TPU v7x, 128 devices: a whole 4x4x4 slice. The times are simulated.
128 devices in a mesh: gx: 8 (over x, core), gy: 16 (over z, y).
Axes of the slice: x: 4, y: 4, z: 4, core: 2. Of those that a mesh axis runs over, the one named last changes fastest.
Arguments:
- parent_fields: float32 [5, 4, 384, 6144], P(None, None, 'gx', 'gy'), may hold values from -6 to 6
- parent_velocity: float32 [2, 4, 384, 6144], P(None, None, 'gx', 'gy'), may hold values from -0.3 to 0.3
- parent_mixing: float32 [4, 384, 6144], P(None, 'gx', 'gy'), may hold values from 0.01 to 0.1
- nest_fields: float32 [5, 4, 384, 6144], P(None, None, 'gx', 'gy'), may hold values from -6 to 6
- nest_velocity: float32 [2, 4, 384, 6144], P(None, None, 'gx', 'gy'), may hold values from -0.3 to 0.3
- nest_mixing: float32 [4, 384, 6144], P(None, 'gx', 'gy'), may hold values from 0.01 to 0.1
- nest_anchor: int32 [2], replicated, may hold values from 1 to 3327, as said below
Outputs:
- parent_result: float32 [5, 4, 384, 6144], P(None, None, 'gx', 'gy')
- nest_result: float32 [5, 4, 384, 6144], P(None, None, 'gx', 'gy')
Inputs may be any that keep to these rules, and one draw needn't show every extreme that they name: `nest_anchor`: the row anchor is 1 to 254; the column anchor is 3073 to 3327, so the nest with a rim of one parent cell lies inside the parent grid.
All inputs are finite; a program needn't handle non-finite values.
Results may differ from a plain program's by a relative error of at most 0.00002.
Values sent between devices are 32-bit elements; how exact they have to be, the bound alone decides.
A program may use at most 192 MiB of HBM per device.

v0:
```python
import jax
import jax.numpy as jnp
from jax import lax
from jax.sharding import PartitionSpec as P

SUBSTEPS = 3


third = 1.0 / 3.0
two_thirds = 2.0 / 3.0
nudge_floor = 0.1
relax_width = 4.0


def extended(cells, sides, width):
    for axis, dim in sides:
        count = lax.axis_size(axis)
        ends = count - 1
        head = lax.slice_in_dim(cells, 0, width, axis=dim)
        tail = lax.slice_in_dim(cells, cells.shape[dim] - width, cells.shape[dim], axis=dim)
        cells = jnp.concatenate(
            [
                lax.ppermute(tail, axis, [(i, (i + 1) % count) for i in range(ends)]),
                cells,
                lax.ppermute(head, axis, [((i + 1) % count, i) for i in range(ends)]),
            ],
            axis=dim,
        )
    return cells


def update(values, padded, velocity, mixing):
    western = padded[:, :, :-2, 1:-1]
    eastern = padded[:, :, 2:, 1:-1]
    southern = padded[:, :, 1:-1, :-2]
    northern = padded[:, :, 1:-1, 2:]
    along_rows = velocity[0]
    along_columns = velocity[1]
    upwind = (
        jnp.maximum(along_rows, 0.0) * (values - western)
        + jnp.minimum(along_rows, 0.0) * (eastern - values)
        + jnp.maximum(along_columns, 0.0) * (values - southern)
        + jnp.minimum(along_columns, 0.0) * (northern - values)
    )
    return values - upwind + mixing * (eastern + western + northern + southern - 4.0 * values)


def refine_rows(block):
    lower = block[:, :, :-2]
    centre = block[:, :, 1:-1]
    upper = block[:, :, 2:]
    stacked = jnp.stack(
        (third * lower + two_thirds * centre, centre, two_thirds * centre + third * upper), axis=3
    )
    extent = centre.shape
    return stacked.reshape(extent[0], extent[1], 3 * extent[2], extent[3])


def refine_columns(block):
    lower = block[:, :, :, :-2]
    centre = block[:, :, :, 1:-1]
    upper = block[:, :, :, 2:]
    stacked = jnp.stack(
        (third * lower + two_thirds * centre, centre, two_thirds * centre + third * upper), axis=4
    )
    extent = centre.shape
    return stacked.reshape(extent[0], extent[1], extent[2], 3 * extent[3])


def block_mean(state):
    extent = state.shape
    grouped = state.reshape(extent[0], extent[1], extent[2] // 3, 3, extent[3] // 3, 3)
    return jnp.sum(grouped, axis=(3, 5)) / 9.0


def relax_weight(row_global, column_global, total_rows, total_columns):
    row_distance = jnp.minimum(row_global, total_rows - 1 - row_global)
    column_distance = jnp.minimum(column_global, total_columns - 1 - column_global)
    distance = jnp.minimum(row_distance[:, None], column_distance[None, :]).astype(jnp.float32)
    return nudge_floor + (1.0 - nudge_floor) * jnp.exp(-distance / relax_width)


def take_rows(values, positions, valid):
    picked = jnp.take(values, jnp.clip(positions, 0, values.shape[2] - 1), axis=2)
    return jnp.where(valid[:, None], picked, 0.0)


def take_columns(values, positions, valid):
    picked = jnp.take(values, jnp.clip(positions, 0, values.shape[3] - 1), axis=3)
    return jnp.where(valid, picked, 0.0)


def within(positions, limit):
    return (positions >= 0) & (positions < limit)


def spans(anchor, count, length):
    offsets = (
        jnp.arange(count, dtype=jnp.int32)[:, None] * length
        + jnp.arange(length + 2, dtype=jnp.int32)[None, :]
    )
    return anchor - 1 + offsets.reshape(-1)


def owner_mask(owners, count):
    return (owners[None, :] == jnp.arange(count, dtype=jnp.int32)[:, None]).reshape(-1)


def spread_rows(values, owners, count):
    tiled = jnp.tile(values, (1, 1, count, 1))
    return jnp.where(owner_mask(owners, count)[:, None], tiled, 0.0)


def spread_columns(values, owners, count):
    tiled = jnp.tile(values, (1, 1, 1, count))
    return jnp.where(owner_mask(owners, count), tiled, 0.0)


def per_device(
    parent_fields,
    parent_velocity,
    parent_mixing,
    nest_fields,
    nest_velocity,
    nest_mixing,
    nest_anchor,
):
    row_rank = lax.axis_index("gx")
    column_rank = lax.axis_index("gy")
    row_devices = lax.axis_size("gx")
    column_devices = lax.axis_size("gy")
    fields_count = parent_fields.shape[0]
    levels_count = parent_fields.shape[1]
    parent_rows = parent_fields.shape[2]
    parent_columns = parent_fields.shape[3]
    nest_rows = nest_fields.shape[2]
    nest_columns = nest_fields.shape[3]
    span_rows = nest_rows // 3
    span_columns = nest_columns // 3
    row_anchor = nest_anchor[0]
    column_anchor = nest_anchor[1]
    parent_padded = extended(parent_fields, (("gx", 2), ("gy", 3)), 1)
    parent_next = update(parent_fields, parent_padded, parent_velocity, parent_mixing)
    row_targets = spans(row_anchor, row_devices, span_rows) - row_rank * parent_rows
    column_targets = (
        spans(column_anchor, column_devices, span_columns) - column_rank * parent_columns
    )
    outgoing = take_columns(parent_next, column_targets, within(column_targets, parent_columns))
    incoming = lax.all_to_all(outgoing, "gy", split_axis=3, concat_axis=3, tiled=True)
    partial_block = incoming.reshape(
        fields_count, levels_count, parent_rows, column_devices, span_columns + 2
    ).sum(axis=3)
    outgoing_rows = take_rows(partial_block, row_targets, within(row_targets, parent_rows))
    incoming_rows = lax.all_to_all(outgoing_rows, "gx", split_axis=2, concat_axis=2, tiled=True)
    relay = incoming_rows.reshape(
        fields_count, levels_count, row_devices, span_rows + 2, span_columns + 2
    ).sum(axis=2)
    forcing = refine_columns(refine_rows(relay))
    row_global = row_rank * nest_rows + jnp.arange(nest_rows, dtype=jnp.int32)
    column_global = column_rank * nest_columns + jnp.arange(nest_columns, dtype=jnp.int32)
    weight = relax_weight(
        row_global, column_global, row_devices * nest_rows, column_devices * nest_columns
    )
    state = nest_fields
    for substep in range(SUBSTEPS):
        nest_padded = extended(state, (("gx", 2), ("gy", 3)), 1)
        moved = update(state, nest_padded, nest_velocity, nest_mixing)
        state = moved + weight * (forcing - moved)
    coarse = block_mean(state)
    own_rows = row_anchor + row_rank * span_rows + jnp.arange(span_rows, dtype=jnp.int32)
    own_columns = (
        column_anchor + column_rank * span_columns + jnp.arange(span_columns, dtype=jnp.int32)
    )
    relative_rows = row_rank * parent_rows + jnp.arange(parent_rows, dtype=jnp.int32) - row_anchor
    relative_columns = (
        column_rank * parent_columns + jnp.arange(parent_columns, dtype=jnp.int32) - column_anchor
    )
    rows_valid = within(relative_rows, row_devices * span_rows)
    columns_valid = within(relative_columns, column_devices * span_columns)
    outgoing = spread_columns(coarse, own_columns // parent_columns, column_devices)
    incoming = lax.all_to_all(outgoing, "gy", split_axis=3, concat_axis=3, tiled=True)
    placed = take_columns(incoming, relative_columns, columns_valid)
    outgoing_rows = spread_rows(placed, own_rows // parent_rows, row_devices)
    incoming_rows = lax.all_to_all(outgoing_rows, "gx", split_axis=2, concat_axis=2, tiled=True)
    fed_back = take_rows(incoming_rows, relative_rows, rows_valid)
    covered = rows_valid[:, None] & columns_valid[None, :]
    parent_result = jnp.where(covered, fed_back, parent_next)
    return (parent_result, state)


def solution(mesh):
    placed = (
        P(None, None, "gx", "gy"),
        P(None, None, "gx", "gy"),
        P(None, "gx", "gy"),
        P(None, None, "gx", "gy"),
        P(None, None, "gx", "gy"),
        P(None, "gx", "gy"),
        P(),
    )
    return jax.shard_map(
        per_device,
        mesh=mesh,
        in_specs=placed,
        out_specs=(P(None, None, "gx", "gy"), P(None, None, "gx", "gy")),
        check_vma=False,
    )
```

profile of v0, /device:TPU:1, one launch (start us, length us, event | category | flops | bytes accessed | tf_op | source)
XLA Modules:
  0.0 732.8 jit_solution(10386896655536340189)
XLA Ops:
  1.9 4.5 collective-permute-start.4
  6.4 1.9 collective-permute-start.5
  8.4 1.4 fusion.86
  10.8 2.1 maximum_bitcast_fusion.1
  14.3 3.2 collective-permute-start.6
  17.7 1.3 collective-permute-start.7
  20.7 1.5 collective-permute-done.7
  23.3 3.4 fusion.34
  26.7 3.1 copy.257
  29.8 32.2 %gather_fusion = f32[2080,5,4,48]{3,2,1,0:T(4,128)} fusion(f32[5,4,48,384]{2,1,3,0:T(4,128)} %copy.257, s32[3072]{0:T(1024)S(1)} %copy-done.19), kind=kCustom, calls=%fused_computation | custom fusion | bytes 15982720 | tf_op jit(solution)/shard_map/jit(_take)/gather | solution.py:89
  62.0 15.2 %fusion.87 = f32[2080,5,4,48]{3,2,1,0:T(4,128)} fusion(f32[2080,5,4,48]{3,2,1,0:T(4,128)} %gather_fusion, pred[2080]{0:T(1024)(128)(4,1)S(1)} %copy-done.21, pred[2080]{0:T(1024)(128)(4,1)S(1)} %copy-done.20), kind=kLoop, calls=%fused_computation.195 | loop fusion | flops 3993600 | bytes 15978560
  77.2 26.0 %reshape.359 = f32[16,1,124800]{2,1,0:T(1,128)} reshape(f32[2080,5,4,48]{3,2,1,0:T(4,128)} %fusion.87) | data formatting | bytes 15974400
  103.2 9.4 %all-to-all-start = ((f32[16,1,124800]{2,1,0:T(1,128)}), f32[16,1,124800]{2,1,0:T(1,128)}, u32[]{:S(2)}, u32[]{:S(2)}) async-start(f32[16,1,124800]{2,1,0:T(1,128)} %reshape.359), calls=%async_computation | async-start | bytes 15974400 | tf_op jit(solution)/shard_map/all_to_all | solution.py:149
  113.7 120.9 %all-to-all-done = f32[16,1,124800]{2,1,0:T(1,128)} async-done(((f32[16,1,124800]{2,1,0:T(1,128)}), f32[16,1,124800]{2,1,0:T(1,128)}, u32[]{:S(2)}, u32[]{:S(2)}) %all-to-all-start) | async-done | bytes 7987232 | tf_op jit(solution)/shard_map/all_to_all | solution.py:149
  235.2 24.6 %reduce.4 = f32[16,124800]{1,0:T(8,128)} reduce(f32[16,1,124800]{2,1,0:T(1,128)} %all-to-all-done, f32[]{:T(128)} %broadcast.601), dimensions={1}, to_apply=%all_to_all.12.reduce_sub_computation | reduce | bytes 15974404 | tf_op jit(solution)/shard_map/all_to_all | solution.py:149
  259.8 28.8 %reshape.360 = f32[2080,5,4,48]{3,2,1,0:T(4,128)} reshape(f32[16,124800]{1,0:T(8,128)} %reduce.4) | data formatting | bytes 15974400
  288.6 11.8 %reduce_sum.27 = f32[5,4,48,130]{2,1,0,3:T(4,128)S(1)} reduce(f32[5,4,48,16,130]{2,1,0,4,3:T(4,128)} %bitcast.60, f32[]{:T(128)} %constant.66.clone.1), dimensions={3}, to_apply=%region_0.1 | reduce | flops 1872000 | bytes 8486404 | tf_op jit(solution)/shard_map/reduce_sum | solution.py:152
  300.5 1.6 copy.258
  302.0 4.3 gather_fusion.1
  306.4 4.1 select_bitcast_fusion.2
  310.5 4.3 all-to-all-start.1
  316.1 3.5 collective-permute-start
  319.7 1.9 collective-permute-start.1
  322.7 24.9 %collective-permute-done = f32[5,4,1,384]{3,1,2,0:T(4,128)S(1)} collective-permute-done((f32[5,4,1,384]{3,1,2,0:T(4,128)S(1)}, f32[5,4,1,384]{3,1,2,0:T(4,128)S(1)}, u32[]{:S(2)}, u32[]{:S(2)}) %collective-permute-start) | collective-permute-done | bytes 30752 | tf_op jit(solution)/shard_map/ppermute | solution.py:23
  347.7 2.0 collective-permute-done.1
  350.8 1.3 copy.243
  357.4 1.5 collective-permute-done.3
  362.3 3.6 copy.262
  365.8 3.5 copy.263
  369.4 3.6 multiply_add_fusion.2
  373.1 3.5 collective-permute-start.8
  376.6 1.9 collective-permute-start.9
  378.6 3.2 collective-permute-done.9
  382.5 1.6 collective-permute-start.10
  384.4 1.3 collective-permute-start.11
  387.5 1.3 collective-permute-done.11
  389.9 5.7 multiply_add_fusion.1
  395.7 3.3 collective-permute-start.12
  399.0 1.9 collective-permute-start.13
  401.5 2.7 collective-permute-done.13
  405.6 1.3 copy.281
  406.9 6.1 collective-permute-start.14
  412.9 1.9 copy.283
  416.8 1.8 copy.282
  419.6 1.8 copy.284
  421.4 4.6 multiply_add_fusion
  426.0 61.8 %reshape.322 = f32[5,4,16,3,128,3]{5,4,3,2,1,0:T(8,128)} reshape(f32[5,4,48,384]{3,2,1,0:T(8,128)} %multiply_add_fusion) | data formatting | bytes 2949120 | tf_op jit(solution)/shard_map/reshape | solution.py:72
  487.7 20.5 %reduce_sum.29 = f32[5,4,16,128]{3,2,1,0:T(8,128)S(1)} reduce(f32[5,4,16,3,128,3]{5,4,3,2,1,0:T(8,128)} %reshape.322, f32[]{:T(128)} %constant.66.clone.1), dimensions={3,5}, to_apply=%region_2.3 | reduce | flops 327680 | bytes 1638404 | tf_op jit(solution)/shard_map/reduce_sum | solution.py:73
  508.7 11.5 %bitcast_select_fusion = f32[5,4,16,2048]{2,1,0,3:T(4,128)} fusion(f32[5,4,16,128]{2,1,0,3:T(4,128)S(1)} %copy.286, pred[2048]{0:T(1024)(128)(4,1)S(1)} %fusion.70), kind=kLoop, calls=%fused_computation.5 | loop fusion | flops 655360 | bytes 2787328 | tf_op jit(solution)/shard_map/jit(_where)/select_n | solution.py:116
  520.2 21.1 %reshape.361 = f32[16,1,40960]{2,1,0:T(1,128)} reshape(f32[2048,5,4,16]{3,2,1,0:T(4,128)} %bitcast.61) | data formatting | bytes 5242880
  541.3 8.1 %all-to-all-start.2 = ((f32[16,1,40960]{2,1,0:T(1,128)}), f32[16,1,40960]{2,1,0:T(1,128)S(1)}, u32[]{:S(2)}, u32[]{:S(2)}) async-start(f32[16,1,40960]{2,1,0:T(1,128)} %reshape.361), calls=%async_computation.2 | async-start | bytes 5242880 | tf_op jit(solution)/shard_map/all_to_all | solution.py:181
  552.3 39.2 %all-to-all-done.2 = f32[16,1,40960]{2,1,0:T(1,128)S(1)} async-done(((f32[16,1,40960]{2,1,0:T(1,128)}), f32[16,1,40960]{2,1,0:T(1,128)S(1)}, u32[]{:S(2)}, u32[]{:S(2)}) %all-to-all-start.2) | async-done | bytes 2621472 | tf_op jit(solution)/shard_map/all_to_all | solution.py:181
  591.5 9.1 %reduce.5 = f32[16,40960]{1,0:T(8,128)} reduce(f32[16,1,40960]{2,1,0:T(1,128)S(1)} %all-to-all-done.2, f32[]{:T(128)} %broadcast.601), dimensions={1}, to_apply=%all_to_all.14.reduce_sub_computation | reduce | bytes 5242884 | tf_op jit(solution)/shard_map/all_to_all | solution.py:181
  600.6 25.4 %reshape.362 = f32[2048,5,4,16]{3,2,1,0:T(4,128)} reshape(f32[16,40960]{1,0:T(8,128)} %reduce.5) | data formatting | bytes 5242880
  626.0 17.1 %copy.287 = f32[5,4,16,2048]{2,1,3,0:T(4,128)} copy(f32[5,4,16,2048]{2,1,0,3:T(4,128)} %bitcast.62) | data formatting | bytes 5242880 | tf_op jit(solution)/shard_map/all_to_all | solution.py:181
  643.1 12.3 %gather_fusion.2 = f32[384,5,4,16]{3,2,1,0:T(4,128)} fusion(f32[5,4,16,2048]{2,1,3,0:T(4,128)} %copy.287, s32[1024]{0:T(1024)S(1)} %pad_clamp_fusion.2), kind=kCustom, calls=%fused_computation.2 | custom fusion | bytes 984576 | tf_op jit(solution)/shard_map/jit(_take)/gather | solution.py:89
  655.4 5.9 select_bitcast_fusion.1
  661.3 3.4 copy.288
  664.7 2.9 bitcast_select_fusion.1
  667.6 5.3 all-to-all-start.3
  676.1 42.9 %all-to-all-done.3 = f32[5,4,128,384]{3,1,0,2:T(4,128)} async-done(((f32[5,4,128,384]{3,1,0,2:T(4,128)}), f32[5,4,128,384]{3,1,0,2:T(4,128)}, u32[]{:S(2)}, u32[]{:S(2)}) %all-to-all-start.3) | async-done | bytes 3932192 | tf_op jit(solution)/shard_map/all_to_all | solution.py:184
  719.0 4.7 copy.289
  723.7 3.9 gather_fusion.3
  727.6 4.6 bitcast_select_fusion.2
  (138 shorter events, 33.0 us)
Async XLA Ops:
  0.6 13.0 %copy-start = (f32[5,4,48,384]{3,2,1,0:T(8,128)S(1)}, f32[5,4,48,384]{3,2,1,0:T(8,128)}, u32[]{:S(2)}) copy-start(f32[5,4,48,384]{3,2,1,0:T(8,128)} %param.7) | copy-start | bytes 4423684
  1.9 11.7 %collective-permute-start.4 = (f32[5,4,1,384]{3,1,2,0:T(4,128)S(1)}, f32[5,4,1,384]{3,1,2,0:T(4,128)S(1)}, u32[]{:S(2)}, u32[]{:S(2)}) collective-permute-start(f32[5,4,1,384]{3,1,2,0:T(4,128)S(1)} %copy.294), channel_id=1, source_target_pairs={{0,16},{16,32},{32,48},{48,64},{64,80},{80,96},{96,112},{1,17},{17... | collective-permute-start | bytes 92168 | tf_op jit(solution)/shard_map/ppermute | solution.py:23
  6.4 7.2 collective-permute-start.5
  13.6 9.7 %copy-start.10 = (f32[5,4,1,384]{3,2,1,0:T(1,128)}, f32[5,4,1,384]{3,2,1,0:T(1,128)S(1)}, u32[]{:S(2)}) copy-start(f32[5,4,1,384]{3,2,1,0:T(1,128)S(1)} %copy.248) | copy-start | bytes 92164
  13.7 0.6 copy-start.12
  14.3 6.1 collective-permute-start.6
  17.7 4.4 collective-permute-start.7
  20.7 6.0 copy-start.5
  26.7 3.1 copy-start.19
  29.8 32.2 %copy-start.20 = (pred[2080]{0:T(1024)(128)(4,1)S(1)}, pred[2080]{0:T(1024)(128)(4,1)}, u32[]{:S(2)}) copy-start(pred[2080]{0:T(1024)(128)(4,1)} %reshape.324) | copy-start | bytes 6244
  29.8 32.2 %copy-start.21 = (pred[2080]{0:T(1024)(128)(4,1)S(1)}, pred[2080]{0:T(1024)(128)(4,1)}, u32[]{:S(2)}) copy-start(pred[2080]{0:T(1024)(128)(4,1)} %compare_and_fusion) | copy-start | bytes 6244
  103.2 131.5 %all-to-all-start = ((f32[16,1,124800]{2,1,0:T(1,128)}), f32[16,1,124800]{2,1,0:T(1,128)}, u32[]{:S(2)}, u32[]{:S(2)}) async-start(f32[16,1,124800]{2,1,0:T(1,128)} %reshape.359), calls=%async_computation | async-start | bytes 15974400 | tf_op jit(solution)/shard_map/all_to_all | solution.py:149
  310.5 11.1 %copy-start.9 = (f32[2,4,48,384]{3,2,1,0:T(8,128)S(1)}, f32[2,4,48,384]{3,2,1,0:T(8,128)}, u32[]{:S(2)}) copy-start(f32[2,4,48,384]{3,2,1,0:T(8,128)} %param.11) | copy-start | bytes 1769476
  310.5 49.5 %all-to-all-start.1 = ((f32[5,4,144,130]{3,1,0,2:T(4,128)}), f32[5,4,144,130]{3,1,0,2:T(4,128)S(1)}, u32[]{:S(2)}, u32[]{:S(2)}) async-start(f32[5,4,144,130]{3,1,0,2:T(4,128)} %select_bitcast_fusion.2), calls=%async_computation.1 | async-start | bytes 5898240 | tf_op jit(solution)/shard_map/all_to_all | solution.py:154
  314.8 34.8 %copy-start.3 = (f32[5,4,48,384]{3,2,1,0:T(8,128)S(1)}, f32[5,4,48,384]{3,2,1,0:T(8,128)}, u32[]{:S(2)}) copy-start(f32[5,4,48,384]{3,2,1,0:T(8,128)} %param.10) | copy-start | bytes 4423684
  316.1 31.5 %collective-permute-start = (f32[5,4,1,384]{3,1,2,0:T(4,128)S(1)}, f32[5,4,1,384]{3,1,2,0:T(4,128)S(1)}, u32[]{:S(2)}, u32[]{:S(2)}) collective-permute-start(f32[5,4,1,384]{3,1,2,0:T(4,128)S(1)} %copy.292), channel_id=1, source_target_pairs={{0,16},{16,32},{32,48},{48,64},{64,80},{80,96},{96,112},{1,17},{17... | collective-permute-start | bytes 92168 | tf_op jit(solution)/shard_map/ppermute | solution.py:23
  319.7 30.0 %collective-permute-start.1 = (f32[5,4,1,384]{3,1,2,0:T(4,128)S(1)}, f32[5,4,1,384]{3,1,2,0:T(4,128)S(1)}, u32[]{:S(2)}, u32[]{:S(2)}) collective-permute-start(f32[5,4,1,384]{3,1,2,0:T(4,128)S(1)} %copy.293), channel_id=1, source_target_pairs={{16,0},{32,16},{48,32},{64,48},{80,64},{96,80},{112,96},{17,1},{33... | collective-permute-start | bytes 92168 | tf_op jit(solution)/shard_map/ppermute | solution.py:25
  347.7 3.1 copy-start.13
  349.7 1.1 copy-start.14
  352.1 4.2 collective-permute-start.2
  354.2 4.6 collective-permute-start.3
  365.8 3.6 copy-start.4
  365.8 3.6 copy-start.7
  365.8 3.6 copy-start.8
  373.0 9.2 %copy-start.2 = (f32[5,4,48,384]{3,2,1,0:T(8,128)}, f32[5,4,48,384]{3,2,1,0:T(8,128)S(1)}, u32[]{:S(2)}) copy-start(f32[5,4,48,384]{3,2,1,0:T(8,128)S(1)} %multiply_add_fusion.2) | copy-start | bytes 4423684
  373.1 5.5 collective-permute-start.8
  376.6 5.2 collective-permute-start.9
  378.6 3.8 copy-start.16
  381.9 0.6 copy-start.18
  382.5 3.9 collective-permute-start.10
  384.4 4.4 collective-permute-start.11
  395.7 5.8 collective-permute-start.12
  399.0 5.2 collective-permute-start.13
  401.5 2.8 copy-start.15
  404.3 1.3 copy-start.17
  406.9 9.9 %collective-permute-start.14 = (f32[5,4,50,1]{2,1,3,0:T(4,128)S(1)}, f32[5,4,50,1]{2,1,3,0:T(4,128)}, u32[]{:S(2)}, u32[]{:S(2)}) collective-permute-start(f32[5,4,50,1]{2,1,3,0:T(4,128)S(1)} %copy.281), channel_id=1, source_target_pairs={{0,1},{1,2},{2,3},{3,4},{4,5},{5,6},{6,7},{7,8},{8,9},{9,10},{10,1... | collective-permute-start | bytes 12008 | tf_op jit(solution)/shard_map/ppermute | solution.py:23
  414.9 4.7 collective-permute-start.15
  541.3 50.2 %all-to-all-start.2 = ((f32[16,1,40960]{2,1,0:T(1,128)}), f32[16,1,40960]{2,1,0:T(1,128)S(1)}, u32[]{:S(2)}, u32[]{:S(2)}) async-start(f32[16,1,40960]{2,1,0:T(1,128)} %reshape.361), calls=%async_computation.2 | async-start | bytes 5242880 | tf_op jit(solution)/shard_map/all_to_all | solution.py:181
  667.6 51.4 %all-to-all-start.3 = ((f32[5,4,128,384]{3,1,0,2:T(4,128)}), f32[5,4,128,384]{3,1,0,2:T(4,128)}, u32[]{:S(2)}, u32[]{:S(2)}) async-start(f32[5,4,128,384]{3,1,0,2:T(4,128)} %bitcast_select_fusion.1), calls=%async_computation.3 | async-start | bytes 7864320 | tf_op jit(solution)/shard_map/all_to_all | solution.py:184
  674.8 0.6 copy-start.22
  723.7 3.9 copy-start.1
  723.7 3.9 copy-start.6
  723.7 3.9 copy-start.11
where the time goes:
time: 743 us; the launch traced here: 733 us
  local copies, waits for them, and re-layouts  276 us (37%)
  waiting for transfers between devices  241 us (32%)
  other arithmetic  144 us (19%)
  starting transfers between devices  67.1 us (9%)
    all_to_all x2, waiting for transfers between devices, per_device(): lax.all_to_all(outgoing, 'gy', split_axis=3, concat_axis=3, tiled=True)  160 us
    unnamed x54, local copies, waits for them, and re-layouts  102 us
    reshape x1, local copies, waits for them, and re-layouts, block_mean(): state.reshape(extent[0], extent[1], extent[2] // 3, 3, extent[3] // 3, 3)  61.8 us
    gather x2, local copies, waits for them, and re-layouts, take_columns(): jnp.take(values, jnp.clip(positions, 0, values.shape[3] - 1), axis=3)  44.5 us
    all_to_all x2, waiting for transfers between devices, per_device(): lax.all_to_all(outgoing_rows, 'gx', split_axis=2, concat_axis=2, tiled=True)  42.9 us
    all_to_all x2, other arithmetic, per_device(): lax.all_to_all(outgoing, 'gy', split_axis=3, concat_axis=3, tiled=True)  33.8 us
    ppermute x8, starting transfers between devices, extended(): lax.ppermute(tail, axis, [(i, (i + 1) % count) for i in range(ends)])  27.1 us
    ppermute x8, waiting for transfers between devices, extended(): lax.ppermute(tail, axis, [(i, (i + 1) % count) for i in range(ends)])  24.9 us
  transfers between devices with their start and end apart: 20, of which 11 were waited for; matrix products, arithmetic and copies ran while one was open for 4% of the time, Pallas kernels for 0%

commit v1 on v0

v1 whole, which is shorter than its diff:
```python
import jax
import jax.numpy as jnp
from jax import lax
from jax.sharding import PartitionSpec as P

SUBSTEPS = 3


third = 1.0 / 3.0
two_thirds = 2.0 / 3.0
nudge_floor = 0.1
relax_width = 4.0


def shift_pairs(count, step):
    return [(i, i + step) for i in range(count) if 0 <= i + step < count]


def neighbours(cells):
    rows = lax.axis_size("gx")
    cols = lax.axis_size("gy")
    western = lax.ppermute(cells[:, :, -1:, :], "gx", shift_pairs(rows, 1))
    eastern = lax.ppermute(cells[:, :, :1, :], "gx", shift_pairs(rows, -1))
    southern = lax.ppermute(cells[:, :, :, -1:], "gy", shift_pairs(cols, 1))
    northern = lax.ppermute(cells[:, :, :, :1], "gy", shift_pairs(cols, -1))
    return western, eastern, southern, northern


def update(values, halo, velocity, mixing):
    west_row, east_row, south_col, north_col = halo
    western = jnp.concatenate([west_row, values[:, :, :-1, :]], axis=2)
    eastern = jnp.concatenate([values[:, :, 1:, :], east_row], axis=2)
    southern = jnp.concatenate([south_col, values[:, :, :, :-1]], axis=3)
    northern = jnp.concatenate([values[:, :, :, 1:], north_col], axis=3)
    along_rows = velocity[0]
    along_columns = velocity[1]
    upwind = (
        jnp.maximum(along_rows, 0.0) * (values - western)
        + jnp.minimum(along_rows, 0.0) * (eastern - values)
        + jnp.maximum(along_columns, 0.0) * (values - southern)
        + jnp.minimum(along_columns, 0.0) * (northern - values)
    )
    return values - upwind + mixing * (eastern + western + northern + southern - 4.0 * values)


def refine_rows(block):
    lower = block[:, :, :-2]
    centre = block[:, :, 1:-1]
    upper = block[:, :, 2:]
    stacked = jnp.stack(
        (third * lower + two_thirds * centre, centre, two_thirds * centre + third * upper), axis=3
    )
    extent = centre.shape
    return stacked.reshape(extent[0], extent[1], 3 * extent[2], extent[3])


def refine_columns(block):
    lower = block[:, :, :, :-2]
    centre = block[:, :, :, 1:-1]
    upper = block[:, :, :, 2:]
    stacked = jnp.stack(
        (third * lower + two_thirds * centre, centre, two_thirds * centre + third * upper), axis=4
    )
    extent = centre.shape
    return stacked.reshape(extent[0], extent[1], extent[2], 3 * extent[3])


def block_mean(state):
    extent = state.shape
    grouped = state.reshape(extent[0], extent[1], extent[2] // 3, 3, extent[3] // 3, 3)
    return jnp.sum(grouped, axis=(3, 5)) / 9.0


def relax_weight(row_global, column_global, total_rows, total_columns):
    row_distance = jnp.minimum(row_global, total_rows - 1 - row_global)
    column_distance = jnp.minimum(column_global, total_columns - 1 - column_global)
    distance = jnp.minimum(row_distance[:, None], column_distance[None, :]).astype(jnp.float32)
    return nudge_floor + (1.0 - nudge_floor) * jnp.exp(-distance / relax_width)


def within(positions, limit):
    return (positions >= 0) & (positions < limit)


def column_pairs(count, base, ratio, k, extra):
    pairs = []
    for m in range(count):
        j = ratio * m + k
        p = base + m + extra
        if j < count and p < count:
            pairs.append((p, j))
    return pairs


def per_device(
    parent_fields,
    parent_velocity,
    parent_mixing,
    nest_fields,
    nest_velocity,
    nest_mixing,
    nest_anchor,
):
    row_rank = lax.axis_index("gx")
    column_rank = lax.axis_index("gy")
    row_devices = lax.axis_size("gx")
    column_devices = lax.axis_size("gy")
    parent_rows = parent_fields.shape[2]
    parent_columns = parent_fields.shape[3]
    nest_rows = nest_fields.shape[2]
    nest_columns = nest_fields.shape[3]
    span_rows = nest_rows // 3
    span_columns = nest_columns // 3
    ratio = parent_columns // span_columns
    base = column_devices // 2
    base_column = base * parent_columns
    relay_rows = span_rows + 2
    relay_columns = span_columns + 2
    row_anchor = nest_anchor[0]
    column_anchor = nest_anchor[1]
    offset = column_anchor - 1 - base_column

    parent_next = update(
        parent_fields, neighbours(parent_fields), parent_velocity, parent_mixing
    )

    margin = parent_columns - span_columns
    wide = jnp.pad(parent_next, ((0, 0), (0, 0), (0, 0), (margin, margin)))
    relay_cols = None
    for k in range(ratio):
        for extra in (0, 1):
            if extra == 1 and k == 0:
                continue
            start = margin + span_columns * k + offset - extra * parent_columns
            piece = lax.dynamic_slice_in_dim(wide, start, relay_columns, axis=3)
            moved = lax.ppermute(
                piece, "gy", column_pairs(column_devices, base, ratio, k, extra)
            )
            relay_cols = moved if relay_cols is None else relay_cols + moved

    padded = jnp.pad(relay_cols, ((0, 0), (0, 0), (relay_rows, relay_rows), (0, 0)))
    slots = []
    for target in range(row_devices):
        first = row_anchor - 1 + span_rows * target - parent_rows * row_rank
        first = jnp.clip(first, -relay_rows, parent_rows) + relay_rows
        slots.append(lax.dynamic_slice_in_dim(padded, first, relay_rows, axis=2))
    stacked = jnp.stack(slots, axis=0)
    relay = lax.psum_scatter(stacked, "gx", scatter_dimension=0, tiled=True)[0]

    forcing = refine_columns(refine_rows(relay))
    row_global = row_rank * nest_rows + jnp.arange(nest_rows, dtype=jnp.int32)
    column_global = column_rank * nest_columns + jnp.arange(nest_columns, dtype=jnp.int32)
    weight = relax_weight(
        row_global, column_global, row_devices * nest_rows, column_devices * nest_columns
    )
    state = nest_fields
    for substep in range(SUBSTEPS):
        moved = update(state, neighbours(state), nest_velocity, nest_mixing)
        state = moved + weight * (forcing - moved)

    coarse = block_mean(state)
    gathered = lax.all_gather(coarse, "gx", axis=2, tiled=True)
    total_span = row_devices * span_rows
    gathered = jnp.pad(gathered, ((0, 0), (0, 0), (parent_rows, parent_rows), (0, 0)))
    first = jnp.clip(parent_rows * row_rank - row_anchor, -parent_rows, total_span)
    strip = lax.dynamic_slice_in_dim(gathered, first + parent_rows, parent_rows, axis=2)

    pieces = []
    for extra in (1, 0):
        for k in range(ratio):
            if extra == 1 and k == 0:
                continue
            pairs = [(j, p) for (p, j) in column_pairs(column_devices, base, ratio, k, extra)]
            pieces.append(lax.ppermute(strip, "gy", pairs))
    joined = jnp.concatenate(pieces, axis=3)
    start = (ratio - 1) * span_columns - 1 - offset
    fed_back = lax.dynamic_slice_in_dim(joined, start, parent_columns, axis=3)

    relative_rows = row_rank * parent_rows + jnp.arange(parent_rows, dtype=jnp.int32) - row_anchor
    relative_columns = (
        column_rank * parent_columns + jnp.arange(parent_columns, dtype=jnp.int32) - column_anchor
    )
    rows_valid = within(relative_rows, total_span)
    columns_valid = within(relative_columns, column_devices * span_columns)
    covered = rows_valid[:, None] & columns_valid[None, :]
    parent_result = jnp.where(covered, fed_back, parent_next)
    return (parent_result, state)


def solution(mesh):
    placed = (
        P(None, None, "gx", "gy"),
        P(None, None, "gx", "gy"),
        P(None, "gx", "gy"),
        P(None, None, "gx", "gy"),
        P(None, None, "gx", "gy"),
        P(None, "gx", "gy"),
        P(),
    )
    return jax.shard_map(
        per_device,
        mesh=mesh,
        in_specs=placed,
        out_specs=(P(None, None, "gx", "gy"), P(None, None, "gx", "gy")),
        check_vma=False,
    )
```

time: 743 us -> 441 us (0.59)
  the two profiles are of different devices: /device:TPU:1 before, /device:TPU:73 now
where the time goes in v1:
time: 441 us; the launch traced here: 440 us
  waiting for transfers between devices  178 us (40%)
  local copies, waits for them, and re-layouts  104 us (24%)
  starting transfers between devices  91.2 us (21%)
  other arithmetic  39.5 us (9%)
  between operations  27 us (6%)
    unnamed x3, waiting for transfers between devices  81.9 us
    reshape x1, local copies, waits for them, and re-layouts, block_mean(): state.reshape(extent[0], extent[1], extent[2] // 3, 3, extent[3] // 3, 3)  60.9 us
    ppermute x5, waiting for transfers between devices, per_device(): pieces.append(lax.ppermute(strip, 'gy', pairs))  46.6 us
    all_gather x1, waiting for transfers between devices, per_device(): gathered = lax.all_gather(coarse, 'gx', axis=2, tiled=True)  32.5 us
    ppermute x4, starting transfers between devices, neighbours(): northern = lax.ppermute(cells[:, :, :, :1], 'gy', shift_pairs(cols, -1))  28 us
    reduce_sum x1, other arithmetic, block_mean(): return jnp.sum(grouped, axis=(3, 5)) / 9.0  20.5 us
    ppermute x4, starting transfers between devices, neighbours(): southern = lax.ppermute(cells[:, :, :, -1:], 'gy', shift_pairs(cols, 1))  17.9 us
    ppermute x4, starting transfers between devices, neighbours(): western = lax.ppermute(cells[:, :, -1:, :], 'gx', shift_pairs(rows, 1))  17.9 us
  transfers between devices with their start and end apart: 28, of which 8 were waited for; matrix products, arithmetic and copies ran while one was open for 10% of the time, Pallas kernels for 0%

profile of v1, /device:TPU:73, one launch (start us, length us, event | category | flops | bytes accessed | tf_op | source)
XLA Modules:
  0.0 439.7 jit_solution(16195591423806882408)
XLA Ops:
  7.2 2.4 fusion.26
  9.6 3.2 collective-permute-start.6
  12.8 2.1 collective-permute-start.7
  15.6 4.2 collective-permute-start.4
  20.4 1.9 collective-permute-start.5
  22.4 1.8 fusion.25
  24.1 2.1 fusion.27
  26.2 1.1 fusion.22
  28.0 0.9 maximum_bitcast_fusion.1
  41.0 1.4 copy.336
  42.4 1.4 copy.337
  45.4 4.0 multiply_add_fusion.3
  49.4 1.4 pad_dynamic-slice_fusion.3
  50.8 2.1 collective-permute-start.10
  53.0 1.4 collective-permute-start.11
  54.3 1.4 collective-permute-start.12
  55.7 1.9 collective-permute-start.8
  57.6 1.4 collective-permute-start.9
  59.0 0.9 maximum_bitcast_fusion.3
  59.9 1.9 fusion.21
  61.8 11.4 %collective-permute-done.10 = f32[5,4,48,130]{3,2,1,0:T(8,128)S(1)} collective-permute-done((f32[5,4,48,130]{3,2,1,0:T(8,128)S(1)}, f32[5,4,48,130]{3,2,1,0:T(8,128)S(1)}, u32[]{:S(2)}, u32[]{:S(2)}) %collective-permute-start.10) | collective-permute-done | bytes 499232 | tf_op jit(solution)/shard_map/ppermute | solution.py:136
  73.2 8.7 %collective-permute-start.2 = (f32[5,4,48,1]{3,2,1,0:T(8,128)}, f32[5,4,48,1]{3,2,1,0:T(8,128)}, u32[]{:S(2)}, u32[]{:S(2)}) collective-permute-start(f32[5,4,48,1]{3,2,1,0:T(8,128)} %get-tuple-element.30), channel_id=1, source_target_pairs={{0,1},{1,2},{2,3},{3,4},{4,5},{5,6},{6,7},{7,8},{8,9},{9,10},{10,1... | collective-permute-start | bytes 11528 | tf_op jit(solution)/shard_map/ppermute | solution.py:24
  81.9 20.6 %collective-permute-start.3 = (f32[5,4,48,1]{3,2,1,0:T(8,128)}, f32[5,4,48,1]{3,2,1,0:T(8,128)}, u32[]{:S(2)}, u32[]{:S(2)}) collective-permute-start(f32[5,4,48,1]{3,2,1,0:T(8,128)} %get-tuple-element.31), channel_id=1, source_target_pairs={{1,0},{2,1},{3,2},{4,3},{5,4},{6,5},{7,6},{8,7},{9,8},{10,9},{11,1... | collective-permute-start | bytes 11528 | tf_op jit(solution)/shard_map/ppermute | solution.py:25
  102.6 5.0 %collective-permute-start = (f32[5,4,1,384]{3,1,2,0:T(4,128)}, f32[5,4,1,384]{3,1,2,0:T(4,128)}, u32[]{:S(2)}, u32[]{:S(2)}) collective-permute-start(f32[5,4,1,384]{3,1,2,0:T(4,128)} %copy.336), channel_id=1, source_target_pairs={{0,16},{16,32},{32,48},{48,64},{64,80},{80,96},{96,112},{1,17},{17... | collective-permute-start | bytes 92168 | tf_op jit(solution)/shard_map/ppermute | solution.py:22
  107.6 1.9 collective-permute-start.1
  110.9 0.9 bitcast_dynamic-update-slice_fusion.7
  111.8 0.9 bitcast_dynamic-update-slice_fusion.6
  112.6 0.9 bitcast_dynamic-update-slice_fusion.5
  113.5 0.9 bitcast_dynamic-update-slice_fusion.4
  114.4 0.9 bitcast_dynamic-update-slice_fusion.3
  115.3 0.9 bitcast_dynamic-update-slice_fusion.2
  116.2 0.9 bitcast_dynamic-update-slice_fusion.1
  117.1 0.9 bitcast_dynamic-update-slice_fusion
  118.3 2.1 fusion.23
  121.8 1.4 copy.299
  123.1 1.4 copy.301
  124.5 81.8 %all-reduce.6.cloned.1.call-done = f32[8,5,4,18,130]{4,2,3,1,0:T(4,128)} async-done(((f32[8,5,4,18,130]{4,2,3,1,0:T(4,128)}), f32[8,5,4,18,130]{4,2,3,1,0:T(4,128)}) %all-reduce.6.cloned.1.call-update) | async-done | bytes 1497616
  206.4 1.7 dynamic-slice_bitcast_fusion
  209.7 3.6 copy.317
  213.3 3.4 copy.318
  216.7 4.1 multiply_add_fusion.2
  221.3 3.1 collective-permute-start.15
  224.5 2.2 collective-permute-start.16
  226.7 3.6 collective-permute-start.13
  230.3 2.8 collective-permute-start.14
  233.7 2.2 collective-permute-done.14
  236.3 1.8 multiply_add_fusion.1
  238.6 2.9 collective-permute-start.19
  241.5 3.1 collective-permute-start.20
  244.6 5.0 %collective-permute-start.17 = (f32[5,4,1,384]{3,1,2,0:T(4,128)S(1)}, f32[5,4,1,384]{3,1,2,0:T(4,128)S(1)}, u32[]{:S(2)}, u32[]{:S(2)}) collective-permute-start(f32[5,4,1,384]{3,1,2,0:T(4,128)S(1)} %copy.324), channel_id=1, source_target_pairs={{0,16},{16,32},{32,48},{48,64},{64,80},{80,96},{96,112},{1,17},{17... | collective-permute-start | bytes 92168 | tf_op jit(solution)/shard_map/ppermute | solution.py:22
  249.6 1.9 collective-permute-start.18
  252.1 3.0 collective-permute-done.18
  255.2 1.8 multiply_add_fusion
  257.0 60.9 %reshape.74 = f32[5,4,16,3,128,3]{5,4,3,2,1,0:T(8,128)} reshape(f32[5,4,48,384]{3,2,1,0:T(8,128)S(1)} %multiply_add_fusion) | data formatting | bytes 2949120 | tf_op jit(solution)/shard_map/reshape | solution.py:70
  317.9 20.5 %reduce_sum.9 = f32[5,4,16,128]{3,2,1,0:T(8,128)S(1)} reduce(f32[5,4,16,3,128,3]{5,4,3,2,1,0:T(8,128)} %reshape.74, f32[]{:T(128)} %constant.93.clone.1), dimensions={3,5}, to_apply=%region_1.2 | reduce | flops 327680 | bytes 1638404 | tf_op jit(solution)/shard_map/reduce_sum | solution.py:71
  339.8 32.5 %all-gather.2.cloned.1.call-done = f32[5,4,128,128]{3,1,0,2:T(4,128)} async-done(((f32[5,4,16,128]{3,1,0,2:T(4,128)}), f32[5,4,128,128]{3,1,0,2:T(4,128)}) %all-gather.2.cloned.1.call-update) | async-done | bytes 1310736 | tf_op jit(solution)/shard_map/all_gather | solution.py:162
  372.6 1.3 collective-permute-start.21
  373.9 1.3 collective-permute-start.22
  375.8 5.3 %collective-permute-start.23 = (f32[5,4,48,128]{3,2,1,0:T(8,128)S(1)}, f32[5,4,48,128]{3,2,1,0:T(8,128)S(1)}, u32[]{:S(2)}, u32[]{:S(2)}) collective-permute-start(f32[5,4,48,128]{3,2,1,0:T(8,128)S(1)} %copy.330), channel_id=1, source_target_pairs={{0,8},{3,9},{6,10},{9,11},{12,12},{15,13},{16,24},{19,25},{22,26},... | collective-permute-start | bytes 1474568 | tf_op jit(solution)/shard_map/ppermute | solution.py:174
  381.7 1.3 collective-permute-start.24
  383.1 1.3 collective-permute-start.25
  384.4 35.7 %collective-permute-done.21 = f32[5,4,48,128]{3,2,1,0:T(8,128)S(1)} collective-permute-done((f32[5,4,48,128]{3,2,1,0:T(8,128)S(1)}, f32[5,4,48,128]{3,2,1,0:T(8,128)S(1)}, u32[]{:S(2)}, u32[]{:S(2)}) %collective-permute-start.21) | collective-permute-done | bytes 491552 | tf_op jit(solution)/shard_map/ppermute | solution.py:174
  420.4 10.8 %collective-permute-done.25 = f32[5,4,48,128]{3,2,1,0:T(8,128)S(1)} collective-permute-done((f32[5,4,48,128]{3,2,1,0:T(8,128)S(1)}, f32[5,4,48,128]{3,2,1,0:T(8,128)S(1)}, u32[]{:S(2)}, u32[]{:S(2)}) %collective-permute-start.25) | collective-permute-done | bytes 491552 | tf_op jit(solution)/shard_map/ppermute | solution.py:174
  431.3 1.6 dynamic-slice_select_fusion
  (97 shorter events, 13.6 us)
Async XLA Ops:
  7.2 7.7 %copy-start = (f32[5,4,48,384]{3,2,1,0:T(8,128)S(1)}, f32[5,4,48,384]{3,2,1,0:T(8,128)}, u32[]{:S(2)}) copy-start(f32[5,4,48,384]{3,2,1,0:T(8,128)} %param.7) | copy-start | bytes 4423684
  7.2 199.2 %all-reduce.6.cloned.1.call-start = ((), (), s32[]{:S(2)}) async-start(), calls=%async_computation.1 | async-start | bytes 5898240
  9.6 35.7 %collective-permute-start.6 = (f32[5,4,48,1]{3,2,1,0:T(8,128)}, f32[5,4,48,1]{3,2,1,0:T(8,128)}, u32[]{:S(2)}, u32[]{:S(2)}) collective-permute-start(f32[5,4,48,1]{3,2,1,0:T(8,128)} %get-tuple-element.43), channel_id=1, source_target_pairs={{0,1},{1,2},{2,3},{3,4},{4,5},{5,6},{6,7},{7,8},{8,9},{9,10},{10,1... | collective-permute-start | bytes 11528 | tf_op jit(solution)/shard_map/ppermute | solution.py:24
  12.8 32.5 %collective-permute-start.7 = (f32[5,4,48,1]{3,2,1,0:T(8,128)}, f32[5,4,48,1]{3,2,1,0:T(8,128)}, u32[]{:S(2)}, u32[]{:S(2)}) collective-permute-start(f32[5,4,48,1]{3,2,1,0:T(8,128)} %get-tuple-element.44), channel_id=1, source_target_pairs={{1,0},{2,1},{3,2},{4,3},{5,4},{6,5},{7,6},{8,7},{9,8},{10,9},{11,1... | collective-permute-start | bytes 11528 | tf_op jit(solution)/shard_map/ppermute | solution.py:25
  15.6 28.2 %collective-permute-start.4 = (f32[5,4,1,384]{3,1,2,0:T(4,128)}, f32[5,4,1,384]{3,1,2,0:T(4,128)}, u32[]{:S(2)}, u32[]{:S(2)}) collective-permute-start(f32[5,4,1,384]{3,1,2,0:T(4,128)} %copy.338), channel_id=1, source_target_pairs={{0,16},{16,32},{32,48},{48,64},{64,80},{80,96},{96,112},{1,17},{17... | collective-permute-start | bytes 92168 | tf_op jit(solution)/shard_map/ppermute | solution.py:22
  20.4 24.1 %collective-permute-start.5 = (f32[5,4,1,384]{3,1,2,0:T(4,128)}, f32[5,4,1,384]{3,1,2,0:T(4,128)}, u32[]{:S(2)}, u32[]{:S(2)}) collective-permute-start(f32[5,4,1,384]{3,1,2,0:T(4,128)} %copy.339), channel_id=1, source_target_pairs={{16,0},{32,16},{48,32},{64,48},{80,64},{96,80},{112,96},{17,1},{33... | collective-permute-start | bytes 92168 | tf_op jit(solution)/shard_map/ppermute | solution.py:23
  24.1 2.1 copy-start.1
  26.2 1.8 copy-start.9
  26.2 2.7 copy-start.11
  49.4 1.4 copy-start.2
  49.4 9.6 %copy-start.10 = (f32[2,4,48,384]{3,2,1,0:T(8,128)S(1)}, f32[2,4,48,384]{3,2,1,0:T(8,128)}, u32[]{:S(2)}) copy-start(f32[2,4,48,384]{3,2,1,0:T(8,128)} %param.11) | copy-start | bytes 1769476
  50.8 22.4 %collective-permute-start.10 = (f32[5,4,48,130]{3,2,1,0:T(8,128)S(1)}, f32[5,4,48,130]{3,2,1,0:T(8,128)S(1)}, u32[]{:S(2)}, u32[]{:S(2)}) collective-permute-start(f32[5,4,48,130]{3,2,1,0:T(8,128)S(1)} %get-tuple-element.35), channel_id=1, source_target_pairs={{9,1},{10,4},{11,7},{12,10},{13,13},{25,17},{26,20},{27,23},{28,26... | collective-permute-start | bytes 1497608 | tf_op jit(solution)/shard_map/ppermute | solution.py:136
  53.0 29.0 %collective-permute-start.11 = (f32[5,4,48,130]{3,2,1,0:T(8,128)S(1)}, f32[5,4,48,130]{3,2,1,0:T(8,128)S(1)}, u32[]{:S(2)}, u32[]{:S(2)}) collective-permute-start(f32[5,4,48,130]{3,2,1,0:T(8,128)S(1)} %get-tuple-element.36), channel_id=1, source_target_pairs={{8,2},{9,5},{10,8},{11,11},{12,14},{24,18},{25,21},{26,24},{27,27}... | collective-permute-start | bytes 1497608 | tf_op jit(solution)/shard_map/ppermute | solution.py:136
  54.3 48.2 %collective-permute-start.12 = (f32[5,4,48,130]{3,2,1,0:T(8,128)S(1)}, f32[5,4,48,130]{3,2,1,0:T(8,128)S(1)}, u32[]{:S(2)}, u32[]{:S(2)}) collective-permute-start(f32[5,4,48,130]{3,2,1,0:T(8,128)S(1)} %get-tuple-element.37), channel_id=1, source_target_pairs={{9,2},{10,5},{11,8},{12,11},{13,14},{25,18},{26,21},{27,24},{28,27... | collective-permute-start | bytes 1497608 | tf_op jit(solution)/shard_map/ppermute | solution.py:136
  55.7 51.9 %collective-permute-start.8 = (f32[5,4,48,130]{3,2,1,0:T(8,128)S(1)}, f32[5,4,48,130]{3,2,1,0:T(8,128)S(1)}, u32[]{:S(2)}, u32[]{:S(2)}) collective-permute-start(f32[5,4,48,130]{3,2,1,0:T(8,128)S(1)} %get-tuple-element.38), channel_id=1, source_target_pairs={{8,0},{9,3},{10,6},{11,9},{12,12},{13,15},{24,16},{25,19},{26,22},... | collective-permute-start | bytes 1497608 | tf_op jit(solution)/shard_map/ppermute | solution.py:136
  57.6 52.0 %collective-permute-start.9 = (f32[5,4,48,130]{3,2,1,0:T(8,128)S(1)}, f32[5,4,48,130]{3,2,1,0:T(8,128)S(1)}, u32[]{:S(2)}, u32[]{:S(2)}) collective-permute-start(f32[5,4,48,130]{3,2,1,0:T(8,128)S(1)} %get-tuple-element.34), channel_id=1, source_target_pairs={{8,1},{9,4},{10,7},{11,10},{12,13},{24,17},{25,20},{26,23},{27,26}... | collective-permute-start | bytes 1497608 | tf_op jit(solution)/shard_map/ppermute | solution.py:136
  73.2 143.5 %collective-permute-start.2 = (f32[5,4,48,1]{3,2,1,0:T(8,128)}, f32[5,4,48,1]{3,2,1,0:T(8,128)}, u32[]{:S(2)}, u32[]{:S(2)}) collective-permute-start(f32[5,4,48,1]{3,2,1,0:T(8,128)} %get-tuple-element.30), channel_id=1, source_target_pairs={{0,1},{1,2},{2,3},{3,4},{4,5},{5,6},{6,7},{7,8},{8,9},{9,10},{10,1... | collective-permute-start | bytes 11528 | tf_op jit(solution)/shard_map/ppermute | solution.py:24
  81.9 134.8 %collective-permute-start.3 = (f32[5,4,48,1]{3,2,1,0:T(8,128)}, f32[5,4,48,1]{3,2,1,0:T(8,128)}, u32[]{:S(2)}, u32[]{:S(2)}) collective-permute-start(f32[5,4,48,1]{3,2,1,0:T(8,128)} %get-tuple-element.31), channel_id=1, source_target_pairs={{1,0},{2,1},{3,2},{4,3},{5,4},{6,5},{7,6},{8,7},{9,8},{10,9},{11,1... | collective-permute-start | bytes 11528 | tf_op jit(solution)/shard_map/ppermute | solution.py:25
  102.6 19.2 %collective-permute-start = (f32[5,4,1,384]{3,1,2,0:T(4,128)}, f32[5,4,1,384]{3,1,2,0:T(4,128)}, u32[]{:S(2)}, u32[]{:S(2)}) collective-permute-start(f32[5,4,1,384]{3,1,2,0:T(4,128)} %copy.336), channel_id=1, source_target_pairs={{0,16},{16,32},{32,48},{48,64},{64,80},{80,96},{96,112},{1,17},{17... | collective-permute-start | bytes 92168 | tf_op jit(solution)/shard_map/ppermute | solution.py:22
  107.6 15.5 %collective-permute-start.1 = (f32[5,4,1,384]{3,1,2,0:T(4,128)}, f32[5,4,1,384]{3,1,2,0:T(4,128)}, u32[]{:S(2)}, u32[]{:S(2)}) collective-permute-start(f32[5,4,1,384]{3,1,2,0:T(4,128)} %copy.337), channel_id=1, source_target_pairs={{16,0},{32,16},{48,32},{64,48},{80,64},{96,80},{112,96},{17,1},{33... | collective-permute-start | bytes 92168 | tf_op jit(solution)/shard_map/ppermute | solution.py:23
  118.0 254.3 %all-gather.2.cloned.1.call-start = ((), (), s32[]{:S(2)}) async-start(), calls=%async_computation | async-start | bytes 1474560 | tf_op jit(solution)/shard_map/all_gather | solution.py:162
  118.3 2.8 copy-start.12
  221.3 14.6 %collective-permute-start.15 = (f32[5,4,48,1]{3,2,1,0:T(8,128)S(1)}, f32[5,4,48,1]{3,2,1,0:T(8,128)S(1)}, u32[]{:S(2)}, u32[]{:S(2)}) collective-permute-start(f32[5,4,48,1]{3,2,1,0:T(8,128)S(1)} %get-tuple-element.22), channel_id=1, source_target_pairs={{0,1},{1,2},{2,3},{3,4},{4,5},{5,6},{6,7},{7,8},{8,9},{9,10},{10,1... | collective-permute-start | bytes 11528 | tf_op jit(solution)/shard_map/ppermute | solution.py:24
  224.5 11.8 %collective-permute-start.16 = (f32[5,4,48,1]{3,2,1,0:T(8,128)S(1)}, f32[5,4,48,1]{3,2,1,0:T(8,128)S(1)}, u32[]{:S(2)}, u32[]{:S(2)}) collective-permute-start(f32[5,4,48,1]{3,2,1,0:T(8,128)S(1)} %get-tuple-element.23), channel_id=1, source_target_pairs={{1,0},{2,1},{3,2},{4,3},{5,4},{6,5},{7,6},{8,7},{9,8},{10,9},{11,1... | collective-permute-start | bytes 11528 | tf_op jit(solution)/shard_map/ppermute | solution.py:25
  226.7 7.0 %collective-permute-start.13 = (f32[5,4,1,384]{3,1,2,0:T(4,128)S(1)}, f32[5,4,1,384]{3,1,2,0:T(4,128)S(1)}, u32[]{:S(2)}, u32[]{:S(2)}) collective-permute-start(f32[5,4,1,384]{3,1,2,0:T(4,128)S(1)} %copy.319), channel_id=1, source_target_pairs={{0,16},{16,32},{32,48},{48,64},{64,80},{80,96},{96,112},{1,17},{17... | collective-permute-start | bytes 92168 | tf_op jit(solution)/shard_map/ppermute | solution.py:22
  230.3 6.0 %copy-start.5 = (f32[4,48,384]{2,1,0:T(8,128)S(1)}, f32[4,48,384]{2,1,0:T(8,128)}, u32[]{:S(2)}) copy-start(f32[4,48,384]{2,1,0:T(8,128)} %get-tuple-element.60) | copy-start | bytes 884740
  230.3 6.0 %copy-start.6 = (f32[4,48,384]{2,1,0:T(8,128)S(1)}, f32[4,48,384]{2,1,0:T(8,128)}, u32[]{:S(2)}) copy-start(f32[4,48,384]{2,1,0:T(8,128)} %get-tuple-element.61) | copy-start | bytes 884740
  230.3 6.0 %copy-start.7 = (f32[4,48,384]{2,1,0:T(8,128)S(1)}, f32[4,48,384]{2,1,0:T(8,128)}, u32[]{:S(2)}) copy-start(f32[4,48,384]{2,1,0:T(8,128)} %param.12) | copy-start | bytes 884740
  230.3 6.0 %copy-start.8 = (f32[48,384]{1,0:T(8,128)S(1)}, f32[48,384]{1,0:T(8,128)}, u32[]{:S(2)}) copy-start(f32[48,384]{1,0:T(8,128)} %multiply_add_fusion.4) | copy-start | bytes 221188
  230.3 5.6 %collective-permute-start.14 = (f32[5,4,1,384]{3,1,2,0:T(4,128)S(1)}, f32[5,4,1,384]{3,1,2,0:T(4,128)S(1)}, u32[]{:S(2)}, u32[]{:S(2)}) collective-permute-start(f32[5,4,1,384]{3,1,2,0:T(4,128)S(1)} %copy.321), channel_id=1, source_target_pairs={{16,0},{32,16},{48,32},{64,48},{80,64},{96,80},{112,96},{17,1},{33... | collective-permute-start | bytes 92168 | tf_op jit(solution)/shard_map/ppermute | solution.py:23
  238.6 16.6 %collective-permute-start.19 = (f32[5,4,48,1]{3,2,1,0:T(8,128)S(1)}, f32[5,4,48,1]{3,2,1,0:T(8,128)S(1)}, u32[]{:S(2)}, u32[]{:S(2)}) collective-permute-start(f32[5,4,48,1]{3,2,1,0:T(8,128)S(1)} %get-tuple-element.14), channel_id=1, source_target_pairs={{0,1},{1,2},{2,3},{3,4},{4,5},{5,6},{6,7},{7,8},{8,9},{9,10},{10,1... | collective-permute-start | bytes 11528 | tf_op jit(solution)/shard_map/ppermute | solution.py:24
  241.5 13.7 %collective-permute-start.20 = (f32[5,4,48,1]{3,2,1,0:T(8,128)S(1)}, f32[5,4,48,1]{3,2,1,0:T(8,128)S(1)}, u32[]{:S(2)}, u32[]{:S(2)}) collective-permute-start(f32[5,4,48,1]{3,2,1,0:T(8,128)S(1)} %get-tuple-element.15), channel_id=1, source_target_pairs={{1,0},{2,1},{3,2},{4,3},{5,4},{6,5},{7,6},{8,7},{9,8},{10,9},{11,1... | collective-permute-start | bytes 11528 | tf_op jit(solution)/shard_map/ppermute | solution.py:25
  244.6 7.5 %collective-permute-start.17 = (f32[5,4,1,384]{3,1,2,0:T(4,128)S(1)}, f32[5,4,1,384]{3,1,2,0:T(4,128)S(1)}, u32[]{:S(2)}, u32[]{:S(2)}) collective-permute-start(f32[5,4,1,384]{3,1,2,0:T(4,128)S(1)} %copy.324), channel_id=1, source_target_pairs={{0,16},{16,32},{32,48},{48,64},{64,80},{80,96},{96,112},{1,17},{17... | collective-permute-start | bytes 92168 | tf_op jit(solution)/shard_map/ppermute | solution.py:22
  249.6 5.5 %collective-permute-start.18 = (f32[5,4,1,384]{3,1,2,0:T(4,128)S(1)}, f32[5,4,1,384]{3,1,2,0:T(4,128)S(1)}, u32[]{:S(2)}, u32[]{:S(2)}) collective-permute-start(f32[5,4,1,384]{3,1,2,0:T(4,128)S(1)} %copy.326), channel_id=1, source_target_pairs={{16,0},{32,16},{48,32},{64,48},{80,64},{96,80},{112,96},{17,1},{33... | collective-permute-start | bytes 92168 | tf_op jit(solution)/shard_map/ppermute | solution.py:23
  257.0 61.0 %copy-start.4 = (f32[5,4,48,384]{3,2,1,0:T(8,128)}, f32[5,4,48,384]{3,2,1,0:T(8,128)S(1)}, u32[]{:S(2)}) copy-start(f32[5,4,48,384]{3,2,1,0:T(8,128)S(1)} %multiply_add_fusion) | copy-start | bytes 4423684
  372.6 47.6 %collective-permute-start.21 = (f32[5,4,48,128]{3,2,1,0:T(8,128)S(1)}, f32[5,4,48,128]{3,2,1,0:T(8,128)S(1)}, u32[]{:S(2)}, u32[]{:S(2)}) collective-permute-start(f32[5,4,48,128]{3,2,1,0:T(8,128)S(1)} %copy.330), channel_id=1, source_target_pairs={{1,9},{4,10},{7,11},{10,12},{13,13},{17,25},{20,26},{23,27},{26,28... | collective-permute-start | bytes 1474568 | tf_op jit(solution)/shard_map/ppermute | solution.py:174
  373.9 46.4 %collective-permute-start.22 = (f32[5,4,48,128]{3,2,1,0:T(8,128)S(1)}, f32[5,4,48,128]{3,2,1,0:T(8,128)S(1)}, u32[]{:S(2)}, u32[]{:S(2)}) collective-permute-start(f32[5,4,48,128]{3,2,1,0:T(8,128)S(1)} %copy.330), channel_id=1, source_target_pairs={{2,9},{5,10},{8,11},{11,12},{14,13},{18,25},{21,26},{24,27},{27,28... | collective-permute-start | bytes 1474568 | tf_op jit(solution)/shard_map/ppermute | solution.py:174
  375.8 44.5 %collective-permute-start.23 = (f32[5,4,48,128]{3,2,1,0:T(8,128)S(1)}, f32[5,4,48,128]{3,2,1,0:T(8,128)S(1)}, u32[]{:S(2)}, u32[]{:S(2)}) collective-permute-start(f32[5,4,48,128]{3,2,1,0:T(8,128)S(1)} %copy.330), channel_id=1, source_target_pairs={{0,8},{3,9},{6,10},{9,11},{12,12},{15,13},{16,24},{19,25},{22,26},... | collective-permute-start | bytes 1474568 | tf_op jit(solution)/shard_map/ppermute | solution.py:174
  381.7 38.6 %collective-permute-start.24 = (f32[5,4,48,128]{3,2,1,0:T(8,128)S(1)}, f32[5,4,48,128]{3,2,1,0:T(8,128)S(1)}, u32[]{:S(2)}, u32[]{:S(2)}) collective-permute-start(f32[5,4,48,128]{3,2,1,0:T(8,128)S(1)} %copy.330), channel_id=1, source_target_pairs={{1,8},{4,9},{7,10},{10,11},{13,12},{17,24},{20,25},{23,26},{26,27}... | collective-permute-start | bytes 1474568 | tf_op jit(solution)/shard_map/ppermute | solution.py:174
  383.1 48.1 %collective-permute-start.25 = (f32[5,4,48,128]{3,2,1,0:T(8,128)S(1)}, f32[5,4,48,128]{3,2,1,0:T(8,128)S(1)}, u32[]{:S(2)}, u32[]{:S(2)}) collective-permute-start(f32[5,4,48,128]{3,2,1,0:T(8,128)S(1)} %copy.330), channel_id=1, source_target_pairs={{2,8},{5,9},{8,10},{11,11},{14,12},{18,24},{21,25},{24,26},{27,27}... | collective-permute-start | bytes 1474568 | tf_op jit(solution)/shard_map/ppermute | solution.py:174
  420.3 11.0 %copy-start.3 = (f32[5,4,48,384]{3,2,1,0:T(8,128)S(1)}, f32[5,4,48,384]{3,2,1,0:T(8,128)}, u32[]{:S(2)}) copy-start(f32[5,4,48,384]{3,2,1,0:T(8,128)} %copy-done.2) | copy-start | bytes 4423684
Sparse Core Ops, SparseCore 0:
  118.2 88.1 all-reduce.5
  339.3 32.9 all-gather.1

commit v2 on v1

--- a/solution.py
+++ b/solution.py
@@ -65,10 +65,17 @@
     return stacked.reshape(extent[0], extent[1], extent[2], 3 * extent[3])
 
 
+def grouping(count):
+    rows = jnp.arange(count, dtype=jnp.int32)[:, None] // 3
+    return (rows == jnp.arange(count // 3, dtype=jnp.int32)[None, :]).astype(jnp.float32)
+
+
 def block_mean(state):
     extent = state.shape
-    grouped = state.reshape(extent[0], extent[1], extent[2] // 3, 3, extent[3] // 3, 3)
-    return jnp.sum(grouped, axis=(3, 5)) / 9.0
+    exact = lax.Precision.HIGHEST
+    across = jnp.einsum("flrc,cb->flrb", state, grouping(extent[3]), precision=exact)
+    down = jnp.einsum("ra,flrb->flab", grouping(extent[2]), across, precision=exact)
+    return down / 9.0
 
 
 def relax_weight(row_global, column_global, total_rows, total_columns):
@@ -145,7 +152,8 @@
         first = jnp.clip(first, -relay_rows, parent_rows) + relay_rows
         slots.append(lax.dynamic_slice_in_dim(padded, first, relay_rows, axis=2))
     stacked = jnp.stack(slots, axis=0)
-    relay = lax.psum_scatter(stacked, "gx", scatter_dimension=0, tiled=True)[0]
+    received = lax.all_to_all(stacked, "gx", split_axis=0, concat_axis=0, tiled=True)
+    relay = jnp.sum(received, axis=0)
 
     forcing = refine_columns(refine_rows(relay))
     row_global = row_rank * nest_rows + jnp.arange(nest_rows, dtype=jnp.int32)

time: 441 us -> 326 us (0.74)
  local copies, waits for them, and re-layouts: 104 us -> 34.8 us
  waiting for transfers between devices: 178 us -> 138 us
  other arithmetic: 39.5 us -> 23.4 us
  starting transfers between devices: 91.2 us -> 99.6 us
    unnamed x3 -> x1, waiting for transfers between devices: 81.9 us -> 0.02 us
    reshape x1 -> x0, local copies, waits for them, and re-layouts: 60.9 us -> none  [block_mean(): state.reshape(extent[0], extent[1], extent[2] // 3, 3, extent[3] // 3, 3)]
    all_to_all x0 -> x1, waiting for transfers between devices: none -> 29.8 us  [per_device(): lax.all_to_all(stacked, 'gx', split_axis=0, concat_axis=0, tiled=True)]
    reduce_sum x1, other arithmetic: 20.5 us -> 2.46 us  [per_device(): relay = jnp.sum(received, axis=0)]
    ppermute x5, waiting for transfers between devices: 11.4 us -> 25.7 us  [per_device(): lax.ppermute(piece, 'gy', column_pairs(column_devices, base, ratio, k, ex...]
    ppermute x4, starting transfers between devices: 28 us -> 39.5 us  [neighbours(): northern = lax.ppermute(cells[:, :, :, :1], 'gy', shift_pairs(cols, -1))]
    ppermute x4, starting transfers between devices: 17.9 us -> 8.97 us  [neighbours(): southern = lax.ppermute(cells[:, :, :, -1:], 'gy', shift_pairs(cols, 1))]
    ppermute x4, waiting for transfers between devices: 0.01 us -> 8.34 us  [neighbours(): southern = lax.ppermute(cells[:, :, :, -1:], 'gy', shift_pairs(cols, 1))]
  transfers between devices with their start and end apart: 28 -> 28, of which waited for: 8 -> 8; matrix products, arithmetic and copies ran while one was open for 10% -> 12% of each run, Pallas kernels for 0% -> 0%
where the time goes in v2:
time: 326 us; the launch traced here: 324 us
  waiting for transfers between devices  138 us (42%)
  starting transfers between devices  99.6 us (31%)
  local copies, waits for them, and re-layouts  34.8 us (11%)
  between operations  26.7 us (8%)
  other arithmetic  23.4 us (7%)
    ppermute x5, waiting for transfers between devices, per_device(): pieces.append(lax.ppermute(strip, 'gy', pairs))  46.6 us
    ppermute x4, starting transfers between devices, neighbours(): northern = lax.ppermute(cells[:, :, :, :1], 'gy', shift_pairs(cols, -1))  39.5 us
    all_to_all x1, waiting for transfers between devices, per_device(): lax.all_to_all(stacked, 'gx', split_axis=0, concat_axis=0, tiled=True)  29.8 us
    ppermute x5, waiting for transfers between devices, per_device(): lax.ppermute(piece, 'gy', column_pairs(column_devices, base, ratio, k, ex...  25.7 us
    all_gather x1, waiting for transfers between devices, per_device(): gathered = lax.all_gather(coarse, 'gx', axis=2, tiled=True)  25.4 us
    ppermute x4, starting transfers between devices, neighbours(): eastern = lax.ppermute(cells[:, :, :1, :], 'gx', shift_pairs(rows, -1))  13.2 us
    ppermute x5, starting transfers between devices, per_device(): lax.ppermute(piece, 'gy', column_pairs(column_devices, base, ratio, k, ex...  12.3 us
    ppermute x4, starting transfers between devices, neighbours(): western = lax.ppermute(cells[:, :, -1:, :], 'gx', shift_pairs(rows, 1))  10.6 us
  transfers between devices with their start and end apart: 28, of which 8 were waited for; matrix products, arithmetic and copies ran while one was open for 12% of the time, Pallas kernels for 0%

profile of v2, /device:TPU:73, one launch (start us, length us, event | category | flops | bytes accessed | tf_op | source)
XLA Modules:
  0.0 324.4 jit_solution(11071260043738988761)
XLA Ops:
  7.2 2.4 fusion.37
  9.6 2.1 collective-permute-start.7
  11.7 3.2 collective-permute-start.6
  15.6 3.1 collective-permute-start.5
  18.7 3.0 collective-permute-start.4
  21.7 1.6 fusion.38
  23.3 1.8 fusion.36
  25.2 0.9 maximum_bitcast_fusion.1
  33.1 3.7 %multiply_add_fusion.3 = f32[5,4,48,384]{3,2,1,0:T(8,128)S(1)} fusion(f32[5,4,48,384]{3,2,1,0:T(8,128)S(1)} %copy-done, f32[5,4,48,1]{3,2,1,0:T(8,128)} %collective-permute-done.7, f32[5,4,48,383]{3,2,1,0:T(8,128)} %get-tuple-element.38, f32[5,4,48,383]{3,2,1,0:T(8,128)S(1)} %get-tuple-element.37, f32[5,4,48,1]{3,2,1,0:T(8,128)} %collective-permute-done.6, ...), kind=kLoop, calls=%fused_computation.35 | loop fusion | flops 8478720 | bytes 10321920 | tf_op jit(solution)/shard_map/add | solution.py:43
  36.8 2.9 pad_dynamic-slice_fusion.3
  39.8 3.3 %collective-permute-start.12 = (f32[5,4,48,130]{3,2,1,0:T(8,128)}, f32[5,4,48,130]{3,2,1,0:T(8,128)}, u32[]{:S(2)}, u32[]{:S(2)}) collective-permute-start(f32[5,4,48,130]{3,2,1,0:T(8,128)} %get-tuple-element.29), channel_id=1, source_target_pairs={{9,2},{10,5},{11,8},{12,11},{13,14},{25,18},{26,21},{27,24},{28,27... | collective-permute-start | bytes 1497608 | tf_op jit(solution)/shard_map/ppermute | solution.py:143
  43.0 2.2 collective-permute-start.11
  45.3 2.2 collective-permute-start.10
  47.5 2.2 collective-permute-start.8
  49.8 2.3 collective-permute-start.9
  57.7 1.2 fusion.33
  58.9 25.7 %collective-permute-done.12 = f32[5,4,48,130]{3,2,1,0:T(8,128)} collective-permute-done((f32[5,4,48,130]{3,2,1,0:T(8,128)}, f32[5,4,48,130]{3,2,1,0:T(8,128)}, u32[]{:S(2)}, u32[]{:S(2)}) %collective-permute-start.12) | collective-permute-done | bytes 499232 | tf_op jit(solution)/shard_map/ppermute | solution.py:143
  84.6 28.6 %collective-permute-start.3 = (f32[5,4,48,1]{3,2,1,0:T(8,128)}, f32[5,4,48,1]{3,2,1,0:T(8,128)}, u32[]{:S(2)}, u32[]{:S(2)}) collective-permute-start(f32[5,4,48,1]{3,2,1,0:T(8,128)} %get-tuple-element.23), channel_id=1, source_target_pairs={{1,0},{2,1},{3,2},{4,3},{5,4},{6,5},{7,6},{8,7},{9,8},{10,9},{11,1... | collective-permute-start | bytes 11528 | tf_op jit(solution)/shard_map/ppermute | solution.py:25
  113.2 1.9 collective-permute-start.2
  115.1 2.7 collective-permute-start.1
  117.9 2.8 collective-permute-start
  120.7 2.8 add_add_fusion
  123.5 0.9 pad_dynamic-slice_fusion.5
  124.4 0.9 bitcast_dynamic-update-slice_fusion.7
  125.3 0.9 bitcast_dynamic-update-slice_fusion.6
  126.2 0.9 bitcast_dynamic-update-slice_fusion.5
  127.1 0.9 bitcast_dynamic-update-slice_fusion.4
  128.0 0.9 bitcast_dynamic-update-slice_fusion.3
  128.9 0.9 bitcast_dynamic-update-slice_fusion.2
  129.8 0.9 bitcast_dynamic-update-slice_fusion.1
  130.7 0.9 bitcast_dynamic-update-slice_fusion
  131.5 4.6 %all-to-all-start = ((f32[8,5,4,18,130]{4,2,3,1,0:T(4,128)}), f32[8,5,4,18,130]{4,2,3,1,0:T(4,128)}, u32[]{:S(2)}, u32[]{:S(2)}) async-start(f32[8,5,4,18,130]{4,2,3,1,0:T(4,128)} %bitcast_dynamic-update-slice_fusion), calls=%async_computation | async-start | bytes 5898240 | tf_op jit(solution)/shard_map/all_to_all | solution.py:155
  137.1 0.9 maximum_bitcast_fusion.3
  138.0 2.1 fusion.34
  140.1 1.9 fusion.32
  142.0 29.8 %all-to-all-done = f32[8,5,4,18,130]{4,2,3,1,0:T(4,128)} async-done(((f32[8,5,4,18,130]{4,2,3,1,0:T(4,128)}), f32[8,5,4,18,130]{4,2,3,1,0:T(4,128)}, u32[]{:S(2)}, u32[]{:S(2)}) %all-to-all-start) | async-done | bytes 1497632 | tf_op jit(solution)/shard_map/all_to_all | solution.py:155
  171.8 2.5 reduce_sum.9
  176.3 3.6 %copy.41 = f32[5,4,48,128,3]{2,1,4,3,0:T(4,128)} copy(f32[5,4,48,128,3]{3,1,2,0,4:T(4,128)S(1)} %pad_maximum_fusion.8) | data formatting | bytes 2949120 | tf_op jit(solution)/shard_map/stack | solution.py:61
  179.9 3.4 %copy.42 = f32[5,4,48,384]{3,2,1,0:T(8,128)S(1)} copy(f32[5,4,48,384]{2,1,3,0:T(4,128)} %bitcast.62) | data formatting | bytes 2949120 | tf_op jit(solution)/shard_map/reshape | solution.py:65
  183.3 4.1 %multiply_add_fusion.2 = f32[5,4,48,384]{3,2,1,0:T(8,128)S(1)} fusion(f32[5,4,48,384]{3,2,1,0:T(8,128)S(1)} %copy.42, f32[5,4,48,384]{3,2,1,0:T(8,128)S(1)} %copy-done.1, f32[5,4,48,1]{3,2,1,0:T(8,128)} %collective-permute-done.3, f32[5,4,48,383]{3,2,1,0:T(8,128)} %get-tuple-element.25, f32[5,4,48,383]{3,2,1,0:T(8,128)} %get-tuple-element.24, ...), kind=kLoop, calls=%fused_computation.34 | loop fusion | flops 9584640 | bytes 11870208 | tf_op jit(solution)/shard_map/add | solution.py:167
  188.2 3.6 %collective-permute-start.16 = (f32[5,4,48,1]{3,2,1,0:T(8,128)S(1)}, f32[5,4,48,1]{3,2,1,0:T(8,128)S(1)}, u32[]{:S(2)}, u32[]{:S(2)}) collective-permute-start(f32[5,4,48,1]{3,2,1,0:T(8,128)S(1)} %get-tuple-element.15), channel_id=1, source_target_pairs={{1,0},{2,1},{3,2},{4,3},{5,4},{6,5},{7,6},{8,7},{9,8},{10,9},{11,1... | collective-permute-start | bytes 11528 | tf_op jit(solution)/shard_map/ppermute | solution.py:25
  191.9 1.9 collective-permute-start.15
  193.8 3.1 collective-permute-start.14
  196.9 2.6 collective-permute-start.13
  199.8 2.2 collective-permute-done.16
  202.0 4.6 %collective-permute-done.15 = f32[5,4,48,1]{3,2,1,0:T(8,128)S(1)} collective-permute-done((f32[5,4,48,1]{3,2,1,0:T(8,128)S(1)}, f32[5,4,48,1]{3,2,1,0:T(8,128)S(1)}, u32[]{:S(2)}, u32[]{:S(2)}) %collective-permute-start.15) | collective-permute-done | bytes 3872 | tf_op jit(solution)/shard_map/ppermute | solution.py:24
  206.7 1.8 multiply_add_fusion.1
  209.2 5.2 %collective-permute-start.20 = (f32[5,4,48,1]{3,2,1,0:T(8,128)S(1)}, f32[5,4,48,1]{3,2,1,0:T(8,128)S(1)}, u32[]{:S(2)}, u32[]{:S(2)}) collective-permute-start(f32[5,4,48,1]{3,2,1,0:T(8,128)S(1)} %get-tuple-element.7), channel_id=1, source_target_pairs={{1,0},{2,1},{3,2},{4,3},{5,4},{6,5},{7,6},{8,7},{9,8},{10,9},{11,1... | collective-permute-start | bytes 11528 | tf_op jit(solution)/shard_map/ppermute | solution.py:25
  214.4 1.9 collective-permute-start.19
  216.3 4.3 %collective-permute-start.18 = (f32[5,4,1,384]{3,2,1,0:T(1,128)S(1)}, f32[5,4,1,384]{3,2,1,0:T(1,128)S(1)}, u32[]{:S(2)}, u32[]{:S(2)}) collective-permute-start(f32[5,4,1,384]{3,2,1,0:T(1,128)S(1)} %get-tuple-element.3), channel_id=1, source_target_pairs={{16,0},{32,16},{48,32},{64,48},{80,64},{96,80},{112,96},{17,1},{33... | collective-permute-start | bytes 92168 | tf_op jit(solution)/shard_map/ppermute | solution.py:23
  220.6 2.1 collective-permute-start.17
  223.0 3.7 %collective-permute-done.19 = f32[5,4,48,1]{3,2,1,0:T(8,128)S(1)} collective-permute-done((f32[5,4,48,1]{3,2,1,0:T(8,128)S(1)}, f32[5,4,48,1]{3,2,1,0:T(8,128)S(1)}, u32[]{:S(2)}, u32[]{:S(2)}) %collective-permute-start.19) | collective-permute-done | bytes 3872 | tf_op jit(solution)/shard_map/ppermute | solution.py:24
  226.7 1.8 multiply_add_fusion
  229.2 1.0 fusion
  230.8 25.4 %all-gather.2.cloned.1.call-done = f32[5,4,128,128]{3,2,1,0:T(8,128)} async-done(((f32[5,4,16,128]{3,2,1,0:T(8,128)}), f32[5,4,128,128]{3,2,1,0:T(8,128)}) %all-gather.2.cloned.1.call-update) | async-done | bytes 1310736 | tf_op jit(solution)/shard_map/all_gather | solution.py:170
  256.3 0.9 pad_dynamic-slice_fusion.13
  257.2 1.3 collective-permute-start.21
  258.5 1.3 collective-permute-start.22
  260.5 5.3 %collective-permute-start.23 = (f32[5,4,48,128]{3,2,1,0:T(8,128)S(1)}, f32[5,4,48,128]{3,2,1,0:T(8,128)S(1)}, u32[]{:S(2)}, u32[]{:S(2)}) collective-permute-start(f32[5,4,48,128]{3,2,1,0:T(8,128)S(1)} %pad_dynamic-slice_fusion.13), channel_id=1, source_target_pairs={{0,8},{3,9},{6,10},{9,11},{12,12},{15,13},{16,24},{19,25},{22,26},... | collective-permute-start | bytes 1474568 | tf_op jit(solution)/shard_map/ppermute | solution.py:182
  266.4 1.3 collective-permute-start.24
  267.8 1.3 collective-permute-start.25
  269.1 35.8 %collective-permute-done.21 = f32[5,4,48,128]{3,2,1,0:T(8,128)S(1)} collective-permute-done((f32[5,4,48,128]{3,2,1,0:T(8,128)S(1)}, f32[5,4,48,128]{3,2,1,0:T(8,128)S(1)}, u32[]{:S(2)}, u32[]{:S(2)}) %collective-permute-start.21) | collective-permute-done | bytes 491552 | tf_op jit(solution)/shard_map/ppermute | solution.py:182
  305.1 10.8 %collective-permute-done.25 = f32[5,4,48,128]{3,2,1,0:T(8,128)S(1)} collective-permute-done((f32[5,4,48,128]{3,2,1,0:T(8,128)S(1)}, f32[5,4,48,128]{3,2,1,0:T(8,128)S(1)}, u32[]{:S(2)}, u32[]{:S(2)}) %collective-permute-start.25) | collective-permute-done | bytes 491552 | tf_op jit(solution)/shard_map/ppermute | solution.py:182
  316.0 1.6 dynamic-slice_select_fusion
  (77 shorter events, 9.3 us)
Async XLA Ops:
  7.2 7.7 %copy-start = (f32[5,4,48,384]{3,2,1,0:T(8,128)S(1)}, f32[5,4,48,384]{3,2,1,0:T(8,128)}, u32[]{:S(2)}) copy-start(f32[5,4,48,384]{3,2,1,0:T(8,128)} %param.7) | copy-start | bytes 4423684
  9.6 23.5 %collective-permute-start.7 = (f32[5,4,48,1]{3,2,1,0:T(8,128)}, f32[5,4,48,1]{3,2,1,0:T(8,128)}, u32[]{:S(2)}, u32[]{:S(2)}) collective-permute-start(f32[5,4,48,1]{3,2,1,0:T(8,128)} %get-tuple-element.36), channel_id=1, source_target_pairs={{1,0},{2,1},{3,2},{4,3},{5,4},{6,5},{7,6},{8,7},{9,8},{10,9},{11,1... | collective-permute-start | bytes 11528 | tf_op jit(solution)/shard_map/ppermute | solution.py:25
  11.7 21.4 %collective-permute-start.6 = (f32[5,4,48,1]{3,2,1,0:T(8,128)}, f32[5,4,48,1]{3,2,1,0:T(8,128)}, u32[]{:S(2)}, u32[]{:S(2)}) collective-permute-start(f32[5,4,48,1]{3,2,1,0:T(8,128)} %get-tuple-element.35), channel_id=1, source_target_pairs={{0,1},{1,2},{2,3},{3,4},{4,5},{5,6},{6,7},{7,8},{8,9},{9,10},{10,1... | collective-permute-start | bytes 11528 | tf_op jit(solution)/shard_map/ppermute | solution.py:24
  15.6 17.5 %collective-permute-start.5 = (f32[5,4,1,384]{3,2,1,0:T(1,128)}, f32[5,4,1,384]{3,2,1,0:T(1,128)}, u32[]{:S(2)}, u32[]{:S(2)}) collective-permute-start(f32[5,4,1,384]{3,2,1,0:T(1,128)} %get-tuple-element.32), channel_id=1, source_target_pairs={{16,0},{32,16},{48,32},{64,48},{80,64},{96,80},{112,96},{17,1},{33... | collective-permute-start | bytes 92168 | tf_op jit(solution)/shard_map/ppermute | solution.py:23
  18.7 14.4 %collective-permute-start.4 = (f32[5,4,1,384]{3,2,1,0:T(1,128)}, f32[5,4,1,384]{3,2,1,0:T(1,128)}, u32[]{:S(2)}, u32[]{:S(2)}) collective-permute-start(f32[5,4,1,384]{3,2,1,0:T(1,128)} %get-tuple-element.31), channel_id=1, source_target_pairs={{0,16},{16,32},{32,48},{48,64},{64,80},{80,96},{96,112},{1,17},{17... | collective-permute-start | bytes 92168 | tf_op jit(solution)/shard_map/ppermute | solution.py:22
  23.3 1.8 copy-start.9
  25.2 0.9 copy-start.11
  36.8 3.0 copy-start.2
  36.8 20.3 %copy-start.1 = (f32[5,4,48,384]{3,2,1,0:T(8,128)S(1)}, f32[5,4,48,384]{3,2,1,0:T(8,128)}, u32[]{:S(2)}) copy-start(f32[5,4,48,384]{3,2,1,0:T(8,128)} %param.10) | copy-start | bytes 4423684
  39.8 44.8 %collective-permute-start.12 = (f32[5,4,48,130]{3,2,1,0:T(8,128)}, f32[5,4,48,130]{3,2,1,0:T(8,128)}, u32[]{:S(2)}, u32[]{:S(2)}) collective-permute-start(f32[5,4,48,130]{3,2,1,0:T(8,128)} %get-tuple-element.29), channel_id=1, source_target_pairs={{9,2},{10,5},{11,8},{12,11},{13,14},{25,18},{26,21},{27,24},{28,27... | collective-permute-start | bytes 1497608 | tf_op jit(solution)/shard_map/ppermute | solution.py:143
  43.0 70.1 %collective-permute-start.11 = (f32[5,4,48,130]{3,2,1,0:T(8,128)}, f32[5,4,48,130]{3,2,1,0:T(8,128)}, u32[]{:S(2)}, u32[]{:S(2)}) collective-permute-start(f32[5,4,48,130]{3,2,1,0:T(8,128)} %get-tuple-element.28), channel_id=1, source_target_pairs={{8,2},{9,5},{10,8},{11,11},{12,14},{24,18},{25,21},{26,24},{27,27}... | collective-permute-start | bytes 1497608 | tf_op jit(solution)/shard_map/ppermute | solution.py:143
  45.3 69.8 %collective-permute-start.10 = (f32[5,4,48,130]{3,2,1,0:T(8,128)}, f32[5,4,48,130]{3,2,1,0:T(8,128)}, u32[]{:S(2)}, u32[]{:S(2)}) collective-permute-start(f32[5,4,48,130]{3,2,1,0:T(8,128)} %get-tuple-element.27), channel_id=1, source_target_pairs={{9,1},{10,4},{11,7},{12,10},{13,13},{25,17},{26,20},{27,23},{28,26... | collective-permute-start | bytes 1497608 | tf_op jit(solution)/shard_map/ppermute | solution.py:143
  47.5 70.3 %collective-permute-start.8 = (f32[5,4,48,130]{3,2,1,0:T(8,128)S(1)}, f32[5,4,48,130]{3,2,1,0:T(8,128)}, u32[]{:S(2)}, u32[]{:S(2)}) collective-permute-start(f32[5,4,48,130]{3,2,1,0:T(8,128)S(1)} %get-tuple-element.30), channel_id=1, source_target_pairs={{8,0},{9,3},{10,6},{11,9},{12,12},{13,15},{24,16},{25,19},{26,22},... | collective-permute-start | bytes 1497608 | tf_op jit(solution)/shard_map/ppermute | solution.py:143
  49.8 71.0 %collective-permute-start.9 = (f32[5,4,48,130]{3,2,1,0:T(8,128)S(1)}, f32[5,4,48,130]{3,2,1,0:T(8,128)}, u32[]{:S(2)}, u32[]{:S(2)}) collective-permute-start(f32[5,4,48,130]{3,2,1,0:T(8,128)S(1)} %get-tuple-element.26), channel_id=1, source_target_pairs={{8,1},{9,4},{10,7},{11,10},{12,13},{24,17},{25,20},{26,23},{27,26}... | collective-permute-start | bytes 1497608 | tf_op jit(solution)/shard_map/ppermute | solution.py:143
  84.6 98.7 %collective-permute-start.3 = (f32[5,4,48,1]{3,2,1,0:T(8,128)}, f32[5,4,48,1]{3,2,1,0:T(8,128)}, u32[]{:S(2)}, u32[]{:S(2)}) collective-permute-start(f32[5,4,48,1]{3,2,1,0:T(8,128)} %get-tuple-element.23), channel_id=1, source_target_pairs={{1,0},{2,1},{3,2},{4,3},{5,4},{6,5},{7,6},{8,7},{9,8},{10,9},{11,1... | collective-permute-start | bytes 11528 | tf_op jit(solution)/shard_map/ppermute | solution.py:25
  113.2 70.1 %collective-permute-start.2 = (f32[5,4,48,1]{3,2,1,0:T(8,128)}, f32[5,4,48,1]{3,2,1,0:T(8,128)}, u32[]{:S(2)}, u32[]{:S(2)}) collective-permute-start(f32[5,4,48,1]{3,2,1,0:T(8,128)} %get-tuple-element.22), channel_id=1, source_target_pairs={{0,1},{1,2},{2,3},{3,4},{4,5},{5,6},{6,7},{7,8},{8,9},{9,10},{10,1... | collective-permute-start | bytes 11528 | tf_op jit(solution)/shard_map/ppermute | solution.py:24
  115.1 68.2 %collective-permute-start.1 = (f32[5,4,1,384]{3,2,1,0:T(1,128)}, f32[5,4,1,384]{3,2,1,0:T(1,128)}, u32[]{:S(2)}, u32[]{:S(2)}) collective-permute-start(f32[5,4,1,384]{3,2,1,0:T(1,128)} %get-tuple-element.19), channel_id=1, source_target_pairs={{16,0},{32,16},{48,32},{64,48},{80,64},{96,80},{112,96},{17,1},{33... | collective-permute-start | bytes 92168 | tf_op jit(solution)/shard_map/ppermute | solution.py:23
  117.9 65.4 %collective-permute-start = (f32[5,4,1,384]{3,2,1,0:T(1,128)}, f32[5,4,1,384]{3,2,1,0:T(1,128)}, u32[]{:S(2)}, u32[]{:S(2)}) collective-permute-start(f32[5,4,1,384]{3,2,1,0:T(1,128)} %get-tuple-element.18), channel_id=1, source_target_pairs={{0,16},{16,32},{32,48},{48,64},{64,80},{80,96},{96,112},{1,17},{17... | collective-permute-start | bytes 92168 | tf_op jit(solution)/shard_map/ppermute | solution.py:22
  131.5 5.5 %copy-start.10 = (f32[2,4,48,384]{3,2,1,0:T(8,128)S(1)}, f32[2,4,48,384]{3,2,1,0:T(8,128)}, u32[]{:S(2)}) copy-start(f32[2,4,48,384]{3,2,1,0:T(8,128)} %param.11) | copy-start | bytes 1769476
  131.5 40.2 %all-to-all-start = ((f32[8,5,4,18,130]{4,2,3,1,0:T(4,128)}), f32[8,5,4,18,130]{4,2,3,1,0:T(4,128)}, u32[]{:S(2)}, u32[]{:S(2)}) async-start(f32[8,5,4,18,130]{4,2,3,1,0:T(4,128)} %bitcast_dynamic-update-slice_fusion), calls=%async_computation | async-start | bytes 5898240 | tf_op jit(solution)/shard_map/all_to_all | solution.py:155
  136.2 120.1 %all-gather.2.cloned.1.call-start = ((), (), s32[]{:S(2)}) async-start(), calls=%async_computation.1 | async-start | bytes 1474560 | tf_op jit(solution)/shard_map/all_gather | solution.py:170
  188.2 13.8 %collective-permute-start.16 = (f32[5,4,48,1]{3,2,1,0:T(8,128)S(1)}, f32[5,4,48,1]{3,2,1,0:T(8,128)S(1)}, u32[]{:S(2)}, u32[]{:S(2)}) collective-permute-start(f32[5,4,48,1]{3,2,1,0:T(8,128)S(1)} %get-tuple-element.15), channel_id=1, source_target_pairs={{1,0},{2,1},{3,2},{4,3},{5,4},{6,5},{7,6},{8,7},{9,8},{10,9},{11,1... | collective-permute-start | bytes 11528 | tf_op jit(solution)/shard_map/ppermute | solution.py:25
  191.9 14.8 %collective-permute-start.15 = (f32[5,4,48,1]{3,2,1,0:T(8,128)S(1)}, f32[5,4,48,1]{3,2,1,0:T(8,128)S(1)}, u32[]{:S(2)}, u32[]{:S(2)}) collective-permute-start(f32[5,4,48,1]{3,2,1,0:T(8,128)S(1)} %get-tuple-element.14), channel_id=1, source_target_pairs={{0,1},{1,2},{2,3},{3,4},{4,5},{5,6},{6,7},{7,8},{8,9},{9,10},{10,1... | collective-permute-start | bytes 11528 | tf_op jit(solution)/shard_map/ppermute | solution.py:24
  193.8 12.8 %collective-permute-start.14 = (f32[5,4,1,384]{3,2,1,0:T(1,128)S(1)}, f32[5,4,1,384]{3,2,1,0:T(1,128)S(1)}, u32[]{:S(2)}, u32[]{:S(2)}) collective-permute-start(f32[5,4,1,384]{3,2,1,0:T(1,128)S(1)} %get-tuple-element.11), channel_id=1, source_target_pairs={{16,0},{32,16},{48,32},{64,48},{80,64},{96,80},{112,96},{17,1},{33... | collective-permute-start | bytes 92168 | tf_op jit(solution)/shard_map/ppermute | solution.py:23
  196.9 9.8 %copy-start.5 = (f32[4,48,384]{2,1,0:T(8,128)S(1)}, f32[4,48,384]{2,1,0:T(8,128)}, u32[]{:S(2)}) copy-start(f32[4,48,384]{2,1,0:T(8,128)} %get-tuple-element.52) | copy-start | bytes 884740
  196.9 9.8 %copy-start.6 = (f32[4,48,384]{2,1,0:T(8,128)S(1)}, f32[4,48,384]{2,1,0:T(8,128)}, u32[]{:S(2)}) copy-start(f32[4,48,384]{2,1,0:T(8,128)} %get-tuple-element.53) | copy-start | bytes 884740
  196.9 9.8 %copy-start.7 = (f32[4,48,384]{2,1,0:T(8,128)S(1)}, f32[4,48,384]{2,1,0:T(8,128)}, u32[]{:S(2)}) copy-start(f32[4,48,384]{2,1,0:T(8,128)} %param.12) | copy-start | bytes 884740
  196.9 9.8 %copy-start.8 = (f32[48,384]{1,0:T(8,128)S(1)}, f32[48,384]{1,0:T(8,128)}, u32[]{:S(2)}) copy-start(f32[48,384]{1,0:T(8,128)} %multiply_add_fusion.4) | copy-start | bytes 221188
  196.9 9.7 %collective-permute-start.13 = (f32[5,4,1,384]{3,2,1,0:T(1,128)S(1)}, f32[5,4,1,384]{3,2,1,0:T(1,128)S(1)}, u32[]{:S(2)}, u32[]{:S(2)}) collective-permute-start(f32[5,4,1,384]{3,2,1,0:T(1,128)S(1)} %get-tuple-element.10), channel_id=1, source_target_pairs={{0,16},{16,32},{32,48},{48,64},{64,80},{80,96},{96,112},{1,17},{17... | collective-permute-start | bytes 92168 | tf_op jit(solution)/shard_map/ppermute | solution.py:22
  209.2 13.7 %collective-permute-start.20 = (f32[5,4,48,1]{3,2,1,0:T(8,128)S(1)}, f32[5,4,48,1]{3,2,1,0:T(8,128)S(1)}, u32[]{:S(2)}, u32[]{:S(2)}) collective-permute-start(f32[5,4,48,1]{3,2,1,0:T(8,128)S(1)} %get-tuple-element.7), channel_id=1, source_target_pairs={{1,0},{2,1},{3,2},{4,3},{5,4},{6,5},{7,6},{8,7},{9,8},{10,9},{11,1... | collective-permute-start | bytes 11528 | tf_op jit(solution)/shard_map/ppermute | solution.py:25
  214.4 12.3 %collective-permute-start.19 = (f32[5,4,48,1]{3,2,1,0:T(8,128)S(1)}, f32[5,4,48,1]{3,2,1,0:T(8,128)S(1)}, u32[]{:S(2)}, u32[]{:S(2)}) collective-permute-start(f32[5,4,48,1]{3,2,1,0:T(8,128)S(1)} %get-tuple-element.6), channel_id=1, source_target_pairs={{0,1},{1,2},{2,3},{3,4},{4,5},{5,6},{6,7},{7,8},{8,9},{9,10},{10,1... | collective-permute-start | bytes 11528 | tf_op jit(solution)/shard_map/ppermute | solution.py:24
  216.3 10.3 %collective-permute-start.18 = (f32[5,4,1,384]{3,2,1,0:T(1,128)S(1)}, f32[5,4,1,384]{3,2,1,0:T(1,128)S(1)}, u32[]{:S(2)}, u32[]{:S(2)}) collective-permute-start(f32[5,4,1,384]{3,2,1,0:T(1,128)S(1)} %get-tuple-element.3), channel_id=1, source_target_pairs={{16,0},{32,16},{48,32},{64,48},{80,64},{96,80},{112,96},{17,1},{33... | collective-permute-start | bytes 92168 | tf_op jit(solution)/shard_map/ppermute | solution.py:23
  220.6 6.1 %collective-permute-start.17 = (f32[5,4,1,384]{3,2,1,0:T(1,128)S(1)}, f32[5,4,1,384]{3,2,1,0:T(1,128)S(1)}, u32[]{:S(2)}, u32[]{:S(2)}) collective-permute-start(f32[5,4,1,384]{3,2,1,0:T(1,128)S(1)} %get-tuple-element.2), channel_id=1, source_target_pairs={{0,16},{16,32},{32,48},{48,64},{64,80},{80,96},{96,112},{1,17},{17... | collective-permute-start | bytes 92168 | tf_op jit(solution)/shard_map/ppermute | solution.py:22
  228.4 28.8 %copy-start.4 = (f32[5,4,48,384]{3,2,1,0:T(8,128)}, f32[5,4,48,384]{3,2,1,0:T(8,128)S(1)}, u32[]{:S(2)}) copy-start(f32[5,4,48,384]{3,2,1,0:T(8,128)S(1)} %multiply_add_fusion) | copy-start | bytes 4423684
  257.2 47.6 %collective-permute-start.21 = (f32[5,4,48,128]{3,2,1,0:T(8,128)S(1)}, f32[5,4,48,128]{3,2,1,0:T(8,128)S(1)}, u32[]{:S(2)}, u32[]{:S(2)}) collective-permute-start(f32[5,4,48,128]{3,2,1,0:T(8,128)S(1)} %pad_dynamic-slice_fusion.13), channel_id=1, source_target_pairs={{1,9},{4,10},{7,11},{10,12},{13,13},{17,25},{20,26},{23,27},{26,28... | collective-permute-start | bytes 1474568 | tf_op jit(solution)/shard_map/ppermute | solution.py:182
  258.5 46.4 %collective-permute-start.22 = (f32[5,4,48,128]{3,2,1,0:T(8,128)S(1)}, f32[5,4,48,128]{3,2,1,0:T(8,128)S(1)}, u32[]{:S(2)}, u32[]{:S(2)}) collective-permute-start(f32[5,4,48,128]{3,2,1,0:T(8,128)S(1)} %pad_dynamic-slice_fusion.13), channel_id=1, source_target_pairs={{2,9},{5,10},{8,11},{11,12},{14,13},{18,25},{21,26},{24,27},{27,28... | collective-permute-start | bytes 1474568 | tf_op jit(solution)/shard_map/ppermute | solution.py:182
  260.5 44.5 %collective-permute-start.23 = (f32[5,4,48,128]{3,2,1,0:T(8,128)S(1)}, f32[5,4,48,128]{3,2,1,0:T(8,128)S(1)}, u32[]{:S(2)}, u32[]{:S(2)}) collective-permute-start(f32[5,4,48,128]{3,2,1,0:T(8,128)S(1)} %pad_dynamic-slice_fusion.13), channel_id=1, source_target_pairs={{0,8},{3,9},{6,10},{9,11},{12,12},{15,13},{16,24},{19,25},{22,26},... | collective-permute-start | bytes 1474568 | tf_op jit(solution)/shard_map/ppermute | solution.py:182
  266.4 38.6 %collective-permute-start.24 = (f32[5,4,48,128]{3,2,1,0:T(8,128)S(1)}, f32[5,4,48,128]{3,2,1,0:T(8,128)S(1)}, u32[]{:S(2)}, u32[]{:S(2)}) collective-permute-start(f32[5,4,48,128]{3,2,1,0:T(8,128)S(1)} %pad_dynamic-slice_fusion.13), channel_id=1, source_target_pairs={{1,8},{4,9},{7,10},{10,11},{13,12},{17,24},{20,25},{23,26},{26,27}... | collective-permute-start | bytes 1474568 | tf_op jit(solution)/shard_map/ppermute | solution.py:182
  267.8 48.1 %collective-permute-start.25 = (f32[5,4,48,128]{3,2,1,0:T(8,128)S(1)}, f32[5,4,48,128]{3,2,1,0:T(8,128)S(1)}, u32[]{:S(2)}, u32[]{:S(2)}) collective-permute-start(f32[5,4,48,128]{3,2,1,0:T(8,128)S(1)} %pad_dynamic-slice_fusion.13), channel_id=1, source_target_pairs={{2,8},{5,9},{8,10},{11,11},{14,12},{18,24},{21,25},{24,26},{27,27}... | collective-permute-start | bytes 1474568 | tf_op jit(solution)/shard_map/ppermute | solution.py:182
  305.0 11.0 %copy-start.3 = (f32[5,4,48,384]{3,2,1,0:T(8,128)S(1)}, f32[5,4,48,384]{3,2,1,0:T(8,128)}, u32[]{:S(2)}) copy-start(f32[5,4,48,384]{3,2,1,0:T(8,128)} %copy-done.2) | copy-start | bytes 4423684
Sparse Core Ops, SparseCore 0:
  230.3 25.9 all-gather.1

commit v3 on v2

--- a/solution.py
+++ b/solution.py
@@ -1,7 +1,11 @@
 import jax
 import jax.numpy as jnp
 from jax import lax
+from jax.experimental import pallas as pl
+from jax.experimental.pallas import tpu as pltpu
 from jax.sharding import PartitionSpec as P
+
+MESH = pl.DeviceIdType.MESH
 
 SUBSTEPS = 3
 
@@ -97,6 +101,84 @@
         if j < count and p < count:
             pairs.append((p, j))
     return pairs
+
+
+def exchange_kernel(axis, patterns, send_ref, recv_ref, send_sems, recv_sems):
+    me = lax.axis_index(axis)
+    barrier = pltpu.get_barrier_semaphore()
+    links = [pair for pairs, _, _ in patterns for pair in pairs]
+    for a, b in links:
+        @pl.when(me == a)
+        def _():
+            pl.semaphore_signal(barrier, 1, device_id={axis: b}, device_id_type=MESH)
+
+        @pl.when(me == b)
+        def _():
+            pl.semaphore_signal(barrier, 1, device_id={axis: a}, device_id_type=MESH)
+
+    peers = {}
+    for a, b in links:
+        peers[a] = peers.get(a, 0) + 1
+        peers[b] = peers.get(b, 0) + 1
+    for device, count in sorted(peers.items()):
+        @pl.when(me == device)
+        def _():
+            pl.semaphore_wait(barrier, count)
+
+    copies = []
+    for number, (pairs, source, slot) in enumerate(patterns):
+        for a, b in pairs:
+            copy = pltpu.make_async_remote_copy(
+                src_ref=send_ref.at[source],
+                dst_ref=recv_ref.at[slot],
+                send_sem=send_sems.at[number],
+                recv_sem=recv_sems.at[slot],
+                device_id={axis: b},
+                device_id_type=MESH,
+            )
+            copies.append((a, b, copy))
+
+            @pl.when(me == a)
+            def _():
+                copy.start()
+
+    for a, b, copy in copies:
+        @pl.when(me == a)
+        def _():
+            copy.wait_send()
+
+        @pl.when(me == b)
+        def _():
+            copy.wait_recv()
+
+
+def exchange(pieces, patterns, slots, axis, identity):
+    me = lax.axis_index(axis)
+    remote = [([(a, b) for a, b in pairs if a != b], source, slot) for pairs, source, slot in patterns]
+    remote = [entry for entry in remote if entry[0]]
+    shape = pieces.shape[1:]
+    received = pl.pallas_call(
+        lambda *refs: exchange_kernel(axis, remote, *refs),
+        out_shape=jax.ShapeDtypeStruct((slots,) + shape, pieces.dtype),
+        in_specs=[pl.BlockSpec(memory_space=pl.ANY)],
+        out_specs=pl.BlockSpec(memory_space=pl.ANY),
+        scratch_shapes=[
+            pltpu.SemaphoreType.DMA((len(remote),)),
+            pltpu.SemaphoreType.DMA((slots,)),
+        ],
+        compiler_params=pltpu.CompilerParams(collective_id=identity, has_side_effects=True),
+    )(pieces)
+    parts = [received[slot] for slot in range(slots)]
+    for pairs, source, slot in patterns:
+        for a, b in pairs:
+            if a == b:
+                parts[slot] = jnp.where(me == a, pieces[source], parts[slot])
+    return parts
+
+
+def flat(block):
+    size = block.size
+    return block.reshape(size // 128, 128) if size % 128 == 0 else block.reshape(-1, block.shape[-1])
 
 
 def per_device(
@@ -133,17 +215,24 @@
 
     margin = parent_columns - span_columns
     wide = jnp.pad(parent_next, ((0, 0), (0, 0), (0, 0), (margin, margin)))
-    relay_cols = None
-    for k in range(ratio):
-        for extra in (0, 1):
+    pieces = []
+    patterns = []
+    for extra in (0, 1):
+        for k in range(ratio):
             if extra == 1 and k == 0:
                 continue
             start = margin + span_columns * k + offset - extra * parent_columns
             piece = lax.dynamic_slice_in_dim(wide, start, relay_columns, axis=3)
-            moved = lax.ppermute(
-                piece, "gy", column_pairs(column_devices, base, ratio, k, extra)
+            patterns.append(
+                (column_pairs(column_devices, base, ratio, k, extra), len(pieces), extra)
             )
-            relay_cols = moved if relay_cols is None else relay_cols + moved
+            pieces.append(flat(piece))
+    within_part, beyond_part = exchange(jnp.stack(pieces), patterns, 2, "gy", 0)
+    piece_shape = parent_next.shape[:3] + (relay_columns,)
+    straddles = column_rank % ratio != 0
+    relay_cols = within_part.reshape(piece_shape) + jnp.where(
+        straddles, beyond_part.reshape(piece_shape), 0.0
+    )
 
     padded = jnp.pad(relay_cols, ((0, 0), (0, 0), (relay_rows, relay_rows), (0, 0)))
     slots = []
@@ -173,14 +262,15 @@
     first = jnp.clip(parent_rows * row_rank - row_anchor, -parent_rows, total_span)
     strip = lax.dynamic_slice_in_dim(gathered, first + parent_rows, parent_rows, axis=2)
 
-    pieces = []
+    patterns = []
     for extra in (1, 0):
         for k in range(ratio):
             if extra == 1 and k == 0:
                 continue
             pairs = [(j, p) for (p, j) in column_pairs(column_devices, base, ratio, k, extra)]
-            pieces.append(lax.ppermute(strip, "gy", pairs))
-    joined = jnp.concatenate(pieces, axis=3)
+            patterns.append((pairs, 0, len(patterns)))
+    parts = exchange(flat(strip)[None], patterns, len(patterns), "gy", 1)
+    joined = jnp.concatenate([part.reshape(strip.shape) for part in parts], axis=3)
     start = (ratio - 1) * span_columns - 1 - offset
     fed_back = lax.dynamic_slice_in_dim(joined, start, parent_columns, axis=3)
 

time: 326 us -> 332 us (1.018)
  Pallas kernels: 0 us -> 84.3 us
  waiting for transfers between devices: 138 us -> 63.1 us
  starting transfers between devices: 99.6 us -> 63.7 us
  local copies, waits for them, and re-layouts: 34.8 us -> 67 us
    pallas_call x0 -> x2, Pallas kernels: none -> 84.3 us  [exchange(): pl.pallas_call(lambda *refs: exchange_kernel(axis, remote, *refs), out_sh...]
    ppermute x10 -> x0, waiting for transfers between devices: 72.3 us -> none  [the longest x5 46.6 us: per_device(): pieces.append(lax.ppermute(strip, 'gy', pairs))]
    ppermute x4, starting transfers between devices: 39.5 us -> 11.7 us  [neighbours(): northern = lax.ppermute(cells[:, :, :, :1], 'gy', shift_pairs(cols, -1))]
    ppermute x10 -> x0, starting transfers between devices: 22.7 us -> none  [the longest x5 12.3 us: per_device(): lax.ppermute(piece, 'gy', column_pairs(column_devices, base, ratio, k, ex...]
    ppermute x4, starting transfers between devices: 8.97 us -> 23.1 us  [neighbours(): southern = lax.ppermute(cells[:, :, :, -1:], 'gy', shift_pairs(cols, 1))]
    another operation x0 -> x6, local copies, waits for them, and re-layouts: none -> 11.5 us  [per_device(): within_part, beyond_part = exchange(jnp.stack(pieces), patterns, 2, 'gy', 0)]
    unnamed x35 -> x43, local copies, waits for them, and re-layouts: 6.43 us -> 14.3 us
    ppermute x4, waiting for transfers between devices: 8.34 us -> 1.77 us  [neighbours(): southern = lax.ppermute(cells[:, :, :, -1:], 'gy', shift_pairs(cols, 1))]
  transfers between devices with their start and end apart: 28 -> 18, of which waited for: 8 -> 6; matrix products, arithmetic and copies ran while one was open for 12% -> 22% of each run, Pallas kernels for 0% -> 9%
where the time goes in v3:
time: 332 us; the launch traced here: 330 us
  Pallas kernels  84.3 us (25%)
  local copies, waits for them, and re-layouts  67 us (20%)
  starting transfers between devices  63.7 us (19%)
  waiting for transfers between devices  63.1 us (19%)
  between operations  26.7 us (8%)
  other arithmetic  23.2 us (7%)
    pallas_call x2, Pallas kernels, exchange(): pl.pallas_call(lambda *refs: exchange_kernel(axis, remote, *refs), out_sh...  84.3 us
    all_to_all x1, waiting for transfers between devices, per_device(): lax.all_to_all(stacked, 'gx', split_axis=0, concat_axis=0, tiled=True)  29.9 us
    all_gather x1, waiting for transfers between devices, per_device(): gathered = lax.all_gather(coarse, 'gx', axis=2, tiled=True)  27.4 us
    ppermute x4, starting transfers between devices, neighbours(): southern = lax.ppermute(cells[:, :, :, -1:], 'gy', shift_pairs(cols, 1))  23.1 us
    unnamed x43, local copies, waits for them, and re-layouts  14.3 us
    ppermute x4, starting transfers between devices, neighbours(): eastern = lax.ppermute(cells[:, :, :1, :], 'gx', shift_pairs(rows, -1))  12.6 us
    ppermute x4, starting transfers between devices, neighbours(): northern = lax.ppermute(cells[:, :, :, :1], 'gy', shift_pairs(cols, -1))  11.7 us
    another operation x6, local copies, waits for them, and re-layouts, per_device(): within_part, beyond_part = exchange(jnp.stack(pieces), patterns, 2, 'gy', 0)  11.5 us
  transfers between devices with their start and end apart: 18, of which 6 were waited for; matrix products, arithmetic and copies ran while one was open for 22% of the time, Pallas kernels for 9%

profile of v3, /device:TPU:73, one launch (start us, length us, event | category | flops | bytes accessed | tf_op | source)
XLA Modules:
  0.0 329.8 jit_solution(1114658294596606784)
XLA Ops:
  7.2 2.4 fusion.38
  9.6 2.1 collective-permute-start.7
  11.7 3.2 collective-permute-start.6
  15.6 3.1 collective-permute-start.5
  18.7 3.0 collective-permute-start.4
  21.7 2.3 fusion.34
  24.1 2.6 collective-permute-start.3
  26.7 2.1 fusion.39
  28.8 1.8 fusion.37
  31.3 0.9 maximum_bitcast_fusion.1
  44.3 2.7 collective-permute-start.2
  47.0 2.5 collective-permute-start.1
  49.5 3.1 collective-permute-start
  52.6 4.0 %multiply_add_fusion.3 = f32[5,4,48,384]{3,2,1,0:T(8,128)S(1)} fusion(f32[5,4,48,384]{3,2,1,0:T(8,128)S(1)} %copy-done, f32[5,4,48,1]{3,2,1,0:T(8,128)} %collective-permute-done.7, f32[5,4,48,383]{3,2,1,0:T(8,128)} %get-tuple-element.43, f32[5,4,48,383]{3,2,1,0:T(8,128)} %get-tuple-element.42, f32[5,4,48,1]{3,2,1,0:T(8,128)} %collective-permute-done.6, ...), kind=kLoop, calls=%fused_computation.35 | loop fusion | flops 8478720 | bytes 10321920 | tf_op jit(solution)/shard_map/add | solution.py:47
  56.7 2.9 pad_dynamic-slice_fusion
  59.6 1.4 stack_reshape.15
  61.1 1.9 constant_dynamic-update-slice_fusion.4
  62.9 2.6 stack_reshape.16
  65.5 2.6 stack_reshape.17
  68.1 1.4 stack_reshape.18
  69.6 2.6 stack_reshape.19
  72.2 1.9 constant_dynamic-update-slice_fusion.3
  74.1 1.9 constant_dynamic-update-slice_fusion.2
  77.6 28.2 %shard_map.86 = f32[2,975,128]{2,1,0:T(8,128)} custom-call(f32[5,975,128]{2,1,0:T(8,128)} %constant_dynamic-update-slice_fusion.refs_0_), custom_call_target="tpu_custom_call" | custom-call | tf_op jit(solution)/shard_map/pallas_call | solution.py:160
  105.8 2.2 fusion.40
  108.0 3.2 squeeze.32
  111.2 3.2 squeeze.31
  114.4 2.0 select_add_fusion
  118.2 0.9 bitcast_dynamic-update-slice_fusion.6
  119.0 0.9 bitcast_dynamic-update-slice_fusion.5
  119.9 0.9 bitcast_dynamic-update-slice_fusion.4
  120.8 0.9 bitcast_dynamic-update-slice_fusion.3
  121.7 0.9 bitcast_dynamic-update-slice_fusion.2
  122.6 0.9 bitcast_dynamic-update-slice_fusion.1
  123.5 0.9 bitcast_dynamic-update-slice_fusion
  124.3 5.2 %all-to-all-start = ((f32[8,5,4,18,130]{4,2,3,1,0:T(4,128)}), f32[8,5,4,18,130]{4,2,3,1,0:T(4,128)}, u32[]{:S(2)}, u32[]{:S(2)}) async-start(f32[8,5,4,18,130]{4,2,3,1,0:T(4,128)} %bitcast_dynamic-update-slice_fusion), calls=%async_computation | async-start | bytes 5898240 | tf_op jit(solution)/shard_map/all_to_all | solution.py:244
  130.3 0.9 maximum_bitcast_fusion.3
  131.2 2.1 fusion.35
  133.3 1.9 fusion.33
  135.2 29.9 %all-to-all-done = f32[8,5,4,18,130]{4,2,3,1,0:T(4,128)} async-done(((f32[8,5,4,18,130]{4,2,3,1,0:T(4,128)}), f32[8,5,4,18,130]{4,2,3,1,0:T(4,128)}, u32[]{:S(2)}, u32[]{:S(2)}) %all-to-all-start) | async-done | bytes 1497632 | tf_op jit(solution)/shard_map/all_to_all | solution.py:244
  165.1 2.5 reduce_sum.9
  169.7 3.6 %copy.41 = f32[5,4,48,128,3]{2,1,4,3,0:T(4,128)} copy(f32[5,4,48,128,3]{3,1,2,0,4:T(4,128)S(1)} %pad_maximum_fusion.8) | data formatting | bytes 2949120 | tf_op jit(solution)/shard_map/stack | solution.py:65
  173.3 3.4 %copy.42 = f32[5,4,48,384]{3,2,1,0:T(8,128)S(1)} copy(f32[5,4,48,384]{2,1,3,0:T(4,128)} %bitcast.78) | data formatting | bytes 2949120 | tf_op jit(solution)/shard_map/reshape | solution.py:69
  176.7 4.1 %multiply_add_fusion.2 = f32[5,4,48,384]{3,2,1,0:T(8,128)S(1)} fusion(f32[5,4,48,384]{3,2,1,0:T(8,128)S(1)} %copy.42, f32[5,4,48,384]{3,2,1,0:T(8,128)S(1)} %copy-done.1, f32[5,4,48,1]{3,2,1,0:T(8,128)} %collective-permute-done.3, f32[5,4,48,383]{3,2,1,0:T(8,128)} %get-tuple-element.30, f32[5,4,48,383]{3,2,1,0:T(8,128)} %get-tuple-element.29, ...), kind=kLoop, calls=%fused_computation.34 | loop fusion | flops 9584640 | bytes 11870208 | tf_op jit(solution)/shard_map/add | solution.py:256
  181.6 5.1 %collective-permute-start.11 = (f32[5,4,48,1]{3,2,1,0:T(8,128)S(1)}, f32[5,4,48,1]{3,2,1,0:T(8,128)S(1)}, u32[]{:S(2)}, u32[]{:S(2)}) collective-permute-start(f32[5,4,48,1]{3,2,1,0:T(8,128)S(1)} %get-tuple-element.20), channel_id=1, source_target_pairs={{1,0},{2,1},{3,2},{4,3},{5,4},{6,5},{7,6},{8,7},{9,8},{10,9},{11,1... | collective-permute-start | bytes 11528 | tf_op jit(solution)/shard_map/ppermute | solution.py:29
  186.7 13.1 %collective-permute-start.10 = (f32[5,4,48,1]{3,2,1,0:T(8,128)S(1)}, f32[5,4,48,1]{3,2,1,0:T(8,128)S(1)}, u32[]{:S(2)}, u32[]{:S(2)}) collective-permute-start(f32[5,4,48,1]{3,2,1,0:T(8,128)S(1)} %get-tuple-element.19), channel_id=1, source_target_pairs={{0,1},{1,2},{2,3},{3,4},{4,5},{5,6},{6,7},{7,8},{8,9},{9,10},{10,1... | collective-permute-start | bytes 11528 | tf_op jit(solution)/shard_map/ppermute | solution.py:28
  199.8 3.1 collective-permute-start.9
  202.9 2.9 collective-permute-start.8
  206.1 2.5 collective-permute-done.11
  209.5 1.8 multiply_add_fusion.1
  212.1 1.9 collective-permute-start.15
  214.0 4.1 %collective-permute-start.14 = (f32[5,4,48,1]{3,2,1,0:T(8,128)S(1)}, f32[5,4,48,1]{3,2,1,0:T(8,128)S(1)}, u32[]{:S(2)}, u32[]{:S(2)}) collective-permute-start(f32[5,4,48,1]{3,2,1,0:T(8,128)S(1)} %get-tuple-element.11), channel_id=1, source_target_pairs={{0,1},{1,2},{2,3},{3,4},{4,5},{5,6},{6,7},{7,8},{8,9},{9,10},{10,1... | collective-permute-start | bytes 11528 | tf_op jit(solution)/shard_map/ppermute | solution.py:28
  218.1 4.0 %collective-permute-start.13 = (f32[5,4,1,384]{3,2,1,0:T(1,128)S(1)}, f32[5,4,1,384]{3,2,1,0:T(1,128)S(1)}, u32[]{:S(2)}, u32[]{:S(2)}) collective-permute-start(f32[5,4,1,384]{3,2,1,0:T(1,128)S(1)} %get-tuple-element.8), channel_id=1, source_target_pairs={{16,0},{32,16},{48,32},{64,48},{80,64},{96,80},{112,96},{17,1},{33... | collective-permute-start | bytes 92168 | tf_op jit(solution)/shard_map/ppermute | solution.py:27
  222.1 2.1 collective-permute-start.12
  224.4 1.5 collective-permute-done.15
  225.9 0.9 collective-permute-done.14
  226.8 1.7 multiply_add_fusion
  229.4 1.0 fusion
  232.4 27.4 %all-gather.2.cloned.1.call-done = f32[5,4,128,128]{3,2,1,0:T(8,128)} async-done(((f32[5,4,16,128]{3,2,1,0:T(8,128)}), f32[5,4,128,128]{3,2,1,0:T(8,128)}) %all-gather.2.cloned.1.call-update) | async-done | bytes 1310736 | tf_op jit(solution)/shard_map/all_gather | solution.py:259
  259.8 1.7 pad_dynamic-slice_fusion.13
  261.6 56.1 %shard_map.87 = f32[5,960,128]{2,1,0:T(8,128)} custom-call(f32[1,960,128]{2,1,0:T(8,128)} %bitcast.85), custom_call_target="tpu_custom_call" | custom-call | tf_op jit(solution)/shard_map/pallas_call | solution.py:160
  317.7 1.9 fusion.23
  320.1 1.2 copy-done.4
  321.3 1.6 dynamic-slice_select_fusion
  (79 shorter events, 13.8 us)
Async XLA Ops:
  7.2 7.7 %copy-start = (f32[5,4,48,384]{3,2,1,0:T(8,128)S(1)}, f32[5,4,48,384]{3,2,1,0:T(8,128)}, u32[]{:S(2)}) copy-start(f32[5,4,48,384]{3,2,1,0:T(8,128)} %param.7) | copy-start | bytes 4423684
  9.6 34.7 %collective-permute-start.7 = (f32[5,4,48,1]{3,2,1,0:T(8,128)}, f32[5,4,48,1]{3,2,1,0:T(8,128)}, u32[]{:S(2)}, u32[]{:S(2)}) collective-permute-start(f32[5,4,48,1]{3,2,1,0:T(8,128)} %get-tuple-element.41), channel_id=1, source_target_pairs={{1,0},{2,1},{3,2},{4,3},{5,4},{6,5},{7,6},{8,7},{9,8},{10,9},{11,1... | collective-permute-start | bytes 11528 | tf_op jit(solution)/shard_map/ppermute | solution.py:29
  11.7 35.3 %collective-permute-start.6 = (f32[5,4,48,1]{3,2,1,0:T(8,128)}, f32[5,4,48,1]{3,2,1,0:T(8,128)}, u32[]{:S(2)}, u32[]{:S(2)}) collective-permute-start(f32[5,4,48,1]{3,2,1,0:T(8,128)} %get-tuple-element.40), channel_id=1, source_target_pairs={{0,1},{1,2},{2,3},{3,4},{4,5},{5,6},{6,7},{7,8},{8,9},{9,10},{10,1... | collective-permute-start | bytes 11528 | tf_op jit(solution)/shard_map/ppermute | solution.py:28
  15.6 33.9 %collective-permute-start.5 = (f32[5,4,1,384]{3,2,1,0:T(1,128)}, f32[5,4,1,384]{3,2,1,0:T(1,128)}, u32[]{:S(2)}, u32[]{:S(2)}) collective-permute-start(f32[5,4,1,384]{3,2,1,0:T(1,128)} %get-tuple-element.37), channel_id=1, source_target_pairs={{16,0},{32,16},{48,32},{64,48},{80,64},{96,80},{112,96},{17,1},{33... | collective-permute-start | bytes 92168 | tf_op jit(solution)/shard_map/ppermute | solution.py:27
  18.7 33.9 %collective-permute-start.4 = (f32[5,4,1,384]{3,2,1,0:T(1,128)}, f32[5,4,1,384]{3,2,1,0:T(1,128)}, u32[]{:S(2)}, u32[]{:S(2)}) collective-permute-start(f32[5,4,1,384]{3,2,1,0:T(1,128)} %get-tuple-element.36), channel_id=1, source_target_pairs={{0,16},{16,32},{32,48},{48,64},{64,80},{80,96},{96,112},{1,17},{17... | collective-permute-start | bytes 92168 | tf_op jit(solution)/shard_map/ppermute | solution.py:26
  24.1 152.6 %collective-permute-start.3 = (f32[5,4,48,1]{3,2,1,0:T(8,128)}, f32[5,4,48,1]{3,2,1,0:T(8,128)}, u32[]{:S(2)}, u32[]{:S(2)}) collective-permute-start(f32[5,4,48,1]{3,2,1,0:T(8,128)} %get-tuple-element.28), channel_id=1, source_target_pairs={{1,0},{2,1},{3,2},{4,3},{5,4},{6,5},{7,6},{8,7},{9,8},{10,9},{11,1... | collective-permute-start | bytes 11528 | tf_op jit(solution)/shard_map/ppermute | solution.py:29
  28.8 1.9 copy-start.1
  28.8 2.6 copy-start.12
  30.6 1.7 copy-start.14
  44.3 132.3 %collective-permute-start.2 = (f32[5,4,48,1]{3,2,1,0:T(8,128)}, f32[5,4,48,1]{3,2,1,0:T(8,128)}, u32[]{:S(2)}, u32[]{:S(2)}) collective-permute-start(f32[5,4,48,1]{3,2,1,0:T(8,128)} %get-tuple-element.27), channel_id=1, source_target_pairs={{0,1},{1,2},{2,3},{3,4},{4,5},{5,6},{6,7},{7,8},{8,9},{9,10},{10,1... | collective-permute-start | bytes 11528 | tf_op jit(solution)/shard_map/ppermute | solution.py:28
  47.0 129.7 %collective-permute-start.1 = (f32[5,4,1,384]{3,2,1,0:T(1,128)}, f32[5,4,1,384]{3,2,1,0:T(1,128)}, u32[]{:S(2)}, u32[]{:S(2)}) collective-permute-start(f32[5,4,1,384]{3,2,1,0:T(1,128)} %get-tuple-element.24), channel_id=1, source_target_pairs={{16,0},{32,16},{48,32},{64,48},{80,64},{96,80},{112,96},{17,1},{33... | collective-permute-start | bytes 92168 | tf_op jit(solution)/shard_map/ppermute | solution.py:27
  49.5 127.2 %collective-permute-start = (f32[5,4,1,384]{3,2,1,0:T(1,128)}, f32[5,4,1,384]{3,2,1,0:T(1,128)}, u32[]{:S(2)}, u32[]{:S(2)}) collective-permute-start(f32[5,4,1,384]{3,2,1,0:T(1,128)} %get-tuple-element.23), channel_id=1, source_target_pairs={{0,16},{16,32},{32,48},{48,64},{64,80},{80,96},{96,112},{1,17},{17... | collective-permute-start | bytes 92168 | tf_op jit(solution)/shard_map/ppermute | solution.py:26
  56.7 3.0 copy-start.3
  72.1 3.8 %copy-start.10 = (f32[1,975,128]{2,1,0:T(8,128)S(1)}, f32[1,975,128]{2,1,0:T(8,128)}, u32[]{:S(2)}) copy-start(f32[1,975,128]{2,1,0:T(8,128)} %stack_reshape.18) | copy-start | bytes 1497604
  72.1 4.6 %copy-start.9 = (f32[1,975,128]{2,1,0:T(8,128)S(1)}, f32[1,975,128]{2,1,0:T(8,128)}, u32[]{:S(2)}) copy-start(f32[1,975,128]{2,1,0:T(8,128)} %stack_reshape.19) | copy-start | bytes 1497604
  124.3 5.9 %copy-start.13 = (f32[2,4,48,384]{3,2,1,0:T(8,128)S(1)}, f32[2,4,48,384]{3,2,1,0:T(8,128)}, u32[]{:S(2)}) copy-start(f32[2,4,48,384]{3,2,1,0:T(8,128)} %param.11) | copy-start | bytes 1769476
  124.3 40.8 %all-to-all-start = ((f32[8,5,4,18,130]{4,2,3,1,0:T(4,128)}), f32[8,5,4,18,130]{4,2,3,1,0:T(4,128)}, u32[]{:S(2)}, u32[]{:S(2)}) async-start(f32[8,5,4,18,130]{4,2,3,1,0:T(4,128)} %bitcast_dynamic-update-slice_fusion), calls=%async_computation | async-start | bytes 5898240 | tf_op jit(solution)/shard_map/all_to_all | solution.py:244
  129.5 130.3 %all-gather.2.cloned.1.call-start = ((), (), s32[]{:S(2)}) async-start(), calls=%async_computation.1 | async-start | bytes 1474560 | tf_op jit(solution)/shard_map/all_gather | solution.py:259
  181.6 27.0 %collective-permute-start.11 = (f32[5,4,48,1]{3,2,1,0:T(8,128)S(1)}, f32[5,4,48,1]{3,2,1,0:T(8,128)S(1)}, u32[]{:S(2)}, u32[]{:S(2)}) collective-permute-start(f32[5,4,48,1]{3,2,1,0:T(8,128)S(1)} %get-tuple-element.20), channel_id=1, source_target_pairs={{1,0},{2,1},{3,2},{4,3},{5,4},{6,5},{7,6},{8,7},{9,8},{10,9},{11,1... | collective-permute-start | bytes 11528 | tf_op jit(solution)/shard_map/ppermute | solution.py:29
  186.7 22.8 %collective-permute-start.10 = (f32[5,4,48,1]{3,2,1,0:T(8,128)S(1)}, f32[5,4,48,1]{3,2,1,0:T(8,128)S(1)}, u32[]{:S(2)}, u32[]{:S(2)}) collective-permute-start(f32[5,4,48,1]{3,2,1,0:T(8,128)S(1)} %get-tuple-element.19), channel_id=1, source_target_pairs={{0,1},{1,2},{2,3},{3,4},{4,5},{5,6},{6,7},{7,8},{8,9},{9,10},{10,1... | collective-permute-start | bytes 11528 | tf_op jit(solution)/shard_map/ppermute | solution.py:28
  199.8 9.6 %collective-permute-start.9 = (f32[5,4,1,384]{3,2,1,0:T(1,128)S(1)}, f32[5,4,1,384]{3,2,1,0:T(1,128)S(1)}, u32[]{:S(2)}, u32[]{:S(2)}) collective-permute-start(f32[5,4,1,384]{3,2,1,0:T(1,128)S(1)} %get-tuple-element.16), channel_id=1, source_target_pairs={{16,0},{32,16},{48,32},{64,48},{80,64},{96,80},{112,96},{17,1},{33... | collective-permute-start | bytes 92168 | tf_op jit(solution)/shard_map/ppermute | solution.py:27
  202.9 6.6 %copy-start.6 = (f32[4,48,384]{2,1,0:T(8,128)S(1)}, f32[4,48,384]{2,1,0:T(8,128)}, u32[]{:S(2)}) copy-start(f32[4,48,384]{2,1,0:T(8,128)} %get-tuple-element.59) | copy-start | bytes 884740
  202.9 6.6 %copy-start.7 = (f32[4,48,384]{2,1,0:T(8,128)S(1)}, f32[4,48,384]{2,1,0:T(8,128)}, u32[]{:S(2)}) copy-start(f32[4,48,384]{2,1,0:T(8,128)} %get-tuple-element.60) | copy-start | bytes 884740
  202.9 6.6 %copy-start.8 = (f32[4,48,384]{2,1,0:T(8,128)S(1)}, f32[4,48,384]{2,1,0:T(8,128)}, u32[]{:S(2)}) copy-start(f32[4,48,384]{2,1,0:T(8,128)} %param.12) | copy-start | bytes 884740
  202.9 6.6 %copy-start.11 = (f32[48,384]{1,0:T(8,128)S(1)}, f32[48,384]{1,0:T(8,128)}, u32[]{:S(2)}) copy-start(f32[48,384]{1,0:T(8,128)} %multiply_add_fusion.4) | copy-start | bytes 221188
  202.9 6.5 %collective-permute-start.8 = (f32[5,4,1,384]{3,2,1,0:T(1,128)S(1)}, f32[5,4,1,384]{3,2,1,0:T(1,128)S(1)}, u32[]{:S(2)}, u32[]{:S(2)}) collective-permute-start(f32[5,4,1,384]{3,2,1,0:T(1,128)S(1)} %get-tuple-element.15), channel_id=1, source_target_pairs={{0,16},{16,32},{32,48},{48,64},{64,80},{80,96},{96,112},{1,17},{17... | collective-permute-start | bytes 92168 | tf_op jit(solution)/shard_map/ppermute | solution.py:26
  212.1 13.9 %collective-permute-start.15 = (f32[5,4,48,1]{3,2,1,0:T(8,128)S(1)}, f32[5,4,48,1]{3,2,1,0:T(8,128)S(1)}, u32[]{:S(2)}, u32[]{:S(2)}) collective-permute-start(f32[5,4,48,1]{3,2,1,0:T(8,128)S(1)} %get-tuple-element.12), channel_id=1, source_target_pairs={{1,0},{2,1},{3,2},{4,3},{5,4},{6,5},{7,6},{8,7},{9,8},{10,9},{11,1... | collective-permute-start | bytes 11528 | tf_op jit(solution)/shard_map/ppermute | solution.py:29
  214.0 12.8 %collective-permute-start.14 = (f32[5,4,48,1]{3,2,1,0:T(8,128)S(1)}, f32[5,4,48,1]{3,2,1,0:T(8,128)S(1)}, u32[]{:S(2)}, u32[]{:S(2)}) collective-permute-start(f32[5,4,48,1]{3,2,1,0:T(8,128)S(1)} %get-tuple-element.11), channel_id=1, source_target_pairs={{0,1},{1,2},{2,3},{3,4},{4,5},{5,6},{6,7},{7,8},{8,9},{9,10},{10,1... | collective-permute-start | bytes 11528 | tf_op jit(solution)/shard_map/ppermute | solution.py:28
  218.1 8.7 %collective-permute-start.13 = (f32[5,4,1,384]{3,2,1,0:T(1,128)S(1)}, f32[5,4,1,384]{3,2,1,0:T(1,128)S(1)}, u32[]{:S(2)}, u32[]{:S(2)}) collective-permute-start(f32[5,4,1,384]{3,2,1,0:T(1,128)S(1)} %get-tuple-element.8), channel_id=1, source_target_pairs={{16,0},{32,16},{48,32},{64,48},{80,64},{96,80},{112,96},{17,1},{33... | collective-permute-start | bytes 92168 | tf_op jit(solution)/shard_map/ppermute | solution.py:27
  222.1 4.8 %collective-permute-start.12 = (f32[5,4,1,384]{3,2,1,0:T(1,128)S(1)}, f32[5,4,1,384]{3,2,1,0:T(1,128)S(1)}, u32[]{:S(2)}, u32[]{:S(2)}) collective-permute-start(f32[5,4,1,384]{3,2,1,0:T(1,128)S(1)} %get-tuple-element.7), channel_id=1, source_target_pairs={{0,16},{16,32},{32,48},{48,64},{64,80},{80,96},{96,112},{1,17},{17... | collective-permute-start | bytes 92168 | tf_op jit(solution)/shard_map/ppermute | solution.py:26
  228.6 33.0 %copy-start.5 = (f32[5,4,48,384]{3,2,1,0:T(8,128)}, f32[5,4,48,384]{3,2,1,0:T(8,128)S(1)}, u32[]{:S(2)}) copy-start(f32[5,4,48,384]{3,2,1,0:T(8,128)S(1)} %multiply_add_fusion) | copy-start | bytes 4423684
  317.7 2.1 copy-start.2
  320.0 1.4 copy-start.4
Sparse Core Ops, SparseCore 0:
  230.5 29.2 all-gather.1

commit v4 on v3

--- a/solution.py
+++ b/solution.py
@@ -20,13 +20,72 @@
     return [(i, i + step) for i in range(count) if 0 <= i + step < count]
 
 
-def neighbours(cells):
+def halo_kernel(rows, cols, *refs):
+    sources, targets, send_sems, recv_sems = refs[:4], refs[4:8], refs[8], refs[9]
+    x = lax.axis_index("gx")
+    y = lax.axis_index("gy")
+    routes = (("gx", x, 1, rows), ("gx", x, -1, rows), ("gy", y, 1, cols), ("gy", y, -1, cols))
+    barrier = pltpu.get_barrier_semaphore()
+    for axis, own, step, count in routes:
+        @pl.when((own + step >= 0) & (own + step < count))
+        def _():
+            pl.semaphore_signal(barrier, 1, device_id={axis: own + step}, device_id_type=MESH)
+
+    peers = (x + rows - 1) // rows + (2 * rows - 2 - x) // rows
+    peers = peers + (y + cols - 1) // cols + (2 * cols - 2 - y) // cols
+    pl.semaphore_wait(barrier, peers)
+    copies = []
+    for number, (axis, own, step, count) in enumerate(routes):
+        copy = pltpu.make_async_remote_copy(
+            src_ref=sources[number],
+            dst_ref=targets[number],
+            send_sem=send_sems.at[number],
+            recv_sem=recv_sems.at[number],
+            device_id={axis: own + step},
+            device_id_type=MESH,
+        )
+        copies.append((own, step, count, copy))
+
+        @pl.when((own + step >= 0) & (own + step < count))
+        def _():
+            copy.start()
+
+    for own, step, count, copy in copies:
+        @pl.when((own + step >= 0) & (own + step < count))
+        def _():
+            copy.wait_send()
+
+        @pl.when((own - step >= 0) & (own - step < count))
+        def _():
+            copy.wait_recv()
+
+
+def neighbours(cells, identity):
     rows = lax.axis_size("gx")
     cols = lax.axis_size("gy")
-    western = lax.ppermute(cells[:, :, -1:, :], "gx", shift_pairs(rows, 1))
-    eastern = lax.ppermute(cells[:, :, :1, :], "gx", shift_pairs(rows, -1))
-    southern = lax.ppermute(cells[:, :, :, -1:], "gy", shift_pairs(cols, 1))
-    northern = lax.ppermute(cells[:, :, :, :1], "gy", shift_pairs(cols, -1))
+    x = lax.axis_index("gx")
+    y = lax.axis_index("gy")
+    fields, levels, height, width = cells.shape
+    planes = fields * levels
+    sources = (
+        cells[:, :, -1, :].reshape(planes, width),
+        cells[:, :, 0, :].reshape(planes, width),
+        cells[:, :, :, -1].reshape(planes, height),
+        cells[:, :, :, 0].reshape(planes, height),
+    )
+    received = pl.pallas_call(
+        lambda *refs: halo_kernel(rows, cols, *refs),
+        out_shape=tuple(jax.ShapeDtypeStruct(part.shape, part.dtype) for part in sources),
+        in_specs=[pl.BlockSpec(memory_space=pltpu.VMEM)] * 4,
+        out_specs=tuple(pl.BlockSpec(memory_space=pltpu.VMEM) for _ in range(4)),
+        scratch_shapes=[pltpu.SemaphoreType.DMA((4,)), pltpu.SemaphoreType.DMA((4,))],
+        compiler_params=pltpu.CompilerParams(collective_id=identity, has_side_effects=True),
+    )(*sources)
+    western, eastern, southern, northern = received
+    western = jnp.where(x > 0, western, 0.0).reshape(fields, levels, 1, width)
+    eastern = jnp.where(x < rows - 1, eastern, 0.0).reshape(fields, levels, 1, width)
+    southern = jnp.where(y > 0, southern, 0.0).reshape(fields, levels, height, 1)
+    northern = jnp.where(y < cols - 1, northern, 0.0).reshape(fields, levels, height, 1)
     return western, eastern, southern, northern
 
 
@@ -210,7 +269,7 @@
     offset = column_anchor - 1 - base_column
 
     parent_next = update(
-        parent_fields, neighbours(parent_fields), parent_velocity, parent_mixing
+        parent_fields, neighbours(parent_fields, 2), parent_velocity, parent_mixing
     )
 
     margin = parent_columns - span_columns
@@ -252,7 +311,7 @@
     )
     state = nest_fields
     for substep in range(SUBSTEPS):
-        moved = update(state, neighbours(state), nest_velocity, nest_mixing)
+        moved = update(state, neighbours(state, 3 + substep), nest_velocity, nest_mixing)
         state = moved + weight * (forcing - moved)
 
     coarse = block_mean(state)

time: 332 us -> 339 us (1.021)
  starting transfers between devices: 63.7 us -> 5.78 us
  Pallas kernels: 84.3 us -> 142 us
  waiting for transfers between devices: 63.1 us -> 25.5 us
  local copies, waits for them, and re-layouts: 67 us -> 96.1 us
  other arithmetic: 23.2 us -> 40 us
    pallas_call x0 -> x4, Pallas kernels: none -> 62.6 us  [neighbours(): pl.pallas_call(lambda *refs: halo_kernel(rows, cols, *refs), out_shape=tu...]
    ppermute x16 -> x0, starting transfers between devices: 58.5 us -> none  [the longest x4 23.1 us: neighbours(): southern = lax.ppermute(cells[:, :, :, -1:], 'gy', shift_pairs(cols, 1))]
    all_to_all x1, waiting for transfers between devices: 29.9 us -> 0.01 us  [per_device(): lax.all_to_all(stacked, 'gx', split_axis=0, concat_axis=0, tiled=True)]
    reshape x0 -> x16, local copies, waits for them, and re-layouts: none -> 12.8 us  [the longest x4 4.12 us: neighbours(): jnp.where(y > 0, southern, 0.0).reshape(fields, levels, height, 1)]
    another operation x0 -> x16, local copies, waits for them, and re-layouts: none -> 12.1 us  [the longest x4 3.36 us: neighbours(): cells[:, :, -1, :].reshape(planes, width)]
    select_n x0 -> x12, other arithmetic: none -> 10.2 us  [the longest x4 3.76 us: neighbours(): jnp.where(x < rows - 1, eastern, 0.0).reshape(fields, levels, 1, width)]
    ppermute x16 -> x0, waiting for transfers between devices: 5.82 us -> none  [the longest x4 4.03 us: neighbours(): northern = lax.ppermute(cells[:, :, :, :1], 'gy', shift_pairs(cols, -1))]
    add x3, other arithmetic: 7.67 us -> 13.1 us  [per_device(): state = moved + weight * (forcing - moved)]
  transfers between devices with their start and end apart: 18 -> 2, of which waited for: 6 -> 1; matrix products, arithmetic and copies ran while one was open for 22% -> 5% of each run, Pallas kernels for 9% -> 10%
where the time goes in v4:
time: 339 us; the launch traced here: 337 us
  Pallas kernels  142 us (42%)
  local copies, waits for them, and re-layouts  96.1 us (28%)
  other arithmetic  40 us (12%)
  between operations  25.7 us (8%)
  waiting for transfers between devices  25.5 us (8%)
  starting transfers between devices  5.78 us (2%)
    pallas_call x2, Pallas kernels, exchange(): pl.pallas_call(lambda *refs: exchange_kernel(axis, remote, *refs), out_sh...  79.2 us
    pallas_call x4, Pallas kernels, neighbours(): pl.pallas_call(lambda *refs: halo_kernel(rows, cols, *refs), out_shape=tu...  62.6 us
    all_gather x1, waiting for transfers between devices, per_device(): gathered = lax.all_gather(coarse, 'gx', axis=2, tiled=True)  25.4 us
    unnamed x35, local copies, waits for them, and re-layouts  14.2 us
    add x3, other arithmetic, per_device(): state = moved + weight * (forcing - moved)  13.1 us
    slice x4, local copies, waits for them, and re-layouts, update(): southern = jnp.concatenate([south_col, values[:, :, :, :-1]], axis=3)  10.1 us
    another operation x6, local copies, waits for them, and re-layouts, per_device(): within_part, beyond_part = exchange(jnp.stack(pieces), patterns, 2, 'gy', 0)  8.58 us
    slice x4, local copies, waits for them, and re-layouts, update(): western = jnp.concatenate([west_row, values[:, :, :-1, :]], axis=2)  7.39 us
  transfers between devices with their start and end apart: 2, of which 1 were waited for; matrix products, arithmetic and copies ran while one was open for 5% of the time, Pallas kernels for 10%

profile of v4, /device:TPU:73, one launch (start us, length us, event | category | flops | bytes accessed | tf_op | source)
XLA Modules:
  0.0 336.6 jit_solution(6855640979234376351)
XLA Ops:
  7.2 1.2 slice_reduce_fusion.12
  8.4 1.7 slice_reduce_fusion.4
  10.1 3.7 %fusion.31 = (f32[5,4,48,383]{3,2,1,0:T(8,128)S(1)}, f32[5,4,48,383]{3,2,1,0:T(8,128)}) fusion(f32[5,4,48,384]{3,2,1,0:T(8,128)} %param.7), kind=kLoop, calls=%fused_computation.151 | loop fusion | bytes 5882880 | tf_op jit(solution)/shard_map/slice | solution.py:96
  13.8 1.8 fusion.30
  23.7 6.5 %shard_map.87 = (f32[20,384]{1,0:T(8,128)}, f32[20,384]{1,0:T(8,128)}, f32[20,48]{1,0:T(8,128)}, f32[20,48]{1,0:T(8,128)}) custom-call(f32[20,384]{1,0:T(8,128)} %reshape_squeeze.58.refs_0_, f32[20,384]{1,0:T(8,128)} %reshape_squeeze.59.refs_1_, f32[20,48]{1,0:T(8,128)} %reshape_squeeze.60.refs_2_, f32[20,48]{1,0:T(8,128)} %reshape_squeeze.61.refs_3_), custom_call_target="tpu_custom_call" | custom-call | tf_op jit(solution)/shard_map/pallas_call | solution.py:76
  31.1 1.0 reshape.199
  33.0 2.1 maximum_bitcast_fusion.1
  40.9 3.6 %multiply_add_fusion.3 = f32[5,4,48,384]{3,2,1,0:T(8,128)S(1)} fusion(f32[5,4,48,384]{3,2,1,0:T(8,128)S(1)} %copy-done, f32[5,4,48,1]{3,2,1,0:T(8,128)S(1)} %reshape.200, f32[5,4,48,383]{3,2,1,0:T(8,128)} %get-tuple-element.75, f32[5,4,48,383]{3,2,1,0:T(8,128)S(1)} %get-tuple-element.74, f32[5,4,48,1]{3,2,1,0:T(8,128)} %reshape.199, ...), kind=kLoop, calls=%fused_computation.35 | loop fusion | flops 8478720 | bytes 10321920 | tf_op jit(solution)/shard_map/add | solution.py:106
  44.5 2.6 pad_dynamic-slice_fusion
  48.6 2.6 stack_reshape.16
  51.1 1.4 stack_reshape.17
  52.5 1.4 stack_reshape.18
  53.9 1.8 stack_reshape.19
  55.7 1.9 constant_dynamic-update-slice_fusion.3
  57.6 1.9 constant_dynamic-update-slice_fusion.2
  61.2 23.1 %shard_map.88 = f32[2,975,128]{2,1,0:T(8,128)} custom-call(f32[5,975,128]{2,1,0:T(8,128)} %constant_dynamic-update-slice_fusion.refs_0_), custom_call_target="tpu_custom_call" | custom-call | tf_op jit(solution)/shard_map/pallas_call | solution.py:219
  84.2 2.0 fusion.32
  86.3 3.2 squeeze.32
  89.4 2.2 squeeze.31
  91.6 2.0 select_add_fusion
  94.5 0.9 bitcast_dynamic-update-slice_fusion.7
  98.0 0.9 bitcast_dynamic-update-slice_fusion.3
  98.9 0.9 bitcast_dynamic-update-slice_fusion.2
  99.8 0.9 bitcast_dynamic-update-slice_fusion.1
  100.7 0.9 bitcast_dynamic-update-slice_fusion
  101.6 5.8 %all-to-all-start = ((f32[8,5,4,18,130]{4,2,3,1,0:T(4,128)}), f32[8,5,4,18,130]{4,2,3,1,0:T(4,128)}, u32[]{:S(2)}, u32[]{:S(2)}) async-start(f32[8,5,4,18,130]{4,2,3,1,0:T(4,128)} %bitcast_dynamic-update-slice_fusion), calls=%async_computation | async-start | bytes 5898240 | tf_op jit(solution)/shard_map/all_to_all | solution.py:303
  110.5 32.5 %shard_map.86 = (f32[20,384]{1,0:T(8,128)}, f32[20,384]{1,0:T(8,128)}, f32[20,48]{1,0:T(8,128)}, f32[20,48]{1,0:T(8,128)}) custom-call(f32[20,384]{1,0:T(8,128)} %reshape_squeeze.54.refs_0_, f32[20,384]{1,0:T(8,128)} %reshape_squeeze.55.refs_1_, f32[20,48]{1,0:T(8,128)} %reshape_squeeze.56.refs_2_, f32[20,48]{1,0:T(8,128)} %reshape_squeeze.57.refs_3_), custom_call_target="tpu_custom_call" | custom-call | tf_op jit(solution)/shard_map/pallas_call | solution.py:76
  145.1 1.0 reshape.196
  146.1 1.0 reshape.195
  149.2 0.9 maximum_bitcast_fusion.3
  150.1 2.1 fusion.29
  152.2 1.9 fusion.28
  154.1 2.5 reduce_sum.9
  158.6 3.5 %copy.97 = f32[5,4,48,128,3]{2,1,4,3,0:T(4,128)} copy(f32[5,4,48,128,3]{3,1,2,0,4:T(4,128)S(1)} %pad_maximum_fusion.8) | data formatting | bytes 2949120 | tf_op jit(solution)/shard_map/stack | solution.py:124
  162.2 4.5 %copy.98 = f32[5,4,48,384]{3,2,1,0:T(8,128)} copy(f32[5,4,48,384]{2,1,3,0:T(4,128)} %bitcast.78) | data formatting | bytes 2949120 | tf_op jit(solution)/shard_map/reshape | solution.py:128
  166.7 4.5 %multiply_add_fusion.2 = f32[5,4,48,384]{3,2,1,0:T(8,128)S(1)} fusion(f32[5,4,48,384]{3,2,1,0:T(8,128)} %copy.98, f32[5,4,48,384]{3,2,1,0:T(8,128)S(1)} %copy-done.1, f32[5,4,48,1]{3,2,1,0:T(8,128)} %reshape.196, f32[5,4,48,383]{3,2,1,0:T(8,128)} %get-tuple-element.66, f32[5,4,48,383]{3,2,1,0:T(8,128)} %get-tuple-element.65, f32[5,4,48,1]{3,2,1,0:T(8,128)} %reshape.195, ...), kind=kLoop, calls=%fused_computation.34 | loop fusion | flops 9584640 | bytes 11870208 | tf_op jit(solution)/shard_map/add | solution.py:315
  171.9 2.1 fusion.27
  174.0 1.8 fusion.26
  178.3 18.5 %shard_map.89 = (f32[20,384]{1,0:T(8,128)}, f32[20,384]{1,0:T(8,128)}, f32[20,48]{1,0:T(8,128)}, f32[20,48]{1,0:T(8,128)}) custom-call(f32[20,384]{1,0:T(8,128)} %reshape_squeeze.62.refs_0_, f32[20,384]{1,0:T(8,128)} %reshape_squeeze.63.refs_1_, f32[20,48]{1,0:T(8,128)} %reshape_squeeze.64.refs_2_, f32[20,48]{1,0:T(8,128)} %reshape_squeeze.65.refs_3_), custom_call_target="tpu_custom_call" | custom-call | tf_op jit(solution)/shard_map/pallas_call | solution.py:76
  197.5 1.0 reshape.204
  199.2 1.0 reshape.203
  203.0 4.5 %multiply_add_fusion.1 = f32[5,4,48,384]{3,2,1,0:T(8,128)S(1)} fusion(f32[5,4,48,384]{3,2,1,0:T(8,128)} %copy.98, f32[5,4,48,384]{3,2,1,0:T(8,128)S(1)} %multiply_add_fusion.2, f32[5,4,48,1]{3,2,1,0:T(8,128)} %reshape.204, f32[5,4,48,383]{3,2,1,0:T(8,128)} %get-tuple-element.62, f32[5,4,48,383]{3,2,1,0:T(8,128)} %get-tuple-element.61, ...), kind=kLoop, calls=%fused_computation.33 | loop fusion | flops 9584640 | bytes 11870208 | tf_op jit(solution)/shard_map/add | solution.py:315
  208.3 1.1 slice_reduce_fusion
  209.4 2.1 fusion.25
  211.5 1.8 fusion.24
  213.3 1.5 reshape_squeeze.66.refs_0_
  214.8 1.4 reshape_squeeze.67.refs_1_
  216.2 1.3 reshape_squeeze.68.refs_2_
  218.1 5.2 %shard_map.90 = (f32[20,384]{1,0:T(8,128)}, f32[20,384]{1,0:T(8,128)}, f32[20,48]{1,0:T(8,128)}, f32[20,48]{1,0:T(8,128)}) custom-call(f32[20,384]{1,0:T(8,128)} %reshape_squeeze.66.refs_0_, f32[20,384]{1,0:T(8,128)} %reshape_squeeze.67.refs_1_, f32[20,48]{1,0:T(8,128)} %reshape_squeeze.68.refs_2_, f32[20,48]{1,0:T(8,128)} %reshape_squeeze.69.refs_3_), custom_call_target="tpu_custom_call" | custom-call | tf_op jit(solution)/shard_map/pallas_call | solution.py:76
  224.0 1.0 reshape.208
  225.7 1.0 reshape.207
  226.7 1.4 broadcast_select_fusion
  228.1 1.4 reshape.206
  229.5 1.4 broadcast_select_fusion.1
  230.9 1.4 reshape.205
  232.3 4.1 %multiply_add_fusion = f32[5,4,48,384]{3,2,1,0:T(8,128)S(1)} fusion(f32[5,4,48,384]{3,2,1,0:T(8,128)S(1)} %copy-done.2, f32[5,4,48,384]{3,2,1,0:T(8,128)S(1)} %multiply_add_fusion.1, f32[5,4,48,1]{3,2,1,0:T(8,128)} %reshape.208, f32[5,4,48,383]{3,2,1,0:T(8,128)} %get-tuple-element.58, f32[5,4,48,383]{3,2,1,0:T(8,128)} %get-tuple-element.57, ...), kind=kLoop, calls=%fused_computation.32 | loop fusion | flops 9584640 | bytes 11870208 | tf_op jit(solution)/shard_map/add | solution.py:315
  236.5 1.1 copy-done.6
  238.4 0.9 fusion
  241.3 25.4 %all-gather.2.cloned.1.call-done = f32[5,4,128,128]{3,2,1,0:T(8,128)} async-done(((f32[5,4,16,128]{3,2,1,0:T(8,128)}), f32[5,4,128,128]{3,2,1,0:T(8,128)}) %all-gather.2.cloned.1.call-update) | async-done | bytes 1310736 | tf_op jit(solution)/shard_map/all_gather | solution.py:318
  266.7 1.7 pad_dynamic-slice_fusion.13
  268.4 56.1 %shard_map.91 = f32[5,960,128]{2,1,0:T(8,128)} custom-call(f32[1,960,128]{2,1,0:T(8,128)} %bitcast.85), custom_call_target="tpu_custom_call" | custom-call | tf_op jit(solution)/shard_map/pallas_call | solution.py:219
  324.6 1.9 fusion.23
  327.0 1.2 copy-done.5
  328.2 1.6 dynamic-slice_select_fusion
  (87 shorter events, 33.4 us)
Async XLA Ops:
  10.1 3.7 %copy-start = (f32[5,4,48,384]{3,2,1,0:T(8,128)S(1)}, f32[5,4,48,384]{3,2,1,0:T(8,128)}, u32[]{:S(2)}) copy-start(f32[5,4,48,384]{3,2,1,0:T(8,128)} %param.7) | copy-start | bytes 4423684
  13.8 1.8 copy-start.9
  44.5 2.6 copy-start.4
  55.7 3.8 %copy-start.7 = (f32[1,975,128]{2,1,0:T(8,128)S(1)}, f32[1,975,128]{2,1,0:T(8,128)}, u32[]{:S(2)}) copy-start(f32[1,975,128]{2,1,0:T(8,128)} %stack_reshape.18) | copy-start | bytes 1497604
  101.6 5.8 %copy-start.1 = (f32[5,4,48,384]{3,2,1,0:T(8,128)S(1)}, f32[5,4,48,384]{3,2,1,0:T(8,128)}, u32[]{:S(2)}) copy-start(f32[5,4,48,384]{3,2,1,0:T(8,128)} %param.10) | copy-start | bytes 4423684
  101.6 52.5 %all-to-all-start = ((f32[8,5,4,18,130]{4,2,3,1,0:T(4,128)}), f32[8,5,4,18,130]{4,2,3,1,0:T(4,128)}, u32[]{:S(2)}, u32[]{:S(2)}) async-start(f32[8,5,4,18,130]{4,2,3,1,0:T(4,128)} %bitcast_dynamic-update-slice_fusion), calls=%async_computation | async-start | bytes 5898240 | tf_op jit(solution)/shard_map/all_to_all | solution.py:303
  107.4 41.8 %copy-start.8 = (f32[2,4,48,384]{3,2,1,0:T(8,128)S(1)}, f32[2,4,48,384]{3,2,1,0:T(8,128)}, u32[]{:S(2)}) copy-start(f32[2,4,48,384]{3,2,1,0:T(8,128)} %param.11) | copy-start | bytes 1769476
  107.4 159.3 %all-gather.2.cloned.1.call-start = ((), (), s32[]{:S(2)}) async-start(), calls=%async_computation.1 | async-start | bytes 1474560 | tf_op jit(solution)/shard_map/all_gather | solution.py:318
  213.3 19.0 %copy-start.2 = (f32[5,4,48,384]{3,2,1,0:T(8,128)S(1)}, f32[5,4,48,384]{3,2,1,0:T(8,128)}, u32[]{:S(2)}) copy-start(f32[5,4,48,384]{3,2,1,0:T(8,128)} %copy.98) | copy-start | bytes 4423684
  236.5 1.1 copy-start.6
  237.6 0.8 copy-start.10
  324.6 2.1 copy-start.3
  326.9 1.4 copy-start.5
Sparse Core Ops, SparseCore 0:
  239.5 27.1 all-gather.1

commit v5 on v4

--- a/solution.py
+++ b/solution.py
@@ -274,23 +274,46 @@
 
     margin = parent_columns - span_columns
     wide = jnp.pad(parent_next, ((0, 0), (0, 0), (0, 0), (margin, margin)))
+    straddle = (ratio - 1) * span_columns - 2
+    regimes = (
+        lambda k, extra: not (extra == 1 and k == ratio - 2),
+        lambda k, extra: True,
+        lambda k, extra: not (extra == 0 and k == ratio - 1),
+    )
+    regime = (offset > straddle - span_columns).astype(jnp.int32) + (
+        offset > straddle - span_columns + 1
+    ).astype(jnp.int32)
     pieces = []
-    patterns = []
+    routes = []
     for extra in (0, 1):
         for k in range(ratio):
             if extra == 1 and k == 0:
                 continue
             start = margin + span_columns * k + offset - extra * parent_columns
             piece = lax.dynamic_slice_in_dim(wide, start, relay_columns, axis=3)
-            patterns.append(
-                (column_pairs(column_devices, base, ratio, k, extra), len(pieces), extra)
+            routes.append((k, extra, len(pieces)))
+            pieces.append(flat(piece))
+    stacked_pieces = jnp.stack(pieces)
+    branches = []
+    for number, active in enumerate(regimes):
+        patterns = [
+            (column_pairs(column_devices, base, ratio, k, extra), index, extra)
+            for k, extra, index in routes
+            if active(k, extra)
+        ]
+        identity = (0, 6, 7)[number]
+        branches.append(
+            lambda stacked, patterns=patterns, identity=identity: tuple(
+                exchange(stacked, patterns, 2, "gy", identity)
             )
-            pieces.append(flat(piece))
-    within_part, beyond_part = exchange(jnp.stack(pieces), patterns, 2, "gy", 0)
+        )
+    within_part, beyond_part = lax.switch(regime, branches, stacked_pieces)
     piece_shape = parent_next.shape[:3] + (relay_columns,)
-    straddles = column_rank % ratio != 0
-    relay_cols = within_part.reshape(piece_shape) + jnp.where(
-        straddles, beyond_part.reshape(piece_shape), 0.0
+    own_k = column_rank % ratio
+    within_live = jnp.logical_not((regime == 2) & (own_k == ratio - 1))
+    beyond_live = (own_k != 0) & jnp.logical_not((regime == 0) & (own_k == ratio - 2))
+    relay_cols = jnp.where(within_live, within_part.reshape(piece_shape), 0.0) + jnp.where(
+        beyond_live, beyond_part.reshape(piece_shape), 0.0
     )
 
     padded = jnp.pad(relay_cols, ((0, 0), (0, 0), (relay_rows, relay_rows), (0, 0)))
@@ -321,14 +344,27 @@
     first = jnp.clip(parent_rows * row_rank - row_anchor, -parent_rows, total_span)
     strip = lax.dynamic_slice_in_dim(gathered, first + parent_rows, parent_rows, axis=2)
 
-    patterns = []
+    routes = []
     for extra in (1, 0):
         for k in range(ratio):
             if extra == 1 and k == 0:
                 continue
             pairs = [(j, p) for (p, j) in column_pairs(column_devices, base, ratio, k, extra)]
-            patterns.append((pairs, 0, len(patterns)))
-    parts = exchange(flat(strip)[None], patterns, len(patterns), "gy", 1)
+            routes.append((k, extra, pairs))
+    back_branches = []
+    for number, skipped in enumerate(((1, 1), (0, ratio - 1))):
+        patterns = [
+            (pairs, 0, slot) for slot, (k, extra, pairs) in enumerate(routes)
+            if (k, extra) != (skipped[1], skipped[0])
+        ]
+        identity = (1, 8)[number]
+        back_branches.append(
+            lambda sent, patterns=patterns, identity=identity: tuple(
+                exchange(sent, patterns, len(routes), "gy", identity)
+            )
+        )
+    late = (offset > (ratio - 1) * span_columns - span_columns - 1).astype(jnp.int32)
+    parts = lax.switch(late, back_branches, flat(strip)[None])
     joined = jnp.concatenate([part.reshape(strip.shape) for part in parts], axis=3)
     start = (ratio - 1) * span_columns - 1 - offset
     fed_back = lax.dynamic_slice_in_dim(joined, start, parent_columns, axis=3)

time: 339 us -> 321 us (0.947)
  Pallas kernels: 142 us -> 122 us
    pallas_call x2, Pallas kernels: 79.2 us -> 67.4 us  [exchange(): pl.pallas_call(lambda *refs: exchange_kernel(axis, remote, *refs), out_sh...]
    pallas_call x4, Pallas kernels: 62.6 us -> 54.8 us  [neighbours(): pl.pallas_call(lambda *refs: halo_kernel(rows, cols, *refs), out_shape=tu...]
    unnamed x35 -> x37, local copies, waits for them, and re-layouts: 14.2 us -> 12 us
where the time goes in v5:
time: 321 us; the launch traced here: 319 us
  Pallas kernels  122 us (38%)
  local copies, waits for them, and re-layouts  96.1 us (30%)
  other arithmetic  40.5 us (13%)
  between operations  26.6 us (8%)
  waiting for transfers between devices  24.2 us (8%)
  starting transfers between devices  7.09 us (2%)
    pallas_call x2, Pallas kernels, exchange(): pl.pallas_call(lambda *refs: exchange_kernel(axis, remote, *refs), out_sh...  67.4 us
    pallas_call x4, Pallas kernels, neighbours(): pl.pallas_call(lambda *refs: halo_kernel(rows, cols, *refs), out_shape=tu...  54.8 us
    all_gather x1, waiting for transfers between devices, per_device(): gathered = lax.all_gather(coarse, 'gx', axis=2, tiled=True)  24.2 us
    add x3, other arithmetic, per_device(): state = moved + weight * (forcing - moved)  13.1 us
    unnamed x37, local copies, waits for them, and re-layouts  12 us
    another operation x6, local copies, waits for them, and re-layouts, per_device(): stacked_pieces = jnp.stack(pieces)  11.7 us
    slice x4, local copies, waits for them, and re-layouts, update(): southern = jnp.concatenate([south_col, values[:, :, :, :-1]], axis=3)  9.97 us
    slice x4, local copies, waits for them, and re-layouts, update(): western = jnp.concatenate([west_row, values[:, :, :-1, :]], axis=2)  7.26 us
  transfers between devices with their start and end apart: 2, of which 1 were waited for; matrix products, arithmetic and copies ran while one was open for 5% of the time, Pallas kernels for 10%

profile of v5, /device:TPU:73, one launch (start us, length us, event | category | flops | bytes accessed | tf_op | source)
XLA Modules:
  0.0 318.5 jit_solution(15408385525009345435)
XLA Ops:
  7.2 1.2 slice_reduce_fusion.12
  8.4 1.7 slice_reduce_fusion.4
  10.1 3.7 %fusion.35 = (f32[5,4,48,383]{3,2,1,0:T(8,128)S(1)}, f32[5,4,48,383]{3,2,1,0:T(8,128)}) fusion(f32[5,4,48,384]{3,2,1,0:T(8,128)} %param.12), kind=kLoop, calls=%fused_computation.164 | loop fusion | bytes 5882880 | tf_op jit(solution)/shard_map/slice | solution.py:96
  13.7 1.8 fusion.34
  18.0 6.5 %shard_map.87 = (f32[20,384]{1,0:T(8,128)}, f32[20,384]{1,0:T(8,128)}, f32[20,48]{1,0:T(8,128)}, f32[20,48]{1,0:T(8,128)}) custom-call(f32[20,384]{1,0:T(8,128)} %reshape_squeeze.52.refs_0_, f32[20,384]{1,0:T(8,128)} %reshape_squeeze.53.refs_1_, f32[20,48]{1,0:T(8,128)} %reshape_squeeze.54.refs_2_, f32[20,48]{1,0:T(8,128)} %reshape_squeeze.55.refs_3_), custom_call_target="tpu_custom_call" | custom-call | tf_op jit(solution)/shard_map/pallas_call | solution.py:76
  25.5 1.0 reshape.242
  27.4 2.1 maximum_bitcast_fusion.1
  37.1 3.6 %multiply_add_fusion.3 = f32[5,4,48,384]{3,2,1,0:T(8,128)S(1)} fusion(f32[5,4,48,384]{3,2,1,0:T(8,128)S(1)} %copy-done, f32[5,4,48,1]{3,2,1,0:T(8,128)S(1)} %reshape.243, f32[5,4,48,383]{3,2,1,0:T(8,128)} %get-tuple-element.187, f32[5,4,48,383]{3,2,1,0:T(8,128)S(1)} %get-tuple-element.186, f32[5,4,48,1]{3,2,1,0:T(8,128)} %reshape.242, ...), kind=kLoop, calls=%fused_computation.44 | loop fusion | flops 8478720 | bytes 10321920 | tf_op jit(solution)/shard_map/add | solution.py:106
  40.7 3.3 %pad_dynamic-slice_fusion = (f32[5,4,48,130]{3,2,1,0:T(8,128)}, f32[5,4,48,130]{3,2,1,0:T(8,128)}, f32[5,4,48,130]{3,2,1,0:T(8,128)}, f32[5,4,48,130]{3,2,1,0:T(8,128)}, f32[5,4,48,130]{3,2,1,0:T(8,128)S(1)}) fusion(s32[]{:T(128)S(6)} %select_n.265, f32[5,4,48,384]{3,2,1,0:T(8,128)S(1)} %multiply_add_fusion.3, s32[]{:T(128)S(6)} %select_n.262, ...), kind=kLoop, calls=%fused_computation.9 | loop fusion | bytes 3970580 | tf_op jit(solution)/shard_map/dynamic_slice | solution.py:293
  44.0 1.4 stack_reshape.15
  45.3 1.1 constant_dynamic-update-slice_fusion.4
  46.4 2.6 stack_reshape.16
  49.0 2.6 stack_reshape.17
  51.6 2.6 stack_reshape.18
  54.2 2.6 stack_reshape.19
  56.7 1.2 constant_dynamic-update-slice_fusion.3
  57.9 1.1 constant_dynamic-update-slice_fusion.2
  63.7 29.3 %conditional.2 = ((f32[5,4,48,130]{3,2,1,0:T(8,128)}, f32[5,4,48,130]{3,2,1,0:T(8,128)})) conditional(s32[]{:T(128)} %clamp.7, (f32[5,975,128]{2,1,0:T(8,128)S(1)}, f32[5,4,48,130]{3,2,1,0:T(8,128)S(1)}, f32[5,4,48,130]{3,2,1,0:T(8,128)}) %tuple.42, (f32[5,975,128]{2,1,0:T(8,128)S(1)}, f32[5,4,48,130]{3,2,1,0:T(8,128)S(1)}, ...), branch_computations={%region_0.1_spmd, %region_1.2_spmd, %region_2.3_spmd} | conditional | flops 374405 | bytes 11481714 | solution.py:310
  63.8 21.5 %branch_0_fun.2 = f32[2,975,128]{2,1,0:T(8,128)} custom-call(f32[5,975,128]{2,1,0:T(8,128)S(1)} %get-tuple-element.35.refs_0_), custom_call_target="tpu_custom_call" | custom-call | tf_op jit(solution)/shard_map/cond/branch_0_fun/pallas_call | solution.py:219
  85.3 2.1 fusion.23
  87.4 2.2 squeeze.9
  89.7 1.2 select_select_fusion
  90.9 2.2 reshape.191
  93.0 1.3 select_add_fusion
  102.3 7.1 %all-to-all-start = ((f32[8,5,4,18,130]{4,2,3,1,0:T(4,128)}), f32[8,5,4,18,130]{4,2,3,1,0:T(4,128)}, u32[]{:S(2)}, u32[]{:S(2)}) async-start(f32[8,5,4,18,130]{4,2,3,1,0:T(4,128)} %bitcast_dynamic-update-slice_fusion), calls=%async_computation | async-start | bytes 5898240 | tf_op jit(solution)/shard_map/all_to_all | solution.py:326
  112.6 32.5 %shard_map.86 = (f32[20,384]{1,0:T(8,128)}, f32[20,384]{1,0:T(8,128)}, f32[20,48]{1,0:T(8,128)}, f32[20,48]{1,0:T(8,128)}) custom-call(f32[20,384]{1,0:T(8,128)} %reshape_squeeze.48.refs_0_, f32[20,384]{1,0:T(8,128)} %reshape_squeeze.49.refs_1_, f32[20,48]{1,0:T(8,128)} %reshape_squeeze.50.refs_2_, f32[20,48]{1,0:T(8,128)} %reshape_squeeze.51.refs_3_), custom_call_target="tpu_custom_call" | custom-call | tf_op jit(solution)/shard_map/pallas_call | solution.py:76
  147.2 1.0 reshape.239
  148.2 1.1 reshape.238
  151.3 1.0 maximum_bitcast_fusion.3
  152.2 2.2 fusion.33
  154.4 1.8 fusion.32
  156.2 2.5 reduce_sum.9
  160.7 3.6 %copy.313 = f32[5,4,48,128,3]{2,1,4,3,0:T(4,128)} copy(f32[5,4,48,128,3]{3,1,2,0,4:T(4,128)S(1)} %pad_maximum_fusion.8) | data formatting | bytes 2949120 | tf_op jit(solution)/shard_map/stack | solution.py:124
  164.3 4.5 %copy.314 = f32[5,4,48,384]{3,2,1,0:T(8,128)} copy(f32[5,4,48,384]{2,1,3,0:T(4,128)} %bitcast.84) | data formatting | bytes 2949120 | tf_op jit(solution)/shard_map/reshape | solution.py:128
  168.9 4.5 %multiply_add_fusion.2 = f32[5,4,48,384]{3,2,1,0:T(8,128)S(1)} fusion(f32[5,4,48,384]{3,2,1,0:T(8,128)} %copy.314, f32[5,4,48,384]{3,2,1,0:T(8,128)S(1)} %copy-done.1, f32[5,4,48,1]{3,2,1,0:T(8,128)} %reshape.239, f32[5,4,48,383]{3,2,1,0:T(8,128)} %get-tuple-element.178, f32[5,4,48,383]{3,2,1,0:T(8,128)} %get-tuple-element.177, ...), kind=kLoop, calls=%fused_computation.43 | loop fusion | flops 9584640 | bytes 11870208 | tf_op jit(solution)/shard_map/add | solution.py:338
  174.0 2.1 fusion.31
  176.1 1.8 fusion.30
  180.4 8.5 %shard_map.88 = (f32[20,384]{1,0:T(8,128)}, f32[20,384]{1,0:T(8,128)}, f32[20,48]{1,0:T(8,128)}, f32[20,48]{1,0:T(8,128)}) custom-call(f32[20,384]{1,0:T(8,128)} %reshape_squeeze.56.refs_0_, f32[20,384]{1,0:T(8,128)} %reshape_squeeze.57.refs_1_, f32[20,48]{1,0:T(8,128)} %reshape_squeeze.58.refs_2_, f32[20,48]{1,0:T(8,128)} %reshape_squeeze.59.refs_3_), custom_call_target="tpu_custom_call" | custom-call | tf_op jit(solution)/shard_map/pallas_call | solution.py:76
  189.6 1.0 reshape.247
  191.4 1.0 reshape.246
  195.2 4.5 %multiply_add_fusion.1 = f32[5,4,48,384]{3,2,1,0:T(8,128)S(1)} fusion(f32[5,4,48,384]{3,2,1,0:T(8,128)} %copy.314, f32[5,4,48,384]{3,2,1,0:T(8,128)S(1)} %multiply_add_fusion.2, f32[5,4,48,1]{3,2,1,0:T(8,128)} %reshape.247, f32[5,4,48,383]{3,2,1,0:T(8,128)} %get-tuple-element.174, f32[5,4,48,383]{3,2,1,0:T(8,128)} %get-tuple-element.173, ...), kind=kLoop, calls=%fused_computation.42 | loop fusion | flops 9584640 | bytes 11870208 | tf_op jit(solution)/shard_map/add | solution.py:338
  200.5 1.1 slice_reduce_fusion
  201.6 2.1 fusion.29
  203.7 1.8 fusion.28
  205.5 1.5 reshape_squeeze.60.refs_0_
  207.0 1.4 reshape_squeeze.61.refs_1_
  208.4 1.3 reshape_squeeze.62.refs_2_
  210.3 7.3 %shard_map.89 = (f32[20,384]{1,0:T(8,128)}, f32[20,384]{1,0:T(8,128)}, f32[20,48]{1,0:T(8,128)}, f32[20,48]{1,0:T(8,128)}) custom-call(f32[20,384]{1,0:T(8,128)} %reshape_squeeze.60.refs_0_, f32[20,384]{1,0:T(8,128)} %reshape_squeeze.61.refs_1_, f32[20,48]{1,0:T(8,128)} %reshape_squeeze.62.refs_2_, f32[20,48]{1,0:T(8,128)} %reshape_squeeze.63.refs_3_), custom_call_target="tpu_custom_call" | custom-call | tf_op jit(solution)/shard_map/pallas_call | solution.py:76
  218.3 1.0 reshape.251
  220.1 1.0 reshape.250
  221.1 1.4 broadcast_select_fusion.7
  222.5 1.4 reshape.249
  223.9 1.4 broadcast_select_fusion.8
  225.3 1.4 reshape.248
  226.7 4.1 %multiply_add_fusion = f32[5,4,48,384]{3,2,1,0:T(8,128)S(1)} fusion(f32[5,4,48,384]{3,2,1,0:T(8,128)S(1)} %copy-done.2, f32[5,4,48,384]{3,2,1,0:T(8,128)S(1)} %multiply_add_fusion.1, f32[5,4,48,1]{3,2,1,0:T(8,128)} %reshape.251, f32[5,4,48,383]{3,2,1,0:T(8,128)} %get-tuple-element.170, f32[5,4,48,383]{3,2,1,0:T(8,128)} %get-tuple-element.169, ...), kind=kLoop, calls=%fused_computation.41 | loop fusion | flops 9584640 | bytes 11870208 | tf_op jit(solution)/shard_map/add | solution.py:338
  230.8 1.1 copy-done.9
  232.7 1.0 fusion
  235.7 24.2 %all-gather.2.cloned.1.call-done = f32[5,4,128,128]{3,2,1,0:T(8,128)} async-done(((f32[5,4,16,128]{3,2,1,0:T(8,128)}), f32[5,4,128,128]{3,2,1,0:T(8,128)}) %all-gather.2.cloned.1.call-update) | async-done | bytes 1310736 | tf_op jit(solution)/shard_map/all_gather | solution.py:341
  259.9 0.9 pad_dynamic-slice_fusion.13
  260.8 47.8 %conditional.3 = (f32[5,4,48,128]{3,2,1,0:T(8,128)S(1)}, f32[5,4,48,128]{3,2,1,0:T(8,128)S(1)}, f32[5,4,48,128]{3,2,1,0:T(8,128)S(1)}, f32[5,4,48,128]{3,2,1,0:T(8,128)S(1)}, f32[5,4,48,128]{3,2,1,0:T(8,128)S(1)}) conditional(s32[]{:T(128)} %clamp.6, f32[5,4,48,128]{3,2,1,0:T(8,128)S(1)} %pad_dynamic-slice_fusion.13, ...), branch_computations={%region_4.5_spmd, %region_5.6_spmd} | conditional | flops 245764 | bytes 7372880 | solution.py:367
  260.9 45.9 %branch_0_fun.3 = f32[5,960,128]{2,1,0:T(8,128)} custom-call(f32[1,960,128]{2,1,0:T(8,128)S(1)} %bitcast.85), custom_call_target="tpu_custom_call" | custom-call | tf_op jit(solution)/shard_map/cond/branch_0_fun/pallas_call | solution.py:219
  306.7 1.8 fusion.26
  308.9 1.2 copy-done.8
  310.1 1.6 dynamic-slice_select_fusion
  (93 shorter events, 34.9 us)
Async XLA Ops:
  10.1 3.7 %copy-start = (f32[5,4,48,384]{3,2,1,0:T(8,128)S(1)}, f32[5,4,48,384]{3,2,1,0:T(8,128)}, u32[]{:S(2)}) copy-start(f32[5,4,48,384]{3,2,1,0:T(8,128)} %param.12) | copy-start | bytes 4423684
  25.3 4.2 %copy-start.13 = (s32[2]{0:T(128)S(1)}, s32[2]{0:T(128)}, u32[]{:S(2)}) copy-start(s32[2]{0:T(128)} %param.18) | copy-start | bytes 28
  40.7 3.3 %copy-start.7 = (f32[5,4,48,384]{3,2,1,0:T(8,128)}, f32[5,4,48,384]{3,2,1,0:T(8,128)S(1)}, u32[]{:S(2)}) copy-start(f32[5,4,48,384]{3,2,1,0:T(8,128)S(1)} %multiply_add_fusion.3) | copy-start | bytes 4423684
  56.7 2.2 copy-start.11
  56.7 2.3 copy-start.10
  85.3 4.4 %copy-start.5 = (f32[5,4,48,130]{3,2,1,0:T(8,128)S(1)}, f32[5,4,48,130]{3,2,1,0:T(8,128)}, u32[]{:S(2)}) copy-start(f32[5,4,48,130]{3,2,1,0:T(8,128)} %get-tuple-element.33) | copy-start | bytes 1497604 | tf_op jit(solution)/shard_map/cond
  102.3 7.1 %copy-start.1 = (f32[5,4,48,384]{3,2,1,0:T(8,128)S(1)}, f32[5,4,48,384]{3,2,1,0:T(8,128)}, u32[]{:S(2)}) copy-start(f32[5,4,48,384]{3,2,1,0:T(8,128)} %param.15) | copy-start | bytes 4423684
  102.3 53.9 %all-to-all-start = ((f32[8,5,4,18,130]{4,2,3,1,0:T(4,128)}), f32[8,5,4,18,130]{4,2,3,1,0:T(4,128)}, u32[]{:S(2)}, u32[]{:S(2)}) async-start(f32[8,5,4,18,130]{4,2,3,1,0:T(4,128)} %bitcast_dynamic-update-slice_fusion), calls=%async_computation | async-start | bytes 5898240 | tf_op jit(solution)/shard_map/all_to_all | solution.py:326
  109.4 41.9 %copy-start.12 = (f32[2,4,48,384]{3,2,1,0:T(8,128)S(1)}, f32[2,4,48,384]{3,2,1,0:T(8,128)}, u32[]{:S(2)}) copy-start(f32[2,4,48,384]{3,2,1,0:T(8,128)} %param.16) | copy-start | bytes 1769476
  109.4 150.5 %all-gather.2.cloned.1.call-start = ((), (), s32[]{:S(2)}) async-start(), calls=%async_computation.1 | async-start | bytes 1474560 | tf_op jit(solution)/shard_map/all_gather | solution.py:341
  205.5 21.2 %copy-start.2 = (f32[5,4,48,384]{3,2,1,0:T(8,128)S(1)}, f32[5,4,48,384]{3,2,1,0:T(8,128)}, u32[]{:S(2)}) copy-start(f32[5,4,48,384]{3,2,1,0:T(8,128)} %copy.314) | copy-start | bytes 4423684
  230.8 1.1 copy-start.9
  231.9 0.8 copy-start.14
  308.7 1.4 copy-start.8
Sparse Core Ops, SparseCore 0:
  233.8 26.0 all-gather.1

commit v6 on v5

--- a/solution.py
+++ b/solution.py
@@ -233,6 +233,55 @@
             if a == b:
                 parts[slot] = jnp.where(me == a, pieces[source], parts[slot])
     return parts
+
+
+def gather_kernel(axis, count, source, target, send_sems, recv_sems):
+    me = lax.axis_index(axis)
+    barrier = pltpu.get_barrier_semaphore()
+    for delta in range(1, count):
+        pl.semaphore_signal(
+            barrier, 1, device_id={axis: (me + delta) % count}, device_id_type=MESH
+        )
+    pl.semaphore_wait(barrier, count - 1)
+    outgoing = []
+    for delta in range(1, count):
+        copy = pltpu.make_async_remote_copy(
+            src_ref=source,
+            dst_ref=target.at[me],
+            send_sem=send_sems.at[delta - 1],
+            recv_sem=recv_sems.at[delta - 1],
+            device_id={axis: (me + delta) % count},
+            device_id_type=MESH,
+        )
+        copy.start()
+        outgoing.append(copy)
+    target[me] = source[...]
+    for delta, copy in zip(range(1, count), outgoing):
+        copy.wait_send()
+        incoming = pltpu.make_async_remote_copy(
+            src_ref=source,
+            dst_ref=target.at[(me + count - delta) % count],
+            send_sem=send_sems.at[delta - 1],
+            recv_sem=recv_sems.at[delta - 1],
+            device_id={axis: (me + count - delta) % count},
+            device_id_type=MESH,
+        )
+        incoming.wait_recv()
+
+
+def gather(block, axis, identity):
+    count = lax.axis_size(axis)
+    return pl.pallas_call(
+        lambda *refs: gather_kernel(axis, count, *refs),
+        out_shape=jax.ShapeDtypeStruct((count,) + block.shape, block.dtype),
+        in_specs=[pl.BlockSpec(memory_space=pltpu.VMEM)],
+        out_specs=pl.BlockSpec(memory_space=pltpu.VMEM),
+        scratch_shapes=[
+            pltpu.SemaphoreType.DMA((count - 1,)),
+            pltpu.SemaphoreType.DMA((count - 1,)),
+        ],
+        compiler_params=pltpu.CompilerParams(collective_id=identity, has_side_effects=True),
+    )(block)
 
 
 def flat(block):
@@ -338,7 +387,11 @@
         state = moved + weight * (forcing - moved)
 
     coarse = block_mean(state)
-    gathered = lax.all_gather(coarse, "gx", axis=2, tiled=True)
+    fields_count, levels_count = coarse.shape[:2]
+    collected = gather(coarse.reshape((-1,) + coarse.shape[2:]), "gx", 9)
+    gathered = jnp.moveaxis(collected, 0, 1).reshape(
+        fields_count, levels_count, row_devices * span_rows, coarse.shape[3]
+    )
     total_span = row_devices * span_rows
     gathered = jnp.pad(gathered, ((0, 0), (0, 0), (parent_rows, parent_rows), (0, 0)))
     first = jnp.clip(parent_rows * row_rank - row_anchor, -parent_rows, total_span)

time: 321 us -> 303 us (0.944)
  waiting for transfers between devices: 24.2 us -> 0.01 us
  Pallas kernels: 122 us -> 140 us
  between operations: 26.6 us -> 13.8 us
    all_gather x1 -> x0, waiting for transfers between devices: 24.2 us -> none  [per_device(): gathered = lax.all_gather(coarse, 'gx', axis=2, tiled=True)]
    pallas_call x0 -> x1, Pallas kernels: none -> 21 us  [gather(): pl.pallas_call(lambda *refs: gather_kernel(axis, count, *refs), out_shape...]
    unnamed x37 -> x39, local copies, waits for them, and re-layouts: 12 us -> 12.1 us
  transfers between devices with their start and end apart: 2 -> 1, of which waited for: 1 -> 0; matrix products, arithmetic and copies ran while one was open for 5% -> 5% of each run, Pallas kernels for 10% -> 10%
where the time goes in v6:
time: 303 us; the launch traced here: 301 us
  Pallas kernels  140 us (46%)
  local copies, waits for them, and re-layouts  96.8 us (32%)
  other arithmetic  41.2 us (14%)
  between operations  13.8 us (5%)
  starting transfers between devices  7.1 us (2%)
    pallas_call x2, Pallas kernels, exchange(): pl.pallas_call(lambda *refs: exchange_kernel(axis, remote, *refs), out_sh...  66 us
    pallas_call x4, Pallas kernels, neighbours(): pl.pallas_call(lambda *refs: halo_kernel(rows, cols, *refs), out_shape=tu...  53.4 us
    pallas_call x1, Pallas kernels, gather(): pl.pallas_call(lambda *refs: gather_kernel(axis, count, *refs), out_shape...  21 us
    add x3, other arithmetic, per_device(): state = moved + weight * (forcing - moved)  13.1 us
    unnamed x39, local copies, waits for them, and re-layouts  12.1 us
    another operation x6, local copies, waits for them, and re-layouts, per_device(): stacked_pieces = jnp.stack(pieces)  11.7 us
    slice x4, local copies, waits for them, and re-layouts, update(): southern = jnp.concatenate([south_col, values[:, :, :, :-1]], axis=3)  10 us
    slice x4, local copies, waits for them, and re-layouts, update(): western = jnp.concatenate([west_row, values[:, :, :-1, :]], axis=2)  7.29 us
  transfers between devices with their start and end apart: 1, of which 0 were waited for; matrix products, arithmetic and copies ran while one was open for 5% of the time, Pallas kernels for 10%

profile of v6, /device:TPU:73, one launch (start us, length us, event | category | flops | bytes accessed | tf_op | source)
XLA Modules:
  0.0 301.1 jit_solution(13740051670595387570)
XLA Ops:
  0.6 1.2 slice_reduce_fusion.12
  1.9 1.7 slice_reduce_fusion.4
  3.6 3.7 %fusion.34 = (f32[5,4,48,383]{3,2,1,0:T(8,128)S(1)}, f32[5,4,48,383]{3,2,1,0:T(8,128)}) fusion(f32[5,4,48,384]{3,2,1,0:T(8,128)} %param.12), kind=kLoop, calls=%fused_computation.163 | loop fusion | bytes 5882880 | tf_op jit(solution)/shard_map/slice | solution.py:96
  7.2 1.8 fusion.33
  11.5 6.5 %shard_map.87 = (f32[20,384]{1,0:T(8,128)}, f32[20,384]{1,0:T(8,128)}, f32[20,48]{1,0:T(8,128)}, f32[20,48]{1,0:T(8,128)}) custom-call(f32[20,384]{1,0:T(8,128)} %reshape_squeeze.52.refs_0_, f32[20,384]{1,0:T(8,128)} %reshape_squeeze.53.refs_1_, f32[20,48]{1,0:T(8,128)} %reshape_squeeze.54.refs_2_, f32[20,48]{1,0:T(8,128)} %reshape_squeeze.55.refs_3_), custom_call_target="tpu_custom_call" | custom-call | tf_op jit(solution)/shard_map/pallas_call | solution.py:76
  19.0 1.0 reshape.250
  20.9 2.1 maximum_bitcast_fusion.1
  30.6 3.6 %multiply_add_fusion.3 = f32[5,4,48,384]{3,2,1,0:T(8,128)S(1)} fusion(f32[5,4,48,384]{3,2,1,0:T(8,128)S(1)} %copy-done, f32[5,4,48,1]{3,2,1,0:T(8,128)S(1)} %reshape.251, f32[5,4,48,383]{3,2,1,0:T(8,128)} %get-tuple-element.187, f32[5,4,48,383]{3,2,1,0:T(8,128)S(1)} %get-tuple-element.186, f32[5,4,48,1]{3,2,1,0:T(8,128)} %reshape.250, ...), kind=kLoop, calls=%fused_computation.44 | loop fusion | flops 8478720 | bytes 10321920 | tf_op jit(solution)/shard_map/add | solution.py:106
  34.2 3.3 %pad_dynamic-slice_fusion = (f32[5,4,48,130]{3,2,1,0:T(8,128)}, f32[5,4,48,130]{3,2,1,0:T(8,128)}, f32[5,4,48,130]{3,2,1,0:T(8,128)}, f32[5,4,48,130]{3,2,1,0:T(8,128)}, f32[5,4,48,130]{3,2,1,0:T(8,128)S(1)}) fusion(s32[]{:T(128)S(6)} %select_n.265, f32[5,4,48,384]{3,2,1,0:T(8,128)S(1)} %multiply_add_fusion.3, s32[]{:T(128)S(6)} %select_n.262, ...), kind=kLoop, calls=%fused_computation.9 | loop fusion | bytes 3970580 | tf_op jit(solution)/shard_map/dynamic_slice | solution.py:342
  37.5 1.4 stack_reshape.15
  38.9 1.1 constant_dynamic-update-slice_fusion.4
  39.9 2.6 stack_reshape.16
  42.5 2.6 stack_reshape.17
  45.1 2.6 stack_reshape.18
  47.7 2.6 stack_reshape.19
  50.3 1.2 constant_dynamic-update-slice_fusion.3
  51.4 1.1 constant_dynamic-update-slice_fusion.2
  57.8 29.3 %conditional.2 = ((f32[5,4,48,130]{3,2,1,0:T(8,128)}, f32[5,4,48,130]{3,2,1,0:T(8,128)})) conditional(s32[]{:T(128)} %clamp.7, (f32[5,975,128]{2,1,0:T(8,128)S(1)}, f32[5,4,48,130]{3,2,1,0:T(8,128)S(1)}, f32[5,4,48,130]{3,2,1,0:T(8,128)}) %tuple.42, (f32[5,975,128]{2,1,0:T(8,128)S(1)}, f32[5,4,48,130]{3,2,1,0:T(8,128)S(1)}, ...), branch_computations={%region_0.1_spmd, %region_1.2_spmd, %region_2.3_spmd} | conditional | flops 374405 | bytes 11481714 | solution.py:359
  57.8 21.5 %branch_0_fun.2 = f32[2,975,128]{2,1,0:T(8,128)} custom-call(f32[5,975,128]{2,1,0:T(8,128)S(1)} %get-tuple-element.35.refs_0_), custom_call_target="tpu_custom_call" | custom-call | tf_op jit(solution)/shard_map/cond/branch_0_fun/pallas_call | solution.py:219
  79.3 2.1 fusion.22
  81.5 2.2 squeeze.9
  83.7 1.2 select_select_fusion
  84.9 2.2 reshape.195
  87.1 1.3 select_add_fusion
  96.4 7.1 %all-to-all-start = ((f32[8,5,4,18,130]{4,2,3,1,0:T(4,128)}), f32[8,5,4,18,130]{4,2,3,1,0:T(4,128)}, u32[]{:S(2)}, u32[]{:S(2)}) async-start(f32[8,5,4,18,130]{4,2,3,1,0:T(4,128)} %bitcast_dynamic-update-slice_fusion), calls=%async_computation | async-start | bytes 5898240 | tf_op jit(solution)/shard_map/all_to_all | solution.py:375
  108.0 31.2 %shard_map.86 = (f32[20,384]{1,0:T(8,128)}, f32[20,384]{1,0:T(8,128)}, f32[20,48]{1,0:T(8,128)}, f32[20,48]{1,0:T(8,128)}) custom-call(f32[20,384]{1,0:T(8,128)} %reshape_squeeze.48.refs_0_, f32[20,384]{1,0:T(8,128)} %reshape_squeeze.49.refs_1_, f32[20,48]{1,0:T(8,128)} %reshape_squeeze.50.refs_2_, f32[20,48]{1,0:T(8,128)} %reshape_squeeze.51.refs_3_), custom_call_target="tpu_custom_call" | custom-call | tf_op jit(solution)/shard_map/pallas_call | solution.py:76
  142.6 1.0 reshape.247
  143.7 1.0 reshape.246
  146.7 1.0 maximum_bitcast_fusion.3
  147.7 2.2 fusion.32
  149.8 1.8 fusion.31
  151.6 2.5 reduce_sum.9
  156.2 3.6 %copy.316 = f32[5,4,48,128,3]{2,1,4,3,0:T(4,128)} copy(f32[5,4,48,128,3]{3,1,2,0,4:T(4,128)S(1)} %pad_maximum_fusion.8) | data formatting | bytes 2949120 | tf_op jit(solution)/shard_map/stack | solution.py:124
  159.8 4.5 %copy.317 = f32[5,4,48,384]{3,2,1,0:T(8,128)} copy(f32[5,4,48,384]{2,1,3,0:T(4,128)} %bitcast.87) | data formatting | bytes 2949120 | tf_op jit(solution)/shard_map/reshape | solution.py:128
  164.3 4.5 %multiply_add_fusion.2 = f32[5,4,48,384]{3,2,1,0:T(8,128)S(1)} fusion(f32[5,4,48,384]{3,2,1,0:T(8,128)} %copy.317, f32[5,4,48,384]{3,2,1,0:T(8,128)S(1)} %copy-done.1, f32[5,4,48,1]{3,2,1,0:T(8,128)} %reshape.247, f32[5,4,48,383]{3,2,1,0:T(8,128)} %get-tuple-element.178, f32[5,4,48,383]{3,2,1,0:T(8,128)} %get-tuple-element.177, ...), kind=kLoop, calls=%fused_computation.43 | loop fusion | flops 9584640 | bytes 11870208 | tf_op jit(solution)/shard_map/add | solution.py:387
  169.5 2.1 fusion.30
  171.6 1.8 fusion.29
  175.9 8.5 %shard_map.88 = (f32[20,384]{1,0:T(8,128)}, f32[20,384]{1,0:T(8,128)}, f32[20,48]{1,0:T(8,128)}, f32[20,48]{1,0:T(8,128)}) custom-call(f32[20,384]{1,0:T(8,128)} %reshape_squeeze.56.refs_0_, f32[20,384]{1,0:T(8,128)} %reshape_squeeze.57.refs_1_, f32[20,48]{1,0:T(8,128)} %reshape_squeeze.58.refs_2_, f32[20,48]{1,0:T(8,128)} %reshape_squeeze.59.refs_3_), custom_call_target="tpu_custom_call" | custom-call | tf_op jit(solution)/shard_map/pallas_call | solution.py:76
  185.0 1.0 reshape.255
  186.8 1.0 reshape.254
  190.6 4.5 %multiply_add_fusion.1 = f32[5,4,48,384]{3,2,1,0:T(8,128)S(1)} fusion(f32[5,4,48,384]{3,2,1,0:T(8,128)} %copy.317, f32[5,4,48,384]{3,2,1,0:T(8,128)S(1)} %multiply_add_fusion.2, f32[5,4,48,1]{3,2,1,0:T(8,128)} %reshape.255, f32[5,4,48,383]{3,2,1,0:T(8,128)} %get-tuple-element.174, f32[5,4,48,383]{3,2,1,0:T(8,128)} %get-tuple-element.173, ...), kind=kLoop, calls=%fused_computation.42 | loop fusion | flops 9584640 | bytes 11870208 | tf_op jit(solution)/shard_map/add | solution.py:387
  195.9 1.1 slice_reduce_fusion
  197.0 2.1 fusion.28
  199.1 1.8 fusion.27
  200.9 1.5 reshape_squeeze.60.refs_0_
  202.4 1.4 reshape_squeeze.61.refs_1_
  203.8 1.3 reshape_squeeze.62.refs_2_
  205.7 7.3 %shard_map.89 = (f32[20,384]{1,0:T(8,128)}, f32[20,384]{1,0:T(8,128)}, f32[20,48]{1,0:T(8,128)}, f32[20,48]{1,0:T(8,128)}) custom-call(f32[20,384]{1,0:T(8,128)} %reshape_squeeze.60.refs_0_, f32[20,384]{1,0:T(8,128)} %reshape_squeeze.61.refs_1_, f32[20,48]{1,0:T(8,128)} %reshape_squeeze.62.refs_2_, f32[20,48]{1,0:T(8,128)} %reshape_squeeze.63.refs_3_), custom_call_target="tpu_custom_call" | custom-call | tf_op jit(solution)/shard_map/pallas_call | solution.py:76
  213.7 1.0 reshape.259
  215.5 1.0 reshape.258
  216.5 1.4 broadcast_select_fusion.7
  217.9 1.4 reshape.257
  219.3 1.4 broadcast_select_fusion.8
  220.7 1.4 reshape.256
  222.1 4.1 %multiply_add_fusion = f32[5,4,48,384]{3,2,1,0:T(8,128)S(1)} fusion(f32[5,4,48,384]{3,2,1,0:T(8,128)S(1)} %copy-done.2, f32[5,4,48,384]{3,2,1,0:T(8,128)S(1)} %multiply_add_fusion.1, f32[5,4,48,1]{3,2,1,0:T(8,128)} %reshape.259, f32[5,4,48,383]{3,2,1,0:T(8,128)} %get-tuple-element.170, f32[5,4,48,383]{3,2,1,0:T(8,128)} %get-tuple-element.169, ...), kind=kLoop, calls=%fused_computation.41 | loop fusion | flops 9584640 | bytes 11870208 | tf_op jit(solution)/shard_map/add | solution.py:387
  226.2 1.1 copy-done.9
  228.2 0.9 convolution_multiply_fusion
  229.1 21.0 %shard_map.90 = f32[8,20,16,128]{3,2,1,0:T(8,128)} custom-call(f32[20,16,128]{2,1,0:T(8,128)} %bitcast.103), custom_call_target="tpu_custom_call" | custom-call | tf_op jit(solution)/shard_map/pallas_call | solution.py:274
  250.1 1.5 copy.328
  251.7 46.4 %conditional.3 = (f32[5,4,48,128]{3,2,1,0:T(8,128)S(1)}, f32[5,4,48,128]{3,2,1,0:T(8,128)S(1)}, f32[5,4,48,128]{3,2,1,0:T(8,128)S(1)}, f32[5,4,48,128]{3,2,1,0:T(8,128)S(1)}, f32[5,4,48,128]{3,2,1,0:T(8,128)S(1)}) conditional(s32[]{:T(128)} %clamp.6, f32[5,4,48,128]{3,2,1,0:T(8,128)S(1)} %pad_dynamic-slice_fusion.13, ...), branch_computations={%region_4.5_spmd, %region_5.6_spmd} | conditional | flops 245764 | bytes 7372880 | solution.py:420
  251.7 44.5 %branch_0_fun.3 = f32[5,960,128]{2,1,0:T(8,128)} custom-call(f32[1,960,128]{2,1,0:T(8,128)S(1)} %bitcast.88), custom_call_target="tpu_custom_call" | custom-call | tf_op jit(solution)/shard_map/cond/branch_0_fun/pallas_call | solution.py:219
  296.2 1.8 fusion.25
  298.3 1.2 copy-done.8
  299.5 1.6 dynamic-slice_select_fusion
  (94 shorter events, 35.7 us)
Async XLA Ops:
  3.5 3.7 %copy-start = (f32[5,4,48,384]{3,2,1,0:T(8,128)S(1)}, f32[5,4,48,384]{3,2,1,0:T(8,128)}, u32[]{:S(2)}) copy-start(f32[5,4,48,384]{3,2,1,0:T(8,128)} %param.12) | copy-start | bytes 4423684
  18.8 4.2 %copy-start.14 = (s32[2]{0:T(128)S(1)}, s32[2]{0:T(128)}, u32[]{:S(2)}) copy-start(s32[2]{0:T(128)} %param.18) | copy-start | bytes 28
  34.2 3.3 %copy-start.7 = (f32[5,4,48,384]{3,2,1,0:T(8,128)}, f32[5,4,48,384]{3,2,1,0:T(8,128)S(1)}, u32[]{:S(2)}) copy-start(f32[5,4,48,384]{3,2,1,0:T(8,128)S(1)} %multiply_add_fusion.3) | copy-start | bytes 4423684
  50.3 2.2 copy-start.11
  50.3 2.3 copy-start.10
  79.3 4.4 %copy-start.5 = (f32[5,4,48,130]{3,2,1,0:T(8,128)S(1)}, f32[5,4,48,130]{3,2,1,0:T(8,128)}, u32[]{:S(2)}) copy-start(f32[5,4,48,130]{3,2,1,0:T(8,128)} %get-tuple-element.33) | copy-start | bytes 1497604 | tf_op jit(solution)/shard_map/cond
  96.4 7.1 %copy-start.1 = (f32[5,4,48,384]{3,2,1,0:T(8,128)S(1)}, f32[5,4,48,384]{3,2,1,0:T(8,128)}, u32[]{:S(2)}) copy-start(f32[5,4,48,384]{3,2,1,0:T(8,128)} %param.15) | copy-start | bytes 4423684
  96.4 55.2 %all-to-all-start = ((f32[8,5,4,18,130]{4,2,3,1,0:T(4,128)}), f32[8,5,4,18,130]{4,2,3,1,0:T(4,128)}, u32[]{:S(2)}, u32[]{:S(2)}) async-start(f32[8,5,4,18,130]{4,2,3,1,0:T(4,128)} %bitcast_dynamic-update-slice_fusion), calls=%async_computation | async-start | bytes 5898240 | tf_op jit(solution)/shard_map/all_to_all | solution.py:375
  103.5 43.2 %copy-start.12 = (f32[2,4,48,384]{3,2,1,0:T(8,128)S(1)}, f32[2,4,48,384]{3,2,1,0:T(8,128)}, u32[]{:S(2)}) copy-start(f32[2,4,48,384]{3,2,1,0:T(8,128)} %param.16) | copy-start | bytes 1769476
  200.9 21.2 %copy-start.2 = (f32[5,4,48,384]{3,2,1,0:T(8,128)S(1)}, f32[5,4,48,384]{3,2,1,0:T(8,128)}, u32[]{:S(2)}) copy-start(f32[5,4,48,384]{3,2,1,0:T(8,128)} %copy.317) | copy-start | bytes 4423684
  226.2 1.1 copy-start.9
  227.3 0.8 copy-start.15
  298.2 1.4 copy-start.8
  298.2 1.4 copy-start.13

commit v7 on v6

--- a/solution.py
+++ b/solution.py
@@ -50,7 +50,7 @@
         def _():
             copy.start()
 
-    for own, step, count, copy in copies:
+    for number, (own, step, count, copy) in enumerate(copies):
         @pl.when((own + step >= 0) & (own + step < count))
         def _():
             copy.wait_send()
@@ -58,6 +58,10 @@
         @pl.when((own - step >= 0) & (own - step < count))
         def _():
             copy.wait_recv()
+
+        @pl.when((own - step < 0) | (own - step >= count))
+        def _():
+            targets[number][...] = jnp.zeros(targets[number].shape, targets[number].dtype)
 
 
 def neighbours(cells, identity):
@@ -82,10 +86,10 @@
         compiler_params=pltpu.CompilerParams(collective_id=identity, has_side_effects=True),
     )(*sources)
     western, eastern, southern, northern = received
-    western = jnp.where(x > 0, western, 0.0).reshape(fields, levels, 1, width)
-    eastern = jnp.where(x < rows - 1, eastern, 0.0).reshape(fields, levels, 1, width)
-    southern = jnp.where(y > 0, southern, 0.0).reshape(fields, levels, height, 1)
-    northern = jnp.where(y < cols - 1, northern, 0.0).reshape(fields, levels, height, 1)
+    western = western.reshape(fields, levels, 1, width)
+    eastern = eastern.reshape(fields, levels, 1, width)
+    southern = southern.reshape(fields, levels, height, 1)
+    northern = northern.reshape(fields, levels, height, 1)
     return western, eastern, southern, northern
 
 
@@ -126,6 +130,29 @@
     )
     extent = centre.shape
     return stacked.reshape(extent[0], extent[1], extent[2], 3 * extent[3])
+
+
+def refining(count):
+    fine = jnp.arange(3 * count, dtype=jnp.int32)[:, None]
+    coarse = jnp.arange(count + 2, dtype=jnp.int32)[None, :]
+    centre = fine // 3 + 1
+    phase = fine % 3
+    lower = jnp.where(phase == 0, third, jnp.where(phase == 2, 0.0, 0.0))
+    upper = jnp.where(phase == 2, third, 0.0)
+    middle = jnp.where(phase == 1, 1.0, two_thirds)
+    return (
+        jnp.where(coarse == centre, middle, 0.0)
+        + jnp.where(coarse == centre - 1, lower, 0.0)
+        + jnp.where(coarse == centre + 1, upper, 0.0)
+    ).astype(jnp.float32)
+
+
+def refine(block):
+    exact = lax.Precision.HIGHEST
+    rows = block.shape[2] - 2
+    cols = block.shape[3] - 2
+    down = jnp.einsum("ar,flrc->flac", refining(rows), block, precision=exact)
+    return jnp.einsum("flac,bc->flab", down, refining(cols), precision=exact)
 
 
 def grouping(count):
@@ -375,7 +402,7 @@
     received = lax.all_to_all(stacked, "gx", split_axis=0, concat_axis=0, tiled=True)
     relay = jnp.sum(received, axis=0)
 
-    forcing = refine_columns(refine_rows(relay))
+    forcing = refine(relay)
     row_global = row_rank * nest_rows + jnp.arange(nest_rows, dtype=jnp.int32)
     column_global = column_rank * nest_columns + jnp.arange(nest_columns, dtype=jnp.int32)
     weight = relax_weight(

time: 303 us -> 293 us (0.967)
  other arithmetic: 41.2 us -> 25.2 us
  matrix products: 1.76 us -> 8.48 us
    select_n x14 -> x6, other arithmetic: 10.8 us -> 0.06 us  [the longest x2 0.02 us: refining(): centre = fine // 3 + 1]
    dot_general x0 -> x2, matrix products: none -> 6.72 us  [the longest x1 5.74 us: refine(): return jnp.einsum('flac,bc->flab', down, refining(cols), precision=exact)]
    reshape x17 -> x16, local copies, waits for them, and re-layouts: 17.4 us -> 23.1 us  [the longest x4 6.93 us: neighbours(): northern = northern.reshape(fields, levels, height, 1)]
    add x3 -> x2, other arithmetic: 13.1 us -> 8.61 us  [per_device(): state = moved + weight * (forcing - moved)]
    another operation x2 -> x0, local copies, waits for them, and re-layouts: 4.22 us -> none  [the longest x1 3.58 us: refine_columns(): jnp.stack((third * lower + two_thirds * centre, centre, two_thirds * cent...]
    unnamed x39 -> x47, local copies, waits for them, and re-layouts: 12.1 us -> 12.4 us
  transfers between devices with their start and end apart: 1 -> 1, of which waited for: 0 -> 0; matrix products, arithmetic and copies ran while one was open for 5% -> 6% of each run, Pallas kernels for 10% -> 10%
where the time goes in v7:
time: 293 us; the launch traced here: 291 us
  Pallas kernels  139 us (47%)
  local copies, waits for them, and re-layouts  98.3 us (34%)
  other arithmetic  25.2 us (9%)
  between operations  12.8 us (4%)
  matrix products  8.48 us (3%)
  starting transfers between devices  7.1 us (2%)
    pallas_call x2, Pallas kernels, exchange(): pl.pallas_call(lambda *refs: exchange_kernel(axis, remote, *refs), out_sh...  66 us
    pallas_call x4, Pallas kernels, neighbours(): pl.pallas_call(lambda *refs: halo_kernel(rows, cols, *refs), out_shape=tu...  52.1 us
    pallas_call x1, Pallas kernels, gather(): pl.pallas_call(lambda *refs: gather_kernel(axis, count, *refs), out_shape...  21 us
    unnamed x47, local copies, waits for them, and re-layouts  12.4 us
    another operation x6, local copies, waits for them, and re-layouts, per_device(): stacked_pieces = jnp.stack(pieces)  11.7 us
    slice x4, local copies, waits for them, and re-layouts, update(): western = jnp.concatenate([west_row, values[:, :, :-1, :]], axis=2)  9.04 us
    add x2, other arithmetic, per_device(): state = moved + weight * (forcing - moved)  8.61 us
    slice x4, local copies, waits for them, and re-layouts, update(): southern = jnp.concatenate([south_col, values[:, :, :, :-1]], axis=3)  8.41 us
  transfers between devices with their start and end apart: 1, of which 0 were waited for; matrix products, arithmetic and copies ran while one was open for 6% of the time, Pallas kernels for 10%

profile of v7, /device:TPU:73, one launch (start us, length us, event | category | flops | bytes accessed | tf_op | source)
XLA Modules:
  0.0 291.1 jit_solution(1417103819930737007)
XLA Ops:
  0.6 1.2 slice_reduce_fusion.12
  1.9 1.7 slice_reduce_fusion.4
  3.6 3.5 %fusion.59 = (f32[5,4,47,384]{3,2,1,0:T(8,128)S(1)}, f32[5,4,47,384]{3,2,1,0:T(8,128)}) fusion(f32[5,4,48,384]{3,2,1,0:T(8,128)} %param.12), kind=kLoop, calls=%fused_computation.180 | loop fusion | bytes 5775360 | tf_op jit(solution)/shard_map/slice | solution.py:98
  7.0 2.1 fusion.60
  11.6 6.5 %shard_map.87 = (f32[20,384]{1,0:T(8,128)}, f32[20,384]{1,0:T(8,128)}, f32[20,48]{1,0:T(8,128)}, f32[20,48]{1,0:T(8,128)}) custom-call(f32[20,384]{1,0:T(8,128)} %reshape_squeeze.52.refs_0_, f32[20,384]{1,0:T(8,128)} %reshape_squeeze.53.refs_1_, f32[20,48]{1,0:T(8,128)} %reshape_squeeze.54.refs_2_, f32[20,48]{1,0:T(8,128)} %reshape_squeeze.55.refs_3_), custom_call_target="tpu_custom_call" | custom-call | tf_op jit(solution)/shard_map/pallas_call | solution.py:80
  19.1 1.7 reshape.315
  22.4 2.1 maximum_bitcast_fusion.1
  30.7 3.7 %multiply_add_fusion.3 = f32[5,4,48,384]{3,2,1,0:T(8,128)S(1)} fusion(f32[5,4,48,384]{3,2,1,0:T(8,128)S(1)} %copy-done, f32[5,4,48,1]{3,2,1,0:T(8,128)} %reshape.315, f32[5,4,48,383]{3,2,1,0:T(8,128)} %get-tuple-element.151, f32[5,4,48,383]{3,2,1,0:T(8,128)} %get-tuple-element.150, f32[5,4,48,1]{3,2,1,0:T(8,128)S(1)} %reshape.314, ...), kind=kLoop, calls=%fused_computation.43 | loop fusion | flops 8478720 | bytes 10321920 | tf_op jit(solution)/shard_map/add | solution.py:110
  34.4 3.3 %pad_dynamic-slice_fusion = (f32[5,4,48,130]{3,2,1,0:T(8,128)}, f32[5,4,48,130]{3,2,1,0:T(8,128)}, f32[5,4,48,130]{3,2,1,0:T(8,128)}, f32[5,4,48,130]{3,2,1,0:T(8,128)}, f32[5,4,48,130]{3,2,1,0:T(8,128)S(1)}) fusion(s32[]{:T(128)S(6)} %select_n.309, f32[5,4,48,384]{3,2,1,0:T(8,128)S(1)} %multiply_add_fusion.3, s32[]{:T(128)S(6)} %select_n.306, ...), kind=kLoop, calls=%fused_computation.9 | loop fusion | bytes 3970580 | tf_op jit(solution)/shard_map/dynamic_slice | solution.py:369
  37.7 1.4 stack_reshape.15
  39.0 1.1 constant_dynamic-update-slice_fusion.4
  40.1 2.6 stack_reshape.16
  42.7 2.6 stack_reshape.17
  45.3 2.6 stack_reshape.18
  47.8 2.6 stack_reshape.19
  50.4 1.2 constant_dynamic-update-slice_fusion.3
  51.6 1.1 constant_dynamic-update-slice_fusion.2
  58.2 29.3 %conditional.2 = ((f32[5,4,48,130]{3,2,1,0:T(8,128)}, f32[5,4,48,130]{3,2,1,0:T(8,128)})) conditional(s32[]{:T(128)} %clamp.7, (f32[5,975,128]{2,1,0:T(8,128)S(1)}, f32[5,4,48,130]{3,2,1,0:T(8,128)S(1)}, f32[5,4,48,130]{3,2,1,0:T(8,128)}) %tuple.42, (f32[5,975,128]{2,1,0:T(8,128)S(1)}, f32[5,4,48,130]{3,2,1,0:T(8,128)S(1)}, ...), branch_computations={%region_0.1_spmd, %region_1.2_spmd, %region_2.3_spmd} | conditional | flops 374405 | bytes 11481714 | solution.py:386
  58.3 21.5 %branch_0_fun.2 = f32[2,975,128]{2,1,0:T(8,128)} custom-call(f32[5,975,128]{2,1,0:T(8,128)S(1)} %get-tuple-element.35.refs_0_), custom_call_target="tpu_custom_call" | custom-call | tf_op jit(solution)/shard_map/cond/branch_0_fun/pallas_call | solution.py:246
  79.8 2.1 fusion.48
  81.9 2.2 squeeze.9
  84.2 1.2 select_select_fusion
  85.3 2.2 reshape.261
  87.5 1.3 select_add_fusion
  96.8 7.1 %all-to-all-start = ((f32[8,5,4,18,130]{4,2,3,1,0:T(4,128)}), f32[8,5,4,18,130]{4,2,3,1,0:T(4,128)}, u32[]{:S(2)}, u32[]{:S(2)}) async-start(f32[8,5,4,18,130]{4,2,3,1,0:T(4,128)} %bitcast_dynamic-update-slice_fusion), calls=%async_computation | async-start | bytes 5898240 | tf_op jit(solution)/shard_map/all_to_all | solution.py:402
  109.8 29.8 %shard_map.86 = (f32[20,384]{1,0:T(8,128)}, f32[20,384]{1,0:T(8,128)}, f32[20,48]{1,0:T(8,128)}, f32[20,48]{1,0:T(8,128)}) custom-call(f32[20,384]{1,0:T(8,128)} %reshape_squeeze.48.refs_0_, f32[20,384]{1,0:T(8,128)} %reshape_squeeze.49.refs_1_, f32[20,48]{1,0:T(8,128)} %reshape_squeeze.50.refs_2_, f32[20,48]{1,0:T(8,128)} %reshape_squeeze.51.refs_3_), custom_call_target="tpu_custom_call" | custom-call | tf_op jit(solution)/shard_map/pallas_call | solution.py:80
  139.6 1.7 reshape.310
  141.4 1.7 reshape.311
  143.1 1.4 reshape.308
  144.5 1.4 reshape.309
  148.1 1.9 fusion.57
  150.0 2.1 fusion.58
  152.1 2.5 reduce_sum.9
  154.6 1.0 convolution_bitcast_fusion
  156.0 5.7 %multiply_add_fusion.2 = (f32[5,4,48,384]{3,2,1,0:T(8,128)S(1)}, f32[5,4,48,384]{3,2,1,0:T(8,128)}) fusion(f32[5,4,48,384]{3,2,1,0:T(8,128)S(1)} %copy-done.1, f32[5,4,48,1]{3,2,1,0:T(8,128)} %reshape.311, f32[5,4,48,383]{3,2,1,0:T(8,128)} %get-tuple-element.142, f32[5,4,48,383]{3,2,1,0:T(8,128)} %get-tuple-element.141, f32[5,4,48,1]{3,2,1,0:T(8,128)} %reshape.310, ...), kind=kOutput, calls=%fused_computation.42 | convolution fusion | flops 585062400 | bytes 12378624 | tf_op jit(solution)/shard_map/flac,bc->flab/dot_general | solution.py:155
  161.7 1.8 fusion.55
  163.5 2.1 fusion.56
  168.8 8.5 %shard_map.88 = (f32[20,384]{1,0:T(8,128)}, f32[20,384]{1,0:T(8,128)}, f32[20,48]{1,0:T(8,128)}, f32[20,48]{1,0:T(8,128)}) custom-call(f32[20,384]{1,0:T(8,128)} %reshape_squeeze.56.refs_0_, f32[20,384]{1,0:T(8,128)} %reshape_squeeze.57.refs_1_, f32[20,48]{1,0:T(8,128)} %reshape_squeeze.58.refs_2_, f32[20,48]{1,0:T(8,128)} %reshape_squeeze.59.refs_3_), custom_call_target="tpu_custom_call" | custom-call | tf_op jit(solution)/shard_map/pallas_call | solution.py:80
  177.2 1.7 reshape.318
  179.0 1.7 reshape.319
  180.7 1.4 reshape.316
  182.1 1.4 reshape.317
  183.5 4.5 %multiply_add_fusion.1 = f32[5,4,48,384]{3,2,1,0:T(8,128)S(1)} fusion(f32[5,4,48,384]{3,2,1,0:T(8,128)} %get-tuple-element.171, f32[5,4,48,384]{3,2,1,0:T(8,128)S(1)} %get-tuple-element.170, f32[5,4,48,1]{3,2,1,0:T(8,128)} %reshape.319, f32[5,4,48,383]{3,2,1,0:T(8,128)} %get-tuple-element.138, f32[5,4,48,383]{3,2,1,0:T(8,128)} %get-tuple-element.137, ...), kind=kLoop, calls=%fused_computation.41 | loop fusion | flops 9584640 | bytes 11870208 | tf_op jit(solution)/shard_map/add | solution.py:414
  188.0 1.8 fusion.53
  189.8 2.1 fusion.54
  192.7 1.1 slice_reduce_fusion
  193.8 1.4 reshape_squeeze.60.refs_0_
  195.2 1.4 reshape_squeeze.61.refs_1_
  196.6 1.3 reshape_squeeze.62.refs_2_
  198.5 7.3 %shard_map.89 = (f32[20,384]{1,0:T(8,128)}, f32[20,384]{1,0:T(8,128)}, f32[20,48]{1,0:T(8,128)}, f32[20,48]{1,0:T(8,128)}) custom-call(f32[20,384]{1,0:T(8,128)} %reshape_squeeze.60.refs_0_, f32[20,384]{1,0:T(8,128)} %reshape_squeeze.61.refs_1_, f32[20,48]{1,0:T(8,128)} %reshape_squeeze.62.refs_2_, f32[20,48]{1,0:T(8,128)} %reshape_squeeze.63.refs_3_), custom_call_target="tpu_custom_call" | custom-call | tf_op jit(solution)/shard_map/pallas_call | solution.py:80
  205.8 1.7 reshape.322
  207.6 1.7 reshape.323
  209.3 1.4 reshape.320
  210.7 1.4 reshape.321
  212.1 4.1 %multiply_add_fusion = f32[5,4,48,384]{3,2,1,0:T(8,128)S(1)} fusion(f32[5,4,48,384]{3,2,1,0:T(8,128)S(1)} %copy-done.6, f32[5,4,48,384]{3,2,1,0:T(8,128)S(1)} %multiply_add_fusion.1, f32[5,4,48,1]{3,2,1,0:T(8,128)} %reshape.323, f32[5,4,48,383]{3,2,1,0:T(8,128)} %get-tuple-element.134, f32[5,4,48,383]{3,2,1,0:T(8,128)} %get-tuple-element.133, ...), kind=kLoop, calls=%fused_computation.40 | loop fusion | flops 9584640 | bytes 11870208 | tf_op jit(solution)/shard_map/add | solution.py:414
  216.2 1.1 copy-done.9
  218.2 1.0 convolution_multiply_fusion
  219.1 21.0 %shard_map.90 = f32[8,20,16,128]{3,2,1,0:T(8,128)} custom-call(f32[20,16,128]{2,1,0:T(8,128)} %bitcast.102), custom_call_target="tpu_custom_call" | custom-call | tf_op jit(solution)/shard_map/pallas_call | solution.py:301
  240.1 1.5 copy.92
  241.7 46.4 %conditional.3 = (f32[5,4,48,128]{3,2,1,0:T(8,128)S(1)}, f32[5,4,48,128]{3,2,1,0:T(8,128)S(1)}, f32[5,4,48,128]{3,2,1,0:T(8,128)S(1)}, f32[5,4,48,128]{3,2,1,0:T(8,128)S(1)}, f32[5,4,48,128]{3,2,1,0:T(8,128)S(1)}) conditional(s32[]{:T(128)} %clamp.6, f32[5,4,48,128]{3,2,1,0:T(8,128)S(1)} %pad_dynamic-slice_fusion.13, ...), branch_computations={%region_4.5_spmd, %region_5.6_spmd} | conditional | flops 245764 | bytes 7372880 | solution.py:447
  241.7 44.5 %branch_0_fun.3 = f32[5,960,128]{2,1,0:T(8,128)} custom-call(f32[1,960,128]{2,1,0:T(8,128)S(1)} %bitcast.88), custom_call_target="tpu_custom_call" | custom-call | tf_op jit(solution)/shard_map/cond/branch_0_fun/pallas_call | solution.py:246
  286.2 1.8 fusion.51
  288.3 1.2 copy-done.8
  289.5 1.6 dynamic-slice_select_fusion
  (89 shorter events, 27.0 us)
Async XLA Ops:
  3.5 3.5 %copy-start = (f32[5,4,48,384]{3,2,1,0:T(8,128)S(1)}, f32[5,4,48,384]{3,2,1,0:T(8,128)}, u32[]{:S(2)}) copy-start(f32[5,4,48,384]{3,2,1,0:T(8,128)} %param.12) | copy-start | bytes 4423684
  18.1 6.4 %copy-start.19 = (s32[2]{0:T(128)S(1)}, s32[2]{0:T(128)}, u32[]{:S(2)}) copy-start(s32[2]{0:T(128)} %param.18) | copy-start | bytes 28
  34.4 3.3 %copy-start.7 = (f32[5,4,48,384]{3,2,1,0:T(8,128)}, f32[5,4,48,384]{3,2,1,0:T(8,128)S(1)}, u32[]{:S(2)}) copy-start(f32[5,4,48,384]{3,2,1,0:T(8,128)S(1)} %multiply_add_fusion.3) | copy-start | bytes 4423684
  50.4 2.2 copy-start.12
  50.4 2.3 copy-start.11
  79.8 4.4 %copy-start.4 = (f32[5,4,48,130]{3,2,1,0:T(8,128)S(1)}, f32[5,4,48,130]{3,2,1,0:T(8,128)}, u32[]{:S(2)}) copy-start(f32[5,4,48,130]{3,2,1,0:T(8,128)} %get-tuple-element.33) | copy-start | bytes 1497604 | tf_op jit(solution)/shard_map/cond
  96.8 7.2 %copy-start.1 = (f32[5,4,48,384]{3,2,1,0:T(8,128)S(1)}, f32[5,4,48,384]{3,2,1,0:T(8,128)}, u32[]{:S(2)}) copy-start(f32[5,4,48,384]{3,2,1,0:T(8,128)} %param.15) | copy-start | bytes 4423684
  96.8 55.3 %all-to-all-start = ((f32[8,5,4,18,130]{4,2,3,1,0:T(4,128)}), f32[8,5,4,18,130]{4,2,3,1,0:T(4,128)}, u32[]{:S(2)}, u32[]{:S(2)}) async-start(f32[8,5,4,18,130]{4,2,3,1,0:T(4,128)} %bitcast_dynamic-update-slice_fusion), calls=%async_computation | async-start | bytes 5898240 | tf_op jit(solution)/shard_map/all_to_all | solution.py:402
  103.9 43.3 %copy-start.13 = (f32[2,4,48,384]{3,2,1,0:T(8,128)S(1)}, f32[2,4,48,384]{3,2,1,0:T(8,128)}, u32[]{:S(2)}) copy-start(f32[2,4,48,384]{3,2,1,0:T(8,128)} %param.16) | copy-start | bytes 1769476
  103.9 50.7 %copy-start.17 = (s32[48]{0:T(128)}, s32[48]{0:T(128)S(1)}, u32[]{:S(2)}) copy-start(s32[48]{0:T(128)S(1)} %get-tuple-element.176) | copy-start | bytes 580
  154.6 1.4 copy-start.10
  154.6 1.4 copy-start.14
  154.6 1.4 copy-start.16
  191.9 20.1 %copy-start.6 = (f32[5,4,48,384]{3,2,1,0:T(8,128)S(1)}, f32[5,4,48,384]{3,2,1,0:T(8,128)}, u32[]{:S(2)}) copy-start(f32[5,4,48,384]{3,2,1,0:T(8,128)} %get-tuple-element.171) | copy-start | bytes 4423684
  216.2 1.1 copy-start.9
  217.3 0.8 copy-start.18
  288.2 1.4 copy-start.8
  288.2 1.4 copy-start.15

commit v8 on v7

--- a/solution.py
+++ b/solution.py
@@ -309,6 +309,63 @@
         ],
         compiler_params=pltpu.CompilerParams(collective_id=identity, has_side_effects=True),
     )(block)
+
+
+def stencil_kernel(relaxed, *refs):
+    if relaxed:
+        (values, velocity, mixing, western, eastern, southern, northern, forcing, weight, out) = refs
+    else:
+        (values, velocity, mixing, western, eastern, southern, northern, out) = refs
+    levels, height, width = values.shape[1:]
+    row = lax.broadcasted_iota(jnp.int32, (height, width), 0)
+    col = lax.broadcasted_iota(jnp.int32, (height, width), 1)
+    for level in range(levels):
+        q = values[0, level]
+        west = jnp.where(row == 0, western[0, level], pltpu.roll(q, 1, 0))
+        east = jnp.where(row == height - 1, eastern[0, level], pltpu.roll(q, height - 1, 0))
+        south = jnp.where(col == 0, southern[0, level], pltpu.roll(q, 1, 1))
+        north = jnp.where(col == width - 1, northern[0, level], pltpu.roll(q, width - 1, 1))
+        along_rows = velocity[0, level]
+        along_columns = velocity[1, level]
+        upwind = (
+            jnp.maximum(along_rows, 0.0) * (q - west)
+            + jnp.minimum(along_rows, 0.0) * (east - q)
+            + jnp.maximum(along_columns, 0.0) * (q - south)
+            + jnp.minimum(along_columns, 0.0) * (north - q)
+        )
+        moved = q - upwind + mixing[level] * (east + west + north + south - 4.0 * q)
+        if relaxed:
+            moved = moved + weight[...] * (forcing[0, level] - moved)
+        out[0, level] = moved
+
+
+def stencil(values, halo, velocity, mixing, forcing=None, weight=None):
+    fields, levels, height, width = values.shape
+    west_row, east_row, south_col, north_col = halo
+    plane = pl.BlockSpec((1, levels, height, width), lambda f: (f, 0, 0, 0))
+    edge_row = pl.BlockSpec((1, levels, 1, width), lambda f: (f, 0, 0, 0))
+    edge_col = pl.BlockSpec((1, levels, height, 1), lambda f: (f, 0, 0, 0))
+    operands = [values, velocity, mixing, west_row, east_row, south_col, north_col]
+    specs = [
+        plane,
+        pl.BlockSpec(velocity.shape, lambda f: (0, 0, 0, 0)),
+        pl.BlockSpec(mixing.shape, lambda f: (0, 0, 0)),
+        edge_row,
+        edge_row,
+        edge_col,
+        edge_col,
+    ]
+    relaxed = forcing is not None
+    if relaxed:
+        operands += [forcing, weight]
+        specs += [plane, pl.BlockSpec(weight.shape, lambda f: (0, 0))]
+    return pl.pallas_call(
+        lambda *refs: stencil_kernel(relaxed, *refs),
+        out_shape=jax.ShapeDtypeStruct(values.shape, values.dtype),
+        grid=(fields,),
+        in_specs=specs,
+        out_specs=plane,
+    )(*operands)
 
 
 def flat(block):
@@ -344,7 +401,7 @@
     column_anchor = nest_anchor[1]
     offset = column_anchor - 1 - base_column
 
-    parent_next = update(
+    parent_next = stencil(
         parent_fields, neighbours(parent_fields, 2), parent_velocity, parent_mixing
     )
 
@@ -410,8 +467,9 @@
     )
     state = nest_fields
     for substep in range(SUBSTEPS):
-        moved = update(state, neighbours(state, 3 + substep), nest_velocity, nest_mixing)
-        state = moved + weight * (forcing - moved)
+        state = stencil(
+            state, neighbours(state, 3 + substep), nest_velocity, nest_mixing, forcing, weight
+        )
 
     coarse = block_mean(state)
     fields_count, levels_count = coarse.shape[:2]

time: 293 us -> 287 us (0.980)
  Pallas kernels: 139 us -> 162 us
  other arithmetic: 25.2 us -> 7.13 us
  local copies, waits for them, and re-layouts: 98.3 us -> 88.9 us
    pallas_call x0 -> x4, Pallas kernels: none -> 23.6 us  [stencil(): pl.pallas_call(lambda *refs: stencil_kernel(relaxed, *refs), out_shape=ja...]
    slice x8 -> x0, local copies, waits for them, and re-layouts: 17.4 us -> none  [the longest x4 9.04 us: update(): western = jnp.concatenate([west_row, values[:, :, :-1, :]], axis=2)]
    add x3 -> x0, other arithmetic: 12.3 us -> none  [the longest x2 8.61 us: per_device(): state = moved + weight * (forcing - moved)]
    mul x2 -> x0, other arithmetic: 2.97 us -> none  [update(): jnp.maximum(along_rows, 0.0) * (values - western)]
    unnamed x47 -> x19, local copies, waits for them, and re-layouts: 12.4 us -> 11.8 us
  transfers between devices with their start and end apart: 1 -> 1, of which waited for: 0 -> 0; matrix products, arithmetic and copies ran while one was open for 6% -> 5% of each run, Pallas kernels for 10% -> 10%
where the time goes in v8:
time: 287 us; the launch traced here: 285 us
  Pallas kernels  162 us (56%)
  local copies, waits for them, and re-layouts  88.9 us (31%)
  between operations  13 us (5%)
  other arithmetic  7.13 us (2%)
  matrix products  6.98 us (2%)
  starting transfers between devices  6.94 us (2%)
    pallas_call x2, Pallas kernels, exchange(): pl.pallas_call(lambda *refs: exchange_kernel(axis, remote, *refs), out_sh...  66.1 us
    pallas_call x4, Pallas kernels, neighbours(): pl.pallas_call(lambda *refs: halo_kernel(rows, cols, *refs), out_shape=tu...  51.1 us
    pallas_call x4, Pallas kernels, stencil(): pl.pallas_call(lambda *refs: stencil_kernel(relaxed, *refs), out_shape=ja...  23.6 us
    pallas_call x1, Pallas kernels, gather(): pl.pallas_call(lambda *refs: gather_kernel(axis, count, *refs), out_shape...  20.9 us
    unnamed x19, local copies, waits for them, and re-layouts  11.8 us
    another operation x6, local copies, waits for them, and re-layouts, per_device(): stacked_pieces = jnp.stack(pieces)  11.8 us
    reshape x4, local copies, waits for them, and re-layouts, neighbours(): southern = southern.reshape(fields, levels, height, 1)  6.95 us
    all_to_all x1, starting transfers between devices, per_device(): lax.all_to_all(stacked, 'gx', split_axis=0, concat_axis=0, tiled=True)  6.94 us
  transfers between devices with their start and end apart: 1, of which 0 were waited for; matrix products, arithmetic and copies ran while one was open for 5% of the time, Pallas kernels for 10%

profile of v8, /device:TPU:73, one launch (start us, length us, event | category | flops | bytes accessed | tf_op | source)
XLA Modules:
  0.0 284.7 jit_solution(1966670746970440680)
XLA Ops:
  0.6 1.2 slice_reduce_fusion.12
  1.9 1.7 slice_reduce_fusion.4
  3.5 1.3 fusion.53
  13.7 6.5 %shard_map.87 = (f32[20,384]{1,0:T(8,128)}, f32[20,384]{1,0:T(8,128)}, f32[20,48]{1,0:T(8,128)}, f32[20,48]{1,0:T(8,128)}) custom-call(f32[20,384]{1,0:T(8,128)} %reshape_squeeze.52.refs_0_, f32[20,384]{1,0:T(8,128)} %reshape_squeeze.53.refs_1_, f32[20,48]{1,0:T(8,128)} %reshape_squeeze.54.refs_2_, f32[20,48]{1,0:T(8,128)} %reshape_squeeze.55.refs_3_), custom_call_target="tpu_custom_call" | custom-call | tf_op jit(solution)/shard_map/pallas_call | solution.py:80
  20.2 1.7 reshape.275.refs_5_
  21.9 1.7 reshape.276.refs_6_
  23.6 1.4 reshape.255.refs_3_
  25.0 1.4 reshape.256.refs_4_
  26.4 5.6 %shard_map.88 = f32[5,4,48,384]{3,2,1,0:T(8,128)} custom-call(f32[5,4,48,384]{3,2,1,0:T(8,128)} %refs_0_.2, f32[2,4,48,384]{3,2,1,0:T(8,128)} %refs_1_.4, f32[4,48,384]{2,1,0:T(8,128)} %refs_2_.4, f32[5,4,1,384]{3,2,1,0:T(1,128)} %reshape.255.refs_3_, f32[5,4,1,384]{3,2,1,0:T(1,128)} %reshape.256.refs_4_, f32[5,4,48,1]{3,2,1,0:T(8,128)} %reshape.275.refs_5_, ...), custom_call_target="tpu_custom_call" | custom-call | tf_op jit(solution)/shard_map/pallas_call | solution.py:362
  32.0 5.8 %pad_dynamic-slice_fusion = (f32[5,4,48,130]{3,2,1,0:T(8,128)}, f32[5,4,48,130]{3,2,1,0:T(8,128)}, f32[5,4,48,130]{3,2,1,0:T(8,128)}, f32[5,4,48,130]{3,2,1,0:T(8,128)}, f32[5,4,48,130]{3,2,1,0:T(8,128)S(1)}) fusion(s32[]{:T(128)S(6)} %select_n.309, f32[5,4,48,384]{3,2,1,0:T(8,128)} %shard_map.88, s32[]{:T(128)S(6)} %select_n.306, s32[]{:T(128)S(6)} %select_n.307, ...), kind=kLoop, calls=%fused_computation.9 | loop fusion | bytes 3970580 | tf_op jit(solution)/shard_map/dynamic_slice | solution.py:426
  37.8 1.4 stack_reshape.15
  39.2 1.1 constant_dynamic-update-slice_fusion.4
  40.3 2.6 stack_reshape.16
  42.9 2.6 stack_reshape.17
  45.5 2.6 stack_reshape.18
  48.0 2.6 stack_reshape.19
  50.6 1.1 constant_dynamic-update-slice_fusion.3
  51.7 1.1 constant_dynamic-update-slice_fusion.2
  52.8 1.1 constant_dynamic-update-slice_fusion.1
  59.1 29.3 %conditional.2 = ((f32[5,4,48,130]{3,2,1,0:T(8,128)}, f32[5,4,48,130]{3,2,1,0:T(8,128)})) conditional(s32[]{:T(128)} %clamp.7, (f32[5,975,128]{2,1,0:T(8,128)S(1)}, f32[5,4,48,130]{3,2,1,0:T(8,128)S(1)}, f32[5,4,48,130]{3,2,1,0:T(8,128)}) %tuple.42, (f32[5,975,128]{2,1,0:T(8,128)S(1)}, f32[5,4,48,130]{3,2,1,0:T(8,128)S(1)}, ...), branch_computations={%region_0.1_spmd, %region_1.2_spmd, %region_2.3_spmd} | conditional | flops 374405 | bytes 11481714 | solution.py:443
  59.1 21.5 %branch_0_fun.2 = f32[2,975,128]{2,1,0:T(8,128)} custom-call(f32[5,975,128]{2,1,0:T(8,128)S(1)} %get-tuple-element.35.refs_0_), custom_call_target="tpu_custom_call" | custom-call | tf_op jit(solution)/shard_map/cond/branch_0_fun/pallas_call | solution.py:246
  80.6 2.1 fusion.48
  82.7 2.2 squeeze.16
  85.0 1.2 select_select_fusion
  86.2 2.2 reshape.226
  88.3 1.3 select_add_fusion
  91.4 0.9 bitcast_dynamic-update-slice_fusion.6
  94.1 0.9 bitcast_dynamic-update-slice_fusion.3
  97.6 6.9 %all-to-all-start = ((f32[8,5,4,18,130]{4,2,3,1,0:T(4,128)}), f32[8,5,4,18,130]{4,2,3,1,0:T(4,128)S(1)}, u32[]{:S(2)}, u32[]{:S(2)}) async-start(f32[8,5,4,18,130]{4,2,3,1,0:T(4,128)} %bitcast_dynamic-update-slice_fusion), calls=%async_computation | async-start | bytes 5898240 | tf_op jit(solution)/shard_map/all_to_all | solution.py:459
  104.6 1.2 slice_reduce_fusion.14
  105.8 1.7 slice_reduce_fusion.6
  111.2 28.9 %shard_map.86 = (f32[20,384]{1,0:T(8,128)}, f32[20,384]{1,0:T(8,128)}, f32[20,48]{1,0:T(8,128)}, f32[20,48]{1,0:T(8,128)}) custom-call(f32[20,384]{1,0:T(8,128)} %reshape_squeeze.48.refs_0_, f32[20,384]{1,0:T(8,128)} %reshape_squeeze.49.refs_1_, f32[20,48]{1,0:T(8,128)} %reshape_squeeze.50.refs_2_, f32[20,48]{1,0:T(8,128)} %reshape_squeeze.51.refs_3_), custom_call_target="tpu_custom_call" | custom-call | tf_op jit(solution)/shard_map/pallas_call | solution.py:80
  140.1 1.7 reshape.273.refs_5_
  141.9 1.7 reshape.274.refs_6_
  143.6 1.4 reshape.251.refs_3_
  145.0 1.4 reshape.252.refs_4_
  148.7 1.0 convolution_bitcast_fusion
  149.7 2.9 %fusion.1.refs_7_ = f32[5,4,48,384]{3,2,1,0:T(8,128)} fusion(f32[5,4,48,130]{3,2,1,0:T(8,128)S(1)} %convolution_bitcast_fusion, f32[384]{0:T(512)S(1)} %get-tuple-element.146, s32[384]{0:T(512)S(1)} %get-tuple-element.152, f32[384]{0:T(512)S(1)} %get-tuple-element.147, s32[384]{0:T(512)S(1)} %add_select_fusion, f32[384]{0:T(512)S(1)} %compare_select_fusion.2, ...), kind=kOutput, calls=%fused_computation.47 | convolution fusion | flops 575477760 | bytes 1982976 | tf_op jit(solution)/shard_map/flac,bc->flab/dot_general | solution.py:155
  152.6 6.0 %shard_map.89.refs_0_ = f32[5,4,48,384]{3,2,1,0:T(8,128)} custom-call(f32[5,4,48,384]{3,2,1,0:T(8,128)} %refs_0_.3, f32[2,4,48,384]{3,2,1,0:T(8,128)} %refs_1_.7, f32[4,48,384]{2,1,0:T(8,128)} %refs_2_.7, f32[5,4,1,384]{3,2,1,0:T(1,128)} %reshape.251.refs_3_, f32[5,4,1,384]{3,2,1,0:T(1,128)} %reshape.252.refs_4_, f32[5,4,48,1]{3,2,1,0:T(8,128)} %reshape.273.refs_5_, ...), custom_call_target="tpu_custom_call" | custom-call | tf_op jit(solution)/shard_map/pallas_call | solution.py:362
  158.6 1.2 slice_reduce_fusion.10
  159.8 1.7 slice_reduce_fusion.2
  163.9 8.5 %shard_map.90 = (f32[20,384]{1,0:T(8,128)}, f32[20,384]{1,0:T(8,128)}, f32[20,48]{1,0:T(8,128)}, f32[20,48]{1,0:T(8,128)}) custom-call(f32[20,384]{1,0:T(8,128)} %reshape_squeeze.56.refs_0_, f32[20,384]{1,0:T(8,128)} %reshape_squeeze.57.refs_1_, f32[20,48]{1,0:T(8,128)} %reshape_squeeze.58.refs_2_, f32[20,48]{1,0:T(8,128)} %reshape_squeeze.59.refs_3_), custom_call_target="tpu_custom_call" | custom-call | tf_op jit(solution)/shard_map/pallas_call | solution.py:80
  172.4 1.7 reshape.277.refs_5_
  174.2 1.7 reshape.278.refs_6_
  175.9 1.4 reshape.259.refs_3_
  177.3 1.4 reshape.260.refs_4_
  178.7 6.0 %shard_map.91.refs_0_ = f32[5,4,48,384]{3,2,1,0:T(8,128)} custom-call(f32[5,4,48,384]{3,2,1,0:T(8,128)} %shard_map.89.refs_0_, f32[2,4,48,384]{3,2,1,0:T(8,128)} %refs_1_.7, f32[4,48,384]{2,1,0:T(8,128)} %refs_2_.7, f32[5,4,1,384]{3,2,1,0:T(1,128)} %reshape.259.refs_3_, f32[5,4,1,384]{3,2,1,0:T(1,128)} %reshape.260.refs_4_, ...), custom_call_target="tpu_custom_call" | custom-call | tf_op jit(solution)/shard_map/pallas_call | solution.py:362
  184.7 1.2 slice_reduce_fusion.8
  185.9 1.7 slice_reduce_fusion
  190.1 7.3 %shard_map.92 = (f32[20,384]{1,0:T(8,128)}, f32[20,384]{1,0:T(8,128)}, f32[20,48]{1,0:T(8,128)}, f32[20,48]{1,0:T(8,128)}) custom-call(f32[20,384]{1,0:T(8,128)} %reshape_squeeze.60.refs_0_, f32[20,384]{1,0:T(8,128)} %reshape_squeeze.61.refs_1_, f32[20,48]{1,0:T(8,128)} %reshape_squeeze.62.refs_2_, f32[20,48]{1,0:T(8,128)} %reshape_squeeze.63.refs_3_), custom_call_target="tpu_custom_call" | custom-call | tf_op jit(solution)/shard_map/pallas_call | solution.py:80
  197.4 1.7 reshape.279.refs_5_
  199.1 1.7 reshape.280.refs_6_
  200.9 1.4 reshape.263.refs_3_
  202.3 1.4 reshape.264.refs_4_
  203.7 6.0 %shard_map.93 = f32[5,4,48,384]{3,2,1,0:T(8,128)} custom-call(f32[5,4,48,384]{3,2,1,0:T(8,128)} %shard_map.91.refs_0_, f32[2,4,48,384]{3,2,1,0:T(8,128)} %refs_1_.7, f32[4,48,384]{2,1,0:T(8,128)} %refs_2_.7, f32[5,4,1,384]{3,2,1,0:T(1,128)} %reshape.263.refs_3_, f32[5,4,1,384]{3,2,1,0:T(1,128)} %reshape.264.refs_4_, f32[5,4,48,1]{3,2,1,0:T(8,128)} %reshape.279.refs_5_, ...), custom_call_target="tpu_custom_call" | custom-call | tf_op jit(solution)/shard_map/pallas_call | solution.py:362
  209.6 2.2 fusion.9
  211.8 1.0 convolution_multiply_fusion
  212.8 20.9 %shard_map.94 = f32[8,20,16,128]{3,2,1,0:T(8,128)} custom-call(f32[20,16,128]{2,1,0:T(8,128)} %bitcast.84), custom_call_target="tpu_custom_call" | custom-call | tf_op jit(solution)/shard_map/pallas_call | solution.py:301
  233.7 1.5 copy.52
  235.2 46.5 %conditional.3 = (f32[5,4,48,128]{3,2,1,0:T(8,128)S(1)}, f32[5,4,48,128]{3,2,1,0:T(8,128)S(1)}, f32[5,4,48,128]{3,2,1,0:T(8,128)S(1)}, f32[5,4,48,128]{3,2,1,0:T(8,128)S(1)}, f32[5,4,48,128]{3,2,1,0:T(8,128)S(1)}) conditional(s32[]{:T(128)} %clamp.6, f32[5,4,48,128]{3,2,1,0:T(8,128)S(1)} %pad_dynamic-slice_fusion.13, ...), branch_computations={%region_4.5_spmd, %region_5.6_spmd} | conditional | flops 245764 | bytes 7372880 | solution.py:505
  235.2 44.6 %branch_0_fun.3 = f32[5,960,128]{2,1,0:T(8,128)} custom-call(f32[1,960,128]{2,1,0:T(8,128)S(1)} %bitcast.70), custom_call_target="tpu_custom_call" | custom-call | tf_op jit(solution)/shard_map/cond/branch_0_fun/pallas_call | solution.py:246
  279.8 1.8 fusion.51
  281.9 1.2 copy-done.4
  283.1 1.6 dynamic-slice_select_fusion
  (52 shorter events, 19.3 us)
Async XLA Ops:
  50.6 3.3 %copy-start.5 = (f32[1,975,128]{2,1,0:T(8,128)S(1)}, f32[1,975,128]{2,1,0:T(8,128)}, u32[]{:S(2)}) copy-start(f32[1,975,128]{2,1,0:T(8,128)} %stack_reshape.19) | copy-start | bytes 1497604
  80.6 4.4 %copy-start.2 = (f32[5,4,48,130]{3,2,1,0:T(8,128)S(1)}, f32[5,4,48,130]{3,2,1,0:T(8,128)}, u32[]{:S(2)}) copy-start(f32[5,4,48,130]{3,2,1,0:T(8,128)} %get-tuple-element.33) | copy-start | bytes 1497604 | tf_op jit(solution)/shard_map/cond
  97.6 50.3 %all-to-all-start = ((f32[8,5,4,18,130]{4,2,3,1,0:T(4,128)}), f32[8,5,4,18,130]{4,2,3,1,0:T(4,128)S(1)}, u32[]{:S(2)}, u32[]{:S(2)}) async-start(f32[8,5,4,18,130]{4,2,3,1,0:T(4,128)} %bitcast_dynamic-update-slice_fusion), calls=%async_computation | async-start | bytes 5898240 | tf_op jit(solution)/shard_map/all_to_all | solution.py:459
  281.7 1.4 copy-start.4

commit v9 on v8

--- a/solution.py
+++ b/solution.py
@@ -88,8 +88,6 @@
     western, eastern, southern, northern = received
     western = western.reshape(fields, levels, 1, width)
     eastern = eastern.reshape(fields, levels, 1, width)
-    southern = southern.reshape(fields, levels, height, 1)
-    northern = northern.reshape(fields, levels, height, 1)
     return western, eastern, southern, northern
 
 
@@ -319,12 +317,29 @@
     levels, height, width = values.shape[1:]
     row = lax.broadcasted_iota(jnp.int32, (height, width), 0)
     col = lax.broadcasted_iota(jnp.int32, (height, width), 1)
+    eye = (
+        lax.broadcasted_iota(jnp.int32, (height, height), 0)
+        == lax.broadcasted_iota(jnp.int32, (height, height), 1)
+    ).astype(jnp.float32)
+    first = pl.multiple_of(pl.program_id(0) * levels, levels)
+    numbers = (((1,), (1,)), ((), ()))
+    exact = lax.Precision.HIGHEST
+    south_cols = lax.dot_general(
+        eye, southern[pl.ds(first, levels), :], numbers, precision=exact,
+        preferred_element_type=jnp.float32,
+    )
+    north_cols = lax.dot_general(
+        eye, northern[pl.ds(first, levels), :], numbers, precision=exact,
+        preferred_element_type=jnp.float32,
+    )
     for level in range(levels):
         q = values[0, level]
         west = jnp.where(row == 0, western[0, level], pltpu.roll(q, 1, 0))
         east = jnp.where(row == height - 1, eastern[0, level], pltpu.roll(q, height - 1, 0))
-        south = jnp.where(col == 0, southern[0, level], pltpu.roll(q, 1, 1))
-        north = jnp.where(col == width - 1, northern[0, level], pltpu.roll(q, width - 1, 1))
+        south = jnp.where(col == 0, south_cols[:, level:level + 1], pltpu.roll(q, 1, 1))
+        north = jnp.where(
+            col == width - 1, north_cols[:, level:level + 1], pltpu.roll(q, width - 1, 1)
+        )
         along_rows = velocity[0, level]
         along_columns = velocity[1, level]
         upwind = (
@@ -344,7 +359,7 @@
     west_row, east_row, south_col, north_col = halo
     plane = pl.BlockSpec((1, levels, height, width), lambda f: (f, 0, 0, 0))
     edge_row = pl.BlockSpec((1, levels, 1, width), lambda f: (f, 0, 0, 0))
-    edge_col = pl.BlockSpec((1, levels, height, 1), lambda f: (f, 0, 0, 0))
+    edge_col = pl.BlockSpec((fields * levels, height), lambda f: (0, 0))
     operands = [values, velocity, mixing, west_row, east_row, south_col, north_col]
     specs = [
         plane,

time: 287 us -> 273 us (0.951)
  local copies, waits for them, and re-layouts: 88.9 us -> 75 us
    reshape x8 -> x0, local copies, waits for them, and re-layouts: 13.9 us -> none  [the longest x4 6.95 us: neighbours(): southern = southern.reshape(fields, levels, height, 1)]
  transfers between devices with their start and end apart: 1 -> 1, of which waited for: 0 -> 0; matrix products, arithmetic and copies ran while one was open for 5% -> 4% of each run, Pallas kernels for 10% -> 11%
where the time goes in v9:
time: 273 us; the launch traced here: 271 us
  Pallas kernels  161 us (59%)
  local copies, waits for them, and re-layouts  75 us (27%)
  between operations  13 us (5%)
  other arithmetic  7.12 us (3%)
  matrix products  6.99 us (3%)
  starting transfers between devices  6.95 us (3%)
    pallas_call x2, Pallas kernels, exchange(): pl.pallas_call(lambda *refs: exchange_kernel(axis, remote, *refs), out_sh...  66.1 us
    pallas_call x4, Pallas kernels, neighbours(): pl.pallas_call(lambda *refs: halo_kernel(rows, cols, *refs), out_shape=tu...  51.1 us
    pallas_call x4, Pallas kernels, stencil(): pl.pallas_call(lambda *refs: stencil_kernel(relaxed, *refs), out_shape=ja...  23.2 us
    pallas_call x1, Pallas kernels, gather(): pl.pallas_call(lambda *refs: gather_kernel(axis, count, *refs), out_shape...  20.9 us
    unnamed x19, local copies, waits for them, and re-layouts  11.8 us
    another operation x6, local copies, waits for them, and re-layouts, per_device(): stacked_pieces = jnp.stack(pieces)  11.8 us
    all_to_all x1, starting transfers between devices, per_device(): lax.all_to_all(stacked, 'gx', split_axis=0, concat_axis=0, tiled=True)  6.95 us
    slice x4, local copies, waits for them, and re-layouts, neighbours(): cells[:, :, :, 0].reshape(planes, height)  6.65 us
  transfers between devices with their start and end apart: 1, of which 0 were waited for; matrix products, arithmetic and copies ran while one was open for 4% of the time, Pallas kernels for 11%

profile of v9, /device:TPU:73, one launch (start us, length us, event | category | flops | bytes accessed | tf_op | source)
XLA Modules:
  0.0 270.7 jit_solution(11244828980687982373)
XLA Ops:
  0.6 1.2 slice_reduce_fusion.12
  1.9 1.7 slice_reduce_fusion.4
  3.5 1.3 fusion.53
  13.7 6.5 %shard_map.87 = (f32[20,384]{1,0:T(8,128)}, f32[20,384]{1,0:T(8,128)}, f32[20,48]{1,0:T(8,128)}, f32[20,48]{1,0:T(8,128)}) custom-call(f32[20,384]{1,0:T(8,128)} %reshape_squeeze.52.refs_0_, f32[20,384]{1,0:T(8,128)} %reshape_squeeze.53.refs_1_, f32[20,48]{1,0:T(8,128)} %reshape_squeeze.54.refs_2_, f32[20,48]{1,0:T(8,128)} %reshape_squeeze.55.refs_3_), custom_call_target="tpu_custom_call" | custom-call | tf_op jit(solution)/shard_map/pallas_call | solution.py:80
  20.2 1.4 reshape.229.refs_3_
  21.6 1.4 reshape.230.refs_4_
  23.0 5.5 %shard_map.88 = f32[5,4,48,384]{3,2,1,0:T(8,128)} custom-call(f32[5,4,48,384]{3,2,1,0:T(8,128)} %refs_0_.2, f32[2,4,48,384]{3,2,1,0:T(8,128)} %refs_1_.4, f32[4,48,384]{2,1,0:T(8,128)} %refs_2_.4, f32[5,4,1,384]{3,2,1,0:T(1,128)} %reshape.229.refs_3_, f32[5,4,1,384]{3,2,1,0:T(1,128)} %reshape.230.refs_4_, f32[20,48]{1,0:T(8,128)} %get-tuple-element.74.refs_5_, ...), custom_call_target="tpu_custom_call" | custom-call | tf_op jit(solution)/shard_map/pallas_call | solution.py:377
  28.5 5.8 %pad_dynamic-slice_fusion = (f32[5,4,48,130]{3,2,1,0:T(8,128)}, f32[5,4,48,130]{3,2,1,0:T(8,128)}, f32[5,4,48,130]{3,2,1,0:T(8,128)}, f32[5,4,48,130]{3,2,1,0:T(8,128)}, f32[5,4,48,130]{3,2,1,0:T(8,128)S(1)}) fusion(s32[]{:T(128)S(6)} %select_n.309, f32[5,4,48,384]{3,2,1,0:T(8,128)} %shard_map.88, s32[]{:T(128)S(6)} %select_n.306, s32[]{:T(128)S(6)} %select_n.307, ...), kind=kLoop, calls=%fused_computation.9 | loop fusion | bytes 3970580 | tf_op jit(solution)/shard_map/dynamic_slice | solution.py:441
  34.3 1.4 stack_reshape.15
  35.7 1.1 constant_dynamic-update-slice_fusion.4
  36.7 2.6 stack_reshape.16
  39.3 2.6 stack_reshape.17
  41.9 2.6 stack_reshape.18
  44.5 2.6 stack_reshape.19
  47.1 1.1 constant_dynamic-update-slice_fusion.3
  48.2 1.1 constant_dynamic-update-slice_fusion.2
  49.3 1.1 constant_dynamic-update-slice_fusion.1
  55.5 29.3 %conditional.2 = ((f32[5,4,48,130]{3,2,1,0:T(8,128)}, f32[5,4,48,130]{3,2,1,0:T(8,128)})) conditional(s32[]{:T(128)} %clamp.7, (f32[5,975,128]{2,1,0:T(8,128)S(1)}, f32[5,4,48,130]{3,2,1,0:T(8,128)S(1)}, f32[5,4,48,130]{3,2,1,0:T(8,128)}) %tuple.42, (f32[5,975,128]{2,1,0:T(8,128)S(1)}, f32[5,4,48,130]{3,2,1,0:T(8,128)S(1)}, ...), branch_computations={%region_0.1_spmd, %region_1.2_spmd, %region_2.3_spmd} | conditional | flops 374405 | bytes 11481714 | solution.py:458
  55.5 21.5 %branch_0_fun.2 = f32[2,975,128]{2,1,0:T(8,128)} custom-call(f32[5,975,128]{2,1,0:T(8,128)S(1)} %get-tuple-element.35.refs_0_), custom_call_target="tpu_custom_call" | custom-call | tf_op jit(solution)/shard_map/cond/branch_0_fun/pallas_call | solution.py:244
  77.1 2.1 fusion.48
  79.2 2.2 squeeze.16
  81.5 1.2 select_select_fusion
  82.6 2.2 reshape.210
  84.8 1.3 select_add_fusion
  86.1 0.9 pad_dynamic-slice_fusion.5
  87.0 0.9 bitcast_dynamic-update-slice_fusion.7
  87.9 0.9 bitcast_dynamic-update-slice_fusion.6
  88.8 0.9 bitcast_dynamic-update-slice_fusion.5
  89.7 0.9 bitcast_dynamic-update-slice_fusion.4
  90.5 0.9 bitcast_dynamic-update-slice_fusion.3
  91.4 0.9 bitcast_dynamic-update-slice_fusion.2
  92.3 0.9 bitcast_dynamic-update-slice_fusion.1
  93.2 0.9 bitcast_dynamic-update-slice_fusion
  94.1 6.9 %all-to-all-start = ((f32[8,5,4,18,130]{4,2,3,1,0:T(4,128)}), f32[8,5,4,18,130]{4,2,3,1,0:T(4,128)S(1)}, u32[]{:S(2)}, u32[]{:S(2)}) async-start(f32[8,5,4,18,130]{4,2,3,1,0:T(4,128)} %bitcast_dynamic-update-slice_fusion), calls=%async_computation | async-start | bytes 5898240 | tf_op jit(solution)/shard_map/all_to_all | solution.py:474
  101.1 1.2 slice_reduce_fusion.14
  102.3 1.7 slice_reduce_fusion.6
  107.7 28.9 %shard_map.86 = (f32[20,384]{1,0:T(8,128)}, f32[20,384]{1,0:T(8,128)}, f32[20,48]{1,0:T(8,128)}, f32[20,48]{1,0:T(8,128)}) custom-call(f32[20,384]{1,0:T(8,128)} %reshape_squeeze.48.refs_0_, f32[20,384]{1,0:T(8,128)} %reshape_squeeze.49.refs_1_, f32[20,48]{1,0:T(8,128)} %reshape_squeeze.50.refs_2_, f32[20,48]{1,0:T(8,128)} %reshape_squeeze.51.refs_3_), custom_call_target="tpu_custom_call" | custom-call | tf_op jit(solution)/shard_map/pallas_call | solution.py:80
  136.6 1.4 reshape.227.refs_3_
  138.0 1.4 reshape.228.refs_4_
  140.9 0.8 reduce_sum.9
  141.7 1.0 convolution_bitcast_fusion
  142.7 2.9 %fusion.1.refs_7_ = f32[5,4,48,384]{3,2,1,0:T(8,128)} fusion(f32[5,4,48,130]{3,2,1,0:T(8,128)S(1)} %convolution_bitcast_fusion, f32[384]{0:T(512)S(1)} %get-tuple-element.146, s32[384]{0:T(512)S(1)} %get-tuple-element.152, f32[384]{0:T(512)S(1)} %get-tuple-element.147, s32[384]{0:T(512)S(1)} %add_select_fusion, f32[384]{0:T(512)S(1)} %compare_select_fusion.2, ...), kind=kOutput, calls=%fused_computation.47 | convolution fusion | flops 575477760 | bytes 1982976 | tf_op jit(solution)/shard_map/flac,bc->flab/dot_general | solution.py:153
  145.6 5.9 %shard_map.89.refs_0_ = f32[5,4,48,384]{3,2,1,0:T(8,128)} custom-call(f32[5,4,48,384]{3,2,1,0:T(8,128)} %refs_0_.3, f32[2,4,48,384]{3,2,1,0:T(8,128)} %refs_1_.7, f32[4,48,384]{2,1,0:T(8,128)} %refs_2_.7, f32[5,4,1,384]{3,2,1,0:T(1,128)} %reshape.227.refs_3_, f32[5,4,1,384]{3,2,1,0:T(1,128)} %reshape.228.refs_4_, f32[20,48]{1,0:T(8,128)} %get-tuple-element.70.refs_5_, ...), custom_call_target="tpu_custom_call" | custom-call | tf_op jit(solution)/shard_map/pallas_call | solution.py:377
  151.5 1.2 slice_reduce_fusion.10
  152.7 1.7 slice_reduce_fusion.2
  156.8 8.4 %shard_map.90 = (f32[20,384]{1,0:T(8,128)}, f32[20,384]{1,0:T(8,128)}, f32[20,48]{1,0:T(8,128)}, f32[20,48]{1,0:T(8,128)}) custom-call(f32[20,384]{1,0:T(8,128)} %reshape_squeeze.56.refs_0_, f32[20,384]{1,0:T(8,128)} %reshape_squeeze.57.refs_1_, f32[20,48]{1,0:T(8,128)} %reshape_squeeze.58.refs_2_, f32[20,48]{1,0:T(8,128)} %reshape_squeeze.59.refs_3_), custom_call_target="tpu_custom_call" | custom-call | tf_op jit(solution)/shard_map/pallas_call | solution.py:80
  165.3 1.4 reshape.231.refs_3_
  166.7 1.4 reshape.232.refs_4_
  168.1 5.9 %shard_map.91.refs_0_ = f32[5,4,48,384]{3,2,1,0:T(8,128)} custom-call(f32[5,4,48,384]{3,2,1,0:T(8,128)} %shard_map.89.refs_0_, f32[2,4,48,384]{3,2,1,0:T(8,128)} %refs_1_.7, f32[4,48,384]{2,1,0:T(8,128)} %refs_2_.7, f32[5,4,1,384]{3,2,1,0:T(1,128)} %reshape.231.refs_3_, f32[5,4,1,384]{3,2,1,0:T(1,128)} %reshape.232.refs_4_, ...), custom_call_target="tpu_custom_call" | custom-call | tf_op jit(solution)/shard_map/pallas_call | solution.py:377
  174.0 1.2 slice_reduce_fusion.8
  175.2 1.7 slice_reduce_fusion
  179.4 7.3 %shard_map.92 = (f32[20,384]{1,0:T(8,128)}, f32[20,384]{1,0:T(8,128)}, f32[20,48]{1,0:T(8,128)}, f32[20,48]{1,0:T(8,128)}) custom-call(f32[20,384]{1,0:T(8,128)} %reshape_squeeze.60.refs_0_, f32[20,384]{1,0:T(8,128)} %reshape_squeeze.61.refs_1_, f32[20,48]{1,0:T(8,128)} %reshape_squeeze.62.refs_2_, f32[20,48]{1,0:T(8,128)} %reshape_squeeze.63.refs_3_), custom_call_target="tpu_custom_call" | custom-call | tf_op jit(solution)/shard_map/pallas_call | solution.py:80
  186.7 1.4 reshape.233.refs_3_
  188.1 1.4 reshape.234.refs_4_
  189.5 5.9 %shard_map.93 = f32[5,4,48,384]{3,2,1,0:T(8,128)} custom-call(f32[5,4,48,384]{3,2,1,0:T(8,128)} %shard_map.91.refs_0_, f32[2,4,48,384]{3,2,1,0:T(8,128)} %refs_1_.7, f32[4,48,384]{2,1,0:T(8,128)} %refs_2_.7, f32[5,4,1,384]{3,2,1,0:T(1,128)} %reshape.233.refs_3_, f32[5,4,1,384]{3,2,1,0:T(1,128)} %reshape.234.refs_4_, f32[20,48]{1,0:T(8,128)} %get-tuple-element.84.refs_5_, ...), custom_call_target="tpu_custom_call" | custom-call | tf_op jit(solution)/shard_map/pallas_call | solution.py:377
  195.4 2.2 fusion.9
  197.6 1.0 convolution_multiply_fusion
  198.5 20.9 %shard_map.94 = f32[8,20,16,128]{3,2,1,0:T(8,128)} custom-call(f32[20,16,128]{2,1,0:T(8,128)} %bitcast.84), custom_call_target="tpu_custom_call" | custom-call | tf_op jit(solution)/shard_map/pallas_call | solution.py:299
  219.4 1.5 copy.28
  221.0 46.7 %conditional.3 = (f32[5,4,48,128]{3,2,1,0:T(8,128)S(1)}, f32[5,4,48,128]{3,2,1,0:T(8,128)S(1)}, f32[5,4,48,128]{3,2,1,0:T(8,128)S(1)}, f32[5,4,48,128]{3,2,1,0:T(8,128)S(1)}, f32[5,4,48,128]{3,2,1,0:T(8,128)S(1)}) conditional(s32[]{:T(128)} %clamp.6, f32[5,4,48,128]{3,2,1,0:T(8,128)S(1)} %pad_dynamic-slice_fusion.13, ...), branch_computations={%region_4.5_spmd, %region_5.6_spmd} | conditional | flops 245764 | bytes 7372880 | solution.py:520
  221.2 44.6 %branch_0_fun.3 = f32[5,960,128]{2,1,0:T(8,128)} custom-call(f32[1,960,128]{2,1,0:T(8,128)S(1)} %bitcast.70), custom_call_target="tpu_custom_call" | custom-call | tf_op jit(solution)/shard_map/cond/branch_0_fun/pallas_call | solution.py:244
  265.8 1.8 fusion.51
  267.9 1.2 copy-done.4
  269.1 1.6 dynamic-slice_select_fusion
  (44 shorter events, 12.4 us)
Async XLA Ops:
  47.1 3.3 %copy-start.5 = (f32[1,975,128]{2,1,0:T(8,128)S(1)}, f32[1,975,128]{2,1,0:T(8,128)}, u32[]{:S(2)}) copy-start(f32[1,975,128]{2,1,0:T(8,128)} %stack_reshape.19) | copy-start | bytes 1497604
  77.1 4.4 %copy-start.2 = (f32[5,4,48,130]{3,2,1,0:T(8,128)S(1)}, f32[5,4,48,130]{3,2,1,0:T(8,128)}, u32[]{:S(2)}) copy-start(f32[5,4,48,130]{3,2,1,0:T(8,128)} %get-tuple-element.33) | copy-start | bytes 1497604 | tf_op jit(solution)/shard_map/cond
  94.1 46.9 %all-to-all-start = ((f32[8,5,4,18,130]{4,2,3,1,0:T(4,128)}), f32[8,5,4,18,130]{4,2,3,1,0:T(4,128)S(1)}, u32[]{:S(2)}, u32[]{:S(2)}) async-start(f32[8,5,4,18,130]{4,2,3,1,0:T(4,128)} %bitcast_dynamic-update-slice_fusion), calls=%async_computation | async-start | bytes 5898240 | tf_op jit(solution)/shard_map/all_to_all | solution.py:474
  267.7 1.4 copy-start.4

commit v10 on v9

--- a/solution.py
+++ b/solution.py
@@ -64,19 +64,20 @@
             targets[number][...] = jnp.zeros(targets[number].shape, targets[number].dtype)
 
 
-def neighbours(cells, identity):
-    rows = lax.axis_size("gx")
-    cols = lax.axis_size("gy")
-    x = lax.axis_index("gx")
-    y = lax.axis_index("gy")
+def edges(cells):
     fields, levels, height, width = cells.shape
     planes = fields * levels
-    sources = (
+    return (
         cells[:, :, -1, :].reshape(planes, width),
         cells[:, :, 0, :].reshape(planes, width),
         cells[:, :, :, -1].reshape(planes, height),
         cells[:, :, :, 0].reshape(planes, height),
     )
+
+
+def neighbours(sources, identity):
+    rows = lax.axis_size("gx")
+    cols = lax.axis_size("gy")
     received = pl.pallas_call(
         lambda *refs: halo_kernel(rows, cols, *refs),
         out_shape=tuple(jax.ShapeDtypeStruct(part.shape, part.dtype) for part in sources),
@@ -85,10 +86,7 @@
         scratch_shapes=[pltpu.SemaphoreType.DMA((4,)), pltpu.SemaphoreType.DMA((4,))],
         compiler_params=pltpu.CompilerParams(collective_id=identity, has_side_effects=True),
     )(*sources)
-    western, eastern, southern, northern = received
-    western = western.reshape(fields, levels, 1, width)
-    eastern = eastern.reshape(fields, levels, 1, width)
-    return western, eastern, southern, northern
+    return received
 
 
 def update(values, halo, velocity, mixing):
@@ -311,7 +309,8 @@
 
 def stencil_kernel(relaxed, *refs):
     if relaxed:
-        (values, velocity, mixing, western, eastern, southern, northern, forcing, weight, out) = refs
+        (values, velocity, mixing, western, eastern, southern, northern, forcing, weight) = refs[:9]
+        out, last_row, first_row, last_col, first_col = refs[9:]
     else:
         (values, velocity, mixing, western, eastern, southern, northern, out) = refs
     levels, height, width = values.shape[1:]
@@ -332,10 +331,16 @@
         eye, northern[pl.ds(first, levels), :], numbers, precision=exact,
         preferred_element_type=jnp.float32,
     )
+    picks = lax.broadcasted_iota(jnp.int32, (8, width), 1)
+    chosen = lax.broadcasted_iota(jnp.int32, (8, width), 0)
+    ends = ((chosen == 0) & (picks == 0)) | ((chosen == 1) & (picks == width - 1))
+    ends = ends.astype(jnp.float32)
     for level in range(levels):
         q = values[0, level]
-        west = jnp.where(row == 0, western[0, level], pltpu.roll(q, 1, 0))
-        east = jnp.where(row == height - 1, eastern[0, level], pltpu.roll(q, height - 1, 0))
+        west_row = western[pl.ds(first + level, 1), :]
+        east_row = eastern[pl.ds(first + level, 1), :]
+        west = jnp.where(row == 0, west_row, pltpu.roll(q, 1, 0))
+        east = jnp.where(row == height - 1, east_row, pltpu.roll(q, height - 1, 0))
         south = jnp.where(col == 0, south_cols[:, level:level + 1], pltpu.roll(q, 1, 1))
         north = jnp.where(
             col == width - 1, north_cols[:, level:level + 1], pltpu.roll(q, width - 1, 1)
@@ -351,6 +356,13 @@
         moved = q - upwind + mixing[level] * (east + west + north + south - 4.0 * q)
         if relaxed:
             moved = moved + weight[...] * (forcing[0, level] - moved)
+            last_row[pl.ds(first + level, 1), :] = moved[height - 1:height, :]
+            first_row[pl.ds(first + level, 1), :] = moved[0:1, :]
+            sides = lax.dot_general(
+                ends, moved, numbers, precision=exact, preferred_element_type=jnp.float32
+            )
+            first_col[pl.ds(first + level, 1), :] = sides[0:1, :]
+            last_col[pl.ds(first + level, 1), :] = sides[1:2, :]
         out[0, level] = moved
 
 
@@ -358,7 +370,7 @@
     fields, levels, height, width = values.shape
     west_row, east_row, south_col, north_col = halo
     plane = pl.BlockSpec((1, levels, height, width), lambda f: (f, 0, 0, 0))
-    edge_row = pl.BlockSpec((1, levels, 1, width), lambda f: (f, 0, 0, 0))
+    edge_row = pl.BlockSpec((fields * levels, width), lambda f: (0, 0))
     edge_col = pl.BlockSpec((fields * levels, height), lambda f: (0, 0))
     operands = [values, velocity, mixing, west_row, east_row, south_col, north_col]
     specs = [
@@ -371,15 +383,21 @@
         edge_col,
     ]
     relaxed = forcing is not None
+    out_shape = jax.ShapeDtypeStruct(values.shape, values.dtype)
+    out_specs = plane
     if relaxed:
         operands += [forcing, weight]
         specs += [plane, pl.BlockSpec(weight.shape, lambda f: (0, 0))]
+        rows_shape = jax.ShapeDtypeStruct((fields * levels, width), values.dtype)
+        cols_shape = jax.ShapeDtypeStruct((fields * levels, height), values.dtype)
+        out_shape = (out_shape, rows_shape, rows_shape, cols_shape, cols_shape)
+        out_specs = (plane, edge_row, edge_row, edge_col, edge_col)
     return pl.pallas_call(
         lambda *refs: stencil_kernel(relaxed, *refs),
-        out_shape=jax.ShapeDtypeStruct(values.shape, values.dtype),
+        out_shape=out_shape,
         grid=(fields,),
         in_specs=specs,
-        out_specs=plane,
+        out_specs=out_specs,
     )(*operands)
 
 
@@ -417,7 +435,7 @@
     offset = column_anchor - 1 - base_column
 
     parent_next = stencil(
-        parent_fields, neighbours(parent_fields, 2), parent_velocity, parent_mixing
+        parent_fields, neighbours(edges(parent_fields), 2), parent_velocity, parent_mixing
     )
 
     margin = parent_columns - span_columns
@@ -481,9 +499,10 @@
         row_global, column_global, row_devices * nest_rows, column_devices * nest_columns
     )
     state = nest_fields
+    sides = edges(state)
     for substep in range(SUBSTEPS):
-        state = stencil(
-            state, neighbours(state, 3 + substep), nest_velocity, nest_mixing, forcing, weight
+        state, *sides = stencil(
+            state, neighbours(sides, 3 + substep), nest_velocity, nest_mixing, forcing, weight
         )
 
     coarse = block_mean(state)

time: 273 us -> 251 us (0.919)
  local copies, waits for them, and re-layouts: 75 us -> 53.1 us
    reshape x8 -> x0, local copies, waits for them, and re-layouts: 11.2 us -> none  [the longest x4 5.62 us: neighbours(): western = western.reshape(fields, levels, 1, width)]
    slice x8 -> x4, local copies, waits for them, and re-layouts: 11.6 us -> 5.8 us  [the longest x2 3.33 us: edges(): cells[:, :, :, 0].reshape(planes, height)]
    another operation x16 -> x8, local copies, waits for them, and re-layouts: 9.84 us -> 4.93 us  [the longest x2 1.26 us: edges(): cells[:, :, -1, :].reshape(planes, width)]
  transfers between devices with their start and end apart: 1 -> 1, of which waited for: 0 -> 0; matrix products, arithmetic and copies ran while one was open for 4% -> 3% of each run, Pallas kernels for 11% -> 12%
where the time goes in v10:
time: 251 us; the launch traced here: 250 us
  Pallas kernels  163 us (65%)
  local copies, waits for them, and re-layouts  53.1 us (21%)
  between operations  12.2 us (5%)
  other arithmetic  7.05 us (3%)
  matrix products  6.96 us (3%)
  starting transfers between devices  6.93 us (3%)
    pallas_call x2, Pallas kernels, exchange(): pl.pallas_call(lambda *refs: exchange_kernel(axis, remote, *refs), out_sh...  66.1 us
    pallas_call x4, Pallas kernels, neighbours(): pl.pallas_call(lambda *refs: halo_kernel(rows, cols, *refs), out_shape=tu...  51.2 us
    pallas_call x4, Pallas kernels, stencil(): pl.pallas_call(lambda *refs: stencil_kernel(relaxed, *refs), out_shape=ou...  25 us
    pallas_call x1, Pallas kernels, gather(): pl.pallas_call(lambda *refs: gather_kernel(axis, count, *refs), out_shape...  20.9 us
    unnamed x19, local copies, waits for them, and re-layouts  11.9 us
    another operation x6, local copies, waits for them, and re-layouts, per_device(): stacked_pieces = jnp.stack(pieces)  11.7 us
    all_to_all x1, starting transfers between devices, per_device(): lax.all_to_all(stacked, 'gx', split_axis=0, concat_axis=0, tiled=True)  6.93 us
    dynamic_slice x1, local copies, waits for them, and re-layouts, per_device(): piece = lax.dynamic_slice_in_dim(wide, start, relay_columns, axis=3)  5.82 us
  transfers between devices with their start and end apart: 1, of which 0 were waited for; matrix products, arithmetic and copies ran while one was open for 3% of the time, Pallas kernels for 12%

profile of v10, /device:TPU:73, one launch (start us, length us, event | category | flops | bytes accessed | tf_op | source)
XLA Modules:
  0.0 249.6 jit_solution(14876050725988897215)
XLA Ops:
  0.6 1.2 slice_reduce_fusion.4
  1.9 1.7 slice_reduce_fusion
  3.5 1.3 fusion.53
  10.3 0.6 reshape_squeeze.28.refs_0_
  11.0 0.6 reshape_squeeze.29.refs_1_
  11.6 0.6 reshape_squeeze.30.refs_2_
  12.2 0.6 reshape_squeeze.31.refs_3_
  12.8 6.5 %shard_map.87 = (f32[20,384]{1,0:T(8,128)}, f32[20,384]{1,0:T(8,128)}, f32[20,48]{1,0:T(8,128)}, f32[20,48]{1,0:T(8,128)}) custom-call(f32[20,384]{1,0:T(8,128)} %reshape_squeeze.28.refs_0_, f32[20,384]{1,0:T(8,128)} %reshape_squeeze.29.refs_1_, f32[20,48]{1,0:T(8,128)} %reshape_squeeze.30.refs_2_, f32[20,48]{1,0:T(8,128)} %reshape_squeeze.31.refs_3_), custom_call_target="tpu_custom_call" | custom-call | tf_op jit(solution)/shard_map/pallas_call | solution.py:81
  19.3 5.4 %shard_map.88 = f32[5,4,48,384]{3,2,1,0:T(8,128)} custom-call(f32[5,4,48,384]{3,2,1,0:T(8,128)} %refs_0_.2, f32[2,4,48,384]{3,2,1,0:T(8,128)} %refs_1_.4, f32[4,48,384]{2,1,0:T(8,128)} %refs_2_.4, f32[20,384]{1,0:T(8,128)} %get-tuple-element.83.refs_3_, f32[20,384]{1,0:T(8,128)} %get-tuple-element.84.refs_4_, f32[20,48]{1,0:T(8,128)} %get-tuple-element.85.refs_5_, ...), custom_call_target="tpu_custom_call" | custom-call | tf_op jit(solution)/shard_map/pallas_call | solution.py:395
  24.7 5.8 %pad_dynamic-slice_fusion = (f32[5,4,48,130]{3,2,1,0:T(8,128)}, f32[5,4,48,130]{3,2,1,0:T(8,128)}, f32[5,4,48,130]{3,2,1,0:T(8,128)}, f32[5,4,48,130]{3,2,1,0:T(8,128)}, f32[5,4,48,130]{3,2,1,0:T(8,128)S(1)}) fusion(s32[]{:T(128)S(6)} %select_n.309, f32[5,4,48,384]{3,2,1,0:T(8,128)} %shard_map.88, s32[]{:T(128)S(6)} %select_n.306, s32[]{:T(128)S(6)} %select_n.307, ...), kind=kLoop, calls=%fused_computation.9 | loop fusion | bytes 3970580 | tf_op jit(solution)/shard_map/dynamic_slice | solution.py:459
  30.6 1.4 stack_reshape.15
  31.9 1.1 constant_dynamic-update-slice_fusion.4
  33.0 2.6 %stack_reshape.16 = f32[1,975,128]{2,1,0:T(8,128)} reshape(f32[5,4,48,130]{3,2,1,0:T(8,128)} %get-tuple-element.146) | data formatting | bytes 998400 | tf_op jit(solution)/shard_map/stack;reshape | solution.py:462
  35.6 2.6 %stack_reshape.17 = f32[1,975,128]{2,1,0:T(8,128)} reshape(f32[5,4,48,130]{3,2,1,0:T(8,128)} %get-tuple-element.147) | data formatting | bytes 998400 | tf_op jit(solution)/shard_map/stack;reshape | solution.py:462
  38.1 2.6 %stack_reshape.18 = f32[1,975,128]{2,1,0:T(8,128)} reshape(f32[5,4,48,130]{3,2,1,0:T(8,128)} %get-tuple-element.148) | data formatting | bytes 998400 | tf_op jit(solution)/shard_map/stack;reshape | solution.py:462
  40.7 2.6 %stack_reshape.19 = f32[1,975,128]{2,1,0:T(8,128)} reshape(f32[5,4,48,130]{3,2,1,0:T(8,128)} %get-tuple-element.145) | data formatting | bytes 998400 | tf_op jit(solution)/shard_map/stack;reshape | solution.py:462
  43.3 1.1 constant_dynamic-update-slice_fusion.3
  44.5 1.1 constant_dynamic-update-slice_fusion.2
  45.5 1.1 constant_dynamic-update-slice_fusion.1
  51.8 29.3 %conditional.2 = ((f32[5,4,48,130]{3,2,1,0:T(8,128)}, f32[5,4,48,130]{3,2,1,0:T(8,128)})) conditional(s32[]{:T(128)} %clamp.7, (f32[5,975,128]{2,1,0:T(8,128)S(1)}, f32[5,4,48,130]{3,2,1,0:T(8,128)S(1)}, f32[5,4,48,130]{3,2,1,0:T(8,128)}) %tuple.42, (f32[5,975,128]{2,1,0:T(8,128)S(1)}, f32[5,4,48,130]{3,2,1,0:T(8,128)S(1)}, ...), branch_computations={%region_0.1_spmd, %region_1.2_spmd, %region_2.3_spmd} | conditional | flops 374405 | bytes 11481714 | solution.py:476
  51.8 21.5 %branch_0_fun.2 = f32[2,975,128]{2,1,0:T(8,128)} custom-call(f32[5,975,128]{2,1,0:T(8,128)S(1)} %get-tuple-element.35.refs_0_), custom_call_target="tpu_custom_call" | custom-call | tf_op jit(solution)/shard_map/cond/branch_0_fun/pallas_call | solution.py:242
  73.4 2.1 fusion.48
  75.5 2.2 squeeze.16
  77.8 1.2 select_select_fusion
  78.9 2.2 reshape.194
  81.1 1.3 select_add_fusion
  82.4 0.9 pad_dynamic-slice_fusion.5
  83.3 0.9 bitcast_dynamic-update-slice_fusion.7
  84.2 0.9 bitcast_dynamic-update-slice_fusion.6
  85.1 0.9 bitcast_dynamic-update-slice_fusion.5
  86.0 0.9 bitcast_dynamic-update-slice_fusion.4
  86.9 0.9 bitcast_dynamic-update-slice_fusion.3
  87.8 0.9 bitcast_dynamic-update-slice_fusion.2
  88.7 0.9 bitcast_dynamic-update-slice_fusion.1
  89.6 0.9 bitcast_dynamic-update-slice_fusion
  90.5 6.9 %all-to-all-start = ((f32[8,5,4,18,130]{4,2,3,1,0:T(4,128)}), f32[8,5,4,18,130]{4,2,3,1,0:T(4,128)S(1)}, u32[]{:S(2)}, u32[]{:S(2)}) async-start(f32[8,5,4,18,130]{4,2,3,1,0:T(4,128)} %bitcast_dynamic-update-slice_fusion), calls=%async_computation | async-start | bytes 5898240 | tf_op jit(solution)/shard_map/all_to_all | solution.py:492
  97.4 1.2 slice_reduce_fusion.6
  98.7 1.7 slice_reduce_fusion.2
  101.0 0.6 compare_and_fusion
  101.6 0.6 reshape_squeeze.24.refs_0_
  102.3 0.6 reshape_squeeze.25.refs_1_
  102.9 0.6 reshape_squeeze.26.refs_2_
  103.5 0.6 reshape_squeeze.27.refs_3_
  104.1 28.9 %shard_map.86 = (f32[20,384]{1,0:T(8,128)}, f32[20,384]{1,0:T(8,128)}, f32[20,48]{1,0:T(8,128)}, f32[20,48]{1,0:T(8,128)}) custom-call(f32[20,384]{1,0:T(8,128)} %reshape_squeeze.24.refs_0_, f32[20,384]{1,0:T(8,128)} %reshape_squeeze.25.refs_1_, f32[20,48]{1,0:T(8,128)} %reshape_squeeze.26.refs_2_, f32[20,48]{1,0:T(8,128)} %reshape_squeeze.27.refs_3_), custom_call_target="tpu_custom_call" | custom-call | tf_op jit(solution)/shard_map/pallas_call | solution.py:81
  132.9 0.6 fusion.43
  133.7 0.7 multiply_add_fusion.refs_8_
  134.4 0.8 reduce_sum.9
  135.2 1.0 convolution_bitcast_fusion
  136.2 2.9 %fusion.1.refs_7_ = f32[5,4,48,384]{3,2,1,0:T(8,128)} fusion(f32[5,4,48,130]{3,2,1,0:T(8,128)S(1)} %convolution_bitcast_fusion, f32[384]{0:T(512)S(1)} %get-tuple-element.160, s32[384]{0:T(512)S(1)} %get-tuple-element.166, f32[384]{0:T(512)S(1)} %get-tuple-element.161, s32[384]{0:T(512)S(1)} %add_select_fusion, f32[384]{0:T(512)S(1)} %compare_select_fusion.2, ...), kind=kOutput, calls=%fused_computation.43 | convolution fusion | flops 575477760 | bytes 1982976 | tf_op jit(solution)/shard_map/flac,bc->flab/dot_general | solution.py:151
  139.0 6.5 %shard_map.89 = (f32[5,4,48,384]{3,2,1,0:T(8,128)}, f32[20,384]{1,0:T(8,128)}, f32[20,384]{1,0:T(8,128)}, f32[20,48]{1,0:T(8,128)}, f32[20,48]{1,0:T(8,128)}) custom-call(f32[5,4,48,384]{3,2,1,0:T(8,128)} %refs_0_.3, f32[2,4,48,384]{3,2,1,0:T(8,128)} %refs_1_.7, f32[4,48,384]{2,1,0:T(8,128)} %refs_2_.7, f32[20,384]{1,0:T(8,128)} %get-tuple-element.79.refs_3_, ...), custom_call_target="tpu_custom_call" | custom-call | tf_op jit(solution)/shard_map/pallas_call | solution.py:395
  145.5 8.5 %shard_map.90 = (f32[20,384]{1,0:T(8,128)}, f32[20,384]{1,0:T(8,128)}, f32[20,48]{1,0:T(8,128)}, f32[20,48]{1,0:T(8,128)}) custom-call(f32[20,384]{1,0:T(8,128)} %get-tuple-element.90.refs_0_, f32[20,384]{1,0:T(8,128)} %get-tuple-element.91.refs_1_, f32[20,48]{1,0:T(8,128)} %get-tuple-element.92.refs_2_, f32[20,48]{1,0:T(8,128)} %get-tuple-element.93.refs_3_), custom_call_target="tpu_custom_call" | custom-call | tf_op jit(solution)/shard_map/pallas_call | solution.py:81
  154.0 6.5 %shard_map.91 = (f32[5,4,48,384]{3,2,1,0:T(8,128)}, f32[20,384]{1,0:T(8,128)}, f32[20,384]{1,0:T(8,128)}, f32[20,48]{1,0:T(8,128)}, f32[20,48]{1,0:T(8,128)}) custom-call(f32[5,4,48,384]{3,2,1,0:T(8,128)} %get-tuple-element.89.refs_0_, f32[2,4,48,384]{3,2,1,0:T(8,128)} %refs_1_.7, f32[4,48,384]{2,1,0:T(8,128)} %refs_2_.7, ...), custom_call_target="tpu_custom_call" | custom-call | tf_op jit(solution)/shard_map/pallas_call | solution.py:395
  160.6 7.4 %shard_map.92 = (f32[20,384]{1,0:T(8,128)}, f32[20,384]{1,0:T(8,128)}, f32[20,48]{1,0:T(8,128)}, f32[20,48]{1,0:T(8,128)}) custom-call(f32[20,384]{1,0:T(8,128)} %get-tuple-element.99.refs_0_, f32[20,384]{1,0:T(8,128)} %get-tuple-element.100.refs_1_, f32[20,48]{1,0:T(8,128)} %get-tuple-element.101.refs_2_, f32[20,48]{1,0:T(8,128)} %get-tuple-element.102.refs_3_), custom_call_target="tpu_custom_call" | custom-call | tf_op jit(solution)/shard_map/pallas_call | solution.py:81
  168.0 6.5 %shard_map.93 = (f32[5,4,48,384]{3,2,1,0:T(8,128)}, f32[20,384]{1,0:T(8,128)}, f32[20,384]{1,0:T(8,128)}, f32[20,48]{1,0:T(8,128)}, f32[20,48]{1,0:T(8,128)}) custom-call(f32[5,4,48,384]{3,2,1,0:T(8,128)} %get-tuple-element.98.refs_0_, f32[2,4,48,384]{3,2,1,0:T(8,128)} %refs_1_.7, f32[4,48,384]{2,1,0:T(8,128)} %refs_2_.7, ...), custom_call_target="tpu_custom_call" | custom-call | tf_op jit(solution)/shard_map/pallas_call | solution.py:395
  174.5 2.2 fusion.9
  176.7 0.9 convolution_multiply_fusion
  177.6 20.9 %shard_map.94 = f32[8,20,16,128]{3,2,1,0:T(8,128)} custom-call(f32[20,16,128]{2,1,0:T(8,128)} %bitcast.84), custom_call_target="tpu_custom_call" | custom-call | tf_op jit(solution)/shard_map/pallas_call | solution.py:297
  198.5 1.5 copy.28
  200.1 46.5 %conditional.3 = (f32[5,4,48,128]{3,2,1,0:T(8,128)S(1)}, f32[5,4,48,128]{3,2,1,0:T(8,128)S(1)}, f32[5,4,48,128]{3,2,1,0:T(8,128)S(1)}, f32[5,4,48,128]{3,2,1,0:T(8,128)S(1)}, f32[5,4,48,128]{3,2,1,0:T(8,128)S(1)}) conditional(s32[]{:T(128)} %clamp.6, f32[5,4,48,128]{3,2,1,0:T(8,128)S(1)} %pad_dynamic-slice_fusion.13, ...), branch_computations={%region_4.5_spmd, %region_5.6_spmd} | conditional | flops 245764 | bytes 7372880 | solution.py:539
  200.1 44.6 %branch_0_fun.3 = f32[5,960,128]{2,1,0:T(8,128)} custom-call(f32[1,960,128]{2,1,0:T(8,128)S(1)} %bitcast.70), custom_call_target="tpu_custom_call" | custom-call | tf_op jit(solution)/shard_map/cond/branch_0_fun/pallas_call | solution.py:242
  244.7 1.8 fusion.51
  246.5 0.1 broadcast_select_fusion.3
  246.8 1.2 copy-done.4
  248.0 1.6 dynamic-slice_select_fusion
  (24 shorter events, 0.5 us)
Async XLA Ops:
  43.3 3.3 %copy-start.5 = (f32[1,975,128]{2,1,0:T(8,128)S(1)}, f32[1,975,128]{2,1,0:T(8,128)}, u32[]{:S(2)}) copy-start(f32[1,975,128]{2,1,0:T(8,128)} %stack_reshape.19) | copy-start | bytes 1497604
  73.4 4.4 %copy-start.2 = (f32[5,4,48,130]{3,2,1,0:T(8,128)S(1)}, f32[5,4,48,130]{3,2,1,0:T(8,128)}, u32[]{:S(2)}) copy-start(f32[5,4,48,130]{3,2,1,0:T(8,128)} %get-tuple-element.33) | copy-start | bytes 1497604 | tf_op jit(solution)/shard_map/cond
  90.5 44.0 %all-to-all-start = ((f32[8,5,4,18,130]{4,2,3,1,0:T(4,128)}), f32[8,5,4,18,130]{4,2,3,1,0:T(4,128)S(1)}, u32[]{:S(2)}, u32[]{:S(2)}) async-start(f32[8,5,4,18,130]{4,2,3,1,0:T(4,128)} %bitcast_dynamic-update-slice_fusion), calls=%async_computation | async-start | bytes 5898240 | tf_op jit(solution)/shard_map/all_to_all | solution.py:492
  246.6 1.4 copy-start.4

commit v11 on v10

--- a/solution.py
+++ b/solution.py
@@ -258,7 +258,7 @@
     return parts
 
 
-def gather_kernel(axis, count, source, target, send_sems, recv_sems):
+def gather_kernel(axis, count, spread, source, target, send_sems, recv_sems):
     me = lax.axis_index(axis)
     barrier = pltpu.get_barrier_semaphore()
     for delta in range(1, count):
@@ -269,7 +269,7 @@
     outgoing = []
     for delta in range(1, count):
         copy = pltpu.make_async_remote_copy(
-            src_ref=source,
+            src_ref=source.at[(me + delta) % count] if spread else source,
             dst_ref=target.at[me],
             send_sem=send_sems.at[delta - 1],
             recv_sem=recv_sems.at[delta - 1],
@@ -278,11 +278,11 @@
         )
         copy.start()
         outgoing.append(copy)
-    target[me] = source[...]
+    target[me] = source[me] if spread else source[...]
     for delta, copy in zip(range(1, count), outgoing):
         copy.wait_send()
         incoming = pltpu.make_async_remote_copy(
-            src_ref=source,
+            src_ref=source.at[0] if spread else source,
             dst_ref=target.at[(me + count - delta) % count],
             send_sem=send_sems.at[delta - 1],
             recv_sem=recv_sems.at[delta - 1],
@@ -292,11 +292,12 @@
         incoming.wait_recv()
 
 
-def gather(block, axis, identity):
+def gather(block, axis, identity, spread=False):
     count = lax.axis_size(axis)
+    shape = block.shape[1:] if spread else block.shape
     return pl.pallas_call(
-        lambda *refs: gather_kernel(axis, count, *refs),
-        out_shape=jax.ShapeDtypeStruct((count,) + block.shape, block.dtype),
+        lambda *refs: gather_kernel(axis, count, spread, *refs),
+        out_shape=jax.ShapeDtypeStruct((count,) + shape, block.dtype),
         in_specs=[pl.BlockSpec(memory_space=pltpu.VMEM)],
         out_specs=pl.BlockSpec(memory_space=pltpu.VMEM),
         scratch_shapes=[
@@ -489,8 +490,16 @@
         first = jnp.clip(first, -relay_rows, parent_rows) + relay_rows
         slots.append(lax.dynamic_slice_in_dim(padded, first, relay_rows, axis=2))
     stacked = jnp.stack(slots, axis=0)
-    received = lax.all_to_all(stacked, "gx", split_axis=0, concat_axis=0, tiled=True)
-    relay = jnp.sum(received, axis=0)
+    slot_shape = stacked.shape[1:]
+    planes = slot_shape[0] * slot_shape[1] * slot_shape[2]
+    lanes = relay_columns
+    while (planes * lanes) % 128:
+        lanes += 1
+    stacked = jnp.pad(stacked, ((0, 0),) * 4 + ((0, lanes - relay_columns),))
+    stacked = stacked.reshape(row_devices, planes * lanes // 128, 128)
+    received = gather(stacked, "gx", 10, spread=True)
+    received = received.reshape((row_devices,) + slot_shape[:3] + (lanes,))
+    relay = jnp.sum(received[..., :relay_columns], axis=0)
 
     forcing = refine(relay)
     row_global = row_rank * nest_rows + jnp.arange(nest_rows, dtype=jnp.int32)

time: 251 us -> 270 us (1.076)
  local copies, waits for them, and re-layouts: 53.1 us -> 68 us
  starting transfers between devices: 6.93 us -> 0 us
  Pallas kernels: 163 us -> 169 us
  other arithmetic: 7.05 us -> 10.4 us
    pallas_call x1 -> x2, Pallas kernels: 20.9 us -> 50.4 us  [gather(): pl.pallas_call(lambda *refs: gather_kernel(axis, count, spread, *refs), o...]
    pallas_call x4, Pallas kernels: 51.2 us -> 28 us  [neighbours(): pl.pallas_call(lambda *refs: halo_kernel(rows, cols, *refs), out_shape=tu...]
    reshape x0 -> x2, local copies, waits for them, and re-layouts: none -> 9.64 us  [the longest x1 4.96 us: per_device(): stacked = stacked.reshape(row_devices, planes * lanes // 128, 128)]
    all_to_all x1 -> x0, starting transfers between devices: 6.93 us -> none  [per_device(): lax.all_to_all(stacked, 'gx', split_axis=0, concat_axis=0, tiled=True)]
    pad x0 -> x1, local copies, waits for them, and re-layouts: none -> 4.5 us  [per_device(): stacked = jnp.pad(stacked, ((0, 0),) * 4 + ((0, lanes - relay_columns),))]
  transfers between devices with their start and end apart: 1 -> 0, of which waited for: 0 -> 0; matrix products, arithmetic and copies ran while one was open for 3% -> 0% of each run, Pallas kernels for 12% -> 0%
where the time goes in v11:
time: 270 us; the launch traced here: 268 us
  Pallas kernels  169 us (63%)
  local copies, waits for them, and re-layouts  68 us (25%)
  between operations  13.4 us (5%)
  other arithmetic  10.4 us (4%)
  matrix products  6.99 us (3%)
    pallas_call x2, Pallas kernels, exchange(): pl.pallas_call(lambda *refs: exchange_kernel(axis, remote, *refs), out_sh...  65.3 us
    pallas_call x2, Pallas kernels, gather(): pl.pallas_call(lambda *refs: gather_kernel(axis, count, spread, *refs), o...  50.4 us
    pallas_call x4, Pallas kernels, neighbours(): pl.pallas_call(lambda *refs: halo_kernel(rows, cols, *refs), out_shape=tu...  28 us
    pallas_call x4, Pallas kernels, stencil(): pl.pallas_call(lambda *refs: stencil_kernel(relaxed, *refs), out_shape=ou...  25 us
    unnamed x19, local copies, waits for them, and re-layouts  13.9 us
    another operation x6, local copies, waits for them, and re-layouts, per_device(): stacked_pieces = jnp.stack(pieces)  12.8 us
    dynamic_slice x1, local copies, waits for them, and re-layouts, per_device(): piece = lax.dynamic_slice_in_dim(wide, start, relay_columns, axis=3)  5.71 us

profile of v11, /device:TPU:73, one launch (start us, length us, event | category | flops | bytes accessed | tf_op | source)
XLA Modules:
  0.0 267.7 jit_solution(10541653553021001728)
XLA Ops:
  0.6 1.4 fusion.68
  8.7 1.2 slice_reduce_fusion.5
  10.0 0.6 reshape_squeeze.28.refs_0_
  10.6 0.6 reshape_squeeze.29.refs_1_
  11.2 1.7 slice_reduce_fusion.1
  14.1 6.5 %shard_map.87 = (f32[20,384]{1,0:T(8,128)}, f32[20,384]{1,0:T(8,128)}, f32[20,48]{1,0:T(8,128)}, f32[20,48]{1,0:T(8,128)}) custom-call(f32[20,384]{1,0:T(8,128)} %reshape_squeeze.28.refs_0_, f32[20,384]{1,0:T(8,128)} %reshape_squeeze.29.refs_1_, f32[20,48]{1,0:T(8,128)} %reshape_squeeze.30.refs_2_, f32[20,48]{1,0:T(8,128)} %reshape_squeeze.31.refs_3_), custom_call_target="tpu_custom_call" | custom-call | tf_op jit(solution)/shard_map/pallas_call | solution.py:81
  20.6 5.4 %shard_map.88 = f32[5,4,48,384]{3,2,1,0:T(8,128)} custom-call(f32[5,4,48,384]{3,2,1,0:T(8,128)} %refs_0_.2, f32[2,4,48,384]{3,2,1,0:T(8,128)} %refs_1_.4, f32[4,48,384]{2,1,0:T(8,128)} %refs_2_.4, f32[20,384]{1,0:T(8,128)} %get-tuple-element.83.refs_3_, f32[20,384]{1,0:T(8,128)} %get-tuple-element.84.refs_4_, f32[20,48]{1,0:T(8,128)} %get-tuple-element.85.refs_5_, ...), custom_call_target="tpu_custom_call" | custom-call | tf_op jit(solution)/shard_map/pallas_call | solution.py:396
  26.1 5.7 %pad_dynamic-slice_fusion = (f32[5,4,48,130]{3,2,1,0:T(8,128)}, f32[5,4,48,130]{3,2,1,0:T(8,128)}, f32[5,4,48,130]{3,2,1,0:T(8,128)}, f32[5,4,48,130]{3,2,1,0:T(8,128)}, f32[5,4,48,130]{3,2,1,0:T(8,128)S(1)}) fusion(s32[]{:T(128)S(6)} %select_n.309, f32[5,4,48,384]{3,2,1,0:T(8,128)} %shard_map.88, s32[]{:T(128)S(6)} %select_n.306, s32[]{:T(128)S(6)} %select_n.307, ...), kind=kLoop, calls=%fused_computation.9 | loop fusion | bytes 3970580 | tf_op jit(solution)/shard_map/dynamic_slice | solution.py:460
  31.8 1.4 stack_reshape.15
  33.1 1.1 constant_dynamic-update-slice_fusion.4
  34.2 2.6 stack_reshape.16
  36.8 1.1 constant_dynamic-update-slice_fusion.3
  37.9 2.6 stack_reshape.17
  40.4 1.1 constant_dynamic-update-slice_fusion.2
  41.5 2.6 stack_reshape.18
  44.1 1.1 constant_dynamic-update-slice_fusion.1
  45.2 2.6 stack_reshape.19
  47.8 1.1 constant_dynamic-update-slice_fusion
  48.8 29.3 %conditional.2 = ((f32[5,4,48,130]{3,2,1,0:T(8,128)}, f32[5,4,48,130]{3,2,1,0:T(8,128)})) conditional(s32[]{:T(128)} %clamp.7, (f32[5,975,128]{2,1,0:T(8,128)S(1)}, f32[5,4,48,130]{3,2,1,0:T(8,128)S(1)}, f32[5,4,48,130]{3,2,1,0:T(8,128)}) %tuple.42, (f32[5,975,128]{2,1,0:T(8,128)S(1)}, f32[5,4,48,130]{3,2,1,0:T(8,128)S(1)}, ...), branch_computations={%region_0.1_spmd, %region_1.2_spmd, %region_2.3_spmd} | conditional | flops 374405 | bytes 11481714 | solution.py:477
  48.9 21.5 %branch_0_fun.2 = f32[2,975,128]{2,1,0:T(8,128)} custom-call(f32[5,975,128]{2,1,0:T(8,128)S(1)} %get-tuple-element.35.refs_0_), custom_call_target="tpu_custom_call" | custom-call | tf_op jit(solution)/shard_map/cond/branch_0_fun/pallas_call | solution.py:242
  70.4 2.1 fusion.63
  72.5 2.2 squeeze.16
  74.8 1.2 select_select_fusion
  75.9 2.2 reshape.198
  78.1 1.3 select_add_fusion
  80.1 0.9 fusion.1
  81.6 0.9 fusion.3
  83.1 0.9 fusion.5
  84.6 0.9 fusion.7
  86.2 0.9 fusion.9
  87.7 0.9 fusion.11
  89.2 0.9 fusion.13
  90.7 0.9 fusion.15
  91.5 4.5 %pad.18 = f32[8,5,4,18,144]{4,3,2,1,0:T(8,128)} pad(f32[8,5,4,18,130]{4,3,2,1,0:T(8,128)} %fusion.15, f32[]{:T(128)} %constant.188.clone.1), padding=0_0x0_0x0_0x0_0x0_14 | pad | bytes 3156484 | tf_op jit(solution)/shard_map/jit(_pad)/pad | solution.py:498
  96.0 5.0 %reshape.209.refs_0_ = f32[8,405,128]{2,1,0:T(8,128)} reshape(f32[8,5,4,18,144]{4,3,2,1,0:T(8,128)} %pad.18) | data formatting | bytes 3317760 | tf_op jit(solution)/shard_map/reshape | solution.py:499
  101.0 27.7 %shard_map.89 = f32[8,405,128]{2,1,0:T(8,128)} custom-call(f32[8,405,128]{2,1,0:T(8,128)} %reshape.209.refs_0_), custom_call_target="tpu_custom_call" | custom-call | tf_op jit(solution)/shard_map/pallas_call | solution.py:298
  128.7 4.7 %reshape.210 = f32[8,5,4,18,144]{4,3,2,1,0:T(8,128)} reshape(f32[8,405,128]{2,1,0:T(8,128)} %shard_map.89) | data formatting | bytes 3317760 | tf_op jit(solution)/shard_map/reshape | solution.py:501
  133.4 2.5 slice_reduce_fusion
  136.0 1.0 convolution_bitcast_fusion
  137.0 2.9 %fusion.16.refs_7_ = f32[5,4,48,384]{3,2,1,0:T(8,128)} fusion(f32[5,4,48,130]{3,2,1,0:T(8,128)S(1)} %convolution_bitcast_fusion, f32[384]{0:T(512)S(1)} %get-tuple-element.154, s32[384]{0:T(512)S(1)} %get-tuple-element.153, f32[384]{0:T(512)S(1)} %get-tuple-element.155, s32[384]{0:T(512)S(1)} %get-tuple-element.152, f32[384]{0:T(512)S(1)} %compare_select_fusion.2, ...), kind=kOutput, calls=%fused_computation.51 | convolution fusion | flops 575477760 | bytes 1982976 | tf_op jit(solution)/shard_map/flac,bc->flab/dot_general | solution.py:151
  139.9 0.7 multiply_add_fusion.refs_8_
  140.8 0.6 reshape_squeeze.24.refs_0_
  141.5 0.6 reshape_squeeze.25.refs_1_
  143.8 7.8 %shard_map.86 = (f32[20,384]{1,0:T(8,128)}, f32[20,384]{1,0:T(8,128)}, f32[20,48]{1,0:T(8,128)}, f32[20,48]{1,0:T(8,128)}) custom-call(f32[20,384]{1,0:T(8,128)} %reshape_squeeze.24.refs_0_, f32[20,384]{1,0:T(8,128)} %reshape_squeeze.25.refs_1_, f32[20,48]{1,0:T(8,128)} %reshape_squeeze.26.refs_2_, f32[20,48]{1,0:T(8,128)} %reshape_squeeze.27.refs_3_), custom_call_target="tpu_custom_call" | custom-call | tf_op jit(solution)/shard_map/pallas_call | solution.py:81
  151.6 6.5 %shard_map.90 = (f32[5,4,48,384]{3,2,1,0:T(8,128)}, f32[20,384]{1,0:T(8,128)}, f32[20,384]{1,0:T(8,128)}, f32[20,48]{1,0:T(8,128)}, f32[20,48]{1,0:T(8,128)}) custom-call(f32[5,4,48,384]{3,2,1,0:T(8,128)} %refs_0_.3, f32[2,4,48,384]{3,2,1,0:T(8,128)} %refs_1_.7, f32[4,48,384]{2,1,0:T(8,128)} %refs_2_.7, f32[20,384]{1,0:T(8,128)} %get-tuple-element.79.refs_3_, ...), custom_call_target="tpu_custom_call" | custom-call | tf_op jit(solution)/shard_map/pallas_call | solution.py:396
  158.1 6.4 %shard_map.91 = (f32[20,384]{1,0:T(8,128)}, f32[20,384]{1,0:T(8,128)}, f32[20,48]{1,0:T(8,128)}, f32[20,48]{1,0:T(8,128)}) custom-call(f32[20,384]{1,0:T(8,128)} %get-tuple-element.90.refs_0_, f32[20,384]{1,0:T(8,128)} %get-tuple-element.91.refs_1_, f32[20,48]{1,0:T(8,128)} %get-tuple-element.92.refs_2_, f32[20,48]{1,0:T(8,128)} %get-tuple-element.93.refs_3_), custom_call_target="tpu_custom_call" | custom-call | tf_op jit(solution)/shard_map/pallas_call | solution.py:81
  164.5 6.5 %shard_map.92 = (f32[5,4,48,384]{3,2,1,0:T(8,128)}, f32[20,384]{1,0:T(8,128)}, f32[20,384]{1,0:T(8,128)}, f32[20,48]{1,0:T(8,128)}, f32[20,48]{1,0:T(8,128)}) custom-call(f32[5,4,48,384]{3,2,1,0:T(8,128)} %get-tuple-element.89.refs_0_, f32[2,4,48,384]{3,2,1,0:T(8,128)} %refs_1_.7, f32[4,48,384]{2,1,0:T(8,128)} %refs_2_.7, ...), custom_call_target="tpu_custom_call" | custom-call | tf_op jit(solution)/shard_map/pallas_call | solution.py:396
  171.0 7.4 %shard_map.93 = (f32[20,384]{1,0:T(8,128)}, f32[20,384]{1,0:T(8,128)}, f32[20,48]{1,0:T(8,128)}, f32[20,48]{1,0:T(8,128)}) custom-call(f32[20,384]{1,0:T(8,128)} %get-tuple-element.99.refs_0_, f32[20,384]{1,0:T(8,128)} %get-tuple-element.100.refs_1_, f32[20,48]{1,0:T(8,128)} %get-tuple-element.101.refs_2_, f32[20,48]{1,0:T(8,128)} %get-tuple-element.102.refs_3_), custom_call_target="tpu_custom_call" | custom-call | tf_op jit(solution)/shard_map/pallas_call | solution.py:81
  178.4 6.5 %shard_map.94 = (f32[5,4,48,384]{3,2,1,0:T(8,128)}, f32[20,384]{1,0:T(8,128)}, f32[20,384]{1,0:T(8,128)}, f32[20,48]{1,0:T(8,128)}, f32[20,48]{1,0:T(8,128)}) custom-call(f32[5,4,48,384]{3,2,1,0:T(8,128)} %get-tuple-element.98.refs_0_, f32[2,4,48,384]{3,2,1,0:T(8,128)} %refs_1_.7, f32[4,48,384]{2,1,0:T(8,128)} %refs_2_.7, ...), custom_call_target="tpu_custom_call" | custom-call | tf_op jit(solution)/shard_map/pallas_call | solution.py:396
  185.0 2.2 fusion.24
  187.1 0.9 convolution_multiply_fusion
  188.1 22.7 %shard_map.95 = f32[8,20,16,128]{3,2,1,0:T(8,128)} custom-call(f32[20,16,128]{2,1,0:T(8,128)} %bitcast.101), custom_call_target="tpu_custom_call" | custom-call | tf_op jit(solution)/shard_map/pallas_call | solution.py:298
  210.8 1.5 copy.9
  213.0 45.7 %conditional.3 = (f32[5,4,48,128]{3,2,1,0:T(8,128)S(1)}, f32[5,4,48,128]{3,2,1,0:T(8,128)S(1)}, f32[5,4,48,128]{3,2,1,0:T(8,128)S(1)}, f32[5,4,48,128]{3,2,1,0:T(8,128)S(1)}, f32[5,4,48,128]{3,2,1,0:T(8,128)S(1)}) conditional(s32[]{:T(128)} %clamp.6, f32[5,4,48,128]{3,2,1,0:T(8,128)S(1)} %pad_dynamic-slice_fusion.13, ...), branch_computations={%region_4.5_spmd, %region_5.6_spmd} | conditional | flops 245764 | bytes 7372880 | solution.py:548
  213.0 43.8 %branch_0_fun.3 = f32[5,960,128]{2,1,0:T(8,128)} custom-call(f32[1,960,128]{2,1,0:T(8,128)S(1)} %bitcast.87), custom_call_target="tpu_custom_call" | custom-call | tf_op jit(solution)/shard_map/cond/branch_0_fun/pallas_call | solution.py:242
  256.8 1.8 fusion.66
  258.7 0.9 constant_dynamic-update-slice_fusion.9
  259.6 0.9 constant_dynamic-update-slice_fusion.8
  260.5 0.9 constant_dynamic-update-slice_fusion.7
  261.4 0.9 constant_dynamic-update-slice_fusion.6
  262.3 0.9 constant_dynamic-update-slice_fusion.5
  263.2 0.6 compare_and_fusion
  263.8 0.7 fusion.58
  264.6 3.1 %dynamic-slice_select_fusion = f32[5,4,48,384]{3,2,1,0:T(8,128)} fusion(f32[5,4,48,384]{3,2,1,0:T(8,128)S(1)} %copy-done.4, f32[5,4,48,640]{3,2,1,0:T(8,128)} %constant_dynamic-update-slice_fusion.5, s32[]{:T(128)S(6)} %select_n.338, pred[48,384]{1,0:T(8,128)(4,1)S(1)} %broadcast_and_fusion), kind=kLoop, calls=%fused_computation.24 | loop fusion | flops 368640 | bytes 4442116 | tf_op jit(solution)/shard_map/jit(_where)/select_n | solution.py:560
  (25 shorter events, 3.4 us)
Async XLA Ops:
  70.4 4.4 %copy-start.2 = (f32[5,4,48,130]{3,2,1,0:T(8,128)S(1)}, f32[5,4,48,130]{3,2,1,0:T(8,128)}, u32[]{:S(2)}) copy-start(f32[5,4,48,130]{3,2,1,0:T(8,128)} %get-tuple-element.33) | copy-start | bytes 1497604 | tf_op jit(solution)/shard_map/cond
  135.9 4.8 %copy-start.5 = (f32[5,4,48,384]{3,2,1,0:T(8,128)S(1)}, f32[5,4,48,384]{3,2,1,0:T(8,128)}, u32[]{:S(2)}) copy-start(f32[5,4,48,384]{3,2,1,0:T(8,128)} %refs_0_.3) | copy-start | bytes 4423684
  258.7 5.8 %copy-start.4 = (f32[5,4,48,384]{3,2,1,0:T(8,128)S(1)}, f32[5,4,48,384]{3,2,1,0:T(8,128)}, u32[]{:S(2)}) copy-start(f32[5,4,48,384]{3,2,1,0:T(8,128)} %shard_map.88) | copy-start | bytes 4423684

commit v12 on v10

--- a/solution.py
+++ b/solution.py
@@ -185,8 +185,32 @@
     return pairs
 
 
-def exchange_kernel(axis, patterns, send_ref, recv_ref, send_sems, recv_sems):
+def exchange_kernel(axis, patterns, local, send_ref, recv_ref, send_sems, recv_sems):
     me = lax.axis_index(axis)
+    receivers = {}
+    for pairs, _, slot in patterns:
+        for a, b in pairs:
+            receivers.setdefault(slot, set()).add(b)
+    for a, source, slot in local:
+        receivers.setdefault(slot, set()).add(a)
+    for slot in range(recv_ref.shape[0]):
+        idle = None
+        for device in sorted(receivers.get(slot, ())):
+            test = me != device
+            idle = test if idle is None else idle & test
+        if idle is None:
+            recv_ref[slot] = jnp.zeros(recv_ref.shape[1:], recv_ref.dtype)
+            continue
+
+        @pl.when(idle)
+        def _():
+            recv_ref[slot] = jnp.zeros(recv_ref.shape[1:], recv_ref.dtype)
+
+    for a, source, slot in local:
+        @pl.when(me == a)
+        def _():
+            recv_ref[slot] = send_ref[source]
+
     barrier = pltpu.get_barrier_semaphore()
     links = [pair for pairs, _, _ in patterns for pair in pairs]
     for a, b in links:
@@ -235,27 +259,22 @@
 
 
 def exchange(pieces, patterns, slots, axis, identity):
-    me = lax.axis_index(axis)
     remote = [([(a, b) for a, b in pairs if a != b], source, slot) for pairs, source, slot in patterns]
     remote = [entry for entry in remote if entry[0]]
+    local = [(a, source, slot) for pairs, source, slot in patterns for a, b in pairs if a == b]
     shape = pieces.shape[1:]
     received = pl.pallas_call(
-        lambda *refs: exchange_kernel(axis, remote, *refs),
+        lambda *refs: exchange_kernel(axis, remote, local, *refs),
         out_shape=jax.ShapeDtypeStruct((slots,) + shape, pieces.dtype),
-        in_specs=[pl.BlockSpec(memory_space=pl.ANY)],
-        out_specs=pl.BlockSpec(memory_space=pl.ANY),
+        in_specs=[pl.BlockSpec(memory_space=pltpu.VMEM)],
+        out_specs=pl.BlockSpec(memory_space=pltpu.VMEM),
         scratch_shapes=[
             pltpu.SemaphoreType.DMA((len(remote),)),
             pltpu.SemaphoreType.DMA((slots,)),
         ],
         compiler_params=pltpu.CompilerParams(collective_id=identity, has_side_effects=True),
     )(pieces)
-    parts = [received[slot] for slot in range(slots)]
-    for pairs, source, slot in patterns:
-        for a, b in pairs:
-            if a == b:
-                parts[slot] = jnp.where(me == a, pieces[source], parts[slot])
-    return parts
+    return [received[slot] for slot in range(slots)]
 
 
 def gather_kernel(axis, count, source, target, send_sems, recv_sems):
@@ -475,12 +494,7 @@
         )
     within_part, beyond_part = lax.switch(regime, branches, stacked_pieces)
     piece_shape = parent_next.shape[:3] + (relay_columns,)
-    own_k = column_rank % ratio
-    within_live = jnp.logical_not((regime == 2) & (own_k == ratio - 1))
-    beyond_live = (own_k != 0) & jnp.logical_not((regime == 0) & (own_k == ratio - 2))
-    relay_cols = jnp.where(within_live, within_part.reshape(piece_shape), 0.0) + jnp.where(
-        beyond_live, beyond_part.reshape(piece_shape), 0.0
-    )
+    relay_cols = within_part.reshape(piece_shape) + beyond_part.reshape(piece_shape)
 
     padded = jnp.pad(relay_cols, ((0, 0), (0, 0), (relay_rows, relay_rows), (0, 0)))
     slots = []

time: 251 us -> 252 us (level)
  local copies, waits for them, and re-layouts: 53.1 us -> 43.9 us
  Pallas kernels: 163 us -> 170 us
  starting transfers between devices: 6.93 us -> 9.63 us
    pallas_call x2, Pallas kernels: 66.1 us -> 78 us  [exchange(): pl.pallas_call(lambda *refs: exchange_kernel(axis, remote, local, *refs),...]
    pallas_call x4, Pallas kernels: 51.2 us -> 46.1 us  [neighbours(): pl.pallas_call(lambda *refs: halo_kernel(rows, cols, *refs), out_shape=tu...]
    slice x2 -> x1, local copies, waits for them, and re-layouts: 3.91 us -> 0.16 us  [exchange(): return [received[slot] for slot in range(slots)]]
    all_to_all x1, starting transfers between devices: 6.93 us -> 9.63 us  [per_device(): lax.all_to_all(stacked, 'gx', split_axis=0, concat_axis=0, tiled=True)]
where the time goes in v12:
time: 252 us; the launch traced here: 251 us
  Pallas kernels  170 us (67%)
  local copies, waits for them, and re-layouts  43.9 us (17%)
  between operations  13.6 us (5%)
  starting transfers between devices  9.63 us (4%)
  matrix products  7 us (3%)
  other arithmetic  5.79 us (2%)
    pallas_call x2, Pallas kernels, exchange(): pl.pallas_call(lambda *refs: exchange_kernel(axis, remote, local, *refs),...  78 us
    pallas_call x4, Pallas kernels, neighbours(): pl.pallas_call(lambda *refs: halo_kernel(rows, cols, *refs), out_shape=tu...  46.1 us
    pallas_call x4, Pallas kernels, stencil(): pl.pallas_call(lambda *refs: stencil_kernel(relaxed, *refs), out_shape=ou...  25 us
    pallas_call x1, Pallas kernels, gather(): pl.pallas_call(lambda *refs: gather_kernel(axis, count, *refs), out_shape...  21.1 us
    unnamed x19, local copies, waits for them, and re-layouts  11.8 us
    another operation x6, local copies, waits for them, and re-layouts, per_device(): stacked_pieces = jnp.stack(pieces)  10.6 us
    all_to_all x1, starting transfers between devices, per_device(): lax.all_to_all(stacked, 'gx', split_axis=0, concat_axis=0, tiled=True)  9.63 us
    dynamic_slice x1, local copies, waits for them, and re-layouts, per_device(): piece = lax.dynamic_slice_in_dim(wide, start, relay_columns, axis=3)  5.37 us
  transfers between devices with their start and end apart: 1, of which 0 were waited for; matrix products, arithmetic and copies ran while one was open for 3% of the time, Pallas kernels for 12%

profile of v12, /device:TPU:73, one launch (start us, length us, event | category | flops | bytes accessed | tf_op | source)
XLA Modules:
  0.0 250.5 jit_solution(10768303097280242919)
XLA Ops:
  0.6 1.2 slice_reduce_fusion.4
  1.9 1.7 slice_reduce_fusion
  3.5 1.4 fusion.49
  17.0 0.6 reshape_squeeze.28.refs_0_
  17.6 0.6 reshape_squeeze.29.refs_1_
  18.2 0.6 reshape_squeeze.30.refs_2_
  18.8 0.6 reshape_squeeze.31.refs_3_
  19.4 6.5 %shard_map.87 = (f32[20,384]{1,0:T(8,128)}, f32[20,384]{1,0:T(8,128)}, f32[20,48]{1,0:T(8,128)}, f32[20,48]{1,0:T(8,128)}) custom-call(f32[20,384]{1,0:T(8,128)} %reshape_squeeze.28.refs_0_, f32[20,384]{1,0:T(8,128)} %reshape_squeeze.29.refs_1_, f32[20,48]{1,0:T(8,128)} %reshape_squeeze.30.refs_2_, f32[20,48]{1,0:T(8,128)} %reshape_squeeze.31.refs_3_), custom_call_target="tpu_custom_call" | custom-call | tf_op jit(solution)/shard_map/pallas_call | solution.py:81
  25.9 5.4 %shard_map.88 = f32[5,4,48,384]{3,2,1,0:T(8,128)} custom-call(f32[5,4,48,384]{3,2,1,0:T(8,128)} %refs_0_.5, f32[2,4,48,384]{3,2,1,0:T(8,128)} %refs_1_.4, f32[4,48,384]{2,1,0:T(8,128)} %refs_2_.4, f32[20,384]{1,0:T(8,128)} %get-tuple-element.49.refs_3_, f32[20,384]{1,0:T(8,128)} %get-tuple-element.50.refs_4_, f32[20,48]{1,0:T(8,128)} %get-tuple-element.51.refs_5_, ...), custom_call_target="tpu_custom_call" | custom-call | tf_op jit(solution)/shard_map/pallas_call | solution.py:414
  31.4 5.4 %pad_dynamic-slice_fusion.2 = (f32[5,4,48,130]{3,2,1,0:T(8,128)S(1)}, f32[5,4,48,130]{3,2,1,0:T(8,128)}, f32[5,4,48,130]{3,2,1,0:T(8,128)}, f32[5,4,48,130]{3,2,1,0:T(8,128)}, f32[5,4,48,130]{3,2,1,0:T(8,128)S(1)}) fusion(s32[]{:T(128)S(6)} %select_n.206, f32[5,4,48,384]{3,2,1,0:T(8,128)} %shard_map.88, s32[]{:T(128)S(6)} %select_n.203, s32[]{:T(128)S(6)} %select_n.204, ...), kind=kLoop, calls=%fused_computation.5 | loop fusion | bytes 3970580 | tf_op jit(solution)/shard_map/dynamic_slice | solution.py:478
  36.8 1.4 stack_reshape.15
  38.2 1.1 constant_dynamic-update-slice_fusion.4
  39.2 2.6 %stack_reshape.16 = f32[1,975,128]{2,1,0:T(8,128)} reshape(f32[5,4,48,130]{3,2,1,0:T(8,128)} %get-tuple-element.196) | data formatting | bytes 998400 | tf_op jit(solution)/shard_map/stack;reshape | solution.py:481
  41.8 2.6 %stack_reshape.17 = f32[1,975,128]{2,1,0:T(8,128)} reshape(f32[5,4,48,130]{3,2,1,0:T(8,128)} %get-tuple-element.197) | data formatting | bytes 998400 | tf_op jit(solution)/shard_map/stack;reshape | solution.py:481
  44.4 2.6 %stack_reshape.18 = f32[1,975,128]{2,1,0:T(8,128)} reshape(f32[5,4,48,130]{3,2,1,0:T(8,128)} %get-tuple-element.198) | data formatting | bytes 998400 | tf_op jit(solution)/shard_map/stack;reshape | solution.py:481
  47.0 1.4 stack_reshape.19
  48.4 1.1 constant_dynamic-update-slice_fusion.3
  49.5 1.1 constant_dynamic-update-slice_fusion.2
  50.6 1.1 constant_dynamic-update-slice_fusion.1
  51.7 32.9 %conditional.2 = (f32[5,4,84,130]{3,2,1,0:T(8,128)S(1)}) conditional(s32[]{:T(128)} %clamp.7, f32[5,975,128]{2,1,0:T(8,128)S(1)} %constant_dynamic-update-slice_fusion, f32[5,975,128]{2,1,0:T(8,128)S(1)} %constant_dynamic-update-slice_fusion, f32[5,975,128]{2,1,0:T(8,128)S(1)} %constant_dynamic-update-slice_fusion), branch_computations={%region_0.1_spmd, %region_1.2_spmd, %region_2.3_spmd} | conditional | flops 124800 | bytes 3868812 | solution.py:495
  51.7 30.0 %branch_2_fun.2 = f32[2,975,128]{2,1,0:T(8,128)} custom-call(f32[5,975,128]{2,1,0:T(8,128)S(1)} %refs_0_.4), custom_call_target="tpu_custom_call" | custom-call | tf_op jit(solution)/shard_map/cond/branch_2_fun/pallas_call | solution.py:266
  81.8 1.2 slice_add_fusion.2
  83.0 1.2 add.317
  84.2 0.2 pad.19
  84.6 0.6 constant_dynamic-slice_fusion
  85.2 0.9 bitcast_dynamic-update-slice_fusion.7
  86.1 0.9 bitcast_dynamic-update-slice_fusion.6
  87.0 0.9 bitcast_dynamic-update-slice_fusion.5
  87.9 0.9 bitcast_dynamic-update-slice_fusion.4
  88.8 0.9 bitcast_dynamic-update-slice_fusion.3
  89.6 0.9 bitcast_dynamic-update-slice_fusion.2
  90.5 0.9 bitcast_dynamic-update-slice_fusion.1
  91.4 0.9 bitcast_dynamic-update-slice_fusion
  92.3 9.6 %all-to-all-start = ((f32[8,5,4,18,130]{4,2,3,1,0:T(4,128)}), f32[8,5,4,18,130]{4,2,3,1,0:T(4,128)S(1)}, u32[]{:S(2)}, u32[]{:S(2)}) async-start(f32[8,5,4,18,130]{4,2,3,1,0:T(4,128)} %bitcast_dynamic-update-slice_fusion), calls=%async_computation | async-start | bytes 5898240 | tf_op jit(solution)/shard_map/all_to_all | solution.py:506
  101.9 1.2 slice_reduce_fusion.6
  103.2 1.7 slice_reduce_fusion.2
  105.5 0.6 compare_and_fusion
  106.1 0.6 reshape_squeeze.24.refs_0_
  106.8 0.6 reshape_squeeze.25.refs_1_
  107.4 0.6 reshape_squeeze.26.refs_2_
  108.0 0.6 reshape_squeeze.27.refs_3_
  108.6 28.9 %shard_map.86 = (f32[20,384]{1,0:T(8,128)}, f32[20,384]{1,0:T(8,128)}, f32[20,48]{1,0:T(8,128)}, f32[20,48]{1,0:T(8,128)}) custom-call(f32[20,384]{1,0:T(8,128)} %reshape_squeeze.24.refs_0_, f32[20,384]{1,0:T(8,128)} %reshape_squeeze.25.refs_1_, f32[20,48]{1,0:T(8,128)} %reshape_squeeze.26.refs_2_, f32[20,48]{1,0:T(8,128)} %reshape_squeeze.27.refs_3_), custom_call_target="tpu_custom_call" | custom-call | tf_op jit(solution)/shard_map/pallas_call | solution.py:81
  137.5 0.7 fusion.43
  138.3 0.1 broadcast_and_fusion
  138.4 0.7 multiply_add_fusion.refs_8_
  139.1 0.8 reduce_sum.9
  139.9 1.0 convolution_bitcast_fusion
  140.9 2.9 %fusion.1.refs_7_ = f32[5,4,48,384]{3,2,1,0:T(8,128)} fusion(f32[5,4,48,130]{3,2,1,0:T(8,128)S(1)} %convolution_bitcast_fusion, f32[384]{0:T(512)S(1)} %get-tuple-element.202, s32[384]{0:T(512)S(1)} %get-tuple-element.208, f32[384]{0:T(512)S(1)} %get-tuple-element.203, s32[384]{0:T(512)S(1)} %add_select_fusion, f32[384]{0:T(512)S(1)} %compare_select_fusion.2, ...), kind=kOutput, calls=%fused_computation.29 | convolution fusion | flops 575477760 | bytes 1982976 | tf_op jit(solution)/shard_map/flac,bc->flab/dot_general | solution.py:151
  143.8 6.5 %shard_map.89 = (f32[5,4,48,384]{3,2,1,0:T(8,128)}, f32[20,384]{1,0:T(8,128)}, f32[20,384]{1,0:T(8,128)}, f32[20,48]{1,0:T(8,128)}, f32[20,48]{1,0:T(8,128)}) custom-call(f32[5,4,48,384]{3,2,1,0:T(8,128)} %refs_0_.6, f32[2,4,48,384]{3,2,1,0:T(8,128)} %refs_1_.7, f32[4,48,384]{2,1,0:T(8,128)} %refs_2_.7, f32[20,384]{1,0:T(8,128)} %get-tuple-element.45.refs_3_, ...), custom_call_target="tpu_custom_call" | custom-call | tf_op jit(solution)/shard_map/pallas_call | solution.py:414
  150.3 5.0 %shard_map.90 = (f32[20,384]{1,0:T(8,128)}, f32[20,384]{1,0:T(8,128)}, f32[20,48]{1,0:T(8,128)}, f32[20,48]{1,0:T(8,128)}) custom-call(f32[20,384]{1,0:T(8,128)} %get-tuple-element.54.refs_0_, f32[20,384]{1,0:T(8,128)} %get-tuple-element.55.refs_1_, f32[20,48]{1,0:T(8,128)} %get-tuple-element.56.refs_2_, f32[20,48]{1,0:T(8,128)} %get-tuple-element.57.refs_3_), custom_call_target="tpu_custom_call" | custom-call | tf_op jit(solution)/shard_map/pallas_call | solution.py:81
  155.2 6.5 %shard_map.91 = (f32[5,4,48,384]{3,2,1,0:T(8,128)}, f32[20,384]{1,0:T(8,128)}, f32[20,384]{1,0:T(8,128)}, f32[20,48]{1,0:T(8,128)}, f32[20,48]{1,0:T(8,128)}) custom-call(f32[5,4,48,384]{3,2,1,0:T(8,128)} %get-tuple-element.53.refs_0_, f32[2,4,48,384]{3,2,1,0:T(8,128)} %refs_1_.7, f32[4,48,384]{2,1,0:T(8,128)} %refs_2_.7, ...), custom_call_target="tpu_custom_call" | custom-call | tf_op jit(solution)/shard_map/pallas_call | solution.py:414
  161.8 5.7 %shard_map.92 = (f32[20,384]{1,0:T(8,128)}, f32[20,384]{1,0:T(8,128)}, f32[20,48]{1,0:T(8,128)}, f32[20,48]{1,0:T(8,128)}) custom-call(f32[20,384]{1,0:T(8,128)} %get-tuple-element.63.refs_0_, f32[20,384]{1,0:T(8,128)} %get-tuple-element.64.refs_1_, f32[20,48]{1,0:T(8,128)} %get-tuple-element.65.refs_2_, f32[20,48]{1,0:T(8,128)} %get-tuple-element.66.refs_3_), custom_call_target="tpu_custom_call" | custom-call | tf_op jit(solution)/shard_map/pallas_call | solution.py:81
  167.5 6.5 %shard_map.93 = (f32[5,4,48,384]{3,2,1,0:T(8,128)}, f32[20,384]{1,0:T(8,128)}, f32[20,384]{1,0:T(8,128)}, f32[20,48]{1,0:T(8,128)}, f32[20,48]{1,0:T(8,128)}) custom-call(f32[5,4,48,384]{3,2,1,0:T(8,128)} %get-tuple-element.62.refs_0_, f32[2,4,48,384]{3,2,1,0:T(8,128)} %refs_1_.7, f32[4,48,384]{2,1,0:T(8,128)} %refs_2_.7, ...), custom_call_target="tpu_custom_call" | custom-call | tf_op jit(solution)/shard_map/pallas_call | solution.py:414
  174.1 2.2 fusion.9
  176.2 0.9 convolution_multiply_fusion
  177.2 21.1 %shard_map.94 = f32[8,20,16,128]{3,2,1,0:T(8,128)S(1)} custom-call(f32[20,16,128]{2,1,0:T(8,128)} %bitcast.77), custom_call_target="tpu_custom_call" | custom-call | tf_op jit(solution)/shard_map/pallas_call | solution.py:316
  198.3 49.1 %conditional.3 = (f32[5,960,128]{2,1,0:T(8,128)S(1)}) conditional(s32[]{:T(128)} %clamp.6, (f32[20,8,16,128]{3,2,0,1:T(8,128)S(1)}, s32[]{:T(128)}, s32[]{:T(128)}, f32[]{:T(128)}, s32[]{:T(128)}, /*index=5*/s32[]{:T(128)}) %tuple.80, (f32[20,8,16,128]{3,2,0,1:T(8,128)S(1)}, s32[]{:T(128)}, s32[]{:T(128)}, f32[]{:T(128)}, s32[]{:T(128)}, ...), branch_computations={%region_4.5_spmd.clone, %region_5.6_spmd.clone} | conditional | flops 3 | bytes 4423730 | solution.py:553
  198.4 0.1 copy.33
  198.5 0.9 pad_dynamic-slice_fusion.1
  199.4 48.0 %branch_1_fun.4 = f32[5,960,128]{2,1,0:T(8,128)S(1)} custom-call(f32[1,960,128]{2,1,0:T(8,128)} %bitcast.76), custom_call_target="tpu_custom_call" | custom-call | tf_op jit(solution)/shard_map/cond/branch_1_fun/pallas_call | solution.py:266
  247.4 0.2 fusion.48
  247.6 0.0 copy-start
  247.8 1.2 copy-done
  249.0 1.6 dynamic-slice_select_fusion
  (19 shorter events, 0.3 us)
Async XLA Ops:
  48.4 3.3 %copy-start.1 = (f32[1,975,128]{2,1,0:T(8,128)S(1)}, f32[1,975,128]{2,1,0:T(8,128)}, u32[]{:S(2)}) copy-start(f32[1,975,128]{2,1,0:T(8,128)} %stack_reshape.19) | copy-start | bytes 1497604
  92.3 46.8 %all-to-all-start = ((f32[8,5,4,18,130]{4,2,3,1,0:T(4,128)}), f32[8,5,4,18,130]{4,2,3,1,0:T(4,128)S(1)}, u32[]{:S(2)}, u32[]{:S(2)}) async-start(f32[8,5,4,18,130]{4,2,3,1,0:T(4,128)} %bitcast_dynamic-update-slice_fusion), calls=%async_computation | async-start | bytes 5898240 | tf_op jit(solution)/shard_map/all_to_all | solution.py:506
  247.6 1.4 copy-start

commit v13 on v12

--- a/solution.py
+++ b/solution.py
@@ -497,14 +497,13 @@
     relay_cols = within_part.reshape(piece_shape) + beyond_part.reshape(piece_shape)
 
     padded = jnp.pad(relay_cols, ((0, 0), (0, 0), (relay_rows, relay_rows), (0, 0)))
-    slots = []
-    for target in range(row_devices):
-        first = row_anchor - 1 + span_rows * target - parent_rows * row_rank
-        first = jnp.clip(first, -relay_rows, parent_rows) + relay_rows
-        slots.append(lax.dynamic_slice_in_dim(padded, first, relay_rows, axis=2))
-    stacked = jnp.stack(slots, axis=0)
-    received = lax.all_to_all(stacked, "gx", split_axis=0, concat_axis=0, tiled=True)
-    relay = jnp.sum(received, axis=0)
+    targets = jnp.arange(row_devices, dtype=jnp.int32)[:, None]
+    first = row_anchor - 1 + span_rows * targets - parent_rows * row_rank
+    first = jnp.clip(first, -relay_rows, parent_rows) + relay_rows
+    picks = first + jnp.arange(relay_rows, dtype=jnp.int32)[None, :]
+    stacked = jnp.take(padded, picks, axis=2)
+    received = lax.all_to_all(stacked, "gx", split_axis=2, concat_axis=2, tiled=True)
+    relay = jnp.sum(received, axis=2)
 
     forcing = refine(relay)
     row_global = row_rank * nest_rows + jnp.arange(nest_rows, dtype=jnp.int32)

time: 252 us -> 245 us (0.972)
  local copies, waits for them, and re-layouts: 43.9 us -> 39 us
  between operations: 13.6 us -> 9.03 us
  other arithmetic: 5.79 us -> 8.84 us
    unnamed x19 -> x10, local copies, waits for them, and re-layouts: 11.8 us -> 5.56 us
    gather x0 -> x1, local copies, waits for them, and re-layouts: none -> 4.33 us  [per_device(): stacked = jnp.take(padded, picks, axis=2)]
    select_n x0 -> x2, other arithmetic: none -> 4.22 us  [per_device(): stacked = jnp.take(padded, picks, axis=2)]
where the time goes in v13:
time: 245 us; the launch traced here: 243 us
  Pallas kernels  169 us (69%)
  local copies, waits for them, and re-layouts  39 us (16%)
  starting transfers between devices  9.67 us (4%)
  between operations  9.03 us (4%)
  other arithmetic  8.84 us (4%)
  matrix products  6.98 us (3%)
    pallas_call x2, Pallas kernels, exchange(): pl.pallas_call(lambda *refs: exchange_kernel(axis, remote, local, *refs),...  77.1 us
    pallas_call x4, Pallas kernels, neighbours(): pl.pallas_call(lambda *refs: halo_kernel(rows, cols, *refs), out_shape=tu...  46.2 us
    pallas_call x4, Pallas kernels, stencil(): pl.pallas_call(lambda *refs: stencil_kernel(relaxed, *refs), out_shape=ou...  25 us
    pallas_call x1, Pallas kernels, gather(): pl.pallas_call(lambda *refs: gather_kernel(axis, count, *refs), out_shape...  21.2 us
    all_to_all x1, starting transfers between devices, per_device(): lax.all_to_all(stacked, 'gx', split_axis=2, concat_axis=2, tiled=True)  9.67 us
    another operation x6, local copies, waits for them, and re-layouts, per_device(): stacked_pieces = jnp.stack(pieces)  8.57 us
    unnamed x10, local copies, waits for them, and re-layouts  5.56 us
    dynamic_slice x1, local copies, waits for them, and re-layouts, per_device(): piece = lax.dynamic_slice_in_dim(wide, start, relay_columns, axis=3)  5.02 us
  transfers between devices with their start and end apart: 1, of which 0 were waited for; matrix products, arithmetic and copies ran while one was open for 3% of the time, Pallas kernels for 12%

profile of v13, /device:TPU:73, one launch (start us, length us, event | category | flops | bytes accessed | tf_op | source)
XLA Modules:
  0.0 243.2 jit_solution(18150456759791523859)
XLA Ops:
  0.6 1.4 fusion.52
  2.6 0.1 fusion.41
  2.7 0.1 compare_select_fusion
  2.8 1.7 slice_reduce_fusion
  4.4 1.2 slice_reduce_fusion.4
  12.6 0.1 reshape.258
  12.7 0.6 reshape_squeeze.31.refs_3_
  13.3 0.6 reshape_squeeze.30.refs_2_
  13.9 0.6 reshape_squeeze.29.refs_1_
  14.5 0.6 reshape_squeeze.28.refs_0_
  15.2 6.5 %shard_map.87 = (f32[20,384]{1,0:T(8,128)}, f32[20,384]{1,0:T(8,128)}, f32[20,48]{1,0:T(8,128)}, f32[20,48]{1,0:T(8,128)}) custom-call(f32[20,384]{1,0:T(8,128)} %reshape_squeeze.28.refs_0_, f32[20,384]{1,0:T(8,128)} %reshape_squeeze.29.refs_1_, f32[20,48]{1,0:T(8,128)} %reshape_squeeze.30.refs_2_, f32[20,48]{1,0:T(8,128)} %reshape_squeeze.31.refs_3_), custom_call_target="tpu_custom_call" | custom-call | tf_op jit(solution)/shard_map/pallas_call | solution.py:81
  21.7 5.4 %shard_map.88 = f32[5,4,48,384]{3,2,1,0:T(8,128)} custom-call(f32[5,4,48,384]{3,2,1,0:T(8,128)} %refs_0_.5, f32[2,4,48,384]{3,2,1,0:T(8,128)} %refs_1_.4, f32[4,48,384]{2,1,0:T(8,128)} %refs_2_.4, f32[20,384]{1,0:T(8,128)} %get-tuple-element.45.refs_3_, f32[20,384]{1,0:T(8,128)} %get-tuple-element.46.refs_4_, f32[20,48]{1,0:T(8,128)} %get-tuple-element.47.refs_5_, ...), custom_call_target="tpu_custom_call" | custom-call | tf_op jit(solution)/shard_map/pallas_call | solution.py:414
  27.1 5.0 %pad_dynamic-slice_fusion.2 = (f32[5,4,48,130]{3,2,1,0:T(8,128)}, f32[5,4,48,130]{3,2,1,0:T(8,128)}, f32[5,4,48,130]{3,2,1,0:T(8,128)S(1)}, f32[5,4,48,130]{3,2,1,0:T(8,128)S(1)}, f32[5,4,48,130]{3,2,1,0:T(8,128)S(1)}) fusion(s32[]{:T(128)S(6)} %select_n.203, f32[5,4,48,384]{3,2,1,0:T(8,128)} %shard_map.88, s32[]{:T(128)S(6)} %select_n.200, ...), kind=kLoop, calls=%fused_computation.3 | loop fusion | bytes 3970580 | tf_op jit(solution)/shard_map/dynamic_slice | solution.py:478
  32.1 1.8 stack_reshape.19
  33.9 2.6 %stack_reshape.16 = f32[1,975,128]{2,1,0:T(8,128)} reshape(f32[5,4,48,130]{3,2,1,0:T(8,128)} %get-tuple-element.172) | data formatting | bytes 998400 | tf_op jit(solution)/shard_map/stack;reshape | solution.py:481
  36.5 1.4 stack_reshape.17
  37.9 1.4 stack_reshape.18
  39.3 1.4 stack_reshape.15
  40.7 1.1 constant_dynamic-update-slice_fusion.4
  41.8 1.1 constant_dynamic-update-slice_fusion.3
  42.8 1.1 constant_dynamic-update-slice_fusion.2
  43.9 1.1 constant_dynamic-update-slice_fusion.1
  45.0 29.3 %conditional.2 = (f32[2,975,128]{2,1,0:T(8,128)S(1)}) conditional(s32[]{:T(128)} %clamp.13, f32[5,975,128]{2,1,0:T(8,128)S(1)} %constant_dynamic-update-slice_fusion, f32[5,975,128]{2,1,0:T(8,128)S(1)} %constant_dynamic-update-slice_fusion, f32[5,975,128]{2,1,0:T(8,128)S(1)} %constant_dynamic-update-slice_fusion), branch_computations={%region_0.1_spmd, %region_1.2_spmd, %region_2.3_spmd} | conditional | bytes 8 | solution.py:495
  45.0 29.0 %branch_2_fun.1 = f32[2,975,128]{2,1,0:T(8,128)S(1)} custom-call(f32[5,975,128]{2,1,0:T(8,128)S(1)} %refs_0_.4), custom_call_target="tpu_custom_call" | custom-call | tf_op jit(solution)/shard_map/cond/branch_2_fun/pallas_call | solution.py:266
  74.3 0.1 slice_add_fusion
  74.3 1.2 add.344
  75.6 0.6 copy.14
  76.2 0.3 pad.13
  76.5 4.3 %gather_fusion = f32[144,5,4,130]{3,2,1,0:T(4,128)} fusion(f32[5,4,84,130]{3,1,2,0:T(4,128)S(1)} %pad.13, s32[1024]{0:T(1024)S(1)} %pad_clamp_fusion), kind=kCustom, calls=%fused_computation | custom fusion | bytes 2995776 | tf_op jit(solution)/shard_map/jit(_take)/gather | solution.py:504
  80.8 4.1 %select_bitcast_fusion = f32[5,4,8,18,130]{4,1,0,3,2:T(4,128)} fusion(f32[8,18,5,4,130]{4,3,2,1,0:T(4,128)} %bitcast.55, pred[8,18]{1,0:T(8,128)(4,1)S(1)} %fusion.41), kind=kLoop, calls=%fused_computation.8 | loop fusion | flops 374400 | bytes 2995344 | tf_op jit(solution)/shard_map/jit(_take)/select_n | solution.py:504
  84.9 9.7 %all-to-all-start = ((f32[5,4,8,18,130]{4,1,0,3,2:T(4,128)}), f32[5,4,8,18,130]{4,1,0,3,2:T(4,128)S(1)}, u32[]{:S(2)}, u32[]{:S(2)}) async-start(f32[5,4,8,18,130]{4,1,0,3,2:T(4,128)} %select_bitcast_fusion), calls=%async_computation | async-start | bytes 5898240 | tf_op jit(solution)/shard_map/all_to_all | solution.py:505
  95.2 0.6 compare_and_fusion
  95.8 1.7 slice_reduce_fusion.2
  97.5 1.2 slice_reduce_fusion.6
  98.7 0.6 reshape_squeeze.27.refs_3_
  99.3 0.6 reshape_squeeze.26.refs_2_
  99.9 0.6 reshape_squeeze.25.refs_1_
  100.6 0.6 reshape_squeeze.24.refs_0_
  101.2 29.0 %shard_map.86 = (f32[20,384]{1,0:T(8,128)}, f32[20,384]{1,0:T(8,128)}, f32[20,48]{1,0:T(8,128)}, f32[20,48]{1,0:T(8,128)}) custom-call(f32[20,384]{1,0:T(8,128)} %reshape_squeeze.24.refs_0_, f32[20,384]{1,0:T(8,128)} %reshape_squeeze.25.refs_1_, f32[20,48]{1,0:T(8,128)} %reshape_squeeze.26.refs_2_, f32[20,48]{1,0:T(8,128)} %reshape_squeeze.27.refs_3_), custom_call_target="tpu_custom_call" | custom-call | tf_op jit(solution)/shard_map/pallas_call | solution.py:81
  130.2 0.7 fusion.46
  131.0 0.1 broadcast_and_fusion
  131.1 0.7 multiply_add_fusion.refs_8_
  131.8 0.0 all-to-all-done
  131.8 0.7 reduce_sum.9
  132.6 1.0 convolution_bitcast_fusion
  133.5 2.9 %fusion.1.refs_7_ = f32[5,4,48,384]{3,2,1,0:T(8,128)} fusion(f32[5,4,48,130]{3,2,1,0:T(8,128)S(1)} %convolution_bitcast_fusion, f32[384]{0:T(512)S(1)} %get-tuple-element.178, s32[384]{0:T(512)S(1)} %get-tuple-element.184, f32[384]{0:T(512)S(1)} %get-tuple-element.179, s32[384]{0:T(512)S(1)} %add_select_fusion, f32[384]{0:T(512)S(1)} %compare_select_fusion.4, ...), kind=kOutput, calls=%fused_computation.21 | convolution fusion | flops 575477760 | bytes 1982976 | tf_op jit(solution)/shard_map/flac,bc->flab/dot_general | solution.py:151
  136.4 6.5 %shard_map.89 = (f32[5,4,48,384]{3,2,1,0:T(8,128)}, f32[20,384]{1,0:T(8,128)}, f32[20,384]{1,0:T(8,128)}, f32[20,48]{1,0:T(8,128)}, f32[20,48]{1,0:T(8,128)}) custom-call(f32[5,4,48,384]{3,2,1,0:T(8,128)} %refs_0_.6, f32[2,4,48,384]{3,2,1,0:T(8,128)} %refs_1_.7, f32[4,48,384]{2,1,0:T(8,128)} %refs_2_.7, f32[20,384]{1,0:T(8,128)} %get-tuple-element.41.refs_3_, ...), custom_call_target="tpu_custom_call" | custom-call | tf_op jit(solution)/shard_map/pallas_call | solution.py:414
  142.9 5.0 %shard_map.90 = (f32[20,384]{1,0:T(8,128)}, f32[20,384]{1,0:T(8,128)}, f32[20,48]{1,0:T(8,128)}, f32[20,48]{1,0:T(8,128)}) custom-call(f32[20,384]{1,0:T(8,128)} %get-tuple-element.50.refs_0_, f32[20,384]{1,0:T(8,128)} %get-tuple-element.51.refs_1_, f32[20,48]{1,0:T(8,128)} %get-tuple-element.52.refs_2_, f32[20,48]{1,0:T(8,128)} %get-tuple-element.53.refs_3_), custom_call_target="tpu_custom_call" | custom-call | tf_op jit(solution)/shard_map/pallas_call | solution.py:81
  147.9 6.5 %shard_map.91 = (f32[5,4,48,384]{3,2,1,0:T(8,128)}, f32[20,384]{1,0:T(8,128)}, f32[20,384]{1,0:T(8,128)}, f32[20,48]{1,0:T(8,128)}, f32[20,48]{1,0:T(8,128)}) custom-call(f32[5,4,48,384]{3,2,1,0:T(8,128)} %get-tuple-element.49.refs_0_, f32[2,4,48,384]{3,2,1,0:T(8,128)} %refs_1_.7, f32[4,48,384]{2,1,0:T(8,128)} %refs_2_.7, ...), custom_call_target="tpu_custom_call" | custom-call | tf_op jit(solution)/shard_map/pallas_call | solution.py:414
  154.5 5.8 %shard_map.92 = (f32[20,384]{1,0:T(8,128)}, f32[20,384]{1,0:T(8,128)}, f32[20,48]{1,0:T(8,128)}, f32[20,48]{1,0:T(8,128)}) custom-call(f32[20,384]{1,0:T(8,128)} %get-tuple-element.59.refs_0_, f32[20,384]{1,0:T(8,128)} %get-tuple-element.60.refs_1_, f32[20,48]{1,0:T(8,128)} %get-tuple-element.61.refs_2_, f32[20,48]{1,0:T(8,128)} %get-tuple-element.62.refs_3_), custom_call_target="tpu_custom_call" | custom-call | tf_op jit(solution)/shard_map/pallas_call | solution.py:81
  160.2 6.5 %shard_map.93 = (f32[5,4,48,384]{3,2,1,0:T(8,128)}, f32[20,384]{1,0:T(8,128)}, f32[20,384]{1,0:T(8,128)}, f32[20,48]{1,0:T(8,128)}, f32[20,48]{1,0:T(8,128)}) custom-call(f32[5,4,48,384]{3,2,1,0:T(8,128)} %get-tuple-element.58.refs_0_, f32[2,4,48,384]{3,2,1,0:T(8,128)} %refs_1_.7, f32[4,48,384]{2,1,0:T(8,128)} %refs_2_.7, ...), custom_call_target="tpu_custom_call" | custom-call | tf_op jit(solution)/shard_map/pallas_call | solution.py:414
  166.7 2.2 fusion.9
  168.9 0.9 convolution_multiply_fusion
  169.9 21.2 %shard_map.94 = f32[8,20,16,128]{3,2,1,0:T(8,128)S(1)} custom-call(f32[20,16,128]{2,1,0:T(8,128)} %bitcast.67), custom_call_target="tpu_custom_call" | custom-call | tf_op jit(solution)/shard_map/pallas_call | solution.py:316
  191.0 49.0 %conditional.3 = (f32[5,960,128]{2,1,0:T(8,128)S(1)}) conditional(s32[]{:T(128)} %clamp.12, (f32[20,8,16,128]{3,2,0,1:T(8,128)S(1)}, s32[]{:T(128)}, s32[]{:T(128)}, f32[]{:T(128)}, s32[]{:T(128)}, /*index=5*/s32[]{:T(128)}) %tuple.63, (f32[20,8,16,128]{3,2,0,1:T(8,128)S(1)}, s32[]{:T(128)}, s32[]{:T(128)}, f32[]{:T(128)}, s32[]{:T(128)}, ...), branch_computations={%region_4.5_spmd.clone, %region_5.6_spmd.clone} | conditional | flops 3 | bytes 4423730 | solution.py:552
  191.1 0.1 copy.17
  191.2 0.8 pad_dynamic-slice_fusion.1
  192.1 48.0 %branch_1_fun.3 = f32[5,960,128]{2,1,0:T(8,128)S(1)} custom-call(f32[1,960,128]{2,1,0:T(8,128)} %bitcast.66), custom_call_target="tpu_custom_call" | custom-call | tf_op jit(solution)/shard_map/cond/branch_1_fun/pallas_call | solution.py:266
  240.1 0.2 fusion.51
  240.3 0.0 copy-start
  240.5 1.2 copy-done
  241.6 1.6 dynamic-slice_select_fusion
  (18 shorter events, 0.3 us)
Async XLA Ops:
  84.9 46.9 %all-to-all-start = ((f32[5,4,8,18,130]{4,1,0,3,2:T(4,128)}), f32[5,4,8,18,130]{4,1,0,3,2:T(4,128)S(1)}, u32[]{:S(2)}, u32[]{:S(2)}) async-start(f32[5,4,8,18,130]{4,1,0,3,2:T(4,128)} %select_bitcast_fusion), calls=%async_computation | async-start | bytes 5898240 | tf_op jit(solution)/shard_map/all_to_all | solution.py:505
  240.3 1.4 copy-start

commit v14 on v13

--- a/solution.py
+++ b/solution.py
@@ -185,7 +185,9 @@
     return pairs
 
 
-def exchange_kernel(axis, patterns, local, send_ref, recv_ref, send_sems, recv_sems):
+def exchange_kernel(axis, patterns, local, count, *refs):
+    sends = refs[:count]
+    recv_ref, send_sems, recv_sems = refs[count:]
     me = lax.axis_index(axis)
     receivers = {}
     for pairs, _, slot in patterns:
@@ -209,7 +211,7 @@
     for a, source, slot in local:
         @pl.when(me == a)
         def _():
-            recv_ref[slot] = send_ref[source]
+            recv_ref[slot] = sends[source][...]
 
     barrier = pltpu.get_barrier_semaphore()
     links = [pair for pairs, _, _ in patterns for pair in pairs]
@@ -235,7 +237,7 @@
     for number, (pairs, source, slot) in enumerate(patterns):
         for a, b in pairs:
             copy = pltpu.make_async_remote_copy(
-                src_ref=send_ref.at[source],
+                src_ref=sends[source],
                 dst_ref=recv_ref.at[slot],
                 send_sem=send_sems.at[number],
                 recv_sem=recv_sems.at[slot],
@@ -262,18 +264,18 @@
     remote = [([(a, b) for a, b in pairs if a != b], source, slot) for pairs, source, slot in patterns]
     remote = [entry for entry in remote if entry[0]]
     local = [(a, source, slot) for pairs, source, slot in patterns for a, b in pairs if a == b]
-    shape = pieces.shape[1:]
+    shape = pieces[0].shape
     received = pl.pallas_call(
-        lambda *refs: exchange_kernel(axis, remote, local, *refs),
-        out_shape=jax.ShapeDtypeStruct((slots,) + shape, pieces.dtype),
-        in_specs=[pl.BlockSpec(memory_space=pltpu.VMEM)],
+        lambda *refs: exchange_kernel(axis, remote, local, len(pieces), *refs),
+        out_shape=jax.ShapeDtypeStruct((slots,) + shape, pieces[0].dtype),
+        in_specs=[pl.BlockSpec(memory_space=pltpu.VMEM)] * len(pieces),
         out_specs=pl.BlockSpec(memory_space=pltpu.VMEM),
         scratch_shapes=[
             pltpu.SemaphoreType.DMA((len(remote),)),
             pltpu.SemaphoreType.DMA((slots,)),
         ],
         compiler_params=pltpu.CompilerParams(collective_id=identity, has_side_effects=True),
-    )(pieces)
+    )(*pieces)
     return [received[slot] for slot in range(slots)]
 
 
@@ -478,7 +480,7 @@
             piece = lax.dynamic_slice_in_dim(wide, start, relay_columns, axis=3)
             routes.append((k, extra, len(pieces)))
             pieces.append(flat(piece))
-    stacked_pieces = jnp.stack(pieces)
+    stacked_pieces = tuple(pieces)
     branches = []
     for number, active in enumerate(regimes):
         patterns = [
@@ -549,7 +551,7 @@
             )
         )
     late = (offset > (ratio - 1) * span_columns - span_columns - 1).astype(jnp.int32)
-    parts = lax.switch(late, back_branches, flat(strip)[None])
+    parts = lax.switch(late, back_branches, (flat(strip),))
     joined = jnp.concatenate([part.reshape(strip.shape) for part in parts], axis=3)
     start = (ratio - 1) * span_columns - 1 - offset
     fed_back = lax.dynamic_slice_in_dim(joined, start, parent_columns, axis=3)

time: 245 us -> 237 us (0.967)
  between operations: 9.03 us -> 2.78 us
  loops' own time: 0.26 us -> 6.49 us
  local copies, waits for them, and re-layouts: 39 us -> 34.9 us
  starting transfers between devices: 9.67 us -> 7.13 us
    reshape x0 -> x6, local copies, waits for them, and re-layouts: none -> 11.7 us  [the longest x5 10.5 us: flat(): block.reshape(size // 128, 128)]
    another operation x7 -> x0, local copies, waits for them, and re-layouts: 8.72 us -> none  [the longest x6 8.57 us: per_device(): stacked_pieces = jnp.stack(pieces)]
    pallas_call x2, Pallas kernels: 77.1 us -> 69.7 us  [exchange(): pl.pallas_call(lambda *refs: exchange_kernel(axis, remote, local, len(pie...]
    pallas_call x4, Pallas kernels: 46.2 us -> 53.4 us  [neighbours(): pl.pallas_call(lambda *refs: halo_kernel(rows, cols, *refs), out_shape=tu...]
    another operation x1, loops' own time: 0.21 us -> 6.47 us  [per_device(): within_part, beyond_part = lax.switch(regime, branches, stacked_pieces)]
    unnamed x10 -> x6, local copies, waits for them, and re-layouts: 5.56 us -> 0.14 us
    all_to_all x1, starting transfers between devices: 9.67 us -> 7.13 us  [per_device(): lax.all_to_all(stacked, 'gx', split_axis=2, concat_axis=2, tiled=True)]
  transfers between devices with their start and end apart: 1 -> 1, of which waited for: 0 -> 0; matrix products, arithmetic and copies ran while one was open for 3% -> 2% of each run, Pallas kernels for 12% -> 13%
where the time goes in v14:
time: 237 us; the launch traced here: 236 us
  Pallas kernels  167 us (70%)
  local copies, waits for them, and re-layouts  34.9 us (15%)
  other arithmetic  10.6 us (4%)
  starting transfers between devices  7.13 us (3%)
  matrix products  6.97 us (3%)
  loops' own time  6.49 us (3%)
  between operations  2.78 us (1%)
    pallas_call x2, Pallas kernels, exchange(): pl.pallas_call(lambda *refs: exchange_kernel(axis, remote, local, len(pie...  69.7 us
    pallas_call x4, Pallas kernels, neighbours(): pl.pallas_call(lambda *refs: halo_kernel(rows, cols, *refs), out_shape=tu...  53.4 us
    pallas_call x4, Pallas kernels, stencil(): pl.pallas_call(lambda *refs: stencil_kernel(relaxed, *refs), out_shape=ou...  24.1 us
    pallas_call x1, Pallas kernels, gather(): pl.pallas_call(lambda *refs: gather_kernel(axis, count, *refs), out_shape...  19.9 us
    reshape x5, local copies, waits for them, and re-layouts, flat(): block.reshape(size // 128, 128)  10.5 us
    all_to_all x1, starting transfers between devices, per_device(): lax.all_to_all(stacked, 'gx', split_axis=2, concat_axis=2, tiled=True)  7.13 us
    another operation x1, loops' own time, per_device(): within_part, beyond_part = lax.switch(regime, branches, stacked_pieces)  6.47 us
  transfers between devices with their start and end apart: 1, of which 0 were waited for; matrix products, arithmetic and copies ran while one was open for 2% of the time, Pallas kernels for 13%

profile of v14, /device:TPU:73, one launch (start us, length us, event | category | flops | bytes accessed | tf_op | source)
XLA Modules:
  0.0 236.0 jit_solution(7635914197080110687)
XLA Ops:
  0.6 1.2 slice_reduce_fusion.4
  1.9 1.7 slice_reduce_fusion
  3.5 1.4 fusion.52
  5.5 0.1 compare_select_fusion
  5.6 0.1 fusion.41
  5.7 0.6 reshape_squeeze.28.refs_0_
  6.3 0.6 reshape_squeeze.29.refs_1_
  6.9 0.6 reshape_squeeze.30.refs_2_
  7.5 0.6 reshape_squeeze.31.refs_3_
  8.9 6.6 %shard_map.87 = (f32[20,384]{1,0:T(8,128)}, f32[20,384]{1,0:T(8,128)}, f32[20,48]{1,0:T(8,128)}, f32[20,48]{1,0:T(8,128)}) custom-call(f32[20,384]{1,0:T(8,128)} %reshape_squeeze.28.refs_0_, f32[20,384]{1,0:T(8,128)} %reshape_squeeze.29.refs_1_, f32[20,48]{1,0:T(8,128)} %reshape_squeeze.30.refs_2_, f32[20,48]{1,0:T(8,128)} %reshape_squeeze.31.refs_3_), custom_call_target="tpu_custom_call" | custom-call | tf_op jit(solution)/shard_map/pallas_call | solution.py:81
  15.4 4.5 %shard_map.88 = f32[5,4,48,384]{3,2,1,0:T(8,128)S(1)} custom-call(f32[5,4,48,384]{3,2,1,0:T(8,128)} %refs_0_.2, f32[2,4,48,384]{3,2,1,0:T(8,128)} %refs_1_.4, f32[4,48,384]{2,1,0:T(8,128)} %refs_2_.4, f32[20,384]{1,0:T(8,128)} %get-tuple-element.87.refs_3_, f32[20,384]{1,0:T(8,128)} %get-tuple-element.88.refs_4_, f32[20,48]{1,0:T(8,128)} %get-tuple-element.89.refs_5_, ...), custom_call_target="tpu_custom_call" | custom-call | tf_op jit(solution)/shard_map/pallas_call | solution.py:416
  19.9 43.0 %conditional.2 = (f32[2,975,128]{2,1,0:T(8,128)S(1)}) conditional(s32[]{:T(128)} %clamp.13, (f32[5,4,48,384]{3,2,1,0:T(8,128)S(1)}, f32[]{:T(128)}, s32[]{:T(128)}, s32[]{:T(128)}, s32[]{:T(128)}, /*index=5*/s32[]{:T(128)}, s32[]{:T(128)}, s32[]{:T(128)}, s32[]{:T(128)}, s32[]{:T(128)}, /*index=10*/s32[]{:T(128)}, ...), branch_computations={%region_0.1_spmd.clone.clone, %region_1.2_spmd.clone.clone, %regio... | conditional | flops 19 | bytes 8962810 | solution.py:497
  26.2 2.9 %pad_dynamic-slice_fusion.2 = (f32[5,4,48,130]{3,2,1,0:T(8,128)S(1)}, f32[5,4,48,130]{3,2,1,0:T(8,128)}, f32[5,4,48,130]{3,2,1,0:T(8,128)}, f32[5,4,48,130]{3,2,1,0:T(8,128)S(1)}, f32[5,4,48,130]{3,2,1,0:T(8,128)}) fusion(s32[]{:T(128)S(6)} %select_n.264, f32[5,4,48,384]{3,2,1,0:T(8,128)S(1)} %get-tuple-element.556, f32[]{:T(128)} %get-tuple-element.557, ...), kind=kLoop, calls=%fused_computation.3 | loop fusion | bytes 3970584 | tf_op jit(solution)/shard_map/dynamic_slice | solution.py:480
  29.1 2.6 %reshape.333.refs_0_ = f32[975,128]{1,0:T(8,128)} reshape(f32[5,4,48,130]{3,2,1,0:T(8,128)} %get-tuple-element.644) | data formatting | bytes 998400 | tf_op jit(solution)/shard_map/reshape | solution.py:427
  31.7 2.6 %reshape.334.refs_1_ = f32[975,128]{1,0:T(8,128)} reshape(f32[5,4,48,130]{3,2,1,0:T(8,128)} %get-tuple-element.641) | data formatting | bytes 998400 | tf_op jit(solution)/shard_map/reshape | solution.py:427
  34.3 2.6 %reshape.335.refs_2_ = f32[975,128]{1,0:T(8,128)} reshape(f32[5,4,48,130]{3,2,1,0:T(8,128)} %get-tuple-element.642) | data formatting | bytes 998400 | tf_op jit(solution)/shard_map/reshape | solution.py:427
  36.9 1.4 reshape.336.refs_3_
  38.3 1.4 reshape.337.refs_4_
  39.7 23.1 %branch_0_fun.3 = f32[2,975,128]{2,1,0:T(8,128)S(1)} custom-call(f32[975,128]{1,0:T(8,128)} %reshape.333.refs_0_, f32[975,128]{1,0:T(8,128)} %reshape.334.refs_1_, f32[975,128]{1,0:T(8,128)} %reshape.335.refs_2_, f32[975,128]{1,0:T(8,128)} %reshape.336.refs_3_, f32[975,128]{1,0:T(8,128)} %reshape.337.refs_4_), custom_call_target="tpu_custom_call" | custom-call | tf_op jit(solution)/shard_map/cond/branch_0_fun/pallas_call | solution.py:268
  63.0 0.1 slice_add_fusion
  63.1 1.2 add.344
  64.3 0.6 copy.14
  64.9 0.3 pad.13
  65.2 0.1 reshape.322
  65.3 4.3 %gather_fusion = f32[144,5,4,130]{3,2,1,0:T(4,128)} fusion(f32[5,4,84,130]{3,1,2,0:T(4,128)S(1)} %pad.13, s32[1024]{0:T(1024)S(1)} %pad_clamp_fusion), kind=kCustom, calls=%fused_computation | custom fusion | bytes 2995776 | tf_op jit(solution)/shard_map/jit(_take)/gather | solution.py:506
  69.6 4.1 %select_bitcast_fusion = f32[5,4,8,18,130]{4,1,0,3,2:T(4,128)} fusion(f32[8,18,5,4,130]{4,3,2,1,0:T(4,128)} %bitcast.75, pred[8,18]{1,0:T(8,128)(4,1)S(1)} %fusion.41), kind=kLoop, calls=%fused_computation.18 | loop fusion | flops 374400 | bytes 2995344 | tf_op jit(solution)/shard_map/jit(_take)/select_n | solution.py:506
  73.7 0.0 copy-start
  73.7 7.1 %all-to-all-start = ((f32[5,4,8,18,130]{4,1,0,3,2:T(4,128)}), f32[5,4,8,18,130]{4,1,0,3,2:T(4,128)}, u32[]{:S(2)}, u32[]{:S(2)}) async-start(f32[5,4,8,18,130]{4,1,0,3,2:T(4,128)} %select_bitcast_fusion), calls=%async_computation | async-start | bytes 5898240 | tf_op jit(solution)/shard_map/all_to_all | solution.py:507
  80.9 0.0 copy-done
  80.9 0.2 slice_reduce_fusion.6
  81.1 0.5 slice_reduce_fusion.2
  82.2 0.6 compare_and_fusion
  82.8 0.6 reshape_squeeze.24.refs_0_
  83.4 0.6 reshape_squeeze.25.refs_1_
  84.0 0.6 reshape_squeeze.26.refs_2_
  84.6 0.6 reshape_squeeze.27.refs_3_
  85.2 31.3 %shard_map.86 = (f32[20,384]{1,0:T(8,128)}, f32[20,384]{1,0:T(8,128)}, f32[20,48]{1,0:T(8,128)}, f32[20,48]{1,0:T(8,128)}) custom-call(f32[20,384]{1,0:T(8,128)} %reshape_squeeze.24.refs_0_, f32[20,384]{1,0:T(8,128)} %reshape_squeeze.25.refs_1_, f32[20,48]{1,0:T(8,128)} %reshape_squeeze.26.refs_2_, f32[20,48]{1,0:T(8,128)} %reshape_squeeze.27.refs_3_), custom_call_target="tpu_custom_call" | custom-call | tf_op jit(solution)/shard_map/pallas_call | solution.py:81
  116.5 0.7 fusion.46
  117.3 0.1 broadcast_and_fusion
  117.4 0.7 multiply_add_fusion.refs_8_
  118.2 0.0 all-to-all-done
  118.2 2.5 %reduce_sum.9 = f32[5,4,18,130]{3,1,0,2:T(4,128)S(1)} reduce(f32[5,4,8,18,130]{4,1,0,3,2:T(4,128)} %all-to-all-done, f32[]{:T(128)} %constant.138.clone.1), dimensions={2}, to_apply=%region_3.4 | reduce | flops 327600 | bytes 1684804 | tf_op jit(solution)/shard_map/reduce_sum | solution.py:508
  120.6 1.0 convolution_bitcast_fusion
  121.6 2.9 %fusion.1.refs_7_ = f32[5,4,48,384]{3,2,1,0:T(8,128)} fusion(f32[5,4,48,130]{3,2,1,0:T(8,128)S(1)} %convolution_bitcast_fusion, f32[384]{0:T(512)S(1)} %get-tuple-element.666, s32[384]{0:T(512)S(1)} %get-tuple-element.668, f32[384]{0:T(512)S(1)} %get-tuple-element.667, s32[384]{0:T(512)S(1)} %add_select_fusion, f32[384]{0:T(512)S(1)} %compare_select_fusion.4, ...), kind=kOutput, calls=%fused_computation.31 | convolution fusion | flops 575477760 | bytes 1982976 | tf_op jit(solution)/shard_map/flac,bc->flab/dot_general | solution.py:151
  124.5 6.5 %shard_map.89 = (f32[5,4,48,384]{3,2,1,0:T(8,128)}, f32[20,384]{1,0:T(8,128)}, f32[20,384]{1,0:T(8,128)}, f32[20,48]{1,0:T(8,128)}, f32[20,48]{1,0:T(8,128)}) custom-call(f32[5,4,48,384]{3,2,1,0:T(8,128)} %refs_0_.3, f32[2,4,48,384]{3,2,1,0:T(8,128)} %refs_1_.7, f32[4,48,384]{2,1,0:T(8,128)} %refs_2_.7, f32[20,384]{1,0:T(8,128)} %get-tuple-element.83.refs_3_, ...), custom_call_target="tpu_custom_call" | custom-call | tf_op jit(solution)/shard_map/pallas_call | solution.py:416
  131.0 8.2 %shard_map.90 = (f32[20,384]{1,0:T(8,128)}, f32[20,384]{1,0:T(8,128)}, f32[20,48]{1,0:T(8,128)}, f32[20,48]{1,0:T(8,128)}) custom-call(f32[20,384]{1,0:T(8,128)} %get-tuple-element.92.refs_0_, f32[20,384]{1,0:T(8,128)} %get-tuple-element.93.refs_1_, f32[20,48]{1,0:T(8,128)} %get-tuple-element.94.refs_2_, f32[20,48]{1,0:T(8,128)} %get-tuple-element.95.refs_3_), custom_call_target="tpu_custom_call" | custom-call | tf_op jit(solution)/shard_map/pallas_call | solution.py:81
  139.1 6.5 %shard_map.91 = (f32[5,4,48,384]{3,2,1,0:T(8,128)}, f32[20,384]{1,0:T(8,128)}, f32[20,384]{1,0:T(8,128)}, f32[20,48]{1,0:T(8,128)}, f32[20,48]{1,0:T(8,128)}) custom-call(f32[5,4,48,384]{3,2,1,0:T(8,128)} %get-tuple-element.91.refs_0_, f32[2,4,48,384]{3,2,1,0:T(8,128)} %refs_1_.7, f32[4,48,384]{2,1,0:T(8,128)} %refs_2_.7, ...), custom_call_target="tpu_custom_call" | custom-call | tf_op jit(solution)/shard_map/pallas_call | solution.py:416
  145.7 7.4 %shard_map.92 = (f32[20,384]{1,0:T(8,128)}, f32[20,384]{1,0:T(8,128)}, f32[20,48]{1,0:T(8,128)}, f32[20,48]{1,0:T(8,128)}) custom-call(f32[20,384]{1,0:T(8,128)} %get-tuple-element.101.refs_0_, f32[20,384]{1,0:T(8,128)} %get-tuple-element.102.refs_1_, f32[20,48]{1,0:T(8,128)} %get-tuple-element.103.refs_2_, f32[20,48]{1,0:T(8,128)} %get-tuple-element.104.refs_3_), custom_call_target="tpu_custom_call" | custom-call | tf_op jit(solution)/shard_map/pallas_call | solution.py:81
  153.0 6.5 %shard_map.93 = (f32[5,4,48,384]{3,2,1,0:T(8,128)}, f32[20,384]{1,0:T(8,128)}, f32[20,384]{1,0:T(8,128)}, f32[20,48]{1,0:T(8,128)}, f32[20,48]{1,0:T(8,128)}) custom-call(f32[5,4,48,384]{3,2,1,0:T(8,128)} %get-tuple-element.100.refs_0_, f32[2,4,48,384]{3,2,1,0:T(8,128)} %refs_1_.7, f32[4,48,384]{2,1,0:T(8,128)} %refs_2_.7, ...), custom_call_target="tpu_custom_call" | custom-call | tf_op jit(solution)/shard_map/pallas_call | solution.py:416
  159.6 2.2 fusion.9
  161.8 1.0 convolution_multiply_fusion
  162.7 19.9 %shard_map.94 = f32[8,20,16,128]{3,2,1,0:T(8,128)S(1)} custom-call(f32[20,16,128]{2,1,0:T(8,128)} %bitcast.87), custom_call_target="tpu_custom_call" | custom-call | tf_op jit(solution)/shard_map/pallas_call | solution.py:318
  182.7 49.8 %conditional.3 = (f32[5,960,128]{2,1,0:T(8,128)}) conditional(s32[]{:T(128)} %clamp.12, (f32[20,8,16,128]{3,2,0,1:T(8,128)S(1)}, s32[]{:T(128)}, s32[]{:T(128)}, f32[]{:T(128)}, s32[]{:T(128)}, /*index=5*/s32[]{:T(128)}) %tuple.138, (f32[20,8,16,128]{3,2,0,1:T(8,128)S(1)}, s32[]{:T(128)}, s32[]{:T(128)}, f32[]{:T(128)}, s32[]{:T(128)}, ...), branch_computations={%region_4.5_spmd.clone, %region_5.6_spmd.clone} | conditional | flops 3 | bytes 4423730 | solution.py:554
  182.7 1.2 copy.16
  183.9 1.9 pad_dynamic-slice_fusion
  185.8 46.6 %branch_0_fun.2 = f32[5,960,128]{2,1,0:T(8,128)} custom-call(f32[960,128]{1,0:T(8,128)} %bitcast.85), custom_call_target="tpu_custom_call" | custom-call | tf_op jit(solution)/shard_map/cond/branch_0_fun/pallas_call | solution.py:268
  232.4 1.8 fusion.51
  234.4 1.6 dynamic-slice_select_fusion
  (17 shorter events, 0.3 us)
Async XLA Ops:
  73.7 7.2 %copy-start = (f32[5,4,48,384]{3,2,1,0:T(8,128)S(1)}, f32[5,4,48,384]{3,2,1,0:T(8,128)}, u32[]{:S(2)}) copy-start(f32[5,4,48,384]{3,2,1,0:T(8,128)} %refs_0_.3) | copy-start | bytes 4423684
  73.7 44.4 %all-to-all-start = ((f32[5,4,8,18,130]{4,1,0,3,2:T(4,128)}), f32[5,4,8,18,130]{4,1,0,3,2:T(4,128)}, u32[]{:S(2)}, u32[]{:S(2)}) async-start(f32[5,4,8,18,130]{4,1,0,3,2:T(4,128)} %select_bitcast_fusion), calls=%async_computation | async-start | bytes 5898240 | tf_op jit(solution)/shard_map/all_to_all | solution.py:507

commit v15 on v13

--- a/solution.py
+++ b/solution.py
@@ -326,7 +326,7 @@
     )(block)
 
 
-def stencil_kernel(relaxed, *refs):
+def stencil_kernel(relaxed, margin, *refs):
     if relaxed:
         (values, velocity, mixing, western, eastern, southern, northern, forcing, weight) = refs[:9]
         out, last_row, first_row, last_col, first_col = refs[9:]
@@ -382,10 +382,16 @@
             )
             first_col[pl.ds(first + level, 1), :] = sides[0:1, :]
             last_col[pl.ds(first + level, 1), :] = sides[1:2, :]
-        out[0, level] = moved
-
-
-def stencil(values, halo, velocity, mixing, forcing=None, weight=None):
+        if margin:
+            blank = jnp.zeros((height, margin), moved.dtype)
+            out[0, level, :, :margin] = blank
+            out[0, level, :, margin:margin + width] = moved
+            out[0, level, :, margin + width:] = blank
+        else:
+            out[0, level] = moved
+
+
+def stencil(values, halo, velocity, mixing, forcing=None, weight=None, margin=0):
     fields, levels, height, width = values.shape
     west_row, east_row, south_col, north_col = halo
     plane = pl.BlockSpec((1, levels, height, width), lambda f: (f, 0, 0, 0))
@@ -402,8 +408,10 @@
         edge_col,
     ]
     relaxed = forcing is not None
-    out_shape = jax.ShapeDtypeStruct(values.shape, values.dtype)
-    out_specs = plane
+    out_shape = jax.ShapeDtypeStruct(
+        (fields, levels, height, width + 2 * margin), values.dtype
+    )
+    out_specs = pl.BlockSpec((1, levels, height, width + 2 * margin), lambda f: (f, 0, 0, 0))
     if relaxed:
         operands += [forcing, weight]
         specs += [plane, pl.BlockSpec(weight.shape, lambda f: (0, 0))]
@@ -412,7 +420,7 @@
         out_shape = (out_shape, rows_shape, rows_shape, cols_shape, cols_shape)
         out_specs = (plane, edge_row, edge_row, edge_col, edge_col)
     return pl.pallas_call(
-        lambda *refs: stencil_kernel(relaxed, *refs),
+        lambda *refs: stencil_kernel(relaxed, margin, *refs),
         out_shape=out_shape,
         grid=(fields,),
         in_specs=specs,
@@ -453,12 +461,15 @@
     column_anchor = nest_anchor[1]
     offset = column_anchor - 1 - base_column
 
-    parent_next = stencil(
-        parent_fields, neighbours(edges(parent_fields), 2), parent_velocity, parent_mixing
-    )
-
     margin = parent_columns - span_columns
-    wide = jnp.pad(parent_next, ((0, 0), (0, 0), (0, 0), (margin, margin)))
+    wide = stencil(
+        parent_fields,
+        neighbours(edges(parent_fields), 2),
+        parent_velocity,
+        parent_mixing,
+        margin=margin,
+    )
+    parent_next = wide[:, :, :, margin:margin + parent_columns]
     straddle = (ratio - 1) * span_columns - 2
     regimes = (
         lambda k, extra: not (extra == 1 and k == ratio - 2),

time: 245 us -> 245 us (level)
    unnamed x10 -> x8, local copies, waits for them, and re-layouts: 5.56 us -> 4.41 us
where the time goes in v15:
time: 245 us; the launch traced here: 243 us
  Pallas kernels  170 us (69%)
  local copies, waits for them, and re-layouts  38.6 us (16%)
  other arithmetic  10.3 us (4%)
  starting transfers between devices  9.66 us (4%)
  between operations  8.08 us (3%)
  matrix products  6.97 us (3%)
    pallas_call x2, Pallas kernels, exchange(): pl.pallas_call(lambda *refs: exchange_kernel(axis, remote, local, *refs),...  77.1 us
    pallas_call x4, Pallas kernels, neighbours(): pl.pallas_call(lambda *refs: halo_kernel(rows, cols, *refs), out_shape=tu...  45.6 us
    pallas_call x4, Pallas kernels, stencil(): pl.pallas_call(lambda *refs: stencil_kernel(relaxed, margin, *refs), out_...  25.4 us
    pallas_call x1, Pallas kernels, gather(): pl.pallas_call(lambda *refs: gather_kernel(axis, count, *refs), out_shape...  21.6 us
    all_to_all x1, starting transfers between devices, per_device(): lax.all_to_all(stacked, 'gx', split_axis=2, concat_axis=2, tiled=True)  9.66 us
    another operation x6, local copies, waits for them, and re-layouts, per_device(): stacked_pieces = jnp.stack(pieces)  8.57 us
    dynamic_slice x1, local copies, waits for them, and re-layouts, per_device(): piece = lax.dynamic_slice_in_dim(wide, start, relay_columns, axis=3)  5.85 us
  transfers between devices with their start and end apart: 1, of which 0 were waited for; matrix products, arithmetic and copies ran while one was open for 3% of the time, Pallas kernels for 12%

profile of v15, /device:TPU:73, one launch (start us, length us, event | category | flops | bytes accessed | tf_op | source)
XLA Modules:
  0.0 243.4 jit_solution(4584225174020218918)
XLA Ops:
  0.6 1.3 fusion.52
  2.7 0.1 fusion.41
  2.7 0.1 compare_select_fusion
  2.8 1.7 slice_reduce_fusion
  4.5 1.2 slice_reduce_fusion.4
  11.5 0.1 reshape.258
  11.6 0.6 reshape_squeeze.31.refs_3_
  12.2 0.6 reshape_squeeze.30.refs_2_
  12.8 0.6 reshape_squeeze.29.refs_1_
  13.4 0.6 reshape_squeeze.28.refs_0_
  14.0 6.5 %shard_map.87 = (f32[20,384]{1,0:T(8,128)}, f32[20,384]{1,0:T(8,128)}, f32[20,48]{1,0:T(8,128)}, f32[20,48]{1,0:T(8,128)}) custom-call(f32[20,384]{1,0:T(8,128)} %reshape_squeeze.28.refs_0_, f32[20,384]{1,0:T(8,128)} %reshape_squeeze.29.refs_1_, f32[20,48]{1,0:T(8,128)} %reshape_squeeze.30.refs_2_, f32[20,48]{1,0:T(8,128)} %reshape_squeeze.31.refs_3_), custom_call_target="tpu_custom_call" | custom-call | tf_op jit(solution)/shard_map/pallas_call | solution.py:81
  20.6 5.8 %shard_map.88 = f32[5,4,48,896]{3,2,1,0:T(8,128)} custom-call(f32[5,4,48,384]{3,2,1,0:T(8,128)} %refs_0_.5, f32[2,4,48,384]{3,2,1,0:T(8,128)} %refs_1_.4, f32[4,48,384]{2,1,0:T(8,128)} %refs_2_.4, f32[20,384]{1,0:T(8,128)} %get-tuple-element.45.refs_3_, f32[20,384]{1,0:T(8,128)} %get-tuple-element.46.refs_4_, f32[20,48]{1,0:T(8,128)} %get-tuple-element.47.refs_5_, ...), custom_call_target="tpu_custom_call" | custom-call | tf_op jit(solution)/shard_map/pallas_call | solution.py:422
  26.4 5.8 %constant_dynamic-slice_fusion = (f32[5,4,48,130]{3,2,1,0:T(8,128)}, f32[5,4,48,130]{3,2,1,0:T(8,128)}, f32[5,4,48,130]{3,2,1,0:T(8,128)S(1)}, f32[5,4,48,130]{3,2,1,0:T(8,128)S(1)}, f32[5,4,48,130]{3,2,1,0:T(8,128)S(1)}) fusion(f32[5,4,48,896]{3,2,1,0:T(8,128)} %shard_map.88, s32[]{:T(128)S(6)} %select_n.203, s32[]{:T(128)S(6)} %select_n.202, ...), kind=kLoop, calls=%fused_computation.101 | loop fusion | bytes 4992020 | tf_op jit(solution)/shard_map/dynamic_slice | solution.py:489
  32.2 1.8 stack_reshape.19
  34.0 2.6 %stack_reshape.18 = f32[1,975,128]{2,1,0:T(8,128)} reshape(f32[5,4,48,130]{3,2,1,0:T(8,128)} %get-tuple-element.167) | data formatting | bytes 998400 | tf_op jit(solution)/shard_map/stack;reshape | solution.py:492
  36.6 1.4 stack_reshape.17
  38.0 1.4 stack_reshape.16
  39.4 1.4 stack_reshape.15
  40.8 1.1 constant_dynamic-update-slice_fusion.4
  41.8 1.1 constant_dynamic-update-slice_fusion.3
  42.9 1.1 constant_dynamic-update-slice_fusion.2
  44.0 1.1 constant_dynamic-update-slice_fusion.1
  45.1 29.3 %conditional.2 = (f32[2,975,128]{2,1,0:T(8,128)S(1)}) conditional(s32[]{:T(128)} %clamp.13, f32[5,975,128]{2,1,0:T(8,128)S(1)} %constant_dynamic-update-slice_fusion, f32[5,975,128]{2,1,0:T(8,128)S(1)} %constant_dynamic-update-slice_fusion, f32[5,975,128]{2,1,0:T(8,128)S(1)} %constant_dynamic-update-slice_fusion), branch_computations={%region_0.0_spmd, %region_1.0_spmd, %region_2.0_spmd} | conditional | bytes 8 | solution.py:506
  45.1 29.1 %branch_2_fun.1 = f32[2,975,128]{2,1,0:T(8,128)S(1)} custom-call(f32[5,975,128]{2,1,0:T(8,128)S(1)} %refs_0_.4), custom_call_target="tpu_custom_call" | custom-call | tf_op jit(solution)/shard_map/cond/branch_2_fun/pallas_call | solution.py:266
  74.4 0.1 slice_add_fusion
  74.4 1.2 add.342
  75.6 0.6 copy.14
  76.3 0.3 pad.8
  76.6 4.3 %gather_fusion = f32[144,5,4,130]{3,2,1,0:T(4,128)} fusion(f32[5,4,84,130]{3,1,2,0:T(4,128)S(1)} %pad.8, s32[1024]{0:T(1024)S(1)} %pad_clamp_fusion), kind=kCustom, calls=%fused_computation | custom fusion | bytes 2995776 | tf_op jit(solution)/shard_map/jit(_take)/gather | solution.py:515
  80.9 4.2 %select_bitcast_fusion = f32[5,4,8,18,130]{4,1,0,3,2:T(4,128)} fusion(f32[8,18,5,4,130]{4,3,2,1,0:T(4,128)} %bitcast.55, pred[8,18]{1,0:T(8,128)(4,1)S(1)} %fusion.41), kind=kLoop, calls=%fused_computation.3 | loop fusion | flops 374400 | bytes 2995344 | tf_op jit(solution)/shard_map/jit(_take)/select_n | solution.py:515
  85.0 9.7 %all-to-all-start = ((f32[5,4,8,18,130]{4,1,0,3,2:T(4,128)}), f32[5,4,8,18,130]{4,1,0,3,2:T(4,128)S(1)}, u32[]{:S(2)}, u32[]{:S(2)}) async-start(f32[5,4,8,18,130]{4,1,0,3,2:T(4,128)} %select_bitcast_fusion), calls=%async_computation | async-start | bytes 5898240 | tf_op jit(solution)/shard_map/all_to_all | solution.py:516
  95.4 0.7 compare_and_fusion
  96.1 1.7 slice_reduce_fusion.2
  97.8 1.2 slice_reduce_fusion.6
  99.1 0.6 reshape_squeeze.27.refs_3_
  99.7 0.6 reshape_squeeze.26.refs_2_
  100.3 0.6 reshape_squeeze.25.refs_1_
  100.9 0.6 reshape_squeeze.24.refs_0_
  101.5 28.7 %shard_map.86 = (f32[20,384]{1,0:T(8,128)}, f32[20,384]{1,0:T(8,128)}, f32[20,48]{1,0:T(8,128)}, f32[20,48]{1,0:T(8,128)}) custom-call(f32[20,384]{1,0:T(8,128)} %reshape_squeeze.24.refs_0_, f32[20,384]{1,0:T(8,128)} %reshape_squeeze.25.refs_1_, f32[20,48]{1,0:T(8,128)} %reshape_squeeze.26.refs_2_, f32[20,48]{1,0:T(8,128)} %reshape_squeeze.27.refs_3_), custom_call_target="tpu_custom_call" | custom-call | tf_op jit(solution)/shard_map/pallas_call | solution.py:81
  130.3 0.6 fusion.46
  131.0 0.1 broadcast_and_fusion
  131.0 0.7 multiply_add_fusion.refs_8_
  131.8 0.0 all-to-all-done
  131.8 0.7 reduce_sum.9
  132.5 1.0 convolution_bitcast_fusion
  133.5 2.9 %fusion.1.refs_7_ = f32[5,4,48,384]{3,2,1,0:T(8,128)} fusion(f32[5,4,48,130]{3,2,1,0:T(8,128)S(1)} %convolution_bitcast_fusion, f32[384]{0:T(512)S(1)} %get-tuple-element.178, s32[384]{0:T(512)S(1)} %get-tuple-element.184, f32[384]{0:T(512)S(1)} %get-tuple-element.179, s32[384]{0:T(512)S(1)} %add_select_fusion, f32[384]{0:T(512)S(1)} %compare_select_fusion.4, ...), kind=kOutput, calls=%fused_computation.16 | convolution fusion | flops 575477760 | bytes 1982976 | tf_op jit(solution)/shard_map/flac,bc->flab/dot_general | solution.py:151
  136.4 6.5 %shard_map.89 = (f32[5,4,48,384]{3,2,1,0:T(8,128)}, f32[20,384]{1,0:T(8,128)}, f32[20,384]{1,0:T(8,128)}, f32[20,48]{1,0:T(8,128)}, f32[20,48]{1,0:T(8,128)}) custom-call(f32[5,4,48,384]{3,2,1,0:T(8,128)} %refs_0_.6, f32[2,4,48,384]{3,2,1,0:T(8,128)} %refs_1_.7, f32[4,48,384]{2,1,0:T(8,128)} %refs_2_.7, f32[20,384]{1,0:T(8,128)} %get-tuple-element.41.refs_3_, ...), custom_call_target="tpu_custom_call" | custom-call | tf_op jit(solution)/shard_map/pallas_call | solution.py:422
  142.9 5.0 %shard_map.90 = (f32[20,384]{1,0:T(8,128)}, f32[20,384]{1,0:T(8,128)}, f32[20,48]{1,0:T(8,128)}, f32[20,48]{1,0:T(8,128)}) custom-call(f32[20,384]{1,0:T(8,128)} %get-tuple-element.50.refs_0_, f32[20,384]{1,0:T(8,128)} %get-tuple-element.51.refs_1_, f32[20,48]{1,0:T(8,128)} %get-tuple-element.52.refs_2_, f32[20,48]{1,0:T(8,128)} %get-tuple-element.53.refs_3_), custom_call_target="tpu_custom_call" | custom-call | tf_op jit(solution)/shard_map/pallas_call | solution.py:81
  147.8 6.5 %shard_map.91 = (f32[5,4,48,384]{3,2,1,0:T(8,128)}, f32[20,384]{1,0:T(8,128)}, f32[20,384]{1,0:T(8,128)}, f32[20,48]{1,0:T(8,128)}, f32[20,48]{1,0:T(8,128)}) custom-call(f32[5,4,48,384]{3,2,1,0:T(8,128)} %get-tuple-element.49.refs_0_, f32[2,4,48,384]{3,2,1,0:T(8,128)} %refs_1_.7, f32[4,48,384]{2,1,0:T(8,128)} %refs_2_.7, ...), custom_call_target="tpu_custom_call" | custom-call | tf_op jit(solution)/shard_map/pallas_call | solution.py:422
  154.4 5.4 %shard_map.92 = (f32[20,384]{1,0:T(8,128)}, f32[20,384]{1,0:T(8,128)}, f32[20,48]{1,0:T(8,128)}, f32[20,48]{1,0:T(8,128)}) custom-call(f32[20,384]{1,0:T(8,128)} %get-tuple-element.59.refs_0_, f32[20,384]{1,0:T(8,128)} %get-tuple-element.60.refs_1_, f32[20,48]{1,0:T(8,128)} %get-tuple-element.61.refs_2_, f32[20,48]{1,0:T(8,128)} %get-tuple-element.62.refs_3_), custom_call_target="tpu_custom_call" | custom-call | tf_op jit(solution)/shard_map/pallas_call | solution.py:81
  159.7 6.5 %shard_map.93 = (f32[5,4,48,384]{3,2,1,0:T(8,128)}, f32[20,384]{1,0:T(8,128)}, f32[20,384]{1,0:T(8,128)}, f32[20,48]{1,0:T(8,128)}, f32[20,48]{1,0:T(8,128)}) custom-call(f32[5,4,48,384]{3,2,1,0:T(8,128)} %get-tuple-element.58.refs_0_, f32[2,4,48,384]{3,2,1,0:T(8,128)} %refs_1_.7, f32[4,48,384]{2,1,0:T(8,128)} %refs_2_.7, ...), custom_call_target="tpu_custom_call" | custom-call | tf_op jit(solution)/shard_map/pallas_call | solution.py:422
  166.3 2.2 fusion.9
  168.5 1.0 convolution_multiply_fusion
  169.4 21.6 %shard_map.94 = f32[8,20,16,128]{3,2,1,0:T(8,128)S(1)} custom-call(f32[20,16,128]{2,1,0:T(8,128)} %bitcast.67), custom_call_target="tpu_custom_call" | custom-call | tf_op jit(solution)/shard_map/pallas_call | solution.py:316
  191.0 49.1 %conditional.3 = (f32[5,960,128]{2,1,0:T(8,128)S(1)}) conditional(s32[]{:T(128)} %clamp.12, (f32[20,8,16,128]{3,2,0,1:T(8,128)S(1)}, s32[]{:T(128)}, s32[]{:T(128)}, f32[]{:T(128)}, s32[]{:T(128)}, /*index=5*/s32[]{:T(128)}) %tuple.63, (f32[20,8,16,128]{3,2,0,1:T(8,128)S(1)}, s32[]{:T(128)}, s32[]{:T(128)}, f32[]{:T(128)}, s32[]{:T(128)}, ...), branch_computations={%region_4.5_spmd.clone, %region_5.6_spmd.clone} | conditional | flops 3 | bytes 4423730 | solution.py:563
  191.0 0.1 copy.17
  191.2 0.9 pad_dynamic-slice_fusion.1
  192.0 48.0 %branch_1_fun.3 = f32[5,960,128]{2,1,0:T(8,128)S(1)} custom-call(f32[1,960,128]{2,1,0:T(8,128)} %bitcast.66), custom_call_target="tpu_custom_call" | custom-call | tf_op jit(solution)/shard_map/cond/branch_1_fun/pallas_call | solution.py:266
  240.0 0.2 fusion.51
  240.4 3.0 %slice_select_fusion = f32[5,4,48,384]{3,2,1,0:T(8,128)} fusion(f32[5,4,48,896]{3,2,1,0:T(8,128)} %shard_map.88, f32[5,4,48,640]{3,2,1,0:T(8,128)S(1)} %constant_dynamic-update-slice_fusion.5, s32[]{:T(128)S(6)} %select_n.223, pred[48,384]{1,0:T(8,128)(4,1)S(1)} %broadcast_and_fusion), kind=kLoop, calls=%fused_computation.4 | loop fusion | flops 368640 | bytes 4442116 | tf_op jit(solution)/shard_map/jit(_where)/select_n | solution.py:575
  (18 shorter events, 0.3 us)
Async XLA Ops:
  85.0 46.7 %all-to-all-start = ((f32[5,4,8,18,130]{4,1,0,3,2:T(4,128)}), f32[5,4,8,18,130]{4,1,0,3,2:T(4,128)S(1)}, u32[]{:S(2)}, u32[]{:S(2)}) async-start(f32[5,4,8,18,130]{4,1,0,3,2:T(4,128)} %select_bitcast_fusion), calls=%async_computation | async-start | bytes 5898240 | tf_op jit(solution)/shard_map/all_to_all | solution.py:516

commit v16 on v13

--- a/solution.py
+++ b/solution.py
@@ -501,7 +501,7 @@
     first = row_anchor - 1 + span_rows * targets - parent_rows * row_rank
     first = jnp.clip(first, -relay_rows, parent_rows) + relay_rows
     picks = first + jnp.arange(relay_rows, dtype=jnp.int32)[None, :]
-    stacked = jnp.take(padded, picks, axis=2)
+    stacked = jnp.take(padded, picks, axis=2, mode="clip")
     received = lax.all_to_all(stacked, "gx", split_axis=2, concat_axis=2, tiled=True)
     relay = jnp.sum(received, axis=2)
 

time: 245 us -> 235 us (0.959); the launches traced: 243 us -> 238 us
  other arithmetic: 8.84 us -> 4.53 us
    select_n x2 -> x0, other arithmetic: 4.22 us -> none  [per_device(): stacked = jnp.take(padded, picks, axis=2)]
where the time goes in v16:
time: 235 us; the launch traced here: 238 us
  Pallas kernels  169 us (72%)
  local copies, waits for them, and re-layouts  38.9 us (17%)
  starting transfers between devices  9.68 us (4%)
  between operations  8.31 us (4%)
  matrix products  6.99 us (3%)
  other arithmetic  4.53 us (2%)
    pallas_call x2, Pallas kernels, exchange(): pl.pallas_call(lambda *refs: exchange_kernel(axis, remote, local, *refs),...  77.1 us
    pallas_call x4, Pallas kernels, neighbours(): pl.pallas_call(lambda *refs: halo_kernel(rows, cols, *refs), out_shape=tu...  46.2 us
    pallas_call x4, Pallas kernels, stencil(): pl.pallas_call(lambda *refs: stencil_kernel(relaxed, *refs), out_shape=ou...  25 us
    pallas_call x1, Pallas kernels, gather(): pl.pallas_call(lambda *refs: gather_kernel(axis, count, *refs), out_shape...  21.2 us
    all_to_all x1, starting transfers between devices, per_device(): lax.all_to_all(stacked, 'gx', split_axis=2, concat_axis=2, tiled=True)  9.68 us
    another operation x6, local copies, waits for them, and re-layouts, per_device(): stacked_pieces = jnp.stack(pieces)  8.57 us
    unnamed x10, local copies, waits for them, and re-layouts  5.56 us
    dynamic_slice x1, local copies, waits for them, and re-layouts, per_device(): piece = lax.dynamic_slice_in_dim(wide, start, relay_columns, axis=3)  5.06 us
  transfers between devices with their start and end apart: 1, of which 0 were waited for; matrix products, arithmetic and copies ran while one was open for 3% of the time, Pallas kernels for 12%

profile of v16, /device:TPU:73, one launch (start us, length us, event | category | flops | bytes accessed | tf_op | source)
XLA Modules:
  0.0 238.1 jit_solution(7834759499334307536)
XLA Ops:
  0.6 1.7 slice_reduce_fusion
  2.3 1.2 slice_reduce_fusion.4
  3.5 1.3 fusion.49
  11.7 0.1 iota_add_fusion
  11.7 0.1 reshape.231
  11.8 0.6 reshape_squeeze.31.refs_3_
  12.5 0.6 reshape_squeeze.30.refs_2_
  13.1 0.6 reshape_squeeze.29.refs_1_
  13.7 0.6 reshape_squeeze.28.refs_0_
  14.3 6.5 %shard_map.87 = (f32[20,384]{1,0:T(8,128)}, f32[20,384]{1,0:T(8,128)}, f32[20,48]{1,0:T(8,128)}, f32[20,48]{1,0:T(8,128)}) custom-call(f32[20,384]{1,0:T(8,128)} %reshape_squeeze.28.refs_0_, f32[20,384]{1,0:T(8,128)} %reshape_squeeze.29.refs_1_, f32[20,48]{1,0:T(8,128)} %reshape_squeeze.30.refs_2_, f32[20,48]{1,0:T(8,128)} %reshape_squeeze.31.refs_3_), custom_call_target="tpu_custom_call" | custom-call | tf_op jit(solution)/shard_map/pallas_call | solution.py:81
  20.8 5.4 %shard_map.88 = f32[5,4,48,384]{3,2,1,0:T(8,128)} custom-call(f32[5,4,48,384]{3,2,1,0:T(8,128)} %refs_0_.5, f32[2,4,48,384]{3,2,1,0:T(8,128)} %refs_1_.4, f32[4,48,384]{2,1,0:T(8,128)} %refs_2_.4, f32[20,384]{1,0:T(8,128)} %get-tuple-element.45.refs_3_, f32[20,384]{1,0:T(8,128)} %get-tuple-element.46.refs_4_, f32[20,48]{1,0:T(8,128)} %get-tuple-element.47.refs_5_, ...), custom_call_target="tpu_custom_call" | custom-call | tf_op jit(solution)/shard_map/pallas_call | solution.py:414
  26.3 5.1 %pad_dynamic-slice_fusion.2 = (f32[5,4,48,130]{3,2,1,0:T(8,128)}, f32[5,4,48,130]{3,2,1,0:T(8,128)}, f32[5,4,48,130]{3,2,1,0:T(8,128)S(1)}, f32[5,4,48,130]{3,2,1,0:T(8,128)S(1)}, f32[5,4,48,130]{3,2,1,0:T(8,128)S(1)}) fusion(s32[]{:T(128)S(6)} %select_n.182, f32[5,4,48,384]{3,2,1,0:T(8,128)} %shard_map.88, s32[]{:T(128)S(6)} %select_n.179, ...), kind=kLoop, calls=%fused_computation.3 | loop fusion | bytes 3970580 | tf_op jit(solution)/shard_map/dynamic_slice | solution.py:478
  31.3 1.8 stack_reshape.19
  33.1 2.6 %stack_reshape.16 = f32[1,975,128]{2,1,0:T(8,128)} reshape(f32[5,4,48,130]{3,2,1,0:T(8,128)} %get-tuple-element.172) | data formatting | bytes 998400 | tf_op jit(solution)/shard_map/stack;reshape | solution.py:481
  35.7 1.4 stack_reshape.17
  37.1 1.4 stack_reshape.18
  38.5 1.4 stack_reshape.15
  39.9 1.1 constant_dynamic-update-slice_fusion.4
  40.9 1.1 constant_dynamic-update-slice_fusion.3
  42.0 1.1 constant_dynamic-update-slice_fusion.2
  43.1 1.1 constant_dynamic-update-slice_fusion.1
  44.2 29.3 %conditional.2 = (f32[2,975,128]{2,1,0:T(8,128)S(1)}) conditional(s32[]{:T(128)} %clamp.13, f32[5,975,128]{2,1,0:T(8,128)S(1)} %constant_dynamic-update-slice_fusion, f32[5,975,128]{2,1,0:T(8,128)S(1)} %constant_dynamic-update-slice_fusion, f32[5,975,128]{2,1,0:T(8,128)S(1)} %constant_dynamic-update-slice_fusion), branch_computations={%region_0.1_spmd, %region_1.2_spmd, %region_2.3_spmd} | conditional | bytes 8 | solution.py:495
  44.2 29.0 %branch_2_fun.1 = f32[2,975,128]{2,1,0:T(8,128)S(1)} custom-call(f32[5,975,128]{2,1,0:T(8,128)S(1)} %refs_0_.4), custom_call_target="tpu_custom_call" | custom-call | tf_op jit(solution)/shard_map/cond/branch_2_fun/pallas_call | solution.py:266
  73.5 0.1 slice_add_fusion
  73.5 1.2 add.307
  74.7 0.6 copy.14
  75.4 0.3 pad.13
  75.6 4.3 %gather_fusion = f32[144,5,4,130]{3,2,1,0:T(4,128)} fusion(f32[5,4,84,130]{3,1,2,0:T(4,128)S(1)} %pad.13, s32[1024]{0:T(1024)S(1)} %pad_clamp_fusion), kind=kCustom, calls=%fused_computation | custom fusion | bytes 2995776 | tf_op jit(solution)/shard_map/jit(_take)/gather | solution.py:504
  79.9 9.7 %all-to-all-start = ((f32[5,4,8,18,130]{4,1,0,3,2:T(4,128)}), f32[5,4,8,18,130]{4,1,0,3,2:T(4,128)S(1)}, u32[]{:S(2)}, u32[]{:S(2)}) async-start(f32[5,4,8,18,130]{4,1,0,3,2:T(4,128)} %bitcast.55), calls=%async_computation | async-start | bytes 5898240 | tf_op jit(solution)/shard_map/all_to_all | solution.py:505
  90.2 0.6 compare_and_fusion
  90.8 1.7 slice_reduce_fusion.2
  92.5 1.2 slice_reduce_fusion.6
  93.7 0.6 reshape_squeeze.27.refs_3_
  94.3 0.6 reshape_squeeze.26.refs_2_
  94.9 0.6 reshape_squeeze.25.refs_1_
  95.6 0.6 reshape_squeeze.24.refs_0_
  96.2 29.0 %shard_map.86 = (f32[20,384]{1,0:T(8,128)}, f32[20,384]{1,0:T(8,128)}, f32[20,48]{1,0:T(8,128)}, f32[20,48]{1,0:T(8,128)}) custom-call(f32[20,384]{1,0:T(8,128)} %reshape_squeeze.24.refs_0_, f32[20,384]{1,0:T(8,128)} %reshape_squeeze.25.refs_1_, f32[20,48]{1,0:T(8,128)} %reshape_squeeze.26.refs_2_, f32[20,48]{1,0:T(8,128)} %reshape_squeeze.27.refs_3_), custom_call_target="tpu_custom_call" | custom-call | tf_op jit(solution)/shard_map/pallas_call | solution.py:81
  125.2 0.6 fusion.43
  125.9 0.1 broadcast_and_fusion
  126.0 0.7 multiply_add_fusion.refs_8_
  126.7 0.0 all-to-all-done
  126.7 0.7 reduce_sum.9
  127.5 1.0 convolution_bitcast_fusion
  128.5 2.9 %fusion.1.refs_7_ = f32[5,4,48,384]{3,2,1,0:T(8,128)} fusion(f32[5,4,48,130]{3,2,1,0:T(8,128)S(1)} %convolution_bitcast_fusion, f32[384]{0:T(512)S(1)} %get-tuple-element.178, s32[384]{0:T(512)S(1)} %get-tuple-element.184, f32[384]{0:T(512)S(1)} %get-tuple-element.179, s32[384]{0:T(512)S(1)} %add_select_fusion, f32[384]{0:T(512)S(1)} %compare_select_fusion.2, ...), kind=kOutput, calls=%fused_computation.20 | convolution fusion | flops 575477760 | bytes 1982976 | tf_op jit(solution)/shard_map/flac,bc->flab/dot_general | solution.py:151
  131.4 6.5 %shard_map.89 = (f32[5,4,48,384]{3,2,1,0:T(8,128)}, f32[20,384]{1,0:T(8,128)}, f32[20,384]{1,0:T(8,128)}, f32[20,48]{1,0:T(8,128)}, f32[20,48]{1,0:T(8,128)}) custom-call(f32[5,4,48,384]{3,2,1,0:T(8,128)} %refs_0_.6, f32[2,4,48,384]{3,2,1,0:T(8,128)} %refs_1_.7, f32[4,48,384]{2,1,0:T(8,128)} %refs_2_.7, f32[20,384]{1,0:T(8,128)} %get-tuple-element.41.refs_3_, ...), custom_call_target="tpu_custom_call" | custom-call | tf_op jit(solution)/shard_map/pallas_call | solution.py:414
  137.9 5.0 %shard_map.90 = (f32[20,384]{1,0:T(8,128)}, f32[20,384]{1,0:T(8,128)}, f32[20,48]{1,0:T(8,128)}, f32[20,48]{1,0:T(8,128)}) custom-call(f32[20,384]{1,0:T(8,128)} %get-tuple-element.50.refs_0_, f32[20,384]{1,0:T(8,128)} %get-tuple-element.51.refs_1_, f32[20,48]{1,0:T(8,128)} %get-tuple-element.52.refs_2_, f32[20,48]{1,0:T(8,128)} %get-tuple-element.53.refs_3_), custom_call_target="tpu_custom_call" | custom-call | tf_op jit(solution)/shard_map/pallas_call | solution.py:81
  142.9 6.5 %shard_map.91 = (f32[5,4,48,384]{3,2,1,0:T(8,128)}, f32[20,384]{1,0:T(8,128)}, f32[20,384]{1,0:T(8,128)}, f32[20,48]{1,0:T(8,128)}, f32[20,48]{1,0:T(8,128)}) custom-call(f32[5,4,48,384]{3,2,1,0:T(8,128)} %get-tuple-element.49.refs_0_, f32[2,4,48,384]{3,2,1,0:T(8,128)} %refs_1_.7, f32[4,48,384]{2,1,0:T(8,128)} %refs_2_.7, ...), custom_call_target="tpu_custom_call" | custom-call | tf_op jit(solution)/shard_map/pallas_call | solution.py:414
  149.4 5.7 %shard_map.92 = (f32[20,384]{1,0:T(8,128)}, f32[20,384]{1,0:T(8,128)}, f32[20,48]{1,0:T(8,128)}, f32[20,48]{1,0:T(8,128)}) custom-call(f32[20,384]{1,0:T(8,128)} %get-tuple-element.59.refs_0_, f32[20,384]{1,0:T(8,128)} %get-tuple-element.60.refs_1_, f32[20,48]{1,0:T(8,128)} %get-tuple-element.61.refs_2_, f32[20,48]{1,0:T(8,128)} %get-tuple-element.62.refs_3_), custom_call_target="tpu_custom_call" | custom-call | tf_op jit(solution)/shard_map/pallas_call | solution.py:81
  155.1 6.5 %shard_map.93 = (f32[5,4,48,384]{3,2,1,0:T(8,128)}, f32[20,384]{1,0:T(8,128)}, f32[20,384]{1,0:T(8,128)}, f32[20,48]{1,0:T(8,128)}, f32[20,48]{1,0:T(8,128)}) custom-call(f32[5,4,48,384]{3,2,1,0:T(8,128)} %get-tuple-element.58.refs_0_, f32[2,4,48,384]{3,2,1,0:T(8,128)} %refs_1_.7, f32[4,48,384]{2,1,0:T(8,128)} %refs_2_.7, ...), custom_call_target="tpu_custom_call" | custom-call | tf_op jit(solution)/shard_map/pallas_call | solution.py:414
  161.6 2.2 fusion.9
  163.8 0.9 convolution_multiply_fusion
  164.8 21.2 %shard_map.94 = f32[8,20,16,128]{3,2,1,0:T(8,128)S(1)} custom-call(f32[20,16,128]{2,1,0:T(8,128)} %bitcast.67), custom_call_target="tpu_custom_call" | custom-call | tf_op jit(solution)/shard_map/pallas_call | solution.py:316
  186.0 49.0 %conditional.3 = (f32[5,960,128]{2,1,0:T(8,128)S(1)}) conditional(s32[]{:T(128)} %clamp.12, (f32[20,8,16,128]{3,2,0,1:T(8,128)S(1)}, s32[]{:T(128)}, s32[]{:T(128)}, f32[]{:T(128)}, s32[]{:T(128)}, /*index=5*/s32[]{:T(128)}) %tuple.63, (f32[20,8,16,128]{3,2,0,1:T(8,128)S(1)}, s32[]{:T(128)}, s32[]{:T(128)}, f32[]{:T(128)}, s32[]{:T(128)}, ...), branch_computations={%region_4.5_spmd.clone, %region_5.6_spmd.clone} | conditional | flops 3 | bytes 4423730 | solution.py:552
  186.0 0.1 copy.17
  186.2 0.8 pad_dynamic-slice_fusion.1
  187.0 48.0 %branch_1_fun.3 = f32[5,960,128]{2,1,0:T(8,128)S(1)} custom-call(f32[1,960,128]{2,1,0:T(8,128)} %bitcast.66), custom_call_target="tpu_custom_call" | custom-call | tf_op jit(solution)/shard_map/cond/branch_1_fun/pallas_call | solution.py:266
  235.0 0.2 fusion.48
  235.2 0.0 copy-start
  235.4 1.2 copy-done
  236.6 1.6 dynamic-slice_select_fusion
  (18 shorter events, 0.3 us)
Async XLA Ops:
  79.9 46.8 %all-to-all-start = ((f32[5,4,8,18,130]{4,1,0,3,2:T(4,128)}), f32[5,4,8,18,130]{4,1,0,3,2:T(4,128)S(1)}, u32[]{:S(2)}, u32[]{:S(2)}) async-start(f32[5,4,8,18,130]{4,1,0,3,2:T(4,128)} %bitcast.55), calls=%async_computation | async-start | bytes 5898240 | tf_op jit(solution)/shard_map/all_to_all | solution.py:505
  235.2 1.4 copy-start

commit v17 on v16

--- a/solution.py
+++ b/solution.py
@@ -525,9 +525,8 @@
         fields_count, levels_count, row_devices * span_rows, coarse.shape[3]
     )
     total_span = row_devices * span_rows
-    gathered = jnp.pad(gathered, ((0, 0), (0, 0), (parent_rows, parent_rows), (0, 0)))
-    first = jnp.clip(parent_rows * row_rank - row_anchor, -parent_rows, total_span)
-    strip = lax.dynamic_slice_in_dim(gathered, first + parent_rows, parent_rows, axis=2)
+    picks = parent_rows * row_rank - row_anchor + jnp.arange(parent_rows, dtype=jnp.int32)
+    strip = jnp.take(gathered, jnp.clip(picks, 0, total_span - 1), axis=2, mode="clip")
 
     routes = []
     for extra in (1, 0):

time: 235 us -> 233 us (level); the launches traced: 238 us -> 231 us
  Pallas kernels: 169 us -> 163 us
  starting transfers between devices: 9.68 us -> 6.91 us
    pallas_call x2, Pallas kernels: 77.1 us -> 67 us  [exchange(): pl.pallas_call(lambda *refs: exchange_kernel(axis, remote, local, *refs),...]
    pallas_call x4, Pallas kernels: 46.2 us -> 51.5 us  [neighbours(): pl.pallas_call(lambda *refs: halo_kernel(rows, cols, *refs), out_shape=tu...]
    all_to_all x1, starting transfers between devices: 9.68 us -> 6.91 us  [per_device(): lax.all_to_all(stacked, 'gx', split_axis=2, concat_axis=2, tiled=True)]
  transfers between devices with their start and end apart: 1 -> 1, of which waited for: 0 -> 0; matrix products, arithmetic and copies ran while one was open for 3% -> 3% of each run, Pallas kernels for 12% -> 13%
where the time goes in v17:
time: 233 us; the launch traced here: 231 us
  Pallas kernels  163 us (70%)
  local copies, waits for them, and re-layouts  40.8 us (18%)
  between operations  7.81 us (3%)
  matrix products  6.98 us (3%)
  starting transfers between devices  6.91 us (3%)
  other arithmetic  4.65 us (2%)
    pallas_call x2, Pallas kernels, exchange(): pl.pallas_call(lambda *refs: exchange_kernel(axis, remote, local, *refs),...  67 us
    pallas_call x4, Pallas kernels, neighbours(): pl.pallas_call(lambda *refs: halo_kernel(rows, cols, *refs), out_shape=tu...  51.5 us
    pallas_call x4, Pallas kernels, stencil(): pl.pallas_call(lambda *refs: stencil_kernel(relaxed, *refs), out_shape=ou...  25 us
    pallas_call x1, Pallas kernels, gather(): pl.pallas_call(lambda *refs: gather_kernel(axis, count, *refs), out_shape...  19.8 us
    another operation x6, local copies, waits for them, and re-layouts, per_device(): stacked_pieces = jnp.stack(pieces)  8.57 us
    all_to_all x1, starting transfers between devices, per_device(): lax.all_to_all(stacked, 'gx', split_axis=2, concat_axis=2, tiled=True)  6.91 us
    unnamed x10, local copies, waits for them, and re-layouts  5.56 us
    dynamic_slice x1, local copies, waits for them, and re-layouts, per_device(): piece = lax.dynamic_slice_in_dim(wide, start, relay_columns, axis=3)  5.19 us
  transfers between devices with their start and end apart: 1, of which 0 were waited for; matrix products, arithmetic and copies ran while one was open for 3% of the time, Pallas kernels for 13%

profile of v17, /device:TPU:73, one launch (start us, length us, event | category | flops | bytes accessed | tf_op | source)
XLA Modules:
  0.0 231.4 jit_solution(10521640878007167669)
XLA Ops:
  0.6 1.7 slice_reduce_fusion
  2.3 1.2 slice_reduce_fusion.4
  3.5 1.3 fusion.51
  11.7 0.1 iota_add_fusion
  11.8 0.1 reshape.255
  11.9 0.6 reshape_squeeze.31.refs_3_
  12.5 0.6 reshape_squeeze.30.refs_2_
  13.1 0.6 reshape_squeeze.29.refs_1_
  13.8 0.6 reshape_squeeze.28.refs_0_
  14.4 6.5 %shard_map.87 = (f32[20,384]{1,0:T(8,128)}, f32[20,384]{1,0:T(8,128)}, f32[20,48]{1,0:T(8,128)}, f32[20,48]{1,0:T(8,128)}) custom-call(f32[20,384]{1,0:T(8,128)} %reshape_squeeze.28.refs_0_, f32[20,384]{1,0:T(8,128)} %reshape_squeeze.29.refs_1_, f32[20,48]{1,0:T(8,128)} %reshape_squeeze.30.refs_2_, f32[20,48]{1,0:T(8,128)} %reshape_squeeze.31.refs_3_), custom_call_target="tpu_custom_call" | custom-call | tf_op jit(solution)/shard_map/pallas_call | solution.py:81
  20.9 5.4 %shard_map.88 = f32[5,4,48,384]{3,2,1,0:T(8,128)} custom-call(f32[5,4,48,384]{3,2,1,0:T(8,128)} %refs_0_.5, f32[2,4,48,384]{3,2,1,0:T(8,128)} %refs_1_.4, f32[4,48,384]{2,1,0:T(8,128)} %refs_2_.4, f32[20,384]{1,0:T(8,128)} %get-tuple-element.45.refs_3_, f32[20,384]{1,0:T(8,128)} %get-tuple-element.46.refs_4_, f32[20,48]{1,0:T(8,128)} %get-tuple-element.47.refs_5_, ...), custom_call_target="tpu_custom_call" | custom-call | tf_op jit(solution)/shard_map/pallas_call | solution.py:414
  26.3 5.2 %pad_dynamic-slice_fusion = (f32[5,4,48,130]{3,2,1,0:T(8,128)}, f32[5,4,48,130]{3,2,1,0:T(8,128)}, f32[5,4,48,130]{3,2,1,0:T(8,128)S(1)}, f32[5,4,48,130]{3,2,1,0:T(8,128)S(1)}, f32[5,4,48,130]{3,2,1,0:T(8,128)S(1)}) fusion(s32[]{:T(128)S(6)} %select_n.179, f32[5,4,48,384]{3,2,1,0:T(8,128)} %shard_map.88, s32[]{:T(128)S(6)} %select_n.176, s32[]{:T(128)S(6)} %select_n.177, ...), kind=kLoop, calls=%fused_computation.9 | loop fusion | bytes 3970580 | tf_op jit(solution)/shard_map/dynamic_slice | solution.py:478
  31.5 1.8 stack_reshape.19
  33.3 2.6 %stack_reshape.16 = f32[1,975,128]{2,1,0:T(8,128)} reshape(f32[5,4,48,130]{3,2,1,0:T(8,128)} %get-tuple-element.158) | data formatting | bytes 998400 | tf_op jit(solution)/shard_map/stack;reshape | solution.py:481
  35.9 1.4 stack_reshape.17
  37.3 1.4 stack_reshape.18
  38.7 1.4 stack_reshape.15
  40.1 1.1 constant_dynamic-update-slice_fusion.4
  41.1 1.1 constant_dynamic-update-slice_fusion.3
  42.2 1.1 constant_dynamic-update-slice_fusion.2
  43.3 1.1 constant_dynamic-update-slice_fusion.1
  44.4 21.8 %conditional.2 = (f32[2,975,128]{2,1,0:T(8,128)S(1)}) conditional(s32[]{:T(128)} %clamp.21, f32[5,975,128]{2,1,0:T(8,128)S(1)} %constant_dynamic-update-slice_fusion, f32[5,975,128]{2,1,0:T(8,128)S(1)} %constant_dynamic-update-slice_fusion, f32[5,975,128]{2,1,0:T(8,128)S(1)} %constant_dynamic-update-slice_fusion), branch_computations={%region_0.1_spmd, %region_1.2_spmd, %region_2.3_spmd} | conditional | bytes 8 | solution.py:495
  44.4 21.6 %branch_0_fun.2 = f32[2,975,128]{2,1,0:T(8,128)S(1)} custom-call(f32[5,975,128]{2,1,0:T(8,128)S(1)} %refs_0_.2), custom_call_target="tpu_custom_call" | custom-call | tf_op jit(solution)/shard_map/cond/branch_0_fun/pallas_call | solution.py:266
  66.2 0.1 slice_add_fusion
  66.2 1.2 add.310
  67.5 0.6 copy.27
  68.1 0.3 pad.9
  68.4 4.3 %gather_fusion.2 = f32[144,5,4,130]{3,2,1,0:T(4,128)} fusion(f32[5,4,84,130]{3,1,2,0:T(4,128)S(1)} %pad.9, s32[1024]{0:T(1024)S(1)} %pad_clamp_fusion.2), kind=kCustom, calls=%fused_computation.2 | custom fusion | bytes 2995776 | tf_op jit(solution)/shard_map/jit(_take)/gather | solution.py:504
  72.7 6.9 %all-to-all-start = ((f32[5,4,8,18,130]{4,1,0,3,2:T(4,128)}), f32[5,4,8,18,130]{4,1,0,3,2:T(4,128)S(1)}, u32[]{:S(2)}, u32[]{:S(2)}) async-start(f32[5,4,8,18,130]{4,1,0,3,2:T(4,128)} %bitcast.61), calls=%async_computation | async-start | bytes 5898240 | tf_op jit(solution)/shard_map/all_to_all | solution.py:505
  79.6 0.6 compare_and_fusion
  80.3 1.7 slice_reduce_fusion.2
  81.9 1.2 slice_reduce_fusion.6
  83.2 0.6 reshape_squeeze.27.refs_3_
  83.8 0.6 reshape_squeeze.26.refs_2_
  84.4 0.6 reshape_squeeze.25.refs_1_
  85.0 0.6 reshape_squeeze.24.refs_0_
  85.6 29.5 %shard_map.86 = (f32[20,384]{1,0:T(8,128)}, f32[20,384]{1,0:T(8,128)}, f32[20,48]{1,0:T(8,128)}, f32[20,48]{1,0:T(8,128)}) custom-call(f32[20,384]{1,0:T(8,128)} %reshape_squeeze.24.refs_0_, f32[20,384]{1,0:T(8,128)} %reshape_squeeze.25.refs_1_, f32[20,48]{1,0:T(8,128)} %reshape_squeeze.26.refs_2_, f32[20,48]{1,0:T(8,128)} %reshape_squeeze.27.refs_3_), custom_call_target="tpu_custom_call" | custom-call | tf_op jit(solution)/shard_map/pallas_call | solution.py:81
  115.2 0.6 fusion.45
  115.9 0.1 broadcast_and_fusion
  116.0 0.7 multiply_add_fusion.refs_8_
  116.7 0.0 all-to-all-done
  116.7 0.7 reduce_sum.9
  117.5 1.0 convolution_bitcast_fusion
  118.4 2.9 %fusion.3.refs_7_ = f32[5,4,48,384]{3,2,1,0:T(8,128)} fusion(f32[5,4,48,130]{3,2,1,0:T(8,128)S(1)} %convolution_bitcast_fusion, f32[384]{0:T(512)S(1)} %get-tuple-element.164, s32[384]{0:T(512)S(1)} %get-tuple-element.170, f32[384]{0:T(512)S(1)} %get-tuple-element.165, s32[384]{0:T(512)S(1)} %add_select_fusion, f32[384]{0:T(512)S(1)} %compare_select_fusion.2, ...), kind=kOutput, calls=%fused_computation.26 | convolution fusion | flops 575477760 | bytes 1982976 | tf_op jit(solution)/shard_map/flac,bc->flab/dot_general | solution.py:151
  121.3 6.5 %shard_map.89 = (f32[5,4,48,384]{3,2,1,0:T(8,128)}, f32[20,384]{1,0:T(8,128)}, f32[20,384]{1,0:T(8,128)}, f32[20,48]{1,0:T(8,128)}, f32[20,48]{1,0:T(8,128)}) custom-call(f32[5,4,48,384]{3,2,1,0:T(8,128)} %refs_0_.6, f32[2,4,48,384]{3,2,1,0:T(8,128)} %refs_1_.7, f32[4,48,384]{2,1,0:T(8,128)} %refs_2_.7, f32[20,384]{1,0:T(8,128)} %get-tuple-element.41.refs_3_, ...), custom_call_target="tpu_custom_call" | custom-call | tf_op jit(solution)/shard_map/pallas_call | solution.py:414
  127.8 8.2 %shard_map.90 = (f32[20,384]{1,0:T(8,128)}, f32[20,384]{1,0:T(8,128)}, f32[20,48]{1,0:T(8,128)}, f32[20,48]{1,0:T(8,128)}) custom-call(f32[20,384]{1,0:T(8,128)} %get-tuple-element.50.refs_0_, f32[20,384]{1,0:T(8,128)} %get-tuple-element.51.refs_1_, f32[20,48]{1,0:T(8,128)} %get-tuple-element.52.refs_2_, f32[20,48]{1,0:T(8,128)} %get-tuple-element.53.refs_3_), custom_call_target="tpu_custom_call" | custom-call | tf_op jit(solution)/shard_map/pallas_call | solution.py:81
  136.0 6.5 %shard_map.91 = (f32[5,4,48,384]{3,2,1,0:T(8,128)}, f32[20,384]{1,0:T(8,128)}, f32[20,384]{1,0:T(8,128)}, f32[20,48]{1,0:T(8,128)}, f32[20,48]{1,0:T(8,128)}) custom-call(f32[5,4,48,384]{3,2,1,0:T(8,128)} %get-tuple-element.49.refs_0_, f32[2,4,48,384]{3,2,1,0:T(8,128)} %refs_1_.7, f32[4,48,384]{2,1,0:T(8,128)} %refs_2_.7, ...), custom_call_target="tpu_custom_call" | custom-call | tf_op jit(solution)/shard_map/pallas_call | solution.py:414
  142.5 7.4 %shard_map.92 = (f32[20,384]{1,0:T(8,128)}, f32[20,384]{1,0:T(8,128)}, f32[20,48]{1,0:T(8,128)}, f32[20,48]{1,0:T(8,128)}) custom-call(f32[20,384]{1,0:T(8,128)} %get-tuple-element.59.refs_0_, f32[20,384]{1,0:T(8,128)} %get-tuple-element.60.refs_1_, f32[20,48]{1,0:T(8,128)} %get-tuple-element.61.refs_2_, f32[20,48]{1,0:T(8,128)} %get-tuple-element.62.refs_3_), custom_call_target="tpu_custom_call" | custom-call | tf_op jit(solution)/shard_map/pallas_call | solution.py:81
  149.9 6.5 %shard_map.93 = (f32[5,4,48,384]{3,2,1,0:T(8,128)}, f32[20,384]{1,0:T(8,128)}, f32[20,384]{1,0:T(8,128)}, f32[20,48]{1,0:T(8,128)}, f32[20,48]{1,0:T(8,128)}) custom-call(f32[5,4,48,384]{3,2,1,0:T(8,128)} %get-tuple-element.58.refs_0_, f32[2,4,48,384]{3,2,1,0:T(8,128)} %refs_1_.7, f32[4,48,384]{2,1,0:T(8,128)} %refs_2_.7, ...), custom_call_target="tpu_custom_call" | custom-call | tf_op jit(solution)/shard_map/pallas_call | solution.py:414
  156.4 2.2 fusion.11
  158.6 0.9 convolution_multiply_fusion
  159.6 19.8 %shard_map.94 = f32[8,20,16,128]{3,2,1,0:T(8,128)S(1)} custom-call(f32[20,16,128]{2,1,0:T(8,128)} %bitcast.75), custom_call_target="tpu_custom_call" | custom-call | tf_op jit(solution)/shard_map/pallas_call | solution.py:316
  179.4 48.9 %conditional.3 = (f32[5,960,128]{2,1,0:T(8,128)S(1)}) conditional(s32[]{:T(128)} %clamp.20, (f32[20,8,16,128]{3,2,0,1:T(8,128)S(1)}, s32[]{:T(128)}, s32[]{:T(128)}, s32[]{:T(128)}, s32[48,1]{0,1:T(1,128)S(1)}, /*index=5*/s32[]{:T(128)}) %tuple.62, (f32[20,8,16,128]{3,2,0,1:T(8,128)S(1)}, s32[]{:T(128)}, s32[]{:T(128)}, s32[]{:T(128)}, ...), branch_computations={%region_4.5_spmd, %region_5.6_spmd} | conditional | flops 1121 | bytes 7213856 | solution.py:551
  180.1 0.1 copy.29
  180.2 0.8 copy.23
  181.1 0.9 gather_fusion
  182.0 0.8 copy.24
  182.8 45.5 %branch_0_fun.3 = f32[5,960,128]{2,1,0:T(8,128)S(1)} custom-call(f32[1,960,128]{2,1,0:T(8,128)} %bitcast.73), custom_call_target="tpu_custom_call" | custom-call | tf_op jit(solution)/shard_map/cond/branch_0_fun/pallas_call | solution.py:266
  228.3 0.2 fusion.50
  228.4 0.0 copy-start
  228.7 1.2 copy-done
  229.8 1.6 dynamic-slice_select_fusion
  (21 shorter events, 0.3 us)
Async XLA Ops:
  72.7 44.0 %all-to-all-start = ((f32[5,4,8,18,130]{4,1,0,3,2:T(4,128)}), f32[5,4,8,18,130]{4,1,0,3,2:T(4,128)S(1)}, u32[]{:S(2)}, u32[]{:S(2)}) async-start(f32[5,4,8,18,130]{4,1,0,3,2:T(4,128)} %bitcast.61), calls=%async_computation | async-start | bytes 5898240 | tf_op jit(solution)/shard_map/all_to_all | solution.py:505
  228.4 1.4 copy-start

commit v18 on v16

--- a/solution.py
+++ b/solution.py
@@ -147,8 +147,8 @@
     exact = lax.Precision.HIGHEST
     rows = block.shape[2] - 2
     cols = block.shape[3] - 2
-    down = jnp.einsum("ar,flrc->flac", refining(rows), block, precision=exact)
-    return jnp.einsum("flac,bc->flab", down, refining(cols), precision=exact)
+    across = jnp.einsum("flrc,bc->flrb", block, refining(cols), precision=exact)
+    return jnp.einsum("ar,flrb->flab", refining(rows), across, precision=exact)
 
 
 def grouping(count):

time: 235 us -> 230 us (0.979); the launches traced: 238 us -> 229 us
  Pallas kernels: 169 us -> 163 us
  starting transfers between devices: 9.68 us -> 6.91 us
    pallas_call x2, Pallas kernels: 77.1 us -> 67 us  [exchange(): pl.pallas_call(lambda *refs: exchange_kernel(axis, remote, local, *refs),...]
    pallas_call x4, Pallas kernels: 46.2 us -> 51 us  [neighbours(): pl.pallas_call(lambda *refs: halo_kernel(rows, cols, *refs), out_shape=tu...]
    all_to_all x1, starting transfers between devices: 9.68 us -> 6.91 us  [per_device(): lax.all_to_all(stacked, 'gx', split_axis=2, concat_axis=2, tiled=True)]
  transfers between devices with their start and end apart: 1 -> 1, of which waited for: 0 -> 0; matrix products, arithmetic and copies ran while one was open for 3% -> 3% of each run, Pallas kernels for 12% -> 13%
where the time goes in v18:
time: 230 us; the launch traced here: 229 us
  Pallas kernels  163 us (71%)
  local copies, waits for them, and re-layouts  39.1 us (17%)
  between operations  8.31 us (4%)
  starting transfers between devices  6.91 us (3%)
  matrix products  6.61 us (3%)
  other arithmetic  4.57 us (2%)
    pallas_call x2, Pallas kernels, exchange(): pl.pallas_call(lambda *refs: exchange_kernel(axis, remote, local, *refs),...  67 us
    pallas_call x4, Pallas kernels, neighbours(): pl.pallas_call(lambda *refs: halo_kernel(rows, cols, *refs), out_shape=tu...  51 us
    pallas_call x4, Pallas kernels, stencil(): pl.pallas_call(lambda *refs: stencil_kernel(relaxed, *refs), out_shape=ou...  25 us
    pallas_call x1, Pallas kernels, gather(): pl.pallas_call(lambda *refs: gather_kernel(axis, count, *refs), out_shape...  19.8 us
    another operation x6, local copies, waits for them, and re-layouts, per_device(): stacked_pieces = jnp.stack(pieces)  8.57 us
    all_to_all x1, starting transfers between devices, per_device(): lax.all_to_all(stacked, 'gx', split_axis=2, concat_axis=2, tiled=True)  6.91 us
    unnamed x10, local copies, waits for them, and re-layouts  5.56 us
    dynamic_slice x1, local copies, waits for them, and re-layouts, per_device(): piece = lax.dynamic_slice_in_dim(wide, start, relay_columns, axis=3)  5.19 us
  transfers between devices with their start and end apart: 1, of which 0 were waited for; matrix products, arithmetic and copies ran while one was open for 3% of the time, Pallas kernels for 13%

profile of v18, /device:TPU:73, one launch (start us, length us, event | category | flops | bytes accessed | tf_op | source)
XLA Modules:
  0.0 228.6 jit_solution(4195565912945016903)
XLA Ops:
  0.6 1.7 slice_reduce_fusion
  2.3 1.2 slice_reduce_fusion.4
  3.5 1.3 fusion.49
  11.7 0.1 iota_add_fusion
  11.7 0.1 reshape.231
  11.8 0.6 reshape_squeeze.31.refs_3_
  12.5 0.6 reshape_squeeze.30.refs_2_
  13.1 0.6 reshape_squeeze.29.refs_1_
  13.7 0.6 reshape_squeeze.28.refs_0_
  14.3 6.5 %shard_map.87 = (f32[20,384]{1,0:T(8,128)}, f32[20,384]{1,0:T(8,128)}, f32[20,48]{1,0:T(8,128)}, f32[20,48]{1,0:T(8,128)}) custom-call(f32[20,384]{1,0:T(8,128)} %reshape_squeeze.28.refs_0_, f32[20,384]{1,0:T(8,128)} %reshape_squeeze.29.refs_1_, f32[20,48]{1,0:T(8,128)} %reshape_squeeze.30.refs_2_, f32[20,48]{1,0:T(8,128)} %reshape_squeeze.31.refs_3_), custom_call_target="tpu_custom_call" | custom-call | tf_op jit(solution)/shard_map/pallas_call | solution.py:81
  20.8 5.4 %shard_map.88 = f32[5,4,48,384]{3,2,1,0:T(8,128)} custom-call(f32[5,4,48,384]{3,2,1,0:T(8,128)} %refs_0_.5, f32[2,4,48,384]{3,2,1,0:T(8,128)} %refs_1_.4, f32[4,48,384]{2,1,0:T(8,128)} %refs_2_.4, f32[20,384]{1,0:T(8,128)} %get-tuple-element.45.refs_3_, f32[20,384]{1,0:T(8,128)} %get-tuple-element.46.refs_4_, f32[20,48]{1,0:T(8,128)} %get-tuple-element.47.refs_5_, ...), custom_call_target="tpu_custom_call" | custom-call | tf_op jit(solution)/shard_map/pallas_call | solution.py:414
  26.3 5.2 %pad_dynamic-slice_fusion.2 = (f32[5,4,48,130]{3,2,1,0:T(8,128)}, f32[5,4,48,130]{3,2,1,0:T(8,128)}, f32[5,4,48,130]{3,2,1,0:T(8,128)S(1)}, f32[5,4,48,130]{3,2,1,0:T(8,128)S(1)}, f32[5,4,48,130]{3,2,1,0:T(8,128)S(1)}) fusion(s32[]{:T(128)S(6)} %select_n.182, f32[5,4,48,384]{3,2,1,0:T(8,128)} %shard_map.88, s32[]{:T(128)S(6)} %select_n.179, ...), kind=kLoop, calls=%fused_computation.3 | loop fusion | bytes 3970580 | tf_op jit(solution)/shard_map/dynamic_slice | solution.py:478
  31.5 1.8 stack_reshape.19
  33.3 2.6 %stack_reshape.16 = f32[1,975,128]{2,1,0:T(8,128)} reshape(f32[5,4,48,130]{3,2,1,0:T(8,128)} %get-tuple-element.172) | data formatting | bytes 998400 | tf_op jit(solution)/shard_map/stack;reshape | solution.py:481
  35.8 1.4 stack_reshape.17
  37.2 1.4 stack_reshape.18
  38.6 1.4 stack_reshape.15
  40.0 1.1 constant_dynamic-update-slice_fusion.4
  41.1 1.1 constant_dynamic-update-slice_fusion.3
  42.1 1.1 constant_dynamic-update-slice_fusion.2
  43.2 1.1 constant_dynamic-update-slice_fusion.1
  44.3 21.8 %conditional.2 = (f32[2,975,128]{2,1,0:T(8,128)S(1)}) conditional(s32[]{:T(128)} %clamp.13, f32[5,975,128]{2,1,0:T(8,128)S(1)} %constant_dynamic-update-slice_fusion, f32[5,975,128]{2,1,0:T(8,128)S(1)} %constant_dynamic-update-slice_fusion, f32[5,975,128]{2,1,0:T(8,128)S(1)} %constant_dynamic-update-slice_fusion), branch_computations={%region_0.1_spmd, %region_1.2_spmd, %region_2.3_spmd} | conditional | bytes 8 | solution.py:495
  44.3 21.6 %branch_0_fun.2 = f32[2,975,128]{2,1,0:T(8,128)S(1)} custom-call(f32[5,975,128]{2,1,0:T(8,128)S(1)} %refs_0_.2), custom_call_target="tpu_custom_call" | custom-call | tf_op jit(solution)/shard_map/cond/branch_0_fun/pallas_call | solution.py:266
  66.1 0.1 slice_add_fusion
  66.2 1.2 add.307
  67.4 0.6 copy.14
  68.0 0.3 pad.13
  68.3 4.3 %gather_fusion = f32[144,5,4,130]{3,2,1,0:T(4,128)} fusion(f32[5,4,84,130]{3,1,2,0:T(4,128)S(1)} %pad.13, s32[1024]{0:T(1024)S(1)} %pad_clamp_fusion), kind=kCustom, calls=%fused_computation | custom fusion | bytes 2995776 | tf_op jit(solution)/shard_map/jit(_take)/gather | solution.py:504
  72.6 6.9 %all-to-all-start = ((f32[5,4,8,18,130]{4,1,0,3,2:T(4,128)}), f32[5,4,8,18,130]{4,1,0,3,2:T(4,128)S(1)}, u32[]{:S(2)}, u32[]{:S(2)}) async-start(f32[5,4,8,18,130]{4,1,0,3,2:T(4,128)} %bitcast.55), calls=%async_computation | async-start | bytes 5898240 | tf_op jit(solution)/shard_map/all_to_all | solution.py:505
  80.1 0.6 compare_and_fusion
  80.7 1.7 slice_reduce_fusion.2
  82.4 1.2 slice_reduce_fusion.6
  83.6 0.6 reshape_squeeze.27.refs_3_
  84.2 0.6 reshape_squeeze.26.refs_2_
  84.8 0.6 reshape_squeeze.25.refs_1_
  85.5 0.6 reshape_squeeze.24.refs_0_
  86.1 29.0 %shard_map.86 = (f32[20,384]{1,0:T(8,128)}, f32[20,384]{1,0:T(8,128)}, f32[20,48]{1,0:T(8,128)}, f32[20,48]{1,0:T(8,128)}) custom-call(f32[20,384]{1,0:T(8,128)} %reshape_squeeze.24.refs_0_, f32[20,384]{1,0:T(8,128)} %reshape_squeeze.25.refs_1_, f32[20,48]{1,0:T(8,128)} %reshape_squeeze.26.refs_2_, f32[20,48]{1,0:T(8,128)} %reshape_squeeze.27.refs_3_), custom_call_target="tpu_custom_call" | custom-call | tf_op jit(solution)/shard_map/pallas_call | solution.py:81
  115.1 0.6 fusion.43
  115.8 0.1 broadcast_and_fusion
  115.9 0.7 multiply_add_fusion.refs_8_
  116.6 0.0 all-to-all-done
  116.6 0.7 reduce_sum.9
  117.4 1.0 fusion
  118.4 2.5 %convolution_bitcast_fusion.refs_7_ = f32[5,4,48,384]{3,2,1,0:T(8,128)} fusion(f32[5,4,18,384]{3,2,1,0:T(8,128)S(1)} %fusion, f32[48]{0:T(128)S(1)} %get-tuple-element.180, s32[48]{0:T(128)S(1)} %get-tuple-element.183, f32[48]{0:T(128)S(1)} %get-tuple-element.181, s32[48]{0:T(128)S(1)} %get-tuple-element.182, f32[48]{0:T(128)S(1)} %compare_select_fusion.2, ...), kind=kOutput, calls=%fused_computation.9 | convolution fusion | flops 79633152 | bytes 2028672 | tf_op jit(solution)/shard_map/ar,flrb->flab/dot_general | solution.py:151
  120.9 6.5 %shard_map.89 = (f32[5,4,48,384]{3,2,1,0:T(8,128)}, f32[20,384]{1,0:T(8,128)}, f32[20,384]{1,0:T(8,128)}, f32[20,48]{1,0:T(8,128)}, f32[20,48]{1,0:T(8,128)}) custom-call(f32[5,4,48,384]{3,2,1,0:T(8,128)} %refs_0_.6, f32[2,4,48,384]{3,2,1,0:T(8,128)} %refs_1_.7, f32[4,48,384]{2,1,0:T(8,128)} %refs_2_.7, f32[20,384]{1,0:T(8,128)} %get-tuple-element.41.refs_3_, ...), custom_call_target="tpu_custom_call" | custom-call | tf_op jit(solution)/shard_map/pallas_call | solution.py:414
  127.4 8.2 %shard_map.90 = (f32[20,384]{1,0:T(8,128)}, f32[20,384]{1,0:T(8,128)}, f32[20,48]{1,0:T(8,128)}, f32[20,48]{1,0:T(8,128)}) custom-call(f32[20,384]{1,0:T(8,128)} %get-tuple-element.50.refs_0_, f32[20,384]{1,0:T(8,128)} %get-tuple-element.51.refs_1_, f32[20,48]{1,0:T(8,128)} %get-tuple-element.52.refs_2_, f32[20,48]{1,0:T(8,128)} %get-tuple-element.53.refs_3_), custom_call_target="tpu_custom_call" | custom-call | tf_op jit(solution)/shard_map/pallas_call | solution.py:81
  135.6 6.5 %shard_map.91 = (f32[5,4,48,384]{3,2,1,0:T(8,128)}, f32[20,384]{1,0:T(8,128)}, f32[20,384]{1,0:T(8,128)}, f32[20,48]{1,0:T(8,128)}, f32[20,48]{1,0:T(8,128)}) custom-call(f32[5,4,48,384]{3,2,1,0:T(8,128)} %get-tuple-element.49.refs_0_, f32[2,4,48,384]{3,2,1,0:T(8,128)} %refs_1_.7, f32[4,48,384]{2,1,0:T(8,128)} %refs_2_.7, ...), custom_call_target="tpu_custom_call" | custom-call | tf_op jit(solution)/shard_map/pallas_call | solution.py:414
  142.1 7.4 %shard_map.92 = (f32[20,384]{1,0:T(8,128)}, f32[20,384]{1,0:T(8,128)}, f32[20,48]{1,0:T(8,128)}, f32[20,48]{1,0:T(8,128)}) custom-call(f32[20,384]{1,0:T(8,128)} %get-tuple-element.59.refs_0_, f32[20,384]{1,0:T(8,128)} %get-tuple-element.60.refs_1_, f32[20,48]{1,0:T(8,128)} %get-tuple-element.61.refs_2_, f32[20,48]{1,0:T(8,128)} %get-tuple-element.62.refs_3_), custom_call_target="tpu_custom_call" | custom-call | tf_op jit(solution)/shard_map/pallas_call | solution.py:81
  149.5 6.5 %shard_map.93 = (f32[5,4,48,384]{3,2,1,0:T(8,128)}, f32[20,384]{1,0:T(8,128)}, f32[20,384]{1,0:T(8,128)}, f32[20,48]{1,0:T(8,128)}, f32[20,48]{1,0:T(8,128)}) custom-call(f32[5,4,48,384]{3,2,1,0:T(8,128)} %get-tuple-element.58.refs_0_, f32[2,4,48,384]{3,2,1,0:T(8,128)} %refs_1_.7, f32[4,48,384]{2,1,0:T(8,128)} %refs_2_.7, ...), custom_call_target="tpu_custom_call" | custom-call | tf_op jit(solution)/shard_map/pallas_call | solution.py:414
  156.0 2.2 fusion.9
  158.2 0.9 convolution_multiply_fusion
  159.1 19.8 %shard_map.94 = f32[8,20,16,128]{3,2,1,0:T(8,128)S(1)} custom-call(f32[20,16,128]{2,1,0:T(8,128)} %bitcast.67), custom_call_target="tpu_custom_call" | custom-call | tf_op jit(solution)/shard_map/pallas_call | solution.py:316
  179.0 46.5 %conditional.3 = (f32[5,960,128]{2,1,0:T(8,128)S(1)}) conditional(s32[]{:T(128)} %clamp.12, (f32[20,8,16,128]{3,2,0,1:T(8,128)S(1)}, s32[]{:T(128)}, s32[]{:T(128)}, f32[]{:T(128)}, s32[]{:T(128)}, /*index=5*/s32[]{:T(128)}) %tuple.63, (f32[20,8,16,128]{3,2,0,1:T(8,128)S(1)}, s32[]{:T(128)}, s32[]{:T(128)}, f32[]{:T(128)}, s32[]{:T(128)}, ...), branch_computations={%region_4.5_spmd.clone, %region_5.6_spmd.clone} | conditional | flops 3 | bytes 4423730 | solution.py:552
  179.0 0.1 copy.16
  179.1 0.8 pad_dynamic-slice_fusion
  180.0 45.4 %branch_0_fun.3 = f32[5,960,128]{2,1,0:T(8,128)S(1)} custom-call(f32[1,960,128]{2,1,0:T(8,128)} %bitcast.65), custom_call_target="tpu_custom_call" | custom-call | tf_op jit(solution)/shard_map/cond/branch_0_fun/pallas_call | solution.py:266
  225.4 0.2 fusion.48
  225.6 0.0 copy-start
  225.8 1.2 copy-done
  227.0 1.6 dynamic-slice_select_fusion
  (18 shorter events, 0.3 us)
Async XLA Ops:
  72.6 44.0 %all-to-all-start = ((f32[5,4,8,18,130]{4,1,0,3,2:T(4,128)}), f32[5,4,8,18,130]{4,1,0,3,2:T(4,128)S(1)}, u32[]{:S(2)}, u32[]{:S(2)}) async-start(f32[5,4,8,18,130]{4,1,0,3,2:T(4,128)} %bitcast.55), calls=%async_computation | async-start | bytes 5898240 | tf_op jit(solution)/shard_map/all_to_all | solution.py:505
  225.6 1.4 copy-start
